TPU v7x, 32 devices: a whole 2x2x4 slice. The times are simulated.
32 devices in a mesh: ctx: 8 (over y, x, core), ch: 4 (over z).
Axes of the slice: x: 2, y: 2, z: 4, core: 2. Of those that a mesh axis runs over, the one named last changes fastest.
Arguments:
- query: bfloat16 [8192, 4096], P(('ctx', 'ch')), may hold values from -6 to 6
- key_in: bfloat16 [8192, 4096], P(('ctx', 'ch')), may hold values from -6 to 6
- value: bfloat16 [8192, 4096], P(('ctx', 'ch')), may hold values from -6 to 6
- residues: float32 [4096, 16], P('ch'), may hold values from -0.05 to 0.05
- decay_rates: float32 [4096, 16], P('ch'), may hold values from 2e-05 to 0.03
- skip_gain: float32 [4096], P('ch'), may hold values from 0.5 to 1.5
Outputs:
- output: bfloat16 [8192, 4096], P(('ctx', 'ch'))
All inputs are finite; a program needn't handle non-finite values.
Results may differ from a plain program's by a relative error of at most 0.0056.
Values may be sent and summed in bfloat16 or wider, within the bound.
No kernel may reach another device: no remote copies, remote signals or barrier semaphores. Data moves between devices by JAX's collectives and lax.ppermute only.
A program may use at most 192 MiB of HBM per device.

v0:
```python
import math

import jax
import jax.numpy as jnp
from jax import lax
from jax.sharding import PartitionSpec as P

FILTER_PARTS = 4


HIGHEST = lax.Precision.HIGHEST


def from_behind(value, axis, steps):
    count = lax.axis_size(axis)
    initial, last = (max(0, -steps), min(count, count - steps))
    return lax.ppermute(value, axis, [(source, source + steps) for source in range(initial, last)])


def dft_table(rows_n, cols_n, modulus, angle_sign):
    row_ids = jnp.arange(rows_n, dtype=jnp.int32)[:, None]
    col_ids = jnp.arange(cols_n, dtype=jnp.int32)[None, :]
    phase = (row_ids * col_ids % modulus).astype(jnp.float32) * (
        angle_sign * 2.0 * math.pi / modulus
    )
    return (jnp.cos(phase), jnp.sin(phase))


def stacked_table(cos_tab, sin_tab):
    upper = jnp.stack([cos_tab, -sin_tab], 1)
    lower = jnp.stack([sin_tab, cos_tab], 1)
    return jnp.stack([upper, lower], 0)


def complex_dft(stacked, angle_sign):
    length = stacked.shape[1]
    channels = stacked.shape[2]
    rows_a = 2 ** ((length.bit_length() - 1) // 2)
    rows_b = length // rows_a
    outer_c, outer_s = dft_table(rows_b, rows_b, rows_b, angle_sign)
    twist_c, twist_s = dft_table(rows_b, rows_a, length, angle_sign)
    inner_c, inner_s = dft_table(rows_a, rows_a, rows_a, angle_sign)
    grid_in = stacked.reshape(2, rows_b, rows_a, channels)
    first = jnp.einsum(
        "qkpn,pnac->qkac", stacked_table(outer_c, outer_s), grid_in, precision=HIGHEST
    )
    twist_re = first[0] * twist_c[:, :, None] - first[1] * twist_s[:, :, None]
    twist_im = first[0] * twist_s[:, :, None] + first[1] * twist_c[:, :, None]
    twisted = jnp.stack([twist_re, twist_im])
    second = jnp.einsum(
        "qjpn,pknc->qjkc", stacked_table(inner_c, inner_s), twisted, precision=HIGHEST
    )
    return second.reshape(2, length, channels)


def half_turn(length, angle_sign):
    phase = jnp.arange(length).astype(jnp.float32)[:, None] * (angle_sign * math.pi / length)
    return (jnp.cos(phase), jnp.sin(phase))


def first_bin_of(length):
    return (jnp.arange(length) == 0)[:, None]


def real_forward(window):
    length = window.shape[0] // 2
    channels = window.shape[1]
    folded = window.reshape(length, 2, channels)
    spectrum = complex_dft(jnp.stack([folded[:, 0], folded[:, 1]]), -1.0)
    mirrored = jnp.roll(jnp.flip(spectrum, 1), 1, 1)
    even_part_real = (spectrum[0] + mirrored[0]) * 0.5
    even_part_imaginary = (spectrum[1] - mirrored[1]) * 0.5
    odd_re = (spectrum[1] + mirrored[1]) * 0.5
    odd_im = (mirrored[0] - spectrum[0]) * 0.5
    cos_k, sin_k = half_turn(length, -1.0)
    out_re = even_part_real + cos_k * odd_re - sin_k * odd_im
    out_im = even_part_imaginary + cos_k * odd_im + sin_k * odd_re
    highest_frequency_bin = even_part_real[0:1] - odd_re[0:1]
    out_im = jnp.where(first_bin_of(length), highest_frequency_bin, out_im)
    return jnp.stack([out_re, out_im])


def packed_product(left, right):
    leading_frequency_bin = first_bin_of(left.shape[1])
    prod_re = left[0] * right[0] - left[1] * right[1]
    prod_im = left[0] * right[1] + left[1] * right[0]
    prod_re = jnp.where(leading_frequency_bin, left[0] * right[0], prod_re)
    prod_im = jnp.where(leading_frequency_bin, left[1] * right[1], prod_im)
    return jnp.stack([prod_re, prod_im])


def real_inverse_tail(packed):
    length = packed.shape[1]
    channels = packed.shape[2]
    leading_frequency_bin = first_bin_of(length)
    highest_frequency_bin = packed[1, 0:1]
    output_real = packed[0]
    output_imaginary = jnp.where(leading_frequency_bin, 0.0, packed[1])
    reflected_real = jnp.where(
        leading_frequency_bin, highest_frequency_bin, jnp.roll(jnp.flip(output_real, 0), 1, 0)
    )
    reflected_imaginary = jnp.roll(jnp.flip(output_imaginary, 0), 1, 0)
    even_part_real = (output_real + reflected_real) * 0.5
    even_part_imaginary = (output_imaginary - reflected_imaginary) * 0.5
    difference_real = (output_real - reflected_real) * 0.5
    difference_imaginary = (output_imaginary + reflected_imaginary) * 0.5
    cos_k, sin_k = half_turn(length, 1.0)
    odd_re = difference_real * cos_k - difference_imaginary * sin_k
    odd_im = difference_real * sin_k + difference_imaginary * cos_k
    signal = complex_dft(
        jnp.stack([even_part_real - odd_im, even_part_imaginary + odd_re]), 1.0
    ) * (1.0 / length)
    return jnp.stack([signal[0], signal[1]], axis=1).reshape(2 * length, channels)[length:]


def filter_spectra(residues, decay_rates, length):
    bins = jnp.arange(length, dtype=jnp.int32)[:, None]
    theta = bins.astype(jnp.float32) * (math.pi / length)
    sin_t = jnp.sin(theta)
    half_sin = jnp.sin(theta * 0.5)
    even_bin = bins % 2 == 0
    leading = bins == 0
    spectra_list = []
    for part_index in range(FILTER_PARTS):
        sum_re = jnp.zeros((length, residues.shape[0]), jnp.float32)
        sum_im = jnp.zeros((length, residues.shape[0]), jnp.float32)
        sum_top = jnp.zeros((1, residues.shape[0]), jnp.float32)
        for mode in range(residues.shape[1]):
            rate = decay_rates[:, mode][None, :]
            weight = residues[:, mode][None, :] * jnp.exp(-rate * float(part_index * length))
            ratio = jnp.exp(-rate)
            tail_gap = -jnp.expm1(-rate * float(length))
            numer = jnp.where(even_bin, tail_gap, 2.0 - tail_gap)
            den_re = -jnp.expm1(-rate) + ratio * 2.0 * half_sin * half_sin
            den_im = ratio * sin_t
            scale_mod = weight * numer / (den_re * den_re + den_im * den_im)
            sum_re = sum_re + scale_mod * den_re
            sum_im = sum_im - scale_mod * den_im
            sum_top = sum_top + weight * tail_gap / (1.0 + ratio)
        sum_im = jnp.where(leading, sum_top, sum_im)
        spectra_list.append(jnp.stack([sum_re, sum_im]))
    return spectra_list


def local(query, key_in, value, residues, decay_rates, skip_gain):
    product = (query.astype(jnp.float32) * key_in.astype(jnp.float32)).astype(jnp.bfloat16)
    ctx_block = lax.all_to_all(product, "ch", split_axis=1, concat_axis=0, tiled=True)
    length = ctx_block.shape[0]
    filters = filter_spectra(residues, decay_rates, length)
    earlier = from_behind(ctx_block, "ctx", 1)
    own_spectrum = real_forward(jnp.concatenate([earlier, ctx_block], 0).astype(jnp.float32))
    summed = packed_product(filters[0], own_spectrum)
    moving = own_spectrum
    for step in range(1, FILTER_PARTS):
        moving = from_behind(moving, "ctx", 1)
        summed = summed + packed_product(filters[step], moving)
    convolved = real_inverse_tail(summed)
    mixed = (convolved + skip_gain[None, :] * ctx_block.astype(jnp.float32)).astype(jnp.bfloat16)
    gathered = lax.all_to_all(mixed, "ch", split_axis=0, concat_axis=1, tiled=True)
    return (value.astype(jnp.float32) * gathered.astype(jnp.float32)).astype(jnp.bfloat16)


def solution(mesh):
    return jax.shard_map(
        local,
        mesh=mesh,
        in_specs=(
            P(("ctx", "ch"), None),
            P(("ctx", "ch"), None),
            P(("ctx", "ch"), None),
            P("ch", None),
            P("ch", None),
            P("ch"),
        ),
        out_specs=P(("ctx", "ch"), None),
        check_vma=False,
    )
```

profile of v0, /device:TPU:3, one launch (start us, length us, event | category | flops | bytes accessed | tf_op | source)
XLA Modules:
  0.0 874.8 jit_solution(278917957827728307)
XLA Ops:
  10.8 4.6 all-to-all-start
  16.5 46.7 %all-to-all-done = bf16[256,4,1024]{0,2,1:T(8,128)(2,1)S(1)} async-done(((bf16[256,4,1024]{0,2,1:T(8,128)(2,1)}), bf16[256,4,1024]{0,2,1:T(8,128)(2,1)S(1)}, u32[]{:S(2)}, u32[]{:S(2)}) %all-to-all-start) | async-done | bytes 2097184 | tf_op jit(solution)/shard_map/all_to_all | solution.py:147
  70.8 22.7 %collective-permute-done = bf16[1024,1024]{1,0:T(8,128)(2,1)S(1)} collective-permute-done((bf16[1024,1024]{1,0:T(8,128)(2,1)}, bf16[1024,1024]{1,0:T(8,128)(2,1)S(1)}, u32[]{:S(2)}, u32[]{:S(2)}) %collective-permute-start) | collective-permute-done | bytes 2097184 | tf_op jit(solution)/shard_map/ppermute | solution.py:17
  93.5 6.0 maximum_convert_fusion
  99.5 10.6 %reshape.30706 = f32[1024,2,1024]{2,1,0:T(2,128)} reshape(f32[2048,1024]{1,0:T(8,128)} %maximum_convert_fusion) | data formatting | bytes 16777216 | tf_op jit(solution)/shard_map/convert_element_type | solution.py:151
  110.1 10.0 %fusion.228 = (f32[1024,1,1024]{2,1,0:T(1,128)S(1)}, f32[1024,1,1024]{2,1,0:T(1,128)S(1)}) fusion(f32[1024,2,1024]{2,1,0:T(2,128)} %reshape.30706), kind=kLoop, calls=%fused_computation.607 | loop fusion | bytes 16777216 | tf_op jit(solution)/shard_map/slice | solution.py:69
  126.9 8.7 fusion.178
  138.4 12.7 %fusion.174 = f32[2,32,32,1024]{3,1,2,0:T(8,128)S(1)} fusion(f32[2,32,32,1024]{3,1,2,0:T(8,128)S(1)} %pad_maximum_fusion, f32[1,32,2,32]{3,1,2,0:T(8,128)S(1)} %get-tuple-element.150, f32[1,32,2,32]{3,1,2,0:T(8,128)S(1)} %get-tuple-element.149), kind=kOutput, calls=%fused_computation.378 | convolution fusion | flops 1610616832 | bytes 16793600 | tf_op jit(solution)/shard_map/qjpn,pknc->qjkc/dot_general | solution.py:50
  151.1 4.9 copy.35
  164.5 66.3 %slice.370 = f32[2,1023,1024]{2,1,0:T(8,128)} reverse(f32[2,1023,1024]{2,1,0:T(8,128)} %slice.404), dimensions={1} | reverse | bytes 16760832 | tf_op jit(solution)/shard_map/jit(_roll_static)/slice | solution.py:70
  230.9 4.8 copy.34
  239.7 51.7 %subtract_select_fusion.3 = (f32[1,1024,1024]{2,1,0:T(8,128)}, f32[1,1024,1024]{2,1,0:T(8,128)S(1)}, f32[1,1024,1024]{2,1,0:T(8,128)}, f32[1,1024,1024]{2,1,0:T(8,128)S(1)}, f32[1,1024,1024]{2,1,0:T(8,128)}) fusion(pred[1024]{0:T(1024)(128)(4,1)S(1)} %get-tuple-element.160, f32[1024]{0:T(1024)S(1)} %get-tuple-element.161, ...), kind=kLoop, calls=%fused_computation.170 | loop fusion | flops 257949696 | bytes 42362880 | tf_op jit(solution)/shard_map/jit(_where)/select_n | solution.py:87
  294.8 5.2 collective-permute-start.1
  300.5 89.8 %collective-permute-done.1 = f32[2,1024,1024]{2,1,0:T(8,128)S(1)} collective-permute-done((f32[2,1024,1024]{2,1,0:T(8,128)S(1)}, f32[2,1024,1024]{2,1,0:T(8,128)S(1)}, u32[]{:S(2)}, u32[]{:S(2)}) %collective-permute-start.1) | collective-permute-done | bytes 8388640 | tf_op jit(solution)/shard_map/ppermute | solution.py:17
  390.4 5.3 collective-permute-start.2
  395.7 50.0 %subtract_select_fusion.2 = (f32[1,1024,1024]{2,1,0:T(8,128)}, f32[1,1024,1024]{2,1,0:T(8,128)}, f32[1,1024,1024]{2,1,0:T(8,128)}) fusion(f32[2,1024,1024]{2,1,0:T(8,128)S(1)} %collective-permute-done.1, pred[1024]{0:T(1024)(128)(4,1)S(1)} %get-tuple-element.160, f32[1024]{0:T(1024)S(1)} %bitcast.487, f32[1024]{0:T(1024)S(1)} %get-tuple-element.165, ...), kind=kLoop, calls=%fused_computation.169 | loop fusion | flops 239075328 | bytes 21379072 | tf_op jit(solution)/shard_map/jit(_where)/select_n | solution.py:87
  445.7 40.4 %collective-permute-done.2 = f32[2,1024,1024]{2,1,0:T(8,128)S(1)} collective-permute-done((f32[2,1024,1024]{2,1,0:T(8,128)S(1)}, f32[2,1024,1024]{2,1,0:T(8,128)S(1)}, u32[]{:S(2)}, u32[]{:S(2)}) %collective-permute-start.2) | collective-permute-done | bytes 8388640 | tf_op jit(solution)/shard_map/ppermute | solution.py:17
  486.0 5.3 collective-permute-start.3
  491.3 49.7 %subtract_select_fusion.1 = (f32[1,1024,1024]{2,1,0:T(8,128)}, f32[1,1024,1024]{2,1,0:T(8,128)}, f32[1,1024,1024]{2,1,0:T(8,128)}) fusion(f32[2,1024,1024]{2,1,0:T(8,128)S(1)} %collective-permute-done.2, pred[1024]{0:T(1024)(128)(4,1)S(1)} %get-tuple-element.160, f32[1024]{0:T(1024)S(1)} %bitcast.488, f32[1024]{0:T(1024)S(1)} %get-tuple-element.165, ...), kind=kLoop, calls=%fused_computation.168 | loop fusion | flops 239075328 | bytes 21379072 | tf_op jit(solution)/shard_map/jit(_where)/select_n | solution.py:87
  541.0 40.7 %collective-permute-done.3 = f32[2,1024,1024]{2,1,0:T(8,128)S(1)} collective-permute-done((f32[2,1024,1024]{2,1,0:T(8,128)S(1)}, f32[2,1024,1024]{2,1,0:T(8,128)S(1)}, u32[]{:S(2)}, u32[]{:S(2)}) %collective-permute-start.3) | collective-permute-done | bytes 8388640 | tf_op jit(solution)/shard_map/ppermute | solution.py:17
  581.7 49.2 %subtract_select_fusion = (f32[1,1024,1024]{2,1,0:T(8,128)}, f32[1,1024,1024]{2,1,0:T(8,128)}, f32[1,1024,1024]{2,1,0:T(8,128)}) fusion(f32[2,1024,1024]{2,1,0:T(8,128)S(1)} %collective-permute-done.3, pred[1024]{0:T(1024)(128)(4,1)S(1)} %get-tuple-element.160, f32[1024]{0:T(1024)S(1)} %bitcast.489, f32[1024]{0:T(1024)S(1)} %get-tuple-element.165, ...), kind=kLoop, calls=%fused_computation.167 | loop fusion | flops 239075328 | bytes 21379072 | tf_op jit(solution)/shard_map/jit(_where)/select_n | solution.py:87
  630.8 30.5 %add_select_fusion = (f32[1,1024,1024]{2,1,0:T(8,128)}, f32[1,1024,1024]{2,1,0:T(8,128)}, f32[1,1024,1024]{2,1,0:T(8,128)}, f32[1,1024,1024]{2,1,0:T(8,128)}) fusion(f32[1,1024,1024]{2,1,0:T(8,128)} %get-tuple-element.7, f32[1,1024,1024]{2,1,0:T(8,128)} %get-tuple-element.6, f32[2,1024,1024]{2,1,0:T(8,128)} %copy-done.6, ...), kind=kLoop, calls=%fused_computation.341 | loop fusion | flops 20971520 | bytes 83887104 | tf_op jit(solution)/shard_map/jit(_where)/select_n | solution.py:88
  663.7 11.5 %fusion.4 = f32[2,1024,1024]{2,1,0:T(8,128)S(1)} fusion(f32[1,1024,1024]{2,1,0:T(8,128)} %get-tuple-element.154, f32[1,1024,1024]{2,1,0:T(8,128)S(1)} %copy-done.1, f32[1,1024,1024]{2,1,0:T(8,128)} %get-tuple-element.152, f32[1,1024,1024]{2,1,0:T(8,128)} %get-tuple-element.11, f32[1,1024,1024]{2,1,0:T(8,128)} %get-tuple-element.153, ...), kind=kLoop, calls=%fused_computation.153 | loop fusion | flops 14680064 | bytes 41943040 | tf_op jit(solution)/shard_map/add | solution.py:156
  683.5 33.7 %slice.391 = f32[1023,1024]{1,0:T(8,128)} reverse(f32[1023,1024]{1,0:T(8,128)} %slice.422), dimensions={0} | reverse | bytes 8380416 | tf_op jit(solution)/shard_map/jit(_roll_static)/slice | solution.py:102
  717.1 33.6 %slice.387 = f32[1023,1024]{1,0:T(8,128)} reverse(f32[1023,1024]{1,0:T(8,128)} %slice_bitcast_fusion), dimensions={0} | reverse | bytes 8380416 | tf_op jit(solution)/shard_map/jit(_roll_static)/slice | solution.py:100
  750.7 8.1 add_subtract_fusion
  763.7 8.5 fusion.177
  775.0 12.9 %bitcast_multiply_fusion = f32[2,32,32,1024]{3,1,2,0:T(8,128)S(1)} fusion(f32[2,32,32,1024]{3,1,2,0:T(8,128)S(1)} %pad_maximum_fusion.2, f32[1,32,2,32]{3,1,2,0:T(8,128)S(1)} %get-tuple-element.148, f32[1,32,2,32]{3,1,2,0:T(8,128)S(1)} %get-tuple-element.147), kind=kOutput, calls=%fused_computation.160 | convolution fusion | flops 1612713984 | bytes 16793600 | tf_op jit(solution)/shard_map/qjpn,pknc->qjkc/dot_general | solution.py:50
  795.0 5.2 copy.44
  800.2 6.1 slice.397
  806.3 5.5 copy.45
  823.6 43.5 %all-to-all-done.1 = bf16[4,256,1024]{1,2,0:T(8,128)(2,1)S(1)} async-done(((bf16[4,256,1024]{1,2,0:T(8,128)(2,1)}), bf16[4,256,1024]{1,2,0:T(8,128)(2,1)S(1)}, u32[]{:S(2)}, u32[]{:S(2)}) %all-to-all-start.1) | async-done | bytes 2097184 | tf_op jit(solution)/shard_map/all_to_all | solution.py:159
  (109 shorter events, 89.8 us)
Async XLA Ops:
  7.4 8.4 copy-start.10
  7.4 8.9 %copy-start.11 = (f32[1024,16]{0,1:T(8,128)S(1)}, f32[1024,16]{0,1:T(8,128)}, u32[]{:S(2)}) copy-start(f32[1024,16]{0,1:T(8,128)} %param.9) | copy-start | bytes 196612
  10.8 52.3 %all-to-all-start = ((bf16[256,4,1024]{0,2,1:T(8,128)(2,1)}), bf16[256,4,1024]{0,2,1:T(8,128)(2,1)S(1)}, u32[]{:S(2)}, u32[]{:S(2)}) async-start(bf16[256,4,1024]{0,2,1:T(8,128)(2,1)} %bitcast.244), calls=%async_computation | async-start | bytes 4194304 | tf_op jit(solution)/shard_map/all_to_all | solution.py:147
  63.2 36.3 %copy-start.7 = (bf16[256,4,1024]{0,2,1:T(8,128)(2,1)}, bf16[256,4,1024]{0,2,1:T(8,128)(2,1)S(1)}, u32[]{:S(2)}) copy-start(bf16[256,4,1024]{0,2,1:T(8,128)(2,1)S(1)} %all-to-all-done) | copy-start | bytes 6291460
  65.8 27.7 %collective-permute-start = (bf16[1024,1024]{1,0:T(8,128)(2,1)}, bf16[1024,1024]{1,0:T(8,128)(2,1)S(1)}, u32[]{:S(2)}, u32[]{:S(2)}) collective-permute-start(bf16[1024,1024]{1,0:T(8,128)(2,1)} %bitcast.245), channel_id=1, source_target_pairs={{0,4},{4,8},{8,12},{12,16},{16,20},{20,24},{24,28},{1,5},{5,9},{9,... | collective-permute-start | bytes 6291464 | tf_op jit(solution)/shard_map/ppermute | solution.py:17
  230.9 4.8 copy-start.9
  230.9 7.2 slice-start
  235.6 2.5 slice-start.1
  291.4 2.9 copy-start.2
  291.4 3.4 copy-start.3
  294.8 95.6 %collective-permute-start.1 = (f32[2,1024,1024]{2,1,0:T(8,128)S(1)}, f32[2,1024,1024]{2,1,0:T(8,128)S(1)}, u32[]{:S(2)}, u32[]{:S(2)}) collective-permute-start(f32[2,1024,1024]{2,1,0:T(8,128)S(1)} %pad_maximum_fusion.1), channel_id=1, source_target_pairs={{0,4},{4,8},{8,12},{12,16},{16,20},{20,24},{24,28},{1,5},{5,9},{9,... | collective-permute-start | bytes 25165832 | tf_op jit(solution)/shard_map/ppermute | solution.py:17
  390.4 55.3 %copy-start.4 = (f32[2,1024,1024]{2,1,0:T(8,128)}, f32[2,1024,1024]{2,1,0:T(8,128)S(1)}, u32[]{:S(2)}) copy-start(f32[2,1024,1024]{2,1,0:T(8,128)S(1)} %collective-permute-done.1) | copy-start | bytes 25165828
  390.4 95.7 %collective-permute-start.2 = (f32[2,1024,1024]{2,1,0:T(8,128)S(1)}, f32[2,1024,1024]{2,1,0:T(8,128)S(1)}, u32[]{:S(2)}, u32[]{:S(2)}) collective-permute-start(f32[2,1024,1024]{2,1,0:T(8,128)S(1)} %collective-permute-done.1), channel_id=1, source_target_pairs={{0,4},{4,8},{8,12},{12,16},{16,20},{20,24},{24,28},{1,5},{5,9},{9,... | collective-permute-start | bytes 25165832 | tf_op jit(solution)/shard_map/ppermute | solution.py:17
  486.0 55.0 %copy-start.5 = (f32[2,1024,1024]{2,1,0:T(8,128)}, f32[2,1024,1024]{2,1,0:T(8,128)S(1)}, u32[]{:S(2)}) copy-start(f32[2,1024,1024]{2,1,0:T(8,128)S(1)} %collective-permute-done.2) | copy-start | bytes 25165828
  486.0 95.7 %collective-permute-start.3 = (f32[2,1024,1024]{2,1,0:T(8,128)S(1)}, f32[2,1024,1024]{2,1,0:T(8,128)S(1)}, u32[]{:S(2)}, u32[]{:S(2)}) collective-permute-start(f32[2,1024,1024]{2,1,0:T(8,128)S(1)} %collective-permute-done.2), channel_id=1, source_target_pairs={{0,4},{4,8},{8,12},{12,16},{16,20},{20,24},{24,28},{1,5},{5,9},{9,... | collective-permute-start | bytes 25165832 | tf_op jit(solution)/shard_map/ppermute | solution.py:17
  581.7 49.2 %copy-start.6 = (f32[2,1024,1024]{2,1,0:T(8,128)}, f32[2,1024,1024]{2,1,0:T(8,128)S(1)}, u32[]{:S(2)}) copy-start(f32[2,1024,1024]{2,1,0:T(8,128)S(1)} %collective-permute-done.3) | copy-start | bytes 25165828
  661.4 2.3 copy-start.1
  675.2 3.3 copy-start
  806.3 5.5 copy-start.8
  806.3 5.5 copy-start.12
  815.9 51.2 %all-to-all-start.1 = ((bf16[4,256,1024]{1,2,0:T(8,128)(2,1)}), bf16[4,256,1024]{1,2,0:T(8,128)(2,1)S(1)}, u32[]{:S(2)}, u32[]{:S(2)}) async-start(bf16[4,256,1024]{1,2,0:T(8,128)(2,1)} %add_convert_fusion), calls=%async_computation.1 | async-start | bytes 4194304 | tf_op jit(solution)/shard_map/all_to_all | solution.py:159
where the time goes:
time: 890 us; the launch traced here: 875 us
  waiting for transfers between devices  284 us (32%)
  other arithmetic  280 us (31%)
  local copies, waits for them, and re-layouts  239 us (27%)
  matrix products  42.8 us (5%)
  starting transfers between devices  28.3 us (3%)
    select_n x4, other arithmetic, packed_product(): prod_re = jnp.where(leading_frequency_bin, left[0] * right[0], prod_re)  201 us
    ppermute x4, waiting for transfers between devices, from_behind(): lax.ppermute(value, axis, [(source, source + steps) for source in range(i...  194 us
    slice x3, local copies, waits for them, and re-layouts, real_forward(): mirrored = jnp.roll(jnp.flip(spectrum, 1), 1, 1)  70.7 us
    all_to_all x1, waiting for transfers between devices, local(): lax.all_to_all(product, 'ch', split_axis=1, concat_axis=0, tiled=True)  46.7 us
    all_to_all x1, waiting for transfers between devices, local(): lax.all_to_all(mixed, 'ch', split_axis=0, concat_axis=1, tiled=True)  43.5 us
    slice x2, local copies, waits for them, and re-layouts, real_inverse_tail(): reflected_imaginary = jnp.roll(jnp.flip(output_imaginary, 0), 1, 0)  36.1 us
    slice x2, local copies, waits for them, and re-layouts, real_inverse_tail(): jnp.roll(jnp.flip(output_real, 0), 1, 0)  36 us
    select_n x1, other arithmetic, packed_product(): prod_im = jnp.where(leading_frequency_bin, left[1] * right[1], prod_im)  30.5 us
  transfers between devices with their start and end apart: 6, of which 6 were waited for; matrix products, arithmetic and copies ran while one was open for 12% of the time, Pallas kernels for 0%

commit v1 on v0

v1 whole, which is shorter than its diff:
```python
import functools

import jax
import jax.numpy as jnp
from jax import lax
from jax.experimental import pallas as pl
from jax.experimental.pallas import tpu as pltpu
from jax.sharding import PartitionSpec as P

FILTER_PARTS = 4
LANES = 128
SEGMENTS = 8
WIDE = 4
SHARES = (8, 8, 8, 4, 4)


def from_behind(value, axis, steps):
    count = lax.axis_size(axis)
    return lax.ppermute(value, axis, [(source, source + steps) for source in range(count - steps)])


def rows_of(table, modes):
    return [jnp.broadcast_to(table[m : m + 1, :], (SEGMENTS, table.shape[1])) for m in range(modes)]


def shifted(value, steps, row):
    return jnp.where(row >= steps, pltpu.roll(value, steps, 0), 0.0)


def scan_segments(rate, scr, length):
    modes = rate.shape[0]
    steps = length // SEGMENTS
    decay = rows_of(jnp.exp(-rate), modes)
    state = None
    for i in range(steps):
        tokens = scr[pl.ds(i, SEGMENTS, stride=steps), :]
        if state is None:
            state = [tokens] * modes
        else:
            state = [d * s + tokens for d, s in zip(decay, state)]
    return state


def chain_segments(rate, state, length):
    modes = rate.shape[0]
    steps = length // SEGMENTS
    row = lax.broadcasted_iota(jnp.int32, (SEGMENTS, rate.shape[1]), 0)
    reach = 1
    while reach < SEGMENTS:
        jump = rows_of(jnp.exp(-rate * float(steps * reach)), modes)
        state = [s + j * shifted(s, reach, row) for j, s in zip(jump, state)]
        reach *= 2
    return state


def emit(rate, weight, state, scr, out_scr, length):
    modes = rate.shape[0]
    steps = length // SEGMENTS
    decay = rows_of(jnp.exp(-rate), modes)
    weight = rows_of(weight, modes)
    for i in range(steps):
        tokens = scr[pl.ds(i, SEGMENTS, stride=steps), :]
        state = [d * s + tokens for d, s in zip(decay, state)]
        terms = [w * s for w, s in zip(weight, state)]
        while len(terms) > 1:
            terms = [a + b for a, b in zip(terms[::2], terms[1::2])]
        out_scr[pl.ds(i, SEGMENTS, stride=steps), :] = terms[0]


def product_of(query, key_in):
    return (query.astype(jnp.float32) * key_in.astype(jnp.float32)).astype(jnp.bfloat16)


def over_tiles(ref, body):
    def step(t, carry):
        body(pl.ds(pl.multiple_of(t * LANES, LANES), LANES))
        return carry

    lax.fori_loop(0, ref.shape[1] // LANES, step, 0)


def states_kernel(query, key_in, rate_ref, carry_out, state_out, scr):
    length = query.shape[0]
    modes = rate_ref.shape[1]

    def body(cols):
        scr[...] = product_of(query[:, cols], key_in[:, cols]).astype(jnp.float32)
        rate = rate_ref[0, :, cols]
        state = chain_segments(rate, scan_segments(rate, scr, length), length)
        row = lax.broadcasted_iota(jnp.int32, (SEGMENTS, LANES), 0)
        for m in range(modes):
            carry_out[pl.ds(m * SEGMENTS, SEGMENTS), cols] = shifted(state[m], 1, row)
            state_out[0, pl.ds(m, 1), cols] = state[m][SEGMENTS - 1 :, :]

    over_tiles(query, body)


def own_terms(query, key_in, rate_ref, weight_ref, gain_ref, carry_ref, before_ref, scr, out_scr, cols):
    length = query.shape[0]
    modes = rate_ref.shape[1]
    steps = length // SEGMENTS
    scr[...] = product_of(query[:, cols], key_in[:, cols]).astype(jnp.float32)
    rate = rate_ref[0, :, cols]
    first = (lax.broadcasted_iota(jnp.int32, (SEGMENTS, LANES), 0) * steps).astype(jnp.float32)
    rates = rows_of(rate, modes)
    before = rows_of(before_ref[0, :, cols], modes)
    state = [
        carry_ref[pl.ds(m * SEGMENTS, SEGMENTS), cols] + jnp.exp(-rates[m] * first) * before[m]
        for m in range(modes)
    ]
    emit(rate, weight_ref[0, :, cols], state, scr, out_scr, length)
    return out_scr[...] + gain_ref[0, :, cols] * scr[...]


def gate(value, mixed):
    mixed = mixed.astype(jnp.bfloat16)
    return (value.astype(jnp.float32) * mixed.astype(jnp.float32)).astype(jnp.bfloat16)


def finish_kernel(
    query, key_in, rate_ref, weight_ref, gain_ref, carry_ref, before_ref, value, over_ref, out, scr, out_scr
):
    def body(cols):
        terms = own_terms(
            query, key_in, rate_ref, weight_ref, gain_ref, carry_ref, before_ref, scr, out_scr, cols
        )
        out[:, cols] = gate(value[:, cols], terms - over_ref[:, cols])

    over_tiles(query, body)


def own_kernel(
    query, key_in, rate_ref, weight_ref, gain_ref, carry_ref, before_ref, out, scr, out_scr
):
    def body(cols):
        out[:, cols] = own_terms(
            query, key_in, rate_ref, weight_ref, gain_ref, carry_ref, before_ref, scr, out_scr, cols
        )

    over_tiles(query, body)


def over_terms(past, rate_ref, weight_ref, span, scr, out_scr, cols):
    length = past.shape[0]
    scr[...] = past[:, cols].astype(jnp.float32)
    rate = rate_ref[0, :, cols]
    state = chain_segments(rate, scan_segments(rate, scr, length), length)
    row = lax.broadcasted_iota(jnp.int32, (SEGMENTS, LANES), 0)
    state = [shifted(s, 1, row) for s in state]
    weight = weight_ref[0, :, cols] * jnp.exp(-rate * float(span))
    emit(rate, weight, state, scr, out_scr, length)
    return out_scr[...]


def over_kernel(past, rate_ref, weight_ref, out, scr, out_scr, *, span):
    def body(cols):
        out[:, cols] = over_terms(past, rate_ref, weight_ref, span, scr, out_scr, cols)

    over_tiles(past, body)


def last_kernel(past, rate_ref, weight_ref, terms, value, partial, out, scr, out_scr, *, span):
    del partial

    def body(cols):
        over = over_terms(past, rate_ref, weight_ref, span, scr, out_scr, cols)
        out[:, cols] = gate(value[:, cols], terms[:, cols] - over)

    over_tiles(past, body)


def local(query, key_in, value, residues, decay_rates, skip_gain):
    length, channels = query.shape
    group, modes = residues.shape
    n_ch = channels // group
    wide = min(WIDE * LANES, group)
    part = length * n_ch
    span = FILTER_PARTS * part
    f32 = jnp.float32

    unit = channels // sum(SHARES)
    starts = [unit * sum(SHARES[:k]) for k in range(len(SHARES) + 1)]
    chunks = list(zip(starts[:-1], starts[1:]))
    pasts = [
        from_behind(product_of(query[:, a:b], key_in[:, a:b]), "ctx", FILTER_PARTS) for a, b in chunks
    ]

    def to_all(value):
        spread = jnp.broadcast_to(value[None], (n_ch,) + value.shape)
        return lax.all_to_all(spread, "ch", split_axis=0, concat_axis=0, tiled=True)

    own_rate = decay_rates.T
    rates = to_all(own_rate)
    weights = to_all(residues.T)
    gains = to_all(skip_gain[None])

    def tokens_spec(first, width=wide):
        return pl.BlockSpec((length, width), lambda t: (0, first // width + t))

    def table_spec(first, rows, width=wide):
        per = group // width
        return pl.BlockSpec(
            (1, rows, width), lambda t: ((first // width + t) // per, 0, (first // width + t) % per)
        )

    def carry_spec(first, width=wide):
        return pl.BlockSpec((modes * SEGMENTS, width), lambda t: (0, first // width + t))

    scratch = pltpu.VMEM((length, LANES), f32)

    carries, totals = pl.pallas_call(
        states_kernel,
        grid=(channels // wide,),
        in_specs=[tokens_spec(0), tokens_spec(0), table_spec(0, modes)],
        out_specs=[carry_spec(0), table_spec(0, modes)],
        out_shape=[
            jax.ShapeDtypeStruct((modes * SEGMENTS, channels), f32),
            jax.ShapeDtypeStruct((n_ch, modes, group), f32),
        ],
        scratch_shapes=[scratch],
        name="states",
    )(query, key_in, rates)

    blocks = lax.all_to_all(totals, "ch", split_axis=0, concat_axis=0, tiled=True)
    jump = jnp.exp(-own_rate * float(length))
    tails = [None] * n_ch
    weight_to_end = jnp.ones_like(own_rate)
    running = jnp.zeros_like(own_rate)
    for q in reversed(range(n_ch)):
        running = running + jnp.exp(-own_rate * float(length * (n_ch - 1 - q))) * blocks[q]
        tails[q] = running
    whole = tails[0]
    older = sum(
        jnp.exp(-own_rate * float(part * (j - 1))) * from_behind(whole, "ctx", j)
        for j in range(1, FILTER_PARTS)
    )
    oldest = from_behind(jnp.stack(tails), "ctx", FILTER_PARTS)
    heads = []
    running = jnp.zeros_like(own_rate)
    for q in range(n_ch):
        earlier = older + jnp.exp(-own_rate * float(part * (FILTER_PARTS - 1))) * oldest[q]
        heads.append(running + jnp.exp(-own_rate * float(length * q)) * earlier)
        running = jump * running + blocks[q]
    before = lax.all_to_all(jnp.stack(heads), "ch", split_axis=0, concat_axis=0, tiled=True)

    overs = []
    for (a, b), past in zip(chunks[:-1], pasts[:-1]):
        width = min(wide, b - a)
        overs.append(
            pl.pallas_call(
                functools.partial(over_kernel, span=span),
                grid=((b - a) // width,),
                in_specs=[tokens_spec(0, width), table_spec(a, modes, width), table_spec(a, modes, width)],
                out_specs=tokens_spec(0, width),
                out_shape=jax.ShapeDtypeStruct((length, b - a), f32),
                scratch_shapes=[scratch, scratch],
                name="over",
            )(past, rates, weights)
        )

    def own_specs(first, width):
        return [
            tokens_spec(first, width),
            tokens_spec(first, width),
            table_spec(first, modes, width),
            table_spec(first, modes, width),
            table_spec(first, 1, width),
            carry_spec(first, width),
            table_spec(first, modes, width),
        ]

    own_args = (query, key_in, rates, weights, gains, carries, before)
    result = None
    for (a, b), over in zip(chunks[:-1], overs):
        width = min(wide, b - a)
        extra = [] if result is None else [result]
        kernel = finish_kernel
        if extra:
            def kernel(*refs):
                finish_kernel(*refs[:9], *refs[10:])
        result = pl.pallas_call(
            kernel,
            grid=((b - a) // width,),
            in_specs=own_specs(a, width)
            + [tokens_spec(a, width), tokens_spec(0, width)]
            + [pl.BlockSpec(memory_space=pl.ANY)] * len(extra),
            out_specs=tokens_spec(a, width),
            out_shape=jax.ShapeDtypeStruct((length, channels), jnp.bfloat16),
            scratch_shapes=[scratch, scratch],
            input_output_aliases={9: 0} if extra else {},
            name="finish",
        )(*own_args, value, over, *extra)

    a, b = chunks[-1]
    width = min(wide, b - a)
    terms = pl.pallas_call(
        own_kernel,
        grid=((b - a) // width,),
        in_specs=own_specs(a, width),
        out_specs=tokens_spec(0, width),
        out_shape=jax.ShapeDtypeStruct((length, b - a), f32),
        scratch_shapes=[scratch, scratch],
        name="own",
    )(*own_args)
    return pl.pallas_call(
        functools.partial(last_kernel, span=span),
        grid=((b - a) // width,),
        in_specs=[
            tokens_spec(0, width),
            table_spec(a, modes, width),
            table_spec(a, modes, width),
            tokens_spec(0, width),
            tokens_spec(a, width),
            pl.BlockSpec(memory_space=pl.ANY),
        ],
        out_specs=tokens_spec(a, width),
        out_shape=jax.ShapeDtypeStruct((length, channels), jnp.bfloat16),
        scratch_shapes=[scratch, scratch],
        input_output_aliases={5: 0},
        name="last",
    )(pasts[-1], rates, weights, terms, value, result)


def solution(mesh):
    return jax.shard_map(
        local,
        mesh=mesh,
        in_specs=(
            P(("ctx", "ch"), None),
            P(("ctx", "ch"), None),
            P(("ctx", "ch"), None),
            P("ch", None),
            P("ch", None),
            P("ch"),
        ),
        out_specs=P(("ctx", "ch"), None),
        check_vma=False,
    )
```

time: 890 us -> 157 us (0.18)
  the two profiles are of different devices: /device:TPU:3 before, /device:TPU:0 now
where the time goes in v1:
time: 157 us; the launch traced here: 156 us
  Pallas kernels  64.5 us (41%)
  starting transfers between devices  32.3 us (21%)
  blocking collectives  26.3 us (17%)
  waiting for transfers between devices  22 us (14%)
  other arithmetic  6.71 us (4%)
  local copies, waits for them, and re-layouts  4.32 us (3%)
    pallas_call x4, Pallas kernels, local(): pl.pallas_call(functools.partial(over_kernel, span=span), grid=((b - a) /...  23.8 us
    pallas_call x4, Pallas kernels, local(): pl.pallas_call(kernel, grid=((b - a) // width,), in_specs=own_specs(a, wi...  22.1 us
    ppermute x9, starting transfers between devices, from_behind(): lax.ppermute(value, axis, [(source, source + steps) for source in range(c...  20.6 us
    ppermute x9, waiting for transfers between devices, from_behind(): lax.ppermute(value, axis, [(source, source + steps) for source in range(c...  19.7 us
    all_to_all x1, blocking collectives, to_all(): return lax.all_to_all(spread, 'ch', split_axis=0, concat_axis=0, tiled=True)  15.1 us
    all_to_all x1, blocking collectives, local(): lax.all_to_all(totals, 'ch', split_axis=0, concat_axis=0, tiled=True)  11.2 us
    pallas_call x1, Pallas kernels, local(): pl.pallas_call(states_kernel, grid=(channels // wide,), in_specs=[tokens_...  10.5 us
    all_to_all x2, starting transfers between devices, to_all(): return lax.all_to_all(spread, 'ch', split_axis=0, concat_axis=0, tiled=True)  8.28 us
  transfers between devices with their start and end apart: 12, of which 2 were waited for; matrix products, arithmetic and copies ran while one was open for 5% of the time, Pallas kernels for 32%

profile of v1, /device:TPU:0, one launch (start us, length us, event | category | flops | bytes accessed | tf_op | source)
XLA Modules:
  0.0 156.2 jit_solution(13582016987350509565)
XLA Ops:
  0.0 0.9 broadcast_in_dim.6
  0.9 15.1 %all_to_all.25.rate_ref.refs_2_ = f32[4,16,1024]{2,1,0:T(8,128)} all-to-all(f32[4,16,1024]{2,1,0:T(8,128)S(1)} %broadcast_in_dim.6), channel_id=1, replica_groups=mesh['ctx'=8,'ch'=4] {'ch'}, dimensions={0} | all-to-all | bytes 524288 | tf_op jit(solution)/shard_map/all_to_all | solution.py:190
  16.0 10.5 %states.1 = (f32[128,4096]{1,0:T(8,128)}, f32[4,16,1024]{2,1,0:T(8,128)}) custom-call(bf16[256,4096]{1,0:T(8,128)(2,1)} %refs_0_.5, bf16[256,4096]{1,0:T(8,128)(2,1)} %refs_1_.5, f32[4,16,1024]{2,1,0:T(8,128)} %all_to_all.25.rate_ref.refs_2_), custom_call_target="tpu_custom_call" | custom-call | tf_op jit(solution)/shard_map/states/pallas_call | solution.py:211
  26.5 11.2 %all_to_all.26 = f32[4,16,1024]{2,1,0:T(8,128)S(1)} all-to-all(f32[4,16,1024]{2,1,0:T(8,128)} %get-tuple-element.8), channel_id=1, replica_groups=mesh['ctx'=8,'ch'=4] {'ch'}, dimensions={0} | all-to-all | bytes 524288 | tf_op jit(solution)/shard_map/all_to_all | solution.py:224
  38.3 3.2 %all-to-all-start.2 = ((f32[4,1,1024]{2,1,0:T(1,128)}), f32[4,1,1024]{2,1,0:T(1,128)S(1)}, u32[]{:S(2)}, u32[]{:S(2)}) async-start(f32[4,1,1024]{2,1,0:T(1,128)} %broadcast_in_dim.8), calls=%async_computation.2 | async-start | bytes 32768 | tf_op jit(solution)/shard_map/all_to_all | solution.py:190
  41.6 1.9 %collective-permute-start.1 = (f32[16,1024]{1,0:T(8,128)S(1)}, f32[16,1024]{1,0:T(8,128)}, u32[]{:S(2)}, u32[]{:S(2)}) collective-permute-start(f32[16,1024]{1,0:T(8,128)S(1)} %get-tuple-element.19), channel_id=1, source_target_pairs={{0,4},{4,8},{8,12},{12,16},{16,20},{20,24},{24,28},{1,5},{5,9},{9,... | collective-permute-start | bytes 196616 | tf_op jit(solution)/shard_map/ppermute | solution.py:19
  43.5 4.0 %collective-permute-start.2 = (f32[16,1024]{1,0:T(8,128)S(1)}, f32[16,1024]{1,0:T(8,128)}, u32[]{:S(2)}, u32[]{:S(2)}) collective-permute-start(f32[16,1024]{1,0:T(8,128)S(1)} %get-tuple-element.19), channel_id=1, source_target_pairs={{0,8},{4,12},{8,16},{12,20},{16,24},{20,28},{1,9},{5,13},{9,17},{1... | collective-permute-start | bytes 196616 | tf_op jit(solution)/shard_map/ppermute | solution.py:19
  47.6 4.3 %collective-permute-start.3 = (f32[16,1024]{1,0:T(8,128)S(1)}, f32[16,1024]{1,0:T(8,128)}, u32[]{:S(2)}, u32[]{:S(2)}) collective-permute-start(f32[16,1024]{1,0:T(8,128)S(1)} %get-tuple-element.19), channel_id=1, source_target_pairs={{0,12},{4,16},{8,20},{12,24},{16,28},{1,13},{5,17},{9,21},{13,25},... | collective-permute-start | bytes 196616 | tf_op jit(solution)/shard_map/ppermute | solution.py:19
  52.6 1.4 collective-permute-start.4
  54.0 3.0 %multiply_convert_fusion = (bf16[256,1024]{1,0:T(8,128)(2,1)}, bf16[256,1024]{1,0:T(8,128)(2,1)}, bf16[256,1024]{1,0:T(8,128)(2,1)S(1)}) fusion(bf16[256,4096]{1,0:T(8,128)(2,1)S(1)} %copy-done, bf16[256,4096]{1,0:T(8,128)(2,1)} %refs_0_.5), kind=kLoop, calls=%fused_computation | loop fusion | flops 3145728 | bytes 4718592 | tf_op jit(solution)/shard_map/convert_element_type | solution.py:71
  57.1 2.1 %collective-permute-start.8 = (bf16[256,1024]{1,0:T(8,128)(2,1)}, bf16[256,1024]{1,0:T(8,128)(2,1)}, u32[]{:S(2)}, u32[]{:S(2)}) collective-permute-start(bf16[256,1024]{1,0:T(8,128)(2,1)} %get-tuple-element.11), channel_id=1, source_target_pairs={{0,16},{4,20},{8,24},{12,28},{1,17},{5,21},{9,25},{13,29},{2,18},{... | collective-permute-start | bytes 1572872 | tf_op jit(solution)/shard_map/ppermute | solution.py:19
  59.1 0.7 broadcast_in_dim.7
  59.9 5.0 %all-to-all-start.1 = ((f32[4,16,1024]{2,1,0:T(8,128)}), f32[4,16,1024]{2,1,0:T(8,128)S(1)}, u32[]{:S(2)}, u32[]{:S(2)}) async-start(f32[4,16,1024]{2,1,0:T(8,128)} %broadcast_in_dim.7), calls=%async_computation.1 | async-start | bytes 524288 | tf_op jit(solution)/shard_map/all_to_all | solution.py:190
  64.9 2.1 %collective-permute-start.7 = (bf16[256,1024]{1,0:T(8,128)(2,1)}, bf16[256,1024]{1,0:T(8,128)(2,1)}, u32[]{:S(2)}, u32[]{:S(2)}) collective-permute-start(bf16[256,1024]{1,0:T(8,128)(2,1)} %get-tuple-element.12), channel_id=1, source_target_pairs={{0,16},{4,20},{8,24},{12,28},{1,17},{5,21},{9,25},{13,29},{2,18},{... | collective-permute-start | bytes 1572872 | tf_op jit(solution)/shard_map/ppermute | solution.py:19
  67.0 2.1 %collective-permute-start.6 = (bf16[256,1024]{1,0:T(8,128)(2,1)S(1)}, bf16[256,1024]{1,0:T(8,128)(2,1)}, u32[]{:S(2)}, u32[]{:S(2)}) collective-permute-start(bf16[256,1024]{1,0:T(8,128)(2,1)S(1)} %get-tuple-element.13), channel_id=1, source_target_pairs={{0,16},{4,20},{8,24},{12,28},{1,17},{5,21},{9,25},{13,29},{2,18},{... | collective-permute-start | bytes 1572872 | tf_op jit(solution)/shard_map/ppermute | solution.py:19
  69.1 1.0 fusion.18
  70.9 2.3 %all-to-all-done.1.weight_ref.refs_3_ = f32[4,16,1024]{2,1,0:T(8,128)S(1)} async-done(((f32[4,16,1024]{2,1,0:T(8,128)}), f32[4,16,1024]{2,1,0:T(8,128)S(1)}, u32[]{:S(2)}, u32[]{:S(2)}) %all-to-all-start.1) | async-done | bytes 262176 | tf_op jit(solution)/shard_map/all_to_all | solution.py:190
  73.2 3.4 %all-to-all-start.4 = ((f32[4,16,1024]{2,1,0:T(8,128)}), f32[4,16,1024]{2,1,0:T(8,128)S(1)}, u32[]{:S(2)}, u32[]{:S(2)}) async-start(f32[4,16,1024]{2,1,0:T(8,128)} %pad_maximum_fusion.1), calls=%async_computation.4 | async-start | bytes 524288 | tf_op jit(solution)/shard_map/all_to_all | solution.py:244
  76.6 1.2 multiply_convert_fusion.3
  77.8 1.3 collective-permute-start.5
  79.1 1.3 collective-permute-start
  80.4 19.7 %collective-permute-done.5.past = bf16[256,512]{1,0:T(8,128)(2,1)S(1)} collective-permute-done((bf16[256,512]{1,0:T(8,128)(2,1)S(1)}, bf16[256,512]{1,0:T(8,128)(2,1)S(1)}, u32[]{:S(2)}, u32[]{:S(2)}) %collective-permute-start.5) | collective-permute-done | bytes 262176 | tf_op jit(solution)/shard_map/ppermute | solution.py:19
  100.8 4.1 %over.4.refs_8_ = f32[256,512]{1,0:T(8,128)} custom-call(bf16[256,512]{1,0:T(8,128)(2,1)} %copy-done.5, f32[4,16,1024]{2,1,0:T(8,128)} %all_to_all.25.rate_ref.refs_2_, f32[4,16,1024]{2,1,0:T(8,128)} %copy-done.1), custom_call_target="tpu_custom_call" | custom-call | tf_op jit(solution)/shard_map/over/pallas_call | solution.py:250
  104.9 6.6 %over.7.over_ref = f32[256,1024]{1,0:T(8,128)} custom-call(bf16[256,1024]{1,0:T(8,128)(2,1)} %collective-permute-done.8.past, f32[4,16,1024]{2,1,0:T(8,128)} %all_to_all.25.rate_ref.refs_2_, f32[4,16,1024]{2,1,0:T(8,128)} %copy-done.1), custom_call_target="tpu_custom_call" | custom-call | tf_op jit(solution)/shard_map/over/pallas_call | solution.py:250
  111.5 6.6 %over.6.refs_8_ = f32[256,1024]{1,0:T(8,128)} custom-call(bf16[256,1024]{1,0:T(8,128)(2,1)} %collective-permute-done.7.past, f32[4,16,1024]{2,1,0:T(8,128)} %all_to_all.25.rate_ref.refs_2_, f32[4,16,1024]{2,1,0:T(8,128)} %copy-done.1), custom_call_target="tpu_custom_call" | custom-call | tf_op jit(solution)/shard_map/over/pallas_call | solution.py:250
  118.0 6.5 %over.5.refs_8_ = f32[256,1024]{1,0:T(8,128)} custom-call(bf16[256,1024]{1,0:T(8,128)(2,1)} %collective-permute-done.6.past, f32[4,16,1024]{2,1,0:T(8,128)} %all_to_all.25.rate_ref.refs_2_, f32[4,16,1024]{2,1,0:T(8,128)} %copy-done.1), custom_call_target="tpu_custom_call" | custom-call | tf_op jit(solution)/shard_map/over/pallas_call | solution.py:250
  125.3 3.7 %own.1.terms = f32[256,512]{1,0:T(8,128)} custom-call(bf16[256,4096]{1,0:T(8,128)(2,1)} %refs_0_.5, bf16[256,4096]{1,0:T(8,128)(2,1)} %refs_1_.5, f32[4,16,1024]{2,1,0:T(8,128)} %all_to_all.25.rate_ref.refs_2_, f32[4,16,1024]{2,1,0:T(8,128)} %copy-done.1, f32[4,1,1024]{2,1,0:T(1,128)} %copy-done.4, f32[128,4096]{1,0:T(8,128)} %get-tuple-element.7.carry_ref.refs_5_, ...), custom_call_target="tpu_custom_call" | custom-call | tf_op jit(solution)/shard_map/own/pallas_call | solution.py:296
  129.0 6.0 %finish.4.refs_9_ = bf16[256,4096]{1,0:T(8,128)(2,1)} custom-call(bf16[256,4096]{1,0:T(8,128)(2,1)} %refs_0_.5, bf16[256,4096]{1,0:T(8,128)(2,1)} %refs_1_.5, f32[4,16,1024]{2,1,0:T(8,128)} %all_to_all.25.rate_ref.refs_2_, f32[4,16,1024]{2,1,0:T(8,128)} %copy-done.1, f32[4,1,1024]{2,1,0:T(1,128)} %copy-done.4, ...), custom_call_target="tpu_custom_call" | custom-call | tf_op jit(solution)/shard_map/finish/pallas_call | solution.py:281
  135.0 6.0 %finish.5.refs_9_ = bf16[256,4096]{1,0:T(8,128)(2,1)} custom-call(bf16[256,4096]{1,0:T(8,128)(2,1)} %refs_0_.5, bf16[256,4096]{1,0:T(8,128)(2,1)} %refs_1_.5, f32[4,16,1024]{2,1,0:T(8,128)} %all_to_all.25.rate_ref.refs_2_, f32[4,16,1024]{2,1,0:T(8,128)} %copy-done.1, f32[4,1,1024]{2,1,0:T(1,128)} %copy-done.4, ...), custom_call_target="tpu_custom_call", output_to_operand_aliasing={{}: (9, {})} | custom-call | tf_op jit(solution)/shard_map/finish/pallas_call | solution.py:281
  141.1 6.0 %finish.6.refs_9_ = bf16[256,4096]{1,0:T(8,128)(2,1)} custom-call(bf16[256,4096]{1,0:T(8,128)(2,1)} %refs_0_.5, bf16[256,4096]{1,0:T(8,128)(2,1)} %refs_1_.5, f32[4,16,1024]{2,1,0:T(8,128)} %all_to_all.25.rate_ref.refs_2_, f32[4,16,1024]{2,1,0:T(8,128)} %copy-done.1, f32[4,1,1024]{2,1,0:T(1,128)} %copy-done.4, ...), custom_call_target="tpu_custom_call", output_to_operand_aliasing={{}: (9, {})} | custom-call | tf_op jit(solution)/shard_map/finish/pallas_call | solution.py:281
  147.1 4.0 %finish.7.partial = bf16[256,4096]{1,0:T(8,128)(2,1)} custom-call(bf16[256,4096]{1,0:T(8,128)(2,1)} %refs_0_.5, bf16[256,4096]{1,0:T(8,128)(2,1)} %refs_1_.5, f32[4,16,1024]{2,1,0:T(8,128)} %all_to_all.25.rate_ref.refs_2_, f32[4,16,1024]{2,1,0:T(8,128)} %copy-done.1, f32[4,1,1024]{2,1,0:T(1,128)} %copy-done.4, ...), custom_call_target="tpu_custom_call", output_to_operand_aliasing={{}: (9, {})} | custom-call | tf_op jit(solution)/shard_map/finish/pallas_call | solution.py:281
  151.8 4.4 %last.1 = bf16[256,4096]{1,0:T(8,128)(2,1)} custom-call(bf16[256,512]{1,0:T(8,128)(2,1)} %copy-done.6, f32[4,16,1024]{2,1,0:T(8,128)} %all_to_all.25.rate_ref.refs_2_, f32[4,16,1024]{2,1,0:T(8,128)} %copy-done.1, f32[256,512]{1,0:T(8,128)} %own.1.terms, bf16[256,4096]{1,0:T(8,128)(2,1)} %value.3, ...), custom_call_target="tpu_custom_call", output_to_operand_aliasing={{}: (5, {})} | custom-call | tf_op jit(solution)/shard_map/last/pallas_call | solution.py:305
  (33 shorter events, 4.3 us)
Async XLA Ops:
  16.0 21.7 %copy-start.8 = (f32[1024]{0:T(1024)S(1)}, f32[1024]{0:T(1024)}, u32[]{:S(2)}) copy-start(f32[1024]{0:T(1024)} %param.11) | copy-start | bytes 12292
  16.0 25.6 %copy-start.3 = (f32[1024,16]{0,1:T(8,128)S(1)}, f32[1024,16]{0,1:T(8,128)}, u32[]{:S(2)}) copy-start(f32[1024,16]{0,1:T(8,128)} %param.10) | copy-start | bytes 196612
  16.0 38.0 %copy-start = (bf16[256,4096]{1,0:T(8,128)(2,1)S(1)}, bf16[256,4096]{1,0:T(8,128)(2,1)}, u32[]{:S(2)}) copy-start(bf16[256,4096]{1,0:T(8,128)(2,1)} %refs_1_.5) | copy-start | bytes 6291460
  38.3 20.8 %all-to-all-start.2 = ((f32[4,1,1024]{2,1,0:T(1,128)}), f32[4,1,1024]{2,1,0:T(1,128)S(1)}, u32[]{:S(2)}, u32[]{:S(2)}) async-start(f32[4,1,1024]{2,1,0:T(1,128)} %broadcast_in_dim.8), calls=%async_computation.2 | async-start | bytes 32768 | tf_op jit(solution)/shard_map/all_to_all | solution.py:190
  41.6 23.3 %collective-permute-start.1 = (f32[16,1024]{1,0:T(8,128)S(1)}, f32[16,1024]{1,0:T(8,128)}, u32[]{:S(2)}, u32[]{:S(2)}) collective-permute-start(f32[16,1024]{1,0:T(8,128)S(1)} %get-tuple-element.19), channel_id=1, source_target_pairs={{0,4},{4,8},{8,12},{12,16},{16,20},{20,24},{24,28},{1,5},{5,9},{9,... | collective-permute-start | bytes 196616 | tf_op jit(solution)/shard_map/ppermute | solution.py:19
  43.5 23.5 %collective-permute-start.2 = (f32[16,1024]{1,0:T(8,128)S(1)}, f32[16,1024]{1,0:T(8,128)}, u32[]{:S(2)}, u32[]{:S(2)}) collective-permute-start(f32[16,1024]{1,0:T(8,128)S(1)} %get-tuple-element.19), channel_id=1, source_target_pairs={{0,8},{4,12},{8,16},{12,20},{16,24},{20,28},{1,9},{5,13},{9,17},{1... | collective-permute-start | bytes 196616 | tf_op jit(solution)/shard_map/ppermute | solution.py:19
  47.6 21.6 %collective-permute-start.3 = (f32[16,1024]{1,0:T(8,128)S(1)}, f32[16,1024]{1,0:T(8,128)}, u32[]{:S(2)}, u32[]{:S(2)}) collective-permute-start(f32[16,1024]{1,0:T(8,128)S(1)} %get-tuple-element.19), channel_id=1, source_target_pairs={{0,12},{4,16},{8,20},{12,24},{16,28},{1,13},{5,17},{9,21},{13,25},... | collective-permute-start | bytes 196616 | tf_op jit(solution)/shard_map/ppermute | solution.py:19
  52.6 6.5 %copy-start.7 = (f32[1024,16]{0,1:T(8,128)S(1)}, f32[1024,16]{0,1:T(8,128)}, u32[]{:S(2)}) copy-start(f32[1024,16]{0,1:T(8,128)} %param.9) | copy-start | bytes 196612
  52.6 16.5 %collective-permute-start.4 = (f32[4,16,1024]{2,1,0:T(8,128)}, f32[4,16,1024]{2,1,0:T(8,128)S(1)}, u32[]{:S(2)}, u32[]{:S(2)}) collective-permute-start(f32[4,16,1024]{2,1,0:T(8,128)} %pad_maximum_fusion), channel_id=1, source_target_pairs={{0,16},{4,20},{8,24},{12,28},{1,17},{5,21},{9,25},{13,29},{2,18},{... | collective-permute-start | bytes 786440 | tf_op jit(solution)/shard_map/ppermute | solution.py:19
  57.1 47.8 %collective-permute-start.8 = (bf16[256,1024]{1,0:T(8,128)(2,1)}, bf16[256,1024]{1,0:T(8,128)(2,1)}, u32[]{:S(2)}, u32[]{:S(2)}) collective-permute-start(bf16[256,1024]{1,0:T(8,128)(2,1)} %get-tuple-element.11), channel_id=1, source_target_pairs={{0,16},{4,20},{8,24},{12,28},{1,17},{5,21},{9,25},{13,29},{2,18},{... | collective-permute-start | bytes 1572872 | tf_op jit(solution)/shard_map/ppermute | solution.py:19
  59.1 18.6 %copy-start.4 = (f32[4,1,1024]{2,1,0:T(1,128)}, f32[4,1,1024]{2,1,0:T(1,128)S(1)}, u32[]{:S(2)}) copy-start(f32[4,1,1024]{2,1,0:T(1,128)S(1)} %all-to-all-done.2.gain_ref.refs_4_) | copy-start | bytes 49156
  59.9 13.3 %all-to-all-start.1 = ((f32[4,16,1024]{2,1,0:T(8,128)}), f32[4,16,1024]{2,1,0:T(8,128)S(1)}, u32[]{:S(2)}, u32[]{:S(2)}) async-start(f32[4,16,1024]{2,1,0:T(8,128)} %broadcast_in_dim.7), calls=%async_computation.1 | async-start | bytes 524288 | tf_op jit(solution)/shard_map/all_to_all | solution.py:190
  64.9 46.5 %collective-permute-start.7 = (bf16[256,1024]{1,0:T(8,128)(2,1)}, bf16[256,1024]{1,0:T(8,128)(2,1)}, u32[]{:S(2)}, u32[]{:S(2)}) collective-permute-start(bf16[256,1024]{1,0:T(8,128)(2,1)} %get-tuple-element.12), channel_id=1, source_target_pairs={{0,16},{4,20},{8,24},{12,28},{1,17},{5,21},{9,25},{13,29},{2,18},{... | collective-permute-start | bytes 1572872 | tf_op jit(solution)/shard_map/ppermute | solution.py:19
  67.0 51.0 %collective-permute-start.6 = (bf16[256,1024]{1,0:T(8,128)(2,1)S(1)}, bf16[256,1024]{1,0:T(8,128)(2,1)}, u32[]{:S(2)}, u32[]{:S(2)}) collective-permute-start(bf16[256,1024]{1,0:T(8,128)(2,1)S(1)} %get-tuple-element.13), channel_id=1, source_target_pairs={{0,16},{4,20},{8,24},{12,28},{1,17},{5,21},{9,25},{13,29},{2,18},{... | collective-permute-start | bytes 1572872 | tf_op jit(solution)/shard_map/ppermute | solution.py:19
  73.2 26.9 %copy-start.1 = (f32[4,16,1024]{2,1,0:T(8,128)}, f32[4,16,1024]{2,1,0:T(8,128)S(1)}, u32[]{:S(2)}) copy-start(f32[4,16,1024]{2,1,0:T(8,128)S(1)} %all-to-all-done.1.weight_ref.refs_3_) | copy-start | bytes 786436
  73.2 51.4 %all-to-all-start.4 = ((f32[4,16,1024]{2,1,0:T(8,128)}), f32[4,16,1024]{2,1,0:T(8,128)S(1)}, u32[]{:S(2)}, u32[]{:S(2)}) async-start(f32[4,16,1024]{2,1,0:T(8,128)} %pad_maximum_fusion.1), calls=%async_computation.4 | async-start | bytes 524288 | tf_op jit(solution)/shard_map/all_to_all | solution.py:244
  77.8 22.3 %collective-permute-start.5 = (bf16[256,512]{1,0:T(8,128)(2,1)S(1)}, bf16[256,512]{1,0:T(8,128)(2,1)S(1)}, u32[]{:S(2)}, u32[]{:S(2)}) collective-permute-start(bf16[256,512]{1,0:T(8,128)(2,1)S(1)} %get-tuple-element.14), channel_id=1, source_target_pairs={{0,16},{4,20},{8,24},{12,28},{1,17},{5,21},{9,25},{13,29},{2,18},{... | collective-permute-start | bytes 786440 | tf_op jit(solution)/shard_map/ppermute | solution.py:19
  79.1 72.0 %collective-permute-start = (bf16[256,512]{1,0:T(8,128)(2,1)S(1)}, bf16[256,512]{1,0:T(8,128)(2,1)S(1)}, u32[]{:S(2)}, u32[]{:S(2)}) collective-permute-start(bf16[256,512]{1,0:T(8,128)(2,1)S(1)} %get-tuple-element.15), channel_id=1, source_target_pairs={{0,16},{4,20},{8,24},{12,28},{1,17},{5,21},{9,25},{13,29},{2,18},{... | collective-permute-start | bytes 786440 | tf_op jit(solution)/shard_map/ppermute | solution.py:19
  100.1 0.7 copy-start.5
  124.6 0.7 copy-start.2
  151.1 0.7 copy-start.6

commit v2 on v0

v2 whole, which is shorter than its diff:
```python
import functools

import jax
import jax.numpy as jnp
from jax import lax
from jax.experimental import pallas as pl
from jax.experimental.pallas import tpu as pltpu
from jax.sharding import PartitionSpec as P


FILTER_PARTS = 4
LANES = 128
SEGMENTS = 8
WIDE = 4
RAW_SHARES = (2, 1)
DONE_SHARES = (2, 2, 1)
F32 = jnp.float32


def from_behind(value, axis, steps):
    count = lax.axis_size(axis)
    return lax.ppermute(value, axis, [(source, source + steps) for source in range(count - steps)])


def row_of(table, m):
    return jnp.broadcast_to(table[pl.ds(m, 1), :], (SEGMENTS, LANES))


def shifted(value, steps):
    row = lax.broadcasted_iota(jnp.int32, value.shape, 0)
    return jnp.where(row >= steps, pltpu.roll(value, steps, 0), 0.0)


def step_rows(i):
    return pl.ds(i * SEGMENTS, SEGMENTS)


def over_tiles(width, body):
    def step(t, carry):
        body(t, pl.ds(pl.multiple_of(t * LANES, LANES), LANES))
        return carry

    lax.fori_loop(0, width // LANES, step, 0)


def scan_segments(table, tokens):
    modes = table.shape[1]
    steps = tokens.shape[0] // SEGMENTS
    decay = [row_of(table.at[0], m) for m in range(modes)]
    state = [tokens[step_rows(0), :]] * modes
    for i in range(1, steps):
        now = tokens[step_rows(i), :]
        state = [d * s + now for d, s in zip(decay, state)]
    chained = []
    for m in range(modes):
        value = state[m]
        for level in range(3):
            value = value + row_of(table.at[1 + level], m) * shifted(value, 1 << level)
        chained.append(value)
    return chained


def fill_jumps(table, rate, steps):
    table[0] = jnp.exp(-rate)
    for level in range(3):
        table[1 + level] = jnp.exp(-rate * float(steps << level))


def emit(table, weights, state, tokens, write):
    modes = table.shape[1]
    steps = tokens.shape[0] // SEGMENTS
    decay = [row_of(table.at[0], m) for m in range(modes)]
    weight = [row_of(weights, m) for m in range(modes)]
    for i in range(steps):
        now = tokens[step_rows(i), :]
        state = [d * s + now for d, s in zip(decay, state)]
        terms = [w * s for w, s in zip(weight, state)]
        while len(terms) > 1:
            terms = [a + b for a, b in zip(terms[::2], terms[1::2])]
        write(i, terms[0], now)


def product_kernel(query, key_in, order, *outs):
    product = (query[...].astype(F32) * key_in[...].astype(F32)).astype(jnp.bfloat16)
    product = jnp.dot(order[...], product, preferred_element_type=F32).astype(jnp.bfloat16)
    for out in outs:
        out[...] = product


def states_kernel(product, params, carry_out, state_out, tokens, table, *, modes):
    steps = product.shape[0] // SEGMENTS

    def body(t, cols):
        tokens[...] = product[:, cols].astype(F32)
        fill_jumps(table, params[0, pl.ds(0, modes), cols], steps)
        state = scan_segments(table, tokens)
        for m in range(modes):
            carry_out[pl.ds(m * SEGMENTS, SEGMENTS), cols] = shifted(state[m], 1)
            state_out[t, pl.ds(m, 1), :] = state[m][SEGMENTS - 1 :, :]

    over_tiles(product.shape[1], body)


def combine_kernel(blocks, rate, out, scr, *, window, length):
    count = blocks.shape[0]
    zero = jnp.zeros(blocks.shape[1:], F32)
    rates = rate[...]

    def at(level, b):
        return scr[level, b] if b >= 0 else zero

    for b in range(count):
        scr[0, b] = blocks[b]
    level, reach, covered = 0, 1, None
    total = None
    while True:
        if window & reach:
            if total is None:
                total, covered = [at(level, b) for b in range(count)], reach
            else:
                jump = jnp.exp(-rates * float(length * reach))
                old = total
                total = [
                    at(level, b) + (jump * old[b - reach] if b >= reach else zero) for b in range(count)
                ]
                covered += reach
        if covered == window:
            break
        jump = jnp.exp(-rates * float(length * reach))
        for b in range(count):
            scr[1 - level, b] = at(level, b) + jump * at(level, b - reach)
        level, reach = 1 - level, reach * 2
    out[0] = zero
    for b in range(1, count):
        out[b] = total[b - 1]


def over_kernel(flag, past, params, *rest, span, modes):
    out, tokens, table, weights = rest[-4:]
    steps = past.shape[0] // SEGMENTS

    @pl.when(flag[0] > 0)
    def _():
        def body(t, cols):
            tokens[...] = past[:, cols].astype(F32)
            rate = params[0, pl.ds(0, modes), cols]
            fill_jumps(table, rate, steps)
            weights[...] = params[0, pl.ds(modes, modes), cols] * jnp.exp(-rate * float(span))
            state = [shifted(s, 1) for s in scan_segments(table, tokens)]

            def write(i, value, now):
                out[step_rows(i), cols] = value

            emit(table, weights, state, tokens, write)

        over_tiles(past.shape[1], body)

    @pl.when(flag[0] == 0)
    def _():
        out[...] = jnp.zeros_like(out)


def ahead_kernel(flag, product, params, carry, out, tokens, table, weights, scr, *, span, modes):
    @pl.when(flag[1] > 0)
    def _():
        def body(t, cols):
            tokens[...] = product[:, cols].astype(F32)
            rate = params[0, pl.ds(0, modes), cols]
            table[0] = jnp.exp(-rate)
            weights[...] = params[0, pl.ds(modes, modes), cols] * jnp.exp(-rate * float(span))
            state = [carry[pl.ds(m * SEGMENTS, SEGMENTS), cols] for m in range(modes)]

            def write(i, value, now):
                scr[step_rows(i), :] = value

            emit(table, weights, state, tokens, write)
            out[:, cols] = scr[...].astype(jnp.bfloat16)

        over_tiles(product.shape[1], body)


def finish_kernel(product, params, carry, before, over, value, order, *rest, modes):
    out, tokens, table, weights, scr, mixed = rest[-6:]
    length, width = product.shape
    steps = length // SEGMENTS

    def place(t):
        cols = pl.ds(pl.multiple_of(t * LANES, LANES), LANES)
        plain = lax.dot_general(
            order[...], mixed[:, cols], (((0,), (0,)), ((), ())), preferred_element_type=F32
        )
        out[:, cols] = (value[:, cols].astype(F32) * plain).astype(jnp.bfloat16)

    def body(t, cols):
        place(jnp.maximum(t - 1, 0))
        tokens[...] = product[:, cols].astype(F32)
        rate = params[0, pl.ds(0, modes), cols]
        table[0] = jnp.exp(-rate)
        weights[...] = params[0, pl.ds(modes, modes), cols]
        gain = jnp.broadcast_to(params[0, pl.ds(2 * modes, 1), cols], (SEGMENTS, LANES))
        first = (lax.broadcasted_iota(jnp.int32, (SEGMENTS, LANES), 0) * steps).astype(F32)
        state = []
        for m in range(modes):
            own_rate = jnp.broadcast_to(params[0, pl.ds(m, 1), cols], (SEGMENTS, LANES))
            ahead = jnp.broadcast_to(before[t, pl.ds(m, 1), :], (SEGMENTS, LANES))
            state.append(carry[pl.ds(m * SEGMENTS, SEGMENTS), cols] + jnp.exp(-own_rate * first) * ahead)

        def write(i, value, now):
            scr[step_rows(i), :] = value + gain * now

        emit(table, weights, state, tokens, write)
        mixed[:, cols] = (scr[...] - over[:, cols].astype(F32)).astype(jnp.bfloat16)

    mixed[:, pl.ds(0, LANES)] = jnp.zeros((length, LANES), jnp.bfloat16)
    over_tiles(width, body)
    place(width // LANES - 1)


def shard_program(query, key_in, value, residues, decay_rates, skip_gain):
    length, channels = query.shape
    group, modes = residues.shape
    n_ch, n_ctx = lax.axis_size("ch"), lax.axis_size("ctx")
    devices = n_ctx * n_ch
    per = channels // devices
    wide = min(WIDE * LANES, group)
    part = length * n_ch
    span = FILTER_PARTS * part
    steps = length // SEGMENTS
    tiles = channels // LANES
    bf16 = jnp.bfloat16

    unit = channels // sum(RAW_SHARES + DONE_SHARES)
    shares = (RAW_SHARES + DONE_SHARES)
    unit = channels // 8
    edges = [unit * sum(shares[:k]) for k in range(len(shares) + 1)]
    chunks = list(zip(edges[:-1], edges[1:]))
    raw, done = chunks[: len(RAW_SHARES)], chunks[len(RAW_SHARES) :]

    ctx = lax.axis_index("ctx")
    flags = jnp.stack([ctx >= FILTER_PARTS, ctx + FILTER_PARTS < n_ctx]).astype(jnp.int32)
    smem = pl.BlockSpec(memory_space=pltpu.SMEM)
    hbm = pl.BlockSpec(memory_space=pl.ANY)

    row = jnp.arange(length, dtype=jnp.int32)[:, None]
    col = jnp.arange(length, dtype=jnp.int32)[None, :]
    order = (row % SEGMENTS * steps + row // SEGMENTS == col).astype(bf16)
    order_spec = pl.BlockSpec((length, length), lambda t: (0, 0))

    def tokens_spec(first, width=wide):
        return pl.BlockSpec((length, width), lambda t: (0, first // width + t))

    rows = -(-(2 * modes + 1) // SEGMENTS) * SEGMENTS
    per_group = group // wide

    def params_spec(first):
        return pl.BlockSpec(
            (1, rows, wide), lambda t: ((first // wide + t) // per_group, 0, (first // wide + t) % per_group)
        )

    def carry_spec(first):
        return pl.BlockSpec((modes * SEGMENTS, wide), lambda t: (0, first // wide + t))

    def states_spec(first):
        return pl.BlockSpec((wide // LANES, modes, LANES), lambda t: (first // wide + t, 0, 0))

    tokens_scr = pltpu.VMEM((length, LANES), F32)
    table_scr = pltpu.VMEM((4, modes, LANES), F32)
    weights_scr = pltpu.VMEM((modes, LANES), F32)

    def call(kernel, cols, in_specs, out_specs, out_shape, scratch, args, aliases=None):
        return pl.pallas_call(
            kernel,
            grid=((cols[1] - cols[0]) // wide,),
            in_specs=in_specs,
            out_specs=out_specs,
            out_shape=out_shape,
            scratch_shapes=scratch,
            input_output_aliases=aliases or {},
        )(*args)

    def shape(columns, dtype):
        return jax.ShapeDtypeStruct((length, columns), dtype)

    packed = jnp.concatenate(
        [decay_rates.T, residues.T, skip_gain[None], jnp.zeros((rows - 2 * modes - 1, group), F32)]
    )
    packed = jnp.broadcast_to(packed[None], (n_ch,) + packed.shape)
    params = lax.all_to_all(packed, "ch", split_axis=0, concat_axis=0, tiled=True)

    product, pasts = None, []
    ends = raw + [(raw[-1][1], channels)]
    for k, (a, b) in enumerate(ends):
        extra = [] if product is None else [product]
        sent = k < len(raw)

        def kernel(q, k_in, o, *refs, skip=len(extra)):
            product_kernel(q, k_in, o, *refs[skip:])

        outs = call(
            kernel,
            (a, b),
            [tokens_spec(a), tokens_spec(a), order_spec] + [hbm] * len(extra),
            [tokens_spec(a)] + [tokens_spec(0)] * sent,
            [shape(channels, bf16)] + [shape(b - a, bf16)] * sent,
            [],
            (query, key_in, order, *extra),
            {3: 0} if extra else None,
        )
        product = outs[0]
        if sent:
            pasts.append(from_behind(outs[1], "ctx", FILTER_PARTS))

    carries, totals = call(
        functools.partial(states_kernel, modes=modes),
        (0, channels),
        [tokens_spec(0), params_spec(0)],
        [carry_spec(0), states_spec(0)],
        [
            jax.ShapeDtypeStruct((modes * SEGMENTS, channels), F32),
            jax.ShapeDtypeStruct((tiles, modes, LANES), F32),
        ],
        [tokens_scr, table_scr],
        (product, params),
    )

    def swap(blocks):
        return lax.all_to_all(blocks, ("ctx", "ch"), split_axis=0, concat_axis=0, tiled=True)

    if per >= LANES:
        chips = (per // LANES, modes, LANES)
        totals = totals.reshape((devices,) + chips)
    else:
        chips = (modes, per)
        totals = totals.reshape(tiles, modes, LANES // per, per).transpose(0, 2, 1, 3).reshape((devices,) + chips)
    blocks = swap(totals)
    mine = (ctx * n_ch + lax.axis_index("ch")) * per
    rate_mine = lax.dynamic_slice(
        params, (mine // group, 0, mine % group), (1, modes, per)
    ).reshape(modes, per)
    if per >= LANES:
        rate_mine = rate_mine.reshape(modes, per // LANES, LANES).transpose(1, 0, 2)
    heads = pl.pallas_call(
        functools.partial(combine_kernel, window=FILTER_PARTS * n_ch, length=length),
        out_shape=jax.ShapeDtypeStruct(blocks.shape, F32),
        scratch_shapes=[pltpu.VMEM((2,) + blocks.shape, F32)],
        name="combine",
    )(blocks, rate_mine)
    before = swap(heads)
    if per >= LANES:
        before = before.reshape(tiles, modes, LANES)
    else:
        before = before.reshape(tiles, LANES // per, modes, per).transpose(0, 2, 1, 3).reshape(tiles, modes, LANES)

    aheads = []
    for a, b in done:
        ahead = call(
            functools.partial(ahead_kernel, span=span, modes=modes),
            (a, b),
            [smem, tokens_spec(a), params_spec(a), carry_spec(a)],
            tokens_spec(0),
            shape(b - a, bf16),
            [tokens_scr, table_scr, weights_scr, tokens_scr],
            (flags, product, params, carries),
        )
        aheads.append(from_behind(ahead, "ctx", FILTER_PARTS))

    over = None
    for (a, b), past in zip(raw, pasts):
        extra = [] if over is None else [over]
        over = call(
            functools.partial(over_kernel, span=span, modes=modes),
            (a, b),
            [smem, tokens_spec(0), params_spec(a)] + [hbm] * len(extra),
            tokens_spec(a),
            shape(raw[-1][1], F32),
            [tokens_scr, table_scr, weights_scr],
            (flags, past, params, *extra),
            {3: 0} if extra else None,
        )

    result = None
    last = [((0, raw[-1][1]), over)] + list(zip(done, aheads))
    for (a, b), past in last:
        extra = [] if result is None else [result]
        result = call(
            functools.partial(finish_kernel, modes=modes),
            (a, b),
            [
                tokens_spec(a),
                params_spec(a),
                carry_spec(a),
                states_spec(a),
                tokens_spec(0),
                tokens_spec(a),
                order_spec,
            ]
            + [hbm] * len(extra),
            tokens_spec(a),
            shape(channels, bf16),
            [tokens_scr, table_scr, weights_scr, tokens_scr, pltpu.VMEM((length, wide), bf16)],
            (product, params, carries, before, past, value, order, *extra),
            {7: 0} if extra else None,
        )
    return result


def solution(mesh):
    return jax.shard_map(
        shard_program,
        mesh=mesh,
        in_specs=(
            P(("ctx", "ch"), None),
            P(("ctx", "ch"), None),
            P(("ctx", "ch"), None),
            P("ch", None),
            P("ch", None),
            P("ch"),
        ),
        out_specs=P(("ctx", "ch"), None),
        check_vma=False,
    )
```

time: 890 us -> 117 us (0.13)
  the two profiles are of different devices: /device:TPU:3 before, /device:TPU:6 now
where the time goes in v2:
time: 117 us; the launch traced here: 116 us
  Pallas kernels  57.2 us (49%)
  starting transfers between devices  26.9 us (23%)
  waiting for transfers between devices  20.8 us (18%)
  local copies, waits for them, and re-layouts  8.34 us (7%)
  other arithmetic  2.38 us (2%)
    pallas_call x13, Pallas kernels, call(): pl.pallas_call(kernel, grid=((cols[1] - cols[0]) // wide,), in_specs=in_s...  55.5 us
    all_to_all x2, starting transfers between devices, swap(): lax.all_to_all(blocks, ('ctx', 'ch'), split_axis=0, concat_axis=0, tiled=...  15.5 us
    ppermute x5, waiting for transfers between devices, from_behind(): lax.ppermute(value, axis, [(source, source + steps) for source in range(c...  13.8 us
    all_to_all x1, waiting for transfers between devices, shard_program(): lax.all_to_all(packed, 'ch', split_axis=0, concat_axis=0, tiled=True)  7 us
    ppermute x5, starting transfers between devices, from_behind(): lax.ppermute(value, axis, [(source, source + steps) for source in range(c...  6.56 us
    unnamed x20, local copies, waits for them, and re-layouts  6.05 us
    all_to_all x1, starting transfers between devices, shard_program(): lax.all_to_all(packed, 'ch', split_axis=0, concat_axis=0, tiled=True)  4.87 us
  transfers between devices with their start and end apart: 8, of which 2 were waited for; matrix products, arithmetic and copies ran while one was open for 2% of the time, Pallas kernels for 39%

profile of v2, /device:TPU:6, one launch (start us, length us, event | category | flops | bytes accessed | tf_op | source)
XLA Modules:
  0.0 115.8 jit_solution(3400166307836696770)
XLA Ops:
  0.1 1.0 maximum_maximum_fusion
  1.0 0.9 broadcast_in_dim.16
  2.0 4.9 %all-to-all-start = ((f32[4,40,1024]{2,1,0:T(8,128)}), f32[4,40,1024]{2,1,0:T(8,128)S(1)}, u32[]{:S(2)}, u32[]{:S(2)}) async-start(f32[4,40,1024]{2,1,0:T(8,128)} %broadcast_in_dim.16), calls=%async_computation | async-start | bytes 1310720 | tf_op jit(solution)/shard_map/all_to_all | solution.py:288
  6.8 0.8 fusion.o.order
  7.6 2.5 %shard_map.64 = (bf16[256,4096]{1,0:T(8,128)(2,1)}, bf16[256,1024]{1,0:T(8,128)(2,1)}) custom-call(bf16[256,4096]{1,0:T(8,128)(2,1)} %q.5, bf16[256,4096]{1,0:T(8,128)(2,1)} %k_in.5, bf16[256,256]{1,0:T(8,128)(2,1)} %fusion.o.order), custom_call_target="tpu_custom_call" | custom-call | tf_op jit(solution)/shard_map/pallas_call | solution.py:271
  10.1 2.1 %shard_map.65 = (bf16[256,4096]{1,0:T(8,128)(2,1)}, bf16[256,512]{1,0:T(8,128)(2,1)}) custom-call(bf16[256,4096]{1,0:T(8,128)(2,1)} %q.5, bf16[256,4096]{1,0:T(8,128)(2,1)} %k_in.5, bf16[256,256]{1,0:T(8,128)(2,1)} %fusion.o.order, bf16[256,4096]{1,0:T(8,128)(2,1)} %get-tuple-element.11.refs_0_), custom_call_target="tpu_custom_call", output_to_operand_aliasing={{0}: (3, {})} | custom-call | tf_op jit(solution)/shard_map/pallas_call | solution.py:271
  12.3 4.9 %shard_map.66.product = bf16[256,4096]{1,0:T(8,128)(2,1)} custom-call(bf16[256,4096]{1,0:T(8,128)(2,1)} %q.5, bf16[256,4096]{1,0:T(8,128)(2,1)} %k_in.5, bf16[256,256]{1,0:T(8,128)(2,1)} %fusion.o.order, bf16[256,4096]{1,0:T(8,128)(2,1)} %get-tuple-element.12.refs_0_), custom_call_target="tpu_custom_call", output_to_operand_aliasing={{}: (3, {})} | custom-call | tf_op jit(solution)/shard_map/pallas_call | solution.py:271
  17.1 7.0 %all-to-all-done.params = f32[4,40,1024]{2,1,0:T(8,128)S(1)} async-done(((f32[4,40,1024]{2,1,0:T(8,128)}), f32[4,40,1024]{2,1,0:T(8,128)S(1)}, u32[]{:S(2)}, u32[]{:S(2)}) %all-to-all-start) | async-done | bytes 655392 | tf_op jit(solution)/shard_map/all_to_all | solution.py:288
  24.1 0.9 copy-done
  25.0 8.7 %shard_map.67 = (f32[128,4096]{1,0:T(8,128)}, f32[32,16,128]{2,1,0:T(8,128)}) custom-call(bf16[256,4096]{1,0:T(8,128)(2,1)} %shard_map.66.product, f32[4,40,1024]{2,1,0:T(8,128)} %copy-done), custom_call_target="tpu_custom_call" | custom-call | tf_op jit(solution)/shard_map/pallas_call | solution.py:271
  33.7 3.9 %all-to-all-start.1 = ((f32[32,1,16,128]{3,2,1,0:T(8,128)}), f32[32,1,16,128]{3,2,1,0:T(8,128)S(1)}, u32[]{:S(2)}, u32[]{:S(2)}) async-start(f32[32,1,16,128]{3,2,1,0:T(8,128)} %bitcast.11), calls=%async_computation.1 | async-start | bytes 524288 | tf_op jit(solution)/shard_map/all_to_all | solution.py:327
  37.6 1.3 %collective-permute-start.4 = (bf16[256,1024]{1,0:T(8,128)(2,1)S(1)}, bf16[256,1024]{1,0:T(8,128)(2,1)S(1)}, u32[]{:S(2)}, u32[]{:S(2)}) collective-permute-start(bf16[256,1024]{1,0:T(8,128)(2,1)S(1)} %copy-done.8), channel_id=1, source_target_pairs={{0,16},{4,20},{8,24},{12,28},{1,17},{5,21},{9,25},{13,29},{2,18},{... | collective-permute-start | bytes 1572872 | tf_op jit(solution)/shard_map/ppermute | solution.py:22
  39.6 2.0 %shard_map.70 = bf16[256,1024]{1,0:T(8,128)(2,1)} custom-call(s32[2]{0:T(128)} %add_convert_fusion.flag, bf16[256,4096]{1,0:T(8,128)(2,1)} %shard_map.66.product, f32[4,40,1024]{2,1,0:T(8,128)} %copy-done, f32[128,4096]{1,0:T(8,128)} %get-tuple-element.13.carry), custom_call_target="tpu_custom_call" | custom-call | tf_op jit(solution)/shard_map/pallas_call | solution.py:271
  41.6 1.4 %collective-permute-start.2 = (bf16[256,1024]{1,0:T(8,128)(2,1)}, bf16[256,1024]{1,0:T(8,128)(2,1)S(1)}, u32[]{:S(2)}, u32[]{:S(2)}) collective-permute-start(bf16[256,1024]{1,0:T(8,128)(2,1)} %shard_map.70), channel_id=1, source_target_pairs={{0,16},{4,20},{8,24},{12,28},{1,17},{5,21},{9,25},{13,29},{2,18},{... | collective-permute-start | bytes 1572872 | tf_op jit(solution)/shard_map/ppermute | solution.py:22
  43.0 2.0 %shard_map.69 = bf16[256,1024]{1,0:T(8,128)(2,1)} custom-call(s32[2]{0:T(128)} %add_convert_fusion.flag, bf16[256,4096]{1,0:T(8,128)(2,1)} %shard_map.66.product, f32[4,40,1024]{2,1,0:T(8,128)} %copy-done, f32[128,4096]{1,0:T(8,128)} %get-tuple-element.13.carry), custom_call_target="tpu_custom_call" | custom-call | tf_op jit(solution)/shard_map/pallas_call | solution.py:271
  45.1 1.3 %collective-permute-start.1 = (bf16[256,1024]{1,0:T(8,128)(2,1)}, bf16[256,1024]{1,0:T(8,128)(2,1)S(1)}, u32[]{:S(2)}, u32[]{:S(2)}) collective-permute-start(bf16[256,1024]{1,0:T(8,128)(2,1)} %shard_map.69), channel_id=1, source_target_pairs={{0,16},{4,20},{8,24},{12,28},{1,17},{5,21},{9,25},{13,29},{2,18},{... | collective-permute-start | bytes 1572872 | tf_op jit(solution)/shard_map/ppermute | solution.py:22
  46.4 1.3 %constant_dynamic-slice_fusion.rate = f32[1,16,128]{2,1,0:T(8,128)} fusion(f32[4,40,1024]{2,1,0:T(8,128)} %copy-done, s32[]{:T(128)S(6)} %select_n.65, s32[]{:T(128)S(6)} %select_n.67), kind=kLoop, calls=%fused_computation.13 | loop fusion | bytes 16392 | tf_op jit(solution)/shard_map/dynamic_slice | solution.py:337
  48.4 1.7 %combine.1 = f32[32,1,16,128]{3,2,1,0:T(8,128)} custom-call(f32[32,1,16,128]{3,2,1,0:T(8,128)} %copy-done.2, f32[1,16,128]{2,1,0:T(8,128)} %constant_dynamic-slice_fusion.rate), custom_call_target="tpu_custom_call" | custom-call | tf_op jit(solution)/shard_map/combine/pallas_call | solution.py:342
  50.1 11.6 %all-to-all-start.2 = ((f32[32,1,16,128]{3,2,1,0:T(8,128)}), f32[32,1,16,128]{3,2,1,0:T(8,128)S(1)}, u32[]{:S(2)}, u32[]{:S(2)}) async-start(f32[32,1,16,128]{3,2,1,0:T(8,128)} %combine.1), calls=%async_computation.2 | async-start | bytes 524288 | tf_op jit(solution)/shard_map/all_to_all | solution.py:327
  61.7 1.3 %collective-permute-start.3 = (bf16[256,512]{1,0:T(8,128)(2,1)S(1)}, bf16[256,512]{1,0:T(8,128)(2,1)S(1)}, u32[]{:S(2)}, u32[]{:S(2)}) collective-permute-start(bf16[256,512]{1,0:T(8,128)(2,1)S(1)} %copy-done.9), channel_id=1, source_target_pairs={{0,16},{4,20},{8,24},{12,28},{1,17},{5,21},{9,25},{13,29},{2,18},{... | collective-permute-start | bytes 786440 | tf_op jit(solution)/shard_map/ppermute | solution.py:22
  63.0 1.8 %shard_map.68 = bf16[256,512]{1,0:T(8,128)(2,1)} custom-call(s32[2]{0:T(128)} %add_convert_fusion.flag, bf16[256,4096]{1,0:T(8,128)(2,1)} %shard_map.66.product, f32[4,40,1024]{2,1,0:T(8,128)} %copy-done, f32[128,4096]{1,0:T(8,128)} %get-tuple-element.13.carry), custom_call_target="tpu_custom_call" | custom-call | tf_op jit(solution)/shard_map/pallas_call | solution.py:271
  64.8 1.3 %collective-permute-start = (bf16[256,512]{1,0:T(8,128)(2,1)}, bf16[256,512]{1,0:T(8,128)(2,1)S(1)}, u32[]{:S(2)}, u32[]{:S(2)}) collective-permute-start(bf16[256,512]{1,0:T(8,128)(2,1)} %shard_map.68), channel_id=1, source_target_pairs={{0,16},{4,20},{8,24},{12,28},{1,17},{5,21},{9,25},{13,29},{2,18},{... | collective-permute-start | bytes 786440 | tf_op jit(solution)/shard_map/ppermute | solution.py:22
  66.1 0.8 copy-done.5
  66.9 5.5 %shard_map.71.rest_0_ = f32[256,1536]{1,0:T(8,128)} custom-call(s32[2]{0:T(128)} %add_convert_fusion.flag, bf16[256,1024]{1,0:T(8,128)(2,1)} %copy-done.5, f32[4,40,1024]{2,1,0:T(8,128)} %copy-done), custom_call_target="tpu_custom_call" | custom-call | tf_op jit(solution)/shard_map/pallas_call | solution.py:271
  72.4 13.8 %collective-permute-done.3.past = bf16[256,512]{1,0:T(8,128)(2,1)S(1)} collective-permute-done((bf16[256,512]{1,0:T(8,128)(2,1)S(1)}, bf16[256,512]{1,0:T(8,128)(2,1)S(1)}, u32[]{:S(2)}, u32[]{:S(2)}) %collective-permute-start.3) | collective-permute-done | bytes 262176 | tf_op jit(solution)/shard_map/ppermute | solution.py:22
  86.9 3.6 %shard_map.72.over = f32[256,1536]{1,0:T(8,128)} custom-call(s32[2]{0:T(128)} %add_convert_fusion.flag, bf16[256,512]{1,0:T(8,128)(2,1)} %copy-done.7, f32[4,40,1024]{2,1,0:T(8,128)} %copy-done, f32[256,1536]{1,0:T(8,128)} %shard_map.71.rest_0_), custom_call_target="tpu_custom_call", output_to_operand_aliasing={{}: (3, {})} | custom-call | tf_op jit(solution)/shard_map/pallas_call | solution.py:271
  91.2 7.5 %shard_map.73.rest_0_ = bf16[256,4096]{1,0:T(8,128)(2,1)} custom-call(bf16[256,4096]{1,0:T(8,128)(2,1)} %shard_map.66.product, f32[4,40,1024]{2,1,0:T(8,128)} %copy-done, f32[128,4096]{1,0:T(8,128)} %get-tuple-element.13.carry, f32[32,16,128]{2,1,0:T(8,128)} %bitcast.7, f32[256,1536]{1,0:T(8,128)} %shard_map.72.over, bf16[256,4096]{1,0:T(8,128)(2,1)} %value.7, ...), custom_call_target="tpu_custom_call" | custom-call | tf_op jit(solution)/shard_map/pallas_call | solution.py:271
  98.7 0.8 copy-done.4
  99.5 5.5 %shard_map.74.rest_0_ = bf16[256,4096]{1,0:T(8,128)(2,1)} custom-call(bf16[256,4096]{1,0:T(8,128)(2,1)} %shard_map.66.product, f32[4,40,1024]{2,1,0:T(8,128)} %copy-done, f32[128,4096]{1,0:T(8,128)} %get-tuple-element.13.carry, f32[32,16,128]{2,1,0:T(8,128)} %bitcast.8, bf16[256,1024]{1,0:T(8,128)(2,1)} %copy-done.4, ...), custom_call_target="tpu_custom_call", output_to_operand_aliasing={{}: (7, {})} | custom-call | tf_op jit(solution)/shard_map/pallas_call | solution.py:271
  105.0 0.8 copy-done.3
  105.8 5.5 %shard_map.75.rest_0_ = bf16[256,4096]{1,0:T(8,128)(2,1)} custom-call(bf16[256,4096]{1,0:T(8,128)(2,1)} %shard_map.66.product, f32[4,40,1024]{2,1,0:T(8,128)} %copy-done, f32[128,4096]{1,0:T(8,128)} %get-tuple-element.13.carry, f32[32,16,128]{2,1,0:T(8,128)} %bitcast.9, bf16[256,1024]{1,0:T(8,128)(2,1)} %copy-done.3, ...), custom_call_target="tpu_custom_call", output_to_operand_aliasing={{}: (7, {})} | custom-call | tf_op jit(solution)/shard_map/pallas_call | solution.py:271
  112.1 3.7 %shard_map.76 = bf16[256,4096]{1,0:T(8,128)(2,1)} custom-call(bf16[256,4096]{1,0:T(8,128)(2,1)} %shard_map.66.product, f32[4,40,1024]{2,1,0:T(8,128)} %copy-done, f32[128,4096]{1,0:T(8,128)} %get-tuple-element.13.carry, f32[32,16,128]{2,1,0:T(8,128)} %bitcast.10, bf16[256,512]{1,0:T(8,128)(2,1)} %copy-done.6, ...), custom_call_target="tpu_custom_call", output_to_operand_aliasing={{}: (7, {})} | custom-call | tf_op jit(solution)/shard_map/pallas_call | solution.py:271
  (26 shorter events, 3.6 us)
Async XLA Ops:
  2.0 22.2 %all-to-all-start = ((f32[4,40,1024]{2,1,0:T(8,128)}), f32[4,40,1024]{2,1,0:T(8,128)S(1)}, u32[]{:S(2)}, u32[]{:S(2)}) async-start(f32[4,40,1024]{2,1,0:T(8,128)} %broadcast_in_dim.16), calls=%async_computation | async-start | bytes 1310720 | tf_op jit(solution)/shard_map/all_to_all | solution.py:288
  17.1 20.5 %copy-start.8 = (bf16[256,1024]{1,0:T(8,128)(2,1)S(1)}, bf16[256,1024]{1,0:T(8,128)(2,1)}, u32[]{:S(2)}) copy-start(bf16[256,1024]{1,0:T(8,128)(2,1)} %get-tuple-element.16) | copy-start | bytes 1572868
  24.1 0.9 copy-start
  33.7 14.0 %all-to-all-start.1 = ((f32[32,1,16,128]{3,2,1,0:T(8,128)}), f32[32,1,16,128]{3,2,1,0:T(8,128)S(1)}, u32[]{:S(2)}, u32[]{:S(2)}) async-start(f32[32,1,16,128]{3,2,1,0:T(8,128)} %bitcast.11), calls=%async_computation.1 | async-start | bytes 524288 | tf_op jit(solution)/shard_map/all_to_all | solution.py:327
  37.6 28.5 %collective-permute-start.4 = (bf16[256,1024]{1,0:T(8,128)(2,1)S(1)}, bf16[256,1024]{1,0:T(8,128)(2,1)S(1)}, u32[]{:S(2)}, u32[]{:S(2)}) collective-permute-start(bf16[256,1024]{1,0:T(8,128)(2,1)S(1)} %copy-done.8), channel_id=1, source_target_pairs={{0,16},{4,20},{8,24},{12,28},{1,17},{5,21},{9,25},{13,29},{2,18},{... | collective-permute-start | bytes 1572872 | tf_op jit(solution)/shard_map/ppermute | solution.py:22
  41.6 20.1 %copy-start.9 = (bf16[256,512]{1,0:T(8,128)(2,1)S(1)}, bf16[256,512]{1,0:T(8,128)(2,1)}, u32[]{:S(2)}) copy-start(bf16[256,512]{1,0:T(8,128)(2,1)} %get-tuple-element.15) | copy-start | bytes 786436
  41.6 57.1 %collective-permute-start.2 = (bf16[256,1024]{1,0:T(8,128)(2,1)}, bf16[256,1024]{1,0:T(8,128)(2,1)S(1)}, u32[]{:S(2)}, u32[]{:S(2)}) collective-permute-start(bf16[256,1024]{1,0:T(8,128)(2,1)} %shard_map.70), channel_id=1, source_target_pairs={{0,16},{4,20},{8,24},{12,28},{1,17},{5,21},{9,25},{13,29},{2,18},{... | collective-permute-start | bytes 1572872 | tf_op jit(solution)/shard_map/ppermute | solution.py:22
  45.1 60.0 %collective-permute-start.1 = (bf16[256,1024]{1,0:T(8,128)(2,1)}, bf16[256,1024]{1,0:T(8,128)(2,1)S(1)}, u32[]{:S(2)}, u32[]{:S(2)}) collective-permute-start(bf16[256,1024]{1,0:T(8,128)(2,1)} %shard_map.69), channel_id=1, source_target_pairs={{0,16},{4,20},{8,24},{12,28},{1,17},{5,21},{9,25},{13,29},{2,18},{... | collective-permute-start | bytes 1572872 | tf_op jit(solution)/shard_map/ppermute | solution.py:22
  47.7 0.7 copy-start.2
  50.1 40.4 %all-to-all-start.2 = ((f32[32,1,16,128]{3,2,1,0:T(8,128)}), f32[32,1,16,128]{3,2,1,0:T(8,128)S(1)}, u32[]{:S(2)}, u32[]{:S(2)}) async-start(f32[32,1,16,128]{3,2,1,0:T(8,128)} %combine.1), calls=%async_computation.2 | async-start | bytes 524288 | tf_op jit(solution)/shard_map/all_to_all | solution.py:327
  61.7 24.5 %collective-permute-start.3 = (bf16[256,512]{1,0:T(8,128)(2,1)S(1)}, bf16[256,512]{1,0:T(8,128)(2,1)S(1)}, u32[]{:S(2)}, u32[]{:S(2)}) collective-permute-start(bf16[256,512]{1,0:T(8,128)(2,1)S(1)} %copy-done.9), channel_id=1, source_target_pairs={{0,16},{4,20},{8,24},{12,28},{1,17},{5,21},{9,25},{13,29},{2,18},{... | collective-permute-start | bytes 786440 | tf_op jit(solution)/shard_map/ppermute | solution.py:22
  64.8 46.6 %collective-permute-start = (bf16[256,512]{1,0:T(8,128)(2,1)}, bf16[256,512]{1,0:T(8,128)(2,1)S(1)}, u32[]{:S(2)}, u32[]{:S(2)}) collective-permute-start(bf16[256,512]{1,0:T(8,128)(2,1)} %shard_map.68), channel_id=1, source_target_pairs={{0,16},{4,20},{8,24},{12,28},{1,17},{5,21},{9,25},{13,29},{2,18},{... | collective-permute-start | bytes 786440 | tf_op jit(solution)/shard_map/ppermute | solution.py:22
  66.1 0.8 copy-start.5
  86.2 0.7 copy-start.7
  90.5 0.7 copy-start.1
  98.7 0.8 copy-start.4
  105.0 0.8 copy-start.3
  111.4 0.7 copy-start.6

commit v3 on v2

v3 whole, which is shorter than its diff:
```python
import functools
import math

import jax
import jax.numpy as jnp
from jax import lax
from jax.experimental import pallas as pl
from jax.experimental.pallas import tpu as pltpu
from jax.sharding import PartitionSpec as P


FILTER_PARTS = 4
LANES = 128
SEGMENTS = 8
RAW_SHARES = (2, 2)
DONE_SHARES = (2, 2)
VMEM_BYTES = 16 << 20
F32 = jnp.float32


def from_behind(value, axis, steps):
    count = lax.axis_size(axis)
    return lax.ppermute(value, axis, [(source, source + steps) for source in range(count - steps)])


def row_of(table, m):
    return jnp.broadcast_to(table[pl.ds(m, 1), :], (SEGMENTS, LANES))


def shifted(value, steps):
    row = lax.broadcasted_iota(jnp.int32, value.shape, 0)
    return jnp.where(row >= steps, pltpu.roll(value, steps, 0), 0.0)


def step_rows(i):
    return pl.ds(i * SEGMENTS, SEGMENTS)


def lanes(start):
    return pl.ds(pl.multiple_of(start, LANES), LANES)


def over_tiles(width, body):
    def step(t, carry):
        body(t)
        return carry

    lax.fori_loop(0, width // LANES, step, 0)


def params_at(params, tile, first, count):
    per = params.shape[2] // LANES
    return params.at[tile // per, pl.ds(first, count), lanes(tile % per * LANES)]


def scan_segments(table, tokens):
    modes = table.shape[1]
    steps = tokens.shape[0] // SEGMENTS
    decay = [row_of(table.at[0], m) for m in range(modes)]
    state = [tokens[step_rows(0), :]] * modes
    for i in range(1, steps):
        now = tokens[step_rows(i), :]
        state = [d * s + now for d, s in zip(decay, state)]
    chained = []
    for m in range(modes):
        value = state[m]
        for level in range(3):
            value = value + row_of(table.at[1 + level], m) * shifted(value, 1 << level)
        chained.append(value)
    return chained


def fill_jumps(table, rate, steps):
    table[0] = jnp.exp(-rate)
    for level in range(3):
        table[1 + level] = jnp.exp(-rate * float(steps << level))


def emit(table, weights, state, tokens, write):
    modes = table.shape[1]
    steps = tokens.shape[0] // SEGMENTS
    decay = [row_of(table.at[0], m) for m in range(modes)]
    weight = [row_of(weights, m) for m in range(modes)]
    for i in range(steps):
        now = tokens[step_rows(i), :]
        state = [d * s + now for d, s in zip(decay, state)]
        terms = [w * s for w, s in zip(weight, state)]
        while len(terms) > 1:
            terms = [a + b for a, b in zip(terms[::2], terms[1::2])]
        write(i, terms[0], now)


def fill_order(order):
    length = order.shape[0]
    row = lax.broadcasted_iota(jnp.int32, order.shape, 0)
    col = lax.broadcasted_iota(jnp.int32, order.shape, 1)
    order[...] = jnp.where(row % SEGMENTS * (length // SEGMENTS) + row // SEGMENTS == col, 1.0, 0.0).astype(
        order.dtype
    )


def product_kernel(query, key_in, *refs, first):
    outs, order = refs[:-1], refs[-1]
    fill_order(order)
    start = first
    for out in outs:
        width = out.shape[1]
        wide = math.gcd(width, 4 * LANES)
        for at in range(0, width, wide):
            cols = pl.ds(start + at, wide)
            product = (query[:, cols].astype(F32) * key_in[:, cols].astype(F32)).astype(jnp.bfloat16)
            out[:, pl.ds(at, wide)] = jnp.dot(
                order[...], product, preferred_element_type=F32
            ).astype(jnp.bfloat16)
        start += width


def states_kernel(*refs, modes, count):
    products, params = refs[:count], refs[count]
    carries, state_out = refs[count + 1 : 2 * count + 1], refs[2 * count + 1]
    tokens, table = refs[2 * count + 2 :]
    first = 0
    for product, carry_out in zip(products, carries):
        steps = product.shape[0] // SEGMENTS

        def body(t, first=first, product=product, carry_out=carry_out):
            cols = lanes(t * LANES)
            tokens[...] = product[:, cols].astype(F32)
            fill_jumps(table, params_at(params, first + t, 0, modes)[...], steps)
            state = scan_segments(table, tokens)
            for m in range(modes):
                carry_out[pl.ds(m * SEGMENTS, SEGMENTS), cols] = shifted(state[m], 1)
                state_out[first + t, pl.ds(m, 1), :] = state[m][SEGMENTS - 1 :, :]

        over_tiles(product.shape[1], body)
        first += product.shape[1] // LANES


def combine_kernel(blocks, rate, out, scr, *, window, length):
    count = blocks.shape[0]
    zero = jnp.zeros(blocks.shape[1:], F32)
    rates = rate[...]

    def at(level, b):
        return scr[level, b] if b >= 0 else zero

    for b in range(count):
        scr[0, b] = blocks[b]
    level, reach, covered = 0, 1, None
    total = None
    while True:
        if window & reach:
            if total is None:
                total, covered = [at(level, b) for b in range(count)], reach
            else:
                jump = jnp.exp(-rates * float(length * reach))
                old = total
                total = [
                    at(level, b) + (jump * old[b - reach] if b >= reach else zero) for b in range(count)
                ]
                covered += reach
        if covered == window:
            break
        jump = jnp.exp(-rates * float(length * reach))
        for b in range(count):
            scr[1 - level, b] = at(level, b) + jump * at(level, b - reach)
        level, reach = 1 - level, reach * 2
    out[0] = zero
    for b in range(1, count):
        out[b] = total[b - 1]


def over_kernel(past, params, out, tokens, table, weights, *, span, modes, first):
    steps = past.shape[0] // SEGMENTS
    needed = lax.axis_index("ctx") >= FILTER_PARTS

    @pl.when(needed)
    def _():
        def body(t):
            cols = lanes(t * LANES)
            tokens[...] = past[:, cols].astype(F32)
            rate = params_at(params, first + t, 0, modes)[...]
            fill_jumps(table, rate, steps)
            weights[...] = params_at(params, first + t, modes, modes)[...] * jnp.exp(-rate * float(span))
            state = [shifted(s, 1) for s in scan_segments(table, tokens)]

            def write(i, value, now):
                out[step_rows(i), cols] = value

            emit(table, weights, state, tokens, write)

        over_tiles(past.shape[1], body)

    @pl.when(jnp.logical_not(needed))
    def _():
        out[...] = jnp.zeros_like(out)


def ahead_kernel(product, params, carry, out, tokens, table, weights, scr, *, span, modes, first, n_ctx):
    @pl.when(lax.axis_index("ctx") + FILTER_PARTS < n_ctx)
    def _():
        def body(t):
            cols = lanes(t * LANES)
            tokens[...] = product[:, cols].astype(F32)
            rate = params_at(params, first + t, 0, modes)[...]
            table[0] = jnp.exp(-rate)
            weights[...] = params_at(params, first + t, modes, modes)[...] * jnp.exp(-rate * float(span))
            state = [carry[pl.ds(m * SEGMENTS, SEGMENTS), cols] for m in range(modes)]

            def write(i, value, now):
                scr[step_rows(i), :] = value

            emit(table, weights, state, tokens, write)
            out[:, cols] = scr[...].astype(jnp.bfloat16)

        over_tiles(product.shape[1], body)


def gated(order, mixed, value):
    plain = lax.dot_general(order[...], mixed, (((0,), (0,)), ((), ())), preferred_element_type=F32)
    return (value.astype(F32) * plain).astype(jnp.bfloat16)


def finish_kernel(*refs, modes, count):
    products, params = refs[:count], refs[count]
    carries, before, value = refs[count + 1 : 2 * count + 1], refs[2 * count + 1], refs[2 * count + 2]
    overs = refs[2 * count + 3 : 3 * count + 2]
    out, rest, tokens, table, weights, scr, order, mixed, done, sems = refs[3 * count + 2 :]
    length = value.shape[0]
    steps = length // SEGMENTS
    fill_order(order)
    copies = [None, None]
    first = 0
    for k in range(count):
        product, carry = products[k], carries[k]
        width = product.shape[1]
        slot = k % 2
        last = k == count - 1
        if copies[slot] is not None and not last:
            copies[slot].wait()
            copies[slot] = None

        def place(t, first=first, slot=slot):
            cols = lanes(t * LANES)
            done[slot, :, cols] = gated(order, mixed[:, cols], value[:, lanes((first + t) * LANES)])

        def body(t, first=first, product=product, carry=carry, last=last, place=place, k=k):
            cols = lanes(t * LANES)
            if not last:
                place(jnp.maximum(t - 1, 0))
            tokens[...] = product[:, cols].astype(F32)
            rates = params_at(params, first + t, 0, modes)
            table[0] = jnp.exp(-rates[...])
            weights[...] = params_at(params, first + t, modes, modes)[...]
            gain = row_of(params_at(params, first + t, 2 * modes, 1), 0)
            begin = (lax.broadcasted_iota(jnp.int32, (SEGMENTS, LANES), 0) * steps).astype(F32)
            state = []
            for m in range(modes):
                ahead = row_of(before.at[first + t], m)
                state.append(
                    carry[pl.ds(m * SEGMENTS, SEGMENTS), cols] + jnp.exp(-row_of(rates, m) * begin) * ahead
                )
            if last:

                def write(i, value, now):
                    rest[step_rows(i), cols] = value + gain * now

                emit(table, weights, state, tokens, write)
            else:

                def write(i, value, now):
                    scr[step_rows(i), :] = value + gain * now

                emit(table, weights, state, tokens, write)
                mixed[:, cols] = (scr[...] - overs[k][:, cols].astype(F32)).astype(jnp.bfloat16)

        if k == 0:
            mixed[:, pl.ds(0, LANES)] = jnp.zeros((length, LANES), jnp.bfloat16)
        over_tiles(width, body)
        if not last:
            place(width // LANES - 1)
            copies[slot] = pltpu.make_async_copy(
                done.at[slot, :, pl.ds(0, width)], out.at[:, pl.ds(first * LANES, width)], sems.at[slot]
            )
            copies[slot].start()
        first += width // LANES
    for copy in copies:
        if copy is not None:
            copy.wait()


def last_kernel(rest, over, value, partial, out, order, done, sem):
    del partial
    _, width = rest.shape
    first = value.shape[1] - width
    fill_order(order)
    wide = math.gcd(width, 4 * LANES)
    copies = []
    for k, at in enumerate(range(0, width, wide)):
        cols = pl.ds(at, wide)
        mixed = (rest[:, cols] - over[:, cols].astype(F32)).astype(jnp.bfloat16)
        done[:, cols] = gated(order, mixed, value[:, pl.ds(first + at, wide)])
        copies.append(
            pltpu.make_async_copy(done.at[:, cols], out.at[:, pl.ds(first + at, wide)], sem.at[k])
        )
        copies[-1].start()
    for copy in copies:
        copy.wait()


def shard_program(query, key_in, value, residues, decay_rates, skip_gain):
    length, channels = query.shape
    group, modes = residues.shape
    n_ch, n_ctx = lax.axis_size("ch"), lax.axis_size("ctx")
    devices = n_ctx * n_ch
    per = channels // devices
    span = FILTER_PARTS * length * n_ch
    tiles = channels // LANES
    bf16 = jnp.bfloat16

    shares = RAW_SHARES + DONE_SHARES
    unit = channels // sum(shares)
    widths = [unit * share for share in shares]
    firsts = [sum(widths[:k]) for k in range(len(widths))]
    count, n_raw = len(widths), len(RAW_SHARES)

    vmem = pl.BlockSpec(memory_space=pltpu.VMEM)
    anywhere = pl.BlockSpec(memory_space=pl.ANY)

    def shape(rows, columns, dtype=F32):
        return jax.ShapeDtypeStruct((rows, columns), dtype)

    tokens_scr = pltpu.VMEM((length, LANES), F32)
    table_scr = pltpu.VMEM((4, modes, LANES), F32)
    weights_scr = pltpu.VMEM((modes, LANES), F32)
    order_scr = pltpu.VMEM((length, length), bf16)

    def call(kernel, out_shape, scratch, args, **options):
        specs = dict(in_specs=[vmem] * len(args), out_specs=jax.tree.map(lambda _: vmem, out_shape))
        specs.update(options)
        return pl.pallas_call(
            kernel,
            out_shape=out_shape,
            scratch_shapes=scratch,
            compiler_params=pltpu.CompilerParams(vmem_limit_bytes=VMEM_BYTES),
            **specs,
        )(*args)

    rows = -(-(2 * modes + 1) // SEGMENTS) * SEGMENTS
    packed = jnp.concatenate(
        [decay_rates.T, residues.T, skip_gain[None], jnp.zeros((rows - 2 * modes - 1, group), F32)]
    )
    packed = jnp.broadcast_to(packed[None], (n_ch,) + packed.shape)
    params = lax.all_to_all(packed, "ch", split_axis=0, concat_axis=0, tiled=True)

    products, pasts = [], []
    batches = [[k] for k in range(n_raw)] + [list(range(n_raw, count))]
    for k, batch in enumerate(batches):
        products += call(
            functools.partial(product_kernel, first=firsts[batch[0]]),
            [shape(length, widths[j], bf16) for j in batch],
            [order_scr],
            (query, key_in),
        )
        if k < n_raw:
            pasts.append(from_behind(products[k], "ctx", FILTER_PARTS))

    *carries, totals = call(
        functools.partial(states_kernel, modes=modes, count=count),
        [shape(modes * SEGMENTS, width) for width in widths]
        + [jax.ShapeDtypeStruct((tiles, modes, LANES), F32)],
        [tokens_scr, table_scr],
        (*products, params),
    )

    def swap(blocks):
        return lax.all_to_all(blocks, ("ctx", "ch"), split_axis=0, concat_axis=0, tiled=True)

    mine = (lax.axis_index("ctx") * n_ch + lax.axis_index("ch")) * per
    rate_mine = lax.dynamic_slice(params, (mine // group, 0, mine % group), (1, modes, per))
    rate_mine = rate_mine.reshape(modes, per)
    split = max(per // LANES, 1)
    per_block = (split, modes, per // split)
    rate_mine = rate_mine.reshape(modes, split, per // split).transpose(1, 0, 2)
    if per >= LANES:
        totals = totals.reshape((devices,) + per_block)
    else:
        totals = totals.reshape(tiles, modes, LANES // per, per).transpose(0, 2, 1, 3)
        totals = totals.reshape((devices,) + per_block)
    blocks = swap(totals)
    heads = call(
        functools.partial(combine_kernel, window=FILTER_PARTS * n_ch, length=length),
        jax.ShapeDtypeStruct(blocks.shape, F32),
        [pltpu.VMEM((2,) + blocks.shape, F32)],
        (blocks, rate_mine),
    )
    before = swap(heads)
    if per < LANES:
        before = before.reshape(tiles, LANES // per, modes, per).transpose(0, 2, 1, 3)
    before = before.reshape(tiles, modes, LANES)

    overs = []
    for k in range(n_raw):
        overs.append(
            call(
                functools.partial(over_kernel, span=span, modes=modes, first=firsts[k] // LANES),
                shape(length, widths[k]),
                [tokens_scr, table_scr, weights_scr],
                (pasts[k], params),
            )
        )
    for k in range(n_raw, count):
        ahead = call(
            functools.partial(
                ahead_kernel, span=span, modes=modes, first=firsts[k] // LANES, n_ctx=n_ctx
            ),
            shape(length, widths[k], bf16),
            [tokens_scr, table_scr, weights_scr, tokens_scr],
            (products[k], params, carries[k]),
        )
        overs.append(from_behind(ahead, "ctx", FILTER_PARTS))

    widest = max(widths)
    partial, rest = call(
        functools.partial(finish_kernel, modes=modes, count=count),
        [shape(length, channels, bf16), shape(length, widths[-1])],
        [
            tokens_scr,
            table_scr,
            weights_scr,
            tokens_scr,
            order_scr,
            pltpu.VMEM((length, widest), bf16),
            pltpu.VMEM((2, length, widest), bf16),
            pltpu.SemaphoreType.DMA((2,)),
        ],
        (*products, params, *carries, before, value, *overs[:-1]),
        out_specs=[anywhere, vmem],
    )
    return call(
        last_kernel,
        shape(length, channels, bf16),
        [order_scr, pltpu.VMEM((length, widths[-1]), bf16), pltpu.SemaphoreType.DMA((8,))],
        (rest, overs[-1], value, partial),
        in_specs=[vmem, vmem, vmem, anywhere],
        out_specs=anywhere,
        input_output_aliases={3: 0},
    )


def solution(mesh):
    return jax.shard_map(
        shard_program,
        mesh=mesh,
        in_specs=(
            P(("ctx", "ch"), None),
            P(("ctx", "ch"), None),
            P(("ctx", "ch"), None),
            P("ch", None),
            P("ch", None),
            P("ch"),
        ),
        out_specs=P(("ctx", "ch"), None),
        check_vma=False,
    )
```

time: 117 us -> 122 us (1.043)
  the two profiles are of different devices: /device:TPU:6 before, /device:TPU:0 now
where the time goes in v3:
time: 122 us; the launch traced here: 121 us
  Pallas kernels  40.5 us (33%)
  waiting for transfers between devices  38.8 us (32%)
  starting transfers between devices  25.5 us (21%)
  local copies, waits for them, and re-layouts  14.8 us (12%)
    pallas_call x11, Pallas kernels, call(): pl.pallas_call(kernel, out_shape=out_shape, scratch_shapes=scratch, compi...  40.5 us
    ppermute x4, waiting for transfers between devices, from_behind(): lax.ppermute(value, axis, [(source, source + steps) for source in range(c...  14.9 us
    unnamed x38, local copies, waits for them, and re-layouts  13.9 us
    all_to_all x1, waiting for transfers between devices, shard_program(): lax.all_to_all(packed, 'ch', split_axis=0, concat_axis=0, tiled=True)  12.8 us
    all_to_all x2, waiting for transfers between devices, swap(): lax.all_to_all(blocks, ('ctx', 'ch'), split_axis=0, concat_axis=0, tiled=...  11.1 us
    ppermute x4, starting transfers between devices, from_behind(): lax.ppermute(value, axis, [(source, source + steps) for source in range(c...  10.8 us
    all_to_all x2, starting transfers between devices, swap(): lax.all_to_all(blocks, ('ctx', 'ch'), split_axis=0, concat_axis=0, tiled=...  8.34 us
    all_to_all x1, starting transfers between devices, shard_program(): lax.all_to_all(packed, 'ch', split_axis=0, concat_axis=0, tiled=True)  6.35 us
  transfers between devices with their start and end apart: 7, of which 4 were waited for; matrix products, arithmetic and copies ran while one was open for 0% of the time, Pallas kernels for 25%

profile of v3, /device:TPU:0, one launch (start us, length us, event | category | flops | bytes accessed | tf_op | source)
XLA Modules:
  0.0 120.8 jit_solution(9618470576689051082)
XLA Ops:
  0.1 1.1 maximum_maximum_fusion
  2.1 6.3 %all-to-all-start = ((f32[4,40,1024]{2,1,0:T(8,128)}), f32[4,40,1024]{2,1,0:T(8,128)S(1)}, u32[]{:S(2)}, u32[]{:S(2)}) async-start(f32[4,40,1024]{2,1,0:T(8,128)} %broadcast_in_dim.14), calls=%async_computation | async-start | bytes 1310720 | tf_op jit(solution)/shard_map/all_to_all | solution.py:354
  8.4 1.6 %copy-done.1 = bf16[256,4096]{1,0:T(8,128)(2,1)S(1)} copy-done((bf16[256,4096]{1,0:T(8,128)(2,1)S(1)}, bf16[256,4096]{1,0:T(8,128)(2,1)}, u32[]{:S(2)}) %copy-start.1) | copy-done | bytes 2097176
  10.6 1.2 shard_map.64.refs_0_
  11.8 1.2 shard_map.65.refs_1_
  12.9 12.8 %all-to-all-done.refs_4_.params = f32[4,40,1024]{2,1,0:T(8,128)S(1)} async-done(((f32[4,40,1024]{2,1,0:T(8,128)}), f32[4,40,1024]{2,1,0:T(8,128)S(1)}, u32[]{:S(2)}, u32[]{:S(2)}) %all-to-all-start) | async-done | bytes 655392 | tf_op jit(solution)/shard_map/all_to_all | solution.py:354
  25.7 1.0 copy-done.4
  26.8 8.2 %shard_map.67 = (f32[128,1024]{1,0:T(8,128)S(1)}, f32[128,1024]{1,0:T(8,128)S(1)}, f32[128,1024]{1,0:T(8,128)S(1)}, f32[128,1024]{1,0:T(8,128)S(1)}, f32[32,16,128]{2,1,0:T(8,128)}) custom-call(bf16[256,1024]{1,0:T(8,128)(2,1)} %shard_map.64.refs_0_, bf16[256,1024]{1,0:T(8,128)(2,1)} %shard_map.65.refs_1_, ...), custom_call_target="tpu_custom_call" | custom-call | tf_op jit(solution)/shard_map/pallas_call | solution.py:341
  36.6 3.7 %all-to-all-start.1 = ((f32[32,1,16,128]{3,2,1,0:T(8,128)}), f32[32,1,16,128]{3,2,1,0:T(8,128)S(1)}, u32[]{:S(2)}, u32[]{:S(2)}) async-start(f32[32,1,16,128]{3,2,1,0:T(8,128)} %bitcast.3), calls=%async_computation.1 | async-start | bytes 524288 | tf_op jit(solution)/shard_map/all_to_all | solution.py:377
  40.3 4.5 %collective-permute-start = (bf16[256,1024]{1,0:T(8,128)(2,1)}, bf16[256,1024]{1,0:T(8,128)(2,1)}, u32[]{:S(2)}, u32[]{:S(2)}) collective-permute-start(bf16[256,1024]{1,0:T(8,128)(2,1)} %shard_map.64.refs_0_), channel_id=1, source_target_pairs={{0,16},{4,20},{8,24},{12,28},{1,17},{5,21},{9,25},{13,29},{2,18},{... | collective-permute-start | bytes 1572872 | tf_op jit(solution)/shard_map/ppermute | solution.py:23
  44.8 2.1 %collective-permute-start.1 = (bf16[256,1024]{1,0:T(8,128)(2,1)}, bf16[256,1024]{1,0:T(8,128)(2,1)}, u32[]{:S(2)}, u32[]{:S(2)}) collective-permute-start(bf16[256,1024]{1,0:T(8,128)(2,1)} %shard_map.65.refs_1_), channel_id=1, source_target_pairs={{0,16},{4,20},{8,24},{12,28},{1,17},{5,21},{9,25},{13,29},{2,18},{... | collective-permute-start | bytes 1572872 | tf_op jit(solution)/shard_map/ppermute | solution.py:23
  46.9 3.3 %shard_map.71 = bf16[256,1024]{1,0:T(8,128)(2,1)} custom-call(bf16[256,1024]{1,0:T(8,128)(2,1)S(1)} %get-tuple-element.14.refs_2_.product, f32[4,40,1024]{2,1,0:T(8,128)S(1)} %all-to-all-done.refs_4_.params, f32[128,1024]{1,0:T(8,128)S(1)} %get-tuple-element.18.carry.refs_7_), custom_call_target="tpu_custom_call" | custom-call | tf_op jit(solution)/shard_map/pallas_call | solution.py:341
  50.2 2.1 %collective-permute-start.2 = (bf16[256,1024]{1,0:T(8,128)(2,1)}, bf16[256,1024]{1,0:T(8,128)(2,1)}, u32[]{:S(2)}, u32[]{:S(2)}) collective-permute-start(bf16[256,1024]{1,0:T(8,128)(2,1)} %shard_map.71), channel_id=1, source_target_pairs={{0,16},{4,20},{8,24},{12,28},{1,17},{5,21},{9,25},{13,29},{2,18},{... | collective-permute-start | bytes 1572872 | tf_op jit(solution)/shard_map/ppermute | solution.py:23
  52.2 3.3 %shard_map.73 = bf16[256,1024]{1,0:T(8,128)(2,1)} custom-call(bf16[256,1024]{1,0:T(8,128)(2,1)S(1)} %copy-done.5, f32[4,40,1024]{2,1,0:T(8,128)S(1)} %all-to-all-done.refs_4_.params, f32[128,1024]{1,0:T(8,128)S(1)} %get-tuple-element.19.refs_8_.carry), custom_call_target="tpu_custom_call" | custom-call | tf_op jit(solution)/shard_map/pallas_call | solution.py:341
  55.5 2.1 %collective-permute-start.3 = (bf16[256,1024]{1,0:T(8,128)(2,1)}, bf16[256,1024]{1,0:T(8,128)(2,1)}, u32[]{:S(2)}, u32[]{:S(2)}) collective-permute-start(bf16[256,1024]{1,0:T(8,128)(2,1)} %shard_map.73), channel_id=1, source_target_pairs={{0,16},{4,20},{8,24},{12,28},{1,17},{5,21},{9,25},{13,29},{2,18},{... | collective-permute-start | bytes 1572872 | tf_op jit(solution)/shard_map/ppermute | solution.py:23
  58.4 4.6 %all-to-all-start.2 = ((f32[32,1,16,128]{3,2,1,0:T(8,128)}), f32[32,1,16,128]{3,2,1,0:T(8,128)S(1)}, u32[]{:S(2)}, u32[]{:S(2)}) async-start(f32[32,1,16,128]{3,2,1,0:T(8,128)} %shard_map.68), calls=%async_computation.2 | async-start | bytes 524288 | tf_op jit(solution)/shard_map/all_to_all | solution.py:377
  63.1 1.3 %shard_map.69.refs_11_ = f32[256,1024]{1,0:T(8,128)S(1)} custom-call(bf16[256,1024]{1,0:T(8,128)(2,1)} %collective-permute-done.past, f32[4,40,1024]{2,1,0:T(8,128)S(1)} %all-to-all-done.refs_4_.params), custom_call_target="tpu_custom_call" | custom-call | tf_op jit(solution)/shard_map/pallas_call | solution.py:341
  64.3 1.0 copy-done.7
  65.3 5.3 %collective-permute-done.1.past = bf16[256,1024]{1,0:T(8,128)(2,1)} collective-permute-done((bf16[256,1024]{1,0:T(8,128)(2,1)}, bf16[256,1024]{1,0:T(8,128)(2,1)}, u32[]{:S(2)}, u32[]{:S(2)}) %collective-permute-start.1) | collective-permute-done | bytes 524320 | tf_op jit(solution)/shard_map/ppermute | solution.py:23
  70.5 1.1 shard_map.70.refs_12_
  71.7 1.0 copy-done.9
  72.6 9.6 %collective-permute-done.2.refs_13_ = bf16[256,1024]{1,0:T(8,128)(2,1)} collective-permute-done((bf16[256,1024]{1,0:T(8,128)(2,1)}, bf16[256,1024]{1,0:T(8,128)(2,1)}, u32[]{:S(2)}, u32[]{:S(2)}) %collective-permute-start.2) | collective-permute-done | bytes 524320 | tf_op jit(solution)/shard_map/ppermute | solution.py:23
  82.3 11.1 %all-to-all-done.2 = f32[32,1,16,128]{3,2,1,0:T(8,128)S(1)} async-done(((f32[32,1,16,128]{3,2,1,0:T(8,128)}), f32[32,1,16,128]{3,2,1,0:T(8,128)S(1)}, u32[]{:S(2)}, u32[]{:S(2)}) %all-to-all-start.2) | async-done | bytes 262176 | tf_op jit(solution)/shard_map/all_to_all | solution.py:377
  93.3 1.0 copy-done.6
  94.4 1.2 %copy-done.8 = f32[256,1024]{1,0:T(8,128)S(1)} copy-done((f32[256,1024]{1,0:T(8,128)S(1)}, f32[256,1024]{1,0:T(8,128)}, u32[]{:S(2)}) %copy-start.8) | copy-done | bytes 1048600
  95.6 1.2 %copy-done.10 = f32[256,1024]{1,0:T(8,128)S(1)} copy-done((f32[256,1024]{1,0:T(8,128)S(1)}, f32[256,1024]{1,0:T(8,128)}, u32[]{:S(2)}) %copy-start.10) | copy-done | bytes 1048600
  96.8 1.0 copy-done.12
  97.9 1.0 copy-done.14
  98.9 1.0 copy-done.16
  100.0 1.0 copy-done.18
  101.0 17.5 %shard_map.72 = (bf16[256,4096]{1,0:T(8,128)(2,1)}, f32[256,1024]{1,0:T(8,128)S(1)}) custom-call(bf16[256,1024]{1,0:T(8,128)(2,1)} %shard_map.64.refs_0_, bf16[256,1024]{1,0:T(8,128)(2,1)} %shard_map.65.refs_1_, bf16[256,1024]{1,0:T(8,128)(2,1)S(1)} %get-tuple-element.14.refs_2_.product, bf16[256,1024]{1,0:T(8,128)(2,1)S(1)} %copy-done.6, ...), custom_call_target="tpu_custom_call" | custom-call | tf_op jit(solution)/shard_map/pallas_call | solution.py:341
  118.6 2.2 %shard_map.74 = bf16[256,4096]{1,0:T(8,128)(2,1)} custom-call(f32[256,1024]{1,0:T(8,128)S(1)} %get-tuple-element.21.rest, bf16[256,1024]{1,0:T(8,128)(2,1)} %collective-permute-done.3.over, bf16[256,4096]{1,0:T(8,128)(2,1)S(1)} %copy-done.2, bf16[256,4096]{1,0:T(8,128)(2,1)} %get-tuple-element.22.partial), custom_call_target="tpu_custom_call", output_to_operand_aliasing={{}: (3, {})} | custom-call | tf_op jit(solution)/shard_map/pallas_call | solution.py:341
  (36 shorter events, 4.0 us)
Async XLA Ops:
  0.0 8.4 %copy-start = (bf16[256,4096]{1,0:T(8,128)(2,1)S(1)}, bf16[256,4096]{1,0:T(8,128)(2,1)}, u32[]{:S(2)}) copy-start(bf16[256,4096]{1,0:T(8,128)(2,1)} %query.5) | copy-start | bytes 6291460
  2.1 23.6 %all-to-all-start = ((f32[4,40,1024]{2,1,0:T(8,128)}), f32[4,40,1024]{2,1,0:T(8,128)S(1)}, u32[]{:S(2)}, u32[]{:S(2)}) async-start(f32[4,40,1024]{2,1,0:T(8,128)} %broadcast_in_dim.14), calls=%async_computation | async-start | bytes 1310720 | tf_op jit(solution)/shard_map/all_to_all | solution.py:354
  8.4 1.6 %copy-start.1 = (bf16[256,4096]{1,0:T(8,128)(2,1)S(1)}, bf16[256,4096]{1,0:T(8,128)(2,1)}, u32[]{:S(2)}) copy-start(bf16[256,4096]{1,0:T(8,128)(2,1)} %key_in.5) | copy-start | bytes 6291460
  10.6 1.2 copy-start.3
  25.7 1.0 copy-start.4
  35.0 0.8 copy-start.15
  35.8 0.8 copy-start.17
  36.6 19.0 %copy-start.11 = (f32[128,1024]{1,0:T(8,128)}, f32[128,1024]{1,0:T(8,128)S(1)}, u32[]{:S(2)}) copy-start(f32[128,1024]{1,0:T(8,128)S(1)} %get-tuple-element.18.carry.refs_7_) | copy-start | bytes 1572868
  36.6 19.0 %copy-start.13 = (f32[128,1024]{1,0:T(8,128)}, f32[128,1024]{1,0:T(8,128)S(1)}, u32[]{:S(2)}) copy-start(f32[128,1024]{1,0:T(8,128)S(1)} %get-tuple-element.19.refs_8_.carry) | copy-start | bytes 1572868
  36.6 15.7 %copy-start.5 = (bf16[256,1024]{1,0:T(8,128)(2,1)S(1)}, bf16[256,1024]{1,0:T(8,128)(2,1)}, u32[]{:S(2)}) copy-start(bf16[256,1024]{1,0:T(8,128)(2,1)} %copy-done.3) | copy-start | bytes 1572868
  36.6 21.1 %all-to-all-start.1 = ((f32[32,1,16,128]{3,2,1,0:T(8,128)}), f32[32,1,16,128]{3,2,1,0:T(8,128)S(1)}, u32[]{:S(2)}, u32[]{:S(2)}) async-start(f32[32,1,16,128]{3,2,1,0:T(8,128)} %bitcast.3), calls=%async_computation.1 | async-start | bytes 524288 | tf_op jit(solution)/shard_map/all_to_all | solution.py:377
  40.3 22.8 %collective-permute-start = (bf16[256,1024]{1,0:T(8,128)(2,1)}, bf16[256,1024]{1,0:T(8,128)(2,1)}, u32[]{:S(2)}, u32[]{:S(2)}) collective-permute-start(bf16[256,1024]{1,0:T(8,128)(2,1)} %shard_map.64.refs_0_), channel_id=1, source_target_pairs={{0,16},{4,20},{8,24},{12,28},{1,17},{5,21},{9,25},{13,29},{2,18},{... | collective-permute-start | bytes 1572872 | tf_op jit(solution)/shard_map/ppermute | solution.py:23
  44.8 25.8 %collective-permute-start.1 = (bf16[256,1024]{1,0:T(8,128)(2,1)}, bf16[256,1024]{1,0:T(8,128)(2,1)}, u32[]{:S(2)}, u32[]{:S(2)}) collective-permute-start(bf16[256,1024]{1,0:T(8,128)(2,1)} %shard_map.65.refs_1_), channel_id=1, source_target_pairs={{0,16},{4,20},{8,24},{12,28},{1,17},{5,21},{9,25},{13,29},{2,18},{... | collective-permute-start | bytes 1572872 | tf_op jit(solution)/shard_map/ppermute | solution.py:23
  50.2 32.1 %collective-permute-start.2 = (bf16[256,1024]{1,0:T(8,128)(2,1)}, bf16[256,1024]{1,0:T(8,128)(2,1)}, u32[]{:S(2)}, u32[]{:S(2)}) collective-permute-start(bf16[256,1024]{1,0:T(8,128)(2,1)} %shard_map.71), channel_id=1, source_target_pairs={{0,16},{4,20},{8,24},{12,28},{1,17},{5,21},{9,25},{13,29},{2,18},{... | collective-permute-start | bytes 1572872 | tf_op jit(solution)/shard_map/ppermute | solution.py:23
  55.5 63.0 %collective-permute-start.3 = (bf16[256,1024]{1,0:T(8,128)(2,1)}, bf16[256,1024]{1,0:T(8,128)(2,1)}, u32[]{:S(2)}, u32[]{:S(2)}) collective-permute-start(bf16[256,1024]{1,0:T(8,128)(2,1)} %shard_map.73), channel_id=1, source_target_pairs={{0,16},{4,20},{8,24},{12,28},{1,17},{5,21},{9,25},{13,29},{2,18},{... | collective-permute-start | bytes 1572872 | tf_op jit(solution)/shard_map/ppermute | solution.py:23
  58.4 34.9 %all-to-all-start.2 = ((f32[32,1,16,128]{3,2,1,0:T(8,128)}), f32[32,1,16,128]{3,2,1,0:T(8,128)S(1)}, u32[]{:S(2)}, u32[]{:S(2)}) async-start(f32[32,1,16,128]{3,2,1,0:T(8,128)} %shard_map.68), calls=%async_computation.2 | async-start | bytes 524288 | tf_op jit(solution)/shard_map/all_to_all | solution.py:377
  63.0 30.3 %copy-start.2 = (bf16[256,4096]{1,0:T(8,128)(2,1)S(1)}, bf16[256,4096]{1,0:T(8,128)(2,1)}, u32[]{:S(2)}) copy-start(bf16[256,4096]{1,0:T(8,128)(2,1)} %value.1) | copy-start | bytes 6291460
  64.3 1.0 copy-start.7
  71.7 1.0 copy-start.9
  93.3 1.0 copy-start.6
  94.4 1.2 %copy-start.8 = (f32[256,1024]{1,0:T(8,128)S(1)}, f32[256,1024]{1,0:T(8,128)}, u32[]{:S(2)}) copy-start(f32[256,1024]{1,0:T(8,128)} %copy-done.7) | copy-start | bytes 3145732
  95.6 1.2 %copy-start.10 = (f32[256,1024]{1,0:T(8,128)S(1)}, f32[256,1024]{1,0:T(8,128)}, u32[]{:S(2)}) copy-start(f32[256,1024]{1,0:T(8,128)} %copy-done.9) | copy-start | bytes 3145732
  96.8 1.0 copy-start.12
  97.9 1.0 copy-start.14
  98.9 1.0 copy-start.16
  100.0 1.0 copy-start.18

commit v4 on v3

v4 whole, which is shorter than its diff:
```python
import functools
import math

import jax
import jax.numpy as jnp
from jax import lax
from jax.experimental import pallas as pl
from jax.experimental.pallas import tpu as pltpu
from jax.sharding import PartitionSpec as P


FILTER_PARTS = 4
LANES = 128
SEGMENTS = 8
RAW_SHARES = (2, 2)
DONE_SHARES = (2, 2)
VMEM_BYTES = 16 << 20
F32 = jnp.float32


def from_behind(value, axis, steps):
    count = lax.axis_size(axis)
    return lax.ppermute(value, axis, [(source, source + steps) for source in range(count - steps)])


def ring(parts, axis):
    count = lax.axis_size(axis)
    moved = []
    for k, part in enumerate(parts):
        pairs = [(source, (source + k) % count) for source in range(count)]
        moved.append(lax.ppermute(part, axis, pairs) if k else part)
    return moved


def from_ring(refs, out):
    count = len(refs)
    mine = lax.axis_index("ch")
    for k, ref in enumerate(refs):
        out[(mine - k + count) % count] = ref[...]


def to_ring(whole, refs):
    count = len(refs)
    mine = lax.axis_index("ch")
    for k, ref in enumerate(refs):
        ref[...] = whole[(mine + k) % count]


def row_of(table, m):
    return jnp.broadcast_to(table[pl.ds(m, 1), :], (SEGMENTS, LANES))


def shifted(value, steps):
    row = lax.broadcasted_iota(jnp.int32, value.shape, 0)
    return jnp.where(row >= steps, pltpu.roll(value, steps, 0), 0.0)


def step_rows(i):
    return pl.ds(i * SEGMENTS, SEGMENTS)


def lanes(start):
    return pl.ds(pl.multiple_of(start, LANES), LANES)


def over_tiles(width, body):
    def step(t, carry):
        body(t)
        return carry

    lax.fori_loop(0, width // LANES, step, 0)


def at_tile(table, tile, first=0, count=None):
    per = table.shape[2] // LANES
    count = table.shape[1] if count is None else count
    return table.at[tile // per, pl.ds(first, count), lanes(tile % per * LANES)]


def scan_segments(table, tokens):
    modes = table.shape[1]
    steps = tokens.shape[0] // SEGMENTS
    decay = [row_of(table.at[0], m) for m in range(modes)]
    state = [tokens[step_rows(0), :]] * modes
    for i in range(1, steps):
        now = tokens[step_rows(i), :]
        state = [d * s + now for d, s in zip(decay, state)]
    chained = []
    for m in range(modes):
        value = state[m]
        for level in range(3):
            value = value + row_of(table.at[1 + level], m) * shifted(value, 1 << level)
        chained.append(value)
    return chained


def fill_jumps(table, rate, steps):
    table[0] = jnp.exp(-rate)
    for level in range(3):
        table[1 + level] = jnp.exp(-rate * float(steps << level))


def emit(table, weights, state, tokens, write):
    modes = table.shape[1]
    steps = tokens.shape[0] // SEGMENTS
    decay = [row_of(table.at[0], m) for m in range(modes)]
    weight = [row_of(weights, m) for m in range(modes)]
    for i in range(steps):
        now = tokens[step_rows(i), :]
        state = [d * s + now for d, s in zip(decay, state)]
        terms = [w * s for w, s in zip(weight, state)]
        while len(terms) > 1:
            terms = [a + b for a, b in zip(terms[::2], terms[1::2])]
        write(i, terms[0], now)


def fill_order(order, back=False):
    length = order.shape[0]
    row = lax.broadcasted_iota(jnp.int32, order.shape, 0)
    col = lax.broadcasted_iota(jnp.int32, order.shape, 1)
    inner = length // SEGMENTS if back else SEGMENTS
    order[...] = jnp.where(row % inner * (length // inner) + row // inner == col, 1.0, 0.0).astype(order.dtype)


def product_kernel(query, key_in, *refs, first):
    outs, order = refs[:-1], refs[-1]
    fill_order(order)
    start = first
    for out in outs:
        width = out.shape[1]
        wide = math.gcd(width, 4 * LANES)
        for at in range(0, width, wide):
            cols = pl.ds(start + at, wide)
            product = (query[:, cols].astype(F32) * key_in[:, cols].astype(F32)).astype(jnp.bfloat16)
            out[:, pl.ds(at, wide)] = jnp.dot(
                order[...], product, preferred_element_type=F32
            ).astype(jnp.bfloat16)
        start += width


def states_kernel(*refs, count, n_ch):
    products, parts = refs[:count], refs[count : count + n_ch]
    carries, sums = refs[count + n_ch : 2 * count + n_ch], refs[2 * count + n_ch : 2 * count + 2 * n_ch]
    rates, tokens, table, totals = refs[2 * count + 2 * n_ch :]
    from_ring(parts, rates)
    modes = rates.shape[1]
    first = 0
    for product, carry_out in zip(products, carries):
        steps = product.shape[0] // SEGMENTS

        def body(t, first=first, product=product, carry_out=carry_out):
            cols = lanes(t * LANES)
            tokens[...] = product[:, cols].astype(F32)
            fill_jumps(table, at_tile(rates, first + t)[...], steps)
            state = scan_segments(table, tokens)
            into = at_tile(totals, first + t)
            for m in range(modes):
                carry_out[pl.ds(m * SEGMENTS, SEGMENTS), cols] = shifted(state[m], 1)
                into[pl.ds(m, 1), :] = state[m][SEGMENTS - 1 :, :]

        over_tiles(product.shape[1], body)
        first += product.shape[1] // LANES
    to_ring(totals, sums)


def assemble_kernel(*refs):
    from_ring(refs[:-1], refs[-1])


def tails_kernel(*refs, length):
    *parts, rate, blocks, tails, whole = refs
    from_ring(parts, blocks)
    count = len(parts)
    running = None
    for q in reversed(range(count)):
        now = blocks[q]
        if running is not None:
            now = running + jnp.exp(-rate[...] * float(length * (count - 1 - q))) * now
        running = now
        tails[q] = running
    whole[...] = running


def heads_kernel(*refs, length, parts):
    blocks, rate, oldest, *rest = refs
    wholes, outs, heads = rest[: parts - 1], rest[parts - 1 : -1], rest[-1]
    count = blocks.shape[0]
    rates = rate[...]
    older = wholes[0][...]
    for j in range(1, parts - 1):
        older = older + jnp.exp(-rates * float(length * count * j)) * wholes[j][...]
    last = jnp.exp(-rates * float(length * count * (parts - 1)))
    jump = jnp.exp(-rates * float(length))
    running = None
    for q in range(count):
        earlier = older + last * oldest[q]
        if running is None:
            heads[q] = earlier
            running = blocks[q]
        else:
            heads[q] = running + jnp.exp(-rates * float(length * q)) * earlier
            running = jump * running + blocks[q]
    to_ring(heads, outs)


def over_kernel(past, rates, weighing, out, tokens, table, weights, *, span, first):
    steps = past.shape[0] // SEGMENTS
    modes = rates.shape[1]
    needed = lax.axis_index("ctx") >= FILTER_PARTS

    @pl.when(needed)
    def _():
        def body(t):
            cols = lanes(t * LANES)
            tokens[...] = past[:, cols].astype(F32)
            rate = at_tile(rates, first + t)[...]
            fill_jumps(table, rate, steps)
            weights[...] = at_tile(weighing, first + t, 0, modes)[...] * jnp.exp(-rate * float(span))
            state = [shifted(s, 1) for s in scan_segments(table, tokens)]

            def write(i, value, now):
                out[step_rows(i), cols] = value

            emit(table, weights, state, tokens, write)

        over_tiles(past.shape[1], body)

    @pl.when(jnp.logical_not(needed))
    def _():
        out[...] = jnp.zeros_like(out)


def ahead_kernel(product, rates, weighing, carry, out, tokens, table, weights, scr, *, span, first, n_ctx):
    modes = rates.shape[1]

    @pl.when(lax.axis_index("ctx") + FILTER_PARTS < n_ctx)
    def _():
        def body(t):
            cols = lanes(t * LANES)
            tokens[...] = product[:, cols].astype(F32)
            rate = at_tile(rates, first + t)[...]
            table[0] = jnp.exp(-rate)
            weights[...] = at_tile(weighing, first + t, 0, modes)[...] * jnp.exp(-rate * float(span))
            state = [carry[pl.ds(m * SEGMENTS, SEGMENTS), cols] for m in range(modes)]

            def write(i, value, now):
                scr[step_rows(i), :] = value

            emit(table, weights, state, tokens, write)
            out[:, cols] = scr[...].astype(jnp.bfloat16)

        over_tiles(product.shape[1], body)


def gated(back, mixed, value):
    plain = jnp.dot(back[...], mixed, preferred_element_type=F32)
    return (value.astype(F32) * plain).astype(jnp.bfloat16)


def finish_kernel(*refs, count, n_ch):
    products, carries, overs = refs[:count], refs[count : 2 * count], refs[2 * count : 3 * count - 1]
    refs = refs[3 * count - 1 :]
    befores, (rates, weighing, value, out, rest) = refs[:n_ch], refs[n_ch : n_ch + 5]
    tokens, table, weights, scr, back, before, mixed, done, sems = refs[n_ch + 5 :]
    modes = rates.shape[1]
    length = value.shape[0]
    steps = length // SEGMENTS
    from_ring(befores, before)
    fill_order(back, True)
    copies = [None, None]
    first = 0
    for k in range(count):
        product, carry = products[k], carries[k]
        width = product.shape[1]
        slot = k % 2
        last = k == count - 1

        def body(t, first=first, product=product, carry=carry, last=last, k=k):
            cols = lanes(t * LANES)
            tokens[...] = product[:, cols].astype(F32)
            own = at_tile(rates, first + t)
            table[0] = jnp.exp(-own[...])
            weights[...] = at_tile(weighing, first + t, 0, modes)[...]
            gain = row_of(at_tile(weighing, first + t, modes, 1), 0)
            begin = (lax.broadcasted_iota(jnp.int32, (SEGMENTS, LANES), 0) * steps).astype(F32)
            ahead = at_tile(before, first + t)
            state = []
            for m in range(modes):
                state.append(
                    carry[pl.ds(m * SEGMENTS, SEGMENTS), cols]
                    + jnp.exp(-row_of(own, m) * begin) * row_of(ahead, m)
                )
            if last:

                def write(i, value, now):
                    rest[step_rows(i), cols] = value + gain * now

                emit(table, weights, state, tokens, write)
            else:

                def write(i, value, now):
                    scr[step_rows(i), :] = value + gain * now

                emit(table, weights, state, tokens, write)
                mixed[:, cols] = (scr[...] - overs[k][:, cols].astype(F32)).astype(jnp.bfloat16)

        over_tiles(width, body)
        if not last:
            if copies[slot] is not None:
                copies[slot].wait()
            wide = math.gcd(width, 4 * LANES)
            for at in range(0, width, wide):
                cols = pl.ds(at, wide)
                done[slot, :, cols] = gated(back, mixed[:, cols], value[:, pl.ds(first * LANES + at, wide)])
            copies[slot] = pltpu.make_async_copy(
                done.at[slot, :, pl.ds(0, width)], out.at[:, pl.ds(first * LANES, width)], sems.at[slot]
            )
            copies[slot].start()
        first += width // LANES
    for copy in copies:
        if copy is not None:
            copy.wait()


def last_kernel(rest, over, value, partial, out, back, done, sem):
    del partial
    _, width = rest.shape
    first = value.shape[1] - width
    fill_order(back, True)
    wide = math.gcd(width, 4 * LANES)
    copies = []
    for k, at in enumerate(range(0, width, wide)):
        cols = pl.ds(at, wide)
        mixed = (rest[:, cols] - over[:, cols].astype(F32)).astype(jnp.bfloat16)
        done[:, cols] = gated(back, mixed, value[:, pl.ds(first + at, wide)])
        copies.append(
            pltpu.make_async_copy(done.at[:, cols], out.at[:, pl.ds(first + at, wide)], sem.at[k])
        )
        copies[-1].start()
    for copy in copies:
        copy.wait()


def shard_program(query, key_in, value, residues, decay_rates, skip_gain):
    length, channels = query.shape
    group, modes = residues.shape
    n_ch, n_ctx = lax.axis_size("ch"), lax.axis_size("ctx")
    span = FILTER_PARTS * length * n_ch
    bf16 = jnp.bfloat16

    shares = RAW_SHARES + DONE_SHARES
    unit = channels // sum(shares)
    widths = [unit * share for share in shares]
    firsts = [sum(widths[:k]) for k in range(len(widths))]
    count, n_raw = len(widths), len(RAW_SHARES)

    vmem = pl.BlockSpec(memory_space=pltpu.VMEM)
    anywhere = pl.BlockSpec(memory_space=pl.ANY)

    def shape(rows, columns, dtype=F32):
        return jax.ShapeDtypeStruct((rows, columns), dtype)

    def stack(rows):
        return jax.ShapeDtypeStruct((n_ch, rows, group), F32)

    tokens_scr = pltpu.VMEM((length, LANES), F32)
    table_scr = pltpu.VMEM((4, modes, LANES), F32)
    weights_scr = pltpu.VMEM((modes, LANES), F32)
    order_scr = pltpu.VMEM((length, length), bf16)

    def call(kernel, out_shape, scratch, args, **options):
        specs = dict(in_specs=[vmem] * len(args), out_specs=jax.tree.map(lambda _: vmem, out_shape))
        specs.update(options)
        return pl.pallas_call(
            kernel,
            out_shape=out_shape,
            scratch_shapes=scratch,
            compiler_params=pltpu.CompilerParams(vmem_limit_bytes=VMEM_BYTES),
            **specs,
        )(*args)

    own_rate = decay_rates.T
    rate_parts = ring([own_rate] * n_ch, "ch")

    products, pasts = [], []
    batches = [[k] for k in range(n_raw)] + [list(range(n_raw, count))]
    for k, batch in enumerate(batches):
        products += call(
            functools.partial(product_kernel, first=firsts[batch[0]]),
            [shape(length, widths[j], bf16) for j in batch],
            [order_scr],
            (query, key_in),
        )
        if k < n_raw:
            pasts.append(from_behind(products[k], "ctx", FILTER_PARTS))

    rows = -(-(modes + 1) // SEGMENTS) * SEGMENTS
    own_weight = jnp.concatenate(
        [residues.T, skip_gain[None], jnp.zeros((rows - modes - 1, group), F32)]
    )
    weight_parts = ring([own_weight] * n_ch, "ch")

    outs = call(
        functools.partial(states_kernel, count=count, n_ch=n_ch),
        [shape(modes * SEGMENTS, width) for width in widths] + [shape(modes, group)] * n_ch + [stack(modes)],
        [tokens_scr, table_scr, pltpu.VMEM((n_ch, modes, group), F32)],
        (*products, *rate_parts),
    )
    carries, sums, rates = outs[:count], outs[count:-1], outs[-1]
    sums = ring(sums, "ch")
    weighing = call(assemble_kernel, stack(rows), [], weight_parts)

    overs = []

    def add_over(k):
        overs.append(
            call(
                functools.partial(over_kernel, span=span, first=firsts[k] // LANES),
                shape(length, widths[k]),
                [tokens_scr, table_scr, weights_scr],
                (pasts[k], rates, weighing),
            )
        )

    def ahead_of(k):
        return call(
            functools.partial(ahead_kernel, span=span, first=firsts[k] // LANES, n_ctx=n_ctx),
            shape(length, widths[k], bf16),
            [tokens_scr, table_scr, weights_scr, tokens_scr],
            (products[k], rates, weighing, carries[k]),
        )

    aheads = [ahead_of(k) for k in range(n_raw, count)]
    for k in range(n_raw):
        add_over(k)

    blocks, tails, whole = call(
        functools.partial(tails_kernel, length=length),
        [stack(modes), stack(modes), shape(modes, group)],
        [],
        (*sums, own_rate),
    )
    oldest = from_behind(tails, "ctx", FILTER_PARTS)
    wholes = []
    for j in range(1, FILTER_PARTS):
        wholes.append(from_behind(whole, "ctx", j))
    for ahead in aheads:
        overs.append(from_behind(ahead, "ctx", FILTER_PARTS))
    heads = call(
        functools.partial(heads_kernel, length=length, parts=FILTER_PARTS),
        [shape(modes, group)] * n_ch,
        [pltpu.VMEM((n_ch, modes, group), F32)],
        (blocks, own_rate, oldest, *wholes),
    )
    befores = ring(heads, "ch")

    widest = max(widths)
    partial, rest = call(
        functools.partial(finish_kernel, count=count, n_ch=n_ch),
        [shape(length, channels, bf16), shape(length, widths[-1])],
        [
            tokens_scr,
            table_scr,
            weights_scr,
            tokens_scr,
            order_scr,
            pltpu.VMEM((n_ch, modes, group), F32),
            pltpu.VMEM((length, widest), bf16),
            pltpu.VMEM((2, length, widest), bf16),
            pltpu.SemaphoreType.DMA((2,)),
        ],
        (*products, *carries, *overs[:-1], *befores, rates, weighing, value),
        out_specs=[anywhere, vmem],
    )
    return call(
        last_kernel,
        shape(length, channels, bf16),
        [order_scr, pltpu.VMEM((length, widths[-1]), bf16), pltpu.SemaphoreType.DMA((8,))],
        (rest, overs[-1], value, partial),
        in_specs=[vmem, vmem, vmem, anywhere],
        out_specs=anywhere,
        input_output_aliases={3: 0},
    )


def solution(mesh):
    return jax.shard_map(
        shard_program,
        mesh=mesh,
        in_specs=(
            P(("ctx", "ch"), None),
            P(("ctx", "ch"), None),
            P(("ctx", "ch"), None),
            P("ch", None),
            P("ch", None),
            P("ch"),
        ),
        out_specs=P(("ctx", "ch"), None),
        check_vma=False,
    )
```

time: 122 us -> 107 us (0.88)
  the two profiles are of different devices: /device:TPU:0 before, /device:TPU:4 now
where the time goes in v4:
time: 107 us; the launch traced here: 106 us
  waiting for transfers between devices  42.3 us (40%)
  starting transfers between devices  31.7 us (30%)
  Pallas kernels  28.2 us (26%)
  local copies, waits for them, and re-layouts  3.63 us (3%)
    ppermute x8, waiting for transfers between devices, from_behind(): lax.ppermute(value, axis, [(source, source + steps) for source in range(c...  40.9 us
    pallas_call x13, Pallas kernels, call(): pl.pallas_call(kernel, out_shape=out_shape, scratch_shapes=scratch, compi...  28.2 us
    ppermute x12, starting transfers between devices, ring(): moved.append(lax.ppermute(part, axis, pairs) if k else part)  19 us
    ppermute x8, starting transfers between devices, from_behind(): lax.ppermute(value, axis, [(source, source + steps) for source in range(c...  12.7 us
    unnamed x12, local copies, waits for them, and re-layouts  3.55 us
  transfers between devices with their start and end apart: 20, of which 6 were waited for; matrix products, arithmetic and copies ran while one was open for 0% of the time, Pallas kernels for 19%

profile of v4, /device:TPU:4, one launch (start us, length us, event | category | flops | bytes accessed | tf_op | source)
XLA Modules:
  0.0 106.2 jit_solution(70190353431583487)
XLA Ops:
  0.0 1.6 %collective-permute-start = (f32[16,1024]{1,0:T(8,128)}, f32[16,1024]{1,0:T(8,128)S(1)}, u32[]{:S(2)}, u32[]{:S(2)}) collective-permute-start(f32[16,1024]{1,0:T(8,128)} %bitcast.3), channel_id=1, source_target_pairs={{0,1},{1,2},{2,3},{3,0},{4,5},{5,6},{6,7},{7,4},{8,9},{9,10},{10,1... | collective-permute-start | bytes 196616 | tf_op jit(solution)/shard_map/ppermute | solution.py:31
  1.6 2.6 %collective-permute-start.1 = (f32[16,1024]{1,0:T(8,128)}, f32[16,1024]{1,0:T(8,128)S(1)}, u32[]{:S(2)}, u32[]{:S(2)}) collective-permute-start(f32[16,1024]{1,0:T(8,128)} %bitcast.4), channel_id=1, source_target_pairs={{0,2},{1,3},{2,0},{3,1},{4,6},{5,7},{6,4},{7,5},{8,10},{9,11},{10,... | collective-permute-start | bytes 196616 | tf_op jit(solution)/shard_map/ppermute | solution.py:31
  4.2 1.3 %collective-permute-start.2 = (f32[16,1024]{1,0:T(8,128)}, f32[16,1024]{1,0:T(8,128)S(1)}, u32[]{:S(2)}, u32[]{:S(2)}) collective-permute-start(f32[16,1024]{1,0:T(8,128)} %bitcast.5), channel_id=1, source_target_pairs={{0,3},{1,0},{2,1},{3,2},{4,7},{5,4},{6,5},{7,6},{8,11},{9,8},{10,9... | collective-permute-start | bytes 196616 | tf_op jit(solution)/shard_map/ppermute | solution.py:31
  5.5 1.6 %copy-done = bf16[256,4096]{1,0:T(8,128)(2,1)S(1)} copy-done((bf16[256,4096]{1,0:T(8,128)(2,1)S(1)}, bf16[256,4096]{1,0:T(8,128)(2,1)}, u32[]{:S(2)}) %copy-start) | copy-done | bytes 2097176
  7.1 1.6 %copy-done.1 = bf16[256,4096]{1,0:T(8,128)(2,1)S(1)} copy-done((bf16[256,4096]{1,0:T(8,128)(2,1)S(1)}, bf16[256,4096]{1,0:T(8,128)(2,1)}, u32[]{:S(2)}) %copy-start.1) | copy-done | bytes 2097176
  8.7 0.5 shard_map.66
  10.5 6.4 %shard_map.67 = (f32[128,1024]{1,0:T(8,128)S(1)}, f32[128,1024]{1,0:T(8,128)S(1)}, f32[128,1024]{1,0:T(8,128)S(1)}, f32[128,1024]{1,0:T(8,128)S(1)}, f32[16,1024...) custom-call(bf16[256,1024]{1,0:T(8,128)(2,1)S(1)} %shard_map.64.refs, ...), custom_call_target="tpu_custom_call" | custom-call | tf_op jit(solution)/shard_map/pallas_call | solution.py:374
  17.2 2.7 %collective-permute-start.11 = (f32[16,1024]{1,0:T(8,128)S(1)}, f32[16,1024]{1,0:T(8,128)S(1)}, u32[]{:S(2)}, u32[]{:S(2)}) collective-permute-start(f32[16,1024]{1,0:T(8,128)S(1)} %get-tuple-element.35), channel_id=1, source_target_pairs={{0,3},{1,0},{2,1},{3,2},{4,7},{5,4},{6,5},{7,6},{8,11},{9,8},{10,9... | collective-permute-start | bytes 196616 | tf_op jit(solution)/shard_map/ppermute | solution.py:31
  20.0 1.2 %collective-permute-start.4 = (f32[24,1024]{1,0:T(8,128)S(1)}, f32[24,1024]{1,0:T(8,128)S(1)}, u32[]{:S(2)}, u32[]{:S(2)}) collective-permute-start(f32[24,1024]{1,0:T(8,128)S(1)} %maximum_maximum_fusion.refs_0_), channel_id=1, source_target_pairs={{0,1},{1,2},{2,3},{3,0},{4,5},{5,6},{6,7},{7,4},{8,9},{9,10},{10,1... | collective-permute-start | bytes 294920 | tf_op jit(solution)/shard_map/ppermute | solution.py:31
  21.2 3.2 %collective-permute-start.5 = (f32[24,1024]{1,0:T(8,128)S(1)}, f32[24,1024]{1,0:T(8,128)S(1)}, u32[]{:S(2)}, u32[]{:S(2)}) collective-permute-start(f32[24,1024]{1,0:T(8,128)S(1)} %maximum_maximum_fusion.refs_0_), channel_id=1, source_target_pairs={{0,2},{1,3},{2,0},{3,1},{4,6},{5,7},{6,4},{7,5},{8,10},{9,11},{10,... | collective-permute-start | bytes 294920 | tf_op jit(solution)/shard_map/ppermute | solution.py:31
  24.4 1.3 %collective-permute-start.6 = (f32[24,1024]{1,0:T(8,128)S(1)}, f32[24,1024]{1,0:T(8,128)S(1)}, u32[]{:S(2)}, u32[]{:S(2)}) collective-permute-start(f32[24,1024]{1,0:T(8,128)S(1)} %maximum_maximum_fusion.refs_0_), channel_id=1, source_target_pairs={{0,3},{1,0},{2,1},{3,2},{4,7},{5,4},{6,5},{7,6},{8,11},{9,8},{10,9... | collective-permute-start | bytes 294920 | tf_op jit(solution)/shard_map/ppermute | solution.py:31
  25.7 1.3 %collective-permute-start.7 = (bf16[256,1024]{1,0:T(8,128)(2,1)S(1)}, bf16[256,1024]{1,0:T(8,128)(2,1)S(1)}, u32[]{:S(2)}, u32[]{:S(2)}) collective-permute-start(bf16[256,1024]{1,0:T(8,128)(2,1)S(1)} %shard_map.65.refs_1_), channel_id=1, source_target_pairs={{0,16},{4,20},{8,24},{12,28},{1,17},{5,21},{9,25},{13,29},{2,18},{... | collective-permute-start | bytes 1572872 | tf_op jit(solution)/shard_map/ppermute | solution.py:23
  27.0 1.3 %collective-permute-start.3 = (bf16[256,1024]{1,0:T(8,128)(2,1)S(1)}, bf16[256,1024]{1,0:T(8,128)(2,1)S(1)}, u32[]{:S(2)}, u32[]{:S(2)}) collective-permute-start(bf16[256,1024]{1,0:T(8,128)(2,1)S(1)} %shard_map.64.refs_0_), channel_id=1, source_target_pairs={{0,16},{4,20},{8,24},{12,28},{1,17},{5,21},{9,25},{13,29},{2,18},{... | collective-permute-start | bytes 1572872 | tf_op jit(solution)/shard_map/ppermute | solution.py:23
  28.3 0.5 collective-permute-done.4.refs_1_
  28.8 1.9 %collective-permute-start.13 = (f32[16,1024]{1,0:T(8,128)S(1)}, f32[16,1024]{1,0:T(8,128)S(1)}, u32[]{:S(2)}, u32[]{:S(2)}) collective-permute-start(f32[16,1024]{1,0:T(8,128)S(1)} %get-tuple-element.38), channel_id=1, source_target_pairs={{0,4},{4,8},{8,12},{12,16},{16,20},{20,24},{24,28},{1,5},{5,9},{9,... | collective-permute-start | bytes 196616 | tf_op jit(solution)/shard_map/ppermute | solution.py:23
  30.7 0.9 collective-permute-done.5.refs_2_
  31.7 1.3 %collective-permute-start.8 = (bf16[256,1024]{1,0:T(8,128)(2,1)S(1)}, bf16[256,1024]{1,0:T(8,128)(2,1)S(1)}, u32[]{:S(2)}, u32[]{:S(2)}) collective-permute-start(bf16[256,1024]{1,0:T(8,128)(2,1)S(1)} %shard_map.71), channel_id=1, source_target_pairs={{0,16},{4,20},{8,24},{12,28},{1,17},{5,21},{9,25},{13,29},{2,18},{... | collective-permute-start | bytes 1572872 | tf_op jit(solution)/shard_map/ppermute | solution.py:23
  33.0 1.3 %collective-permute-start.19 = (bf16[256,1024]{1,0:T(8,128)(2,1)S(1)}, bf16[256,1024]{1,0:T(8,128)(2,1)S(1)}, u32[]{:S(2)}, u32[]{:S(2)}) collective-permute-start(bf16[256,1024]{1,0:T(8,128)(2,1)S(1)} %shard_map.75), channel_id=1, source_target_pairs={{0,16},{4,20},{8,24},{12,28},{1,17},{5,21},{9,25},{13,29},{2,18},{... | collective-permute-start | bytes 1572872 | tf_op jit(solution)/shard_map/ppermute | solution.py:23
  34.3 1.0 collective-permute-done.13.refs_3_
  35.4 2.4 %collective-permute-start.14 = (f32[16,1024]{1,0:T(8,128)S(1)}, f32[16,1024]{1,0:T(8,128)S(1)}, u32[]{:S(2)}, u32[]{:S(2)}) collective-permute-start(f32[16,1024]{1,0:T(8,128)S(1)} %get-tuple-element.38), channel_id=1, source_target_pairs={{0,8},{4,12},{8,16},{12,20},{16,24},{20,28},{1,9},{5,13},{9,17},{1... | collective-permute-start | bytes 196616 | tf_op jit(solution)/shard_map/ppermute | solution.py:23
  37.8 8.0 %collective-permute-done.14.refs_4_ = f32[16,1024]{1,0:T(8,128)S(1)} collective-permute-done((f32[16,1024]{1,0:T(8,128)S(1)}, f32[16,1024]{1,0:T(8,128)S(1)}, u32[]{:S(2)}, u32[]{:S(2)}) %collective-permute-start.14) | collective-permute-done | bytes 65568 | tf_op jit(solution)/shard_map/ppermute | solution.py:23
  45.8 1.9 %collective-permute-start.15 = (f32[16,1024]{1,0:T(8,128)S(1)}, f32[16,1024]{1,0:T(8,128)S(1)}, u32[]{:S(2)}, u32[]{:S(2)}) collective-permute-start(f32[16,1024]{1,0:T(8,128)S(1)} %get-tuple-element.38), channel_id=1, source_target_pairs={{0,12},{4,16},{8,20},{12,24},{16,28},{1,13},{5,17},{9,21},{13,25},... | collective-permute-start | bytes 196616 | tf_op jit(solution)/shard_map/ppermute | solution.py:23
  47.7 23.9 %collective-permute-done.15.refs_5_ = f32[16,1024]{1,0:T(8,128)S(1)} collective-permute-done((f32[16,1024]{1,0:T(8,128)S(1)}, f32[16,1024]{1,0:T(8,128)S(1)}, u32[]{:S(2)}, u32[]{:S(2)}) %collective-permute-start.15) | collective-permute-done | bytes 65568 | tf_op jit(solution)/shard_map/ppermute | solution.py:23
  71.6 1.3 %collective-permute-start.12 = (f32[4,16,1024]{2,1,0:T(8,128)S(1)}, f32[4,16,1024]{2,1,0:T(8,128)S(1)}, u32[]{:S(2)}, u32[]{:S(2)}) collective-permute-start(f32[4,16,1024]{2,1,0:T(8,128)S(1)} %get-tuple-element.37), channel_id=1, source_target_pairs={{0,16},{4,20},{8,24},{12,28},{1,17},{5,21},{9,25},{13,29},{2,18},{... | collective-permute-start | bytes 786440 | tf_op jit(solution)/shard_map/ppermute | solution.py:23
  72.9 8.0 %collective-permute-done.12.refs_2_ = f32[4,16,1024]{2,1,0:T(8,128)S(1)} collective-permute-done((f32[4,16,1024]{2,1,0:T(8,128)S(1)}, f32[4,16,1024]{2,1,0:T(8,128)S(1)}, u32[]{:S(2)}, u32[]{:S(2)}) %collective-permute-start.12) | collective-permute-done | bytes 262176 | tf_op jit(solution)/shard_map/ppermute | solution.py:23
  81.0 1.8 %collective-permute-start.16 = (f32[16,1024]{1,0:T(8,128)S(1)}, f32[16,1024]{1,0:T(8,128)S(1)}, u32[]{:S(2)}, u32[]{:S(2)}) collective-permute-start(f32[16,1024]{1,0:T(8,128)S(1)} %get-tuple-element.40), channel_id=1, source_target_pairs={{0,1},{1,2},{2,3},{3,0},{4,5},{5,6},{6,7},{7,4},{8,9},{9,10},{10,1... | collective-permute-start | bytes 196616 | tf_op jit(solution)/shard_map/ppermute | solution.py:31
  82.8 0.4 collective-permute-start.17
  83.2 2.6 %collective-permute-start.18 = (f32[16,1024]{1,0:T(8,128)S(1)}, f32[16,1024]{1,0:T(8,128)S(1)}, u32[]{:S(2)}, u32[]{:S(2)}) collective-permute-start(f32[16,1024]{1,0:T(8,128)S(1)} %get-tuple-element.42), channel_id=1, source_target_pairs={{0,3},{1,0},{2,1},{3,2},{4,7},{5,4},{6,5},{7,6},{8,11},{9,8},{10,9... | collective-permute-start | bytes 196616 | tf_op jit(solution)/shard_map/ppermute | solution.py:31
  85.8 3.7 %shard_map.70.refs_9_ = f32[256,1024]{1,0:T(8,128)S(1)} custom-call(bf16[256,1024]{1,0:T(8,128)(2,1)S(1)} %collective-permute-done.7.past, f32[4,16,1024]{2,1,0:T(8,128)S(1)} %get-tuple-element.31.rates.refs_15_, f32[4,24,1024]{2,1,0:T(8,128)S(1)} %shard_map.68.weighing.refs_16_), custom_call_target="tpu_custom_call" | custom-call | tf_op jit(solution)/shard_map/pallas_call | solution.py:374
  89.4 3.7 %shard_map.69.refs_8_ = f32[256,1024]{1,0:T(8,128)S(1)} custom-call(bf16[256,1024]{1,0:T(8,128)(2,1)S(1)} %collective-permute-done.3.past, f32[4,16,1024]{2,1,0:T(8,128)S(1)} %get-tuple-element.31.rates.refs_15_, f32[4,24,1024]{2,1,0:T(8,128)S(1)} %shard_map.68.weighing.refs_16_), custom_call_target="tpu_custom_call" | custom-call | tf_op jit(solution)/shard_map/pallas_call | solution.py:374
  93.2 11.8 %shard_map.74 = (bf16[256,4096]{1,0:T(8,128)(2,1)}, f32[256,1024]{1,0:T(8,128)S(1)}) custom-call(bf16[256,1024]{1,0:T(8,128)(2,1)S(1)} %shard_map.64.refs_0_, bf16[256,1024]{1,0:T(8,128)(2,1)S(1)} %shard_map.65.refs_1_, bf16[256,1024]{1,0:T(8,128)(2,1)S(1)} %get-tuple-element.25.refs_2_.product, bf16[256,1024]{1,0:T(8,128)(2,1)S(1)} %get-tuple-element.26.refs_3_.product, ...), custom_call_target="tpu_custom_call" | custom-call | tf_op jit(solution)/shard_map/pallas_call | solution.py:374
  105.0 1.1 %shard_map.76 = bf16[256,4096]{1,0:T(8,128)(2,1)} custom-call(f32[256,1024]{1,0:T(8,128)S(1)} %get-tuple-element.43.rest, bf16[256,1024]{1,0:T(8,128)(2,1)S(1)} %collective-permute-done.19.over, bf16[256,4096]{1,0:T(8,128)(2,1)S(1)} %copy-done.2, bf16[256,4096]{1,0:T(8,128)(2,1)} %get-tuple-element.44.partial), custom_call_target="tpu_custom_call", output_to_operand_aliasing={{}: (3, {})} | custom-call | tf_op jit(solution)/shard_map/pallas_call | solution.py:374
  (36 shorter events, 1.9 us)
Async XLA Ops:
  0.0 10.1 %collective-permute-start = (f32[16,1024]{1,0:T(8,128)}, f32[16,1024]{1,0:T(8,128)S(1)}, u32[]{:S(2)}, u32[]{:S(2)}) collective-permute-start(f32[16,1024]{1,0:T(8,128)} %bitcast.3), channel_id=1, source_target_pairs={{0,1},{1,2},{2,3},{3,0},{4,5},{5,6},{6,7},{7,4},{8,9},{9,10},{10,1... | collective-permute-start | bytes 196616 | tf_op jit(solution)/shard_map/ppermute | solution.py:31
  1.6 8.5 %collective-permute-start.1 = (f32[16,1024]{1,0:T(8,128)}, f32[16,1024]{1,0:T(8,128)S(1)}, u32[]{:S(2)}, u32[]{:S(2)}) collective-permute-start(f32[16,1024]{1,0:T(8,128)} %bitcast.4), channel_id=1, source_target_pairs={{0,2},{1,3},{2,0},{3,1},{4,6},{5,7},{6,4},{7,5},{8,10},{9,11},{10,... | collective-permute-start | bytes 196616 | tf_op jit(solution)/shard_map/ppermute | solution.py:31
  4.2 5.9 %collective-permute-start.2 = (f32[16,1024]{1,0:T(8,128)}, f32[16,1024]{1,0:T(8,128)S(1)}, u32[]{:S(2)}, u32[]{:S(2)}) collective-permute-start(f32[16,1024]{1,0:T(8,128)} %bitcast.5), channel_id=1, source_target_pairs={{0,3},{1,0},{2,1},{3,2},{4,7},{5,4},{6,5},{7,6},{8,11},{9,8},{10,9... | collective-permute-start | bytes 196616 | tf_op jit(solution)/shard_map/ppermute | solution.py:31
  5.5 1.6 %copy-start = (bf16[256,4096]{1,0:T(8,128)(2,1)S(1)}, bf16[256,4096]{1,0:T(8,128)(2,1)}, u32[]{:S(2)}) copy-start(bf16[256,4096]{1,0:T(8,128)(2,1)} %query.5) | copy-start | bytes 6291460
  7.1 1.6 %copy-start.1 = (bf16[256,4096]{1,0:T(8,128)(2,1)S(1)}, bf16[256,4096]{1,0:T(8,128)(2,1)}, u32[]{:S(2)}) copy-start(bf16[256,4096]{1,0:T(8,128)(2,1)} %key_in.5) | copy-start | bytes 6291460
  9.6 0.8 copy-start.3
  10.0 9.9 %copy-start.4 = (f32[1024,16]{0,1:T(8,128)S(1)}, f32[1024,16]{0,1:T(8,128)}, u32[]{:S(2)}) copy-start(f32[1024,16]{0,1:T(8,128)} %param.9) | copy-start | bytes 196612
  10.0 9.9 %copy-start.5 = (f32[1024]{0:T(1024)S(1)}, f32[1024]{0:T(1024)}, u32[]{:S(2)}) copy-start(f32[1024]{0:T(1024)} %param.11) | copy-start | bytes 12292
  16.8 7.6 %collective-permute-start.10 = (f32[16,1024]{1,0:T(8,128)S(1)}, f32[16,1024]{1,0:T(8,128)S(1)}, u32[]{:S(2)}, u32[]{:S(2)}) collective-permute-start(f32[16,1024]{1,0:T(8,128)S(1)} %get-tuple-element.34), channel_id=1, source_target_pairs={{0,2},{1,3},{2,0},{3,1},{4,6},{5,7},{6,4},{7,5},{8,10},{9,11},{10,... | collective-permute-start | bytes 196616 | tf_op jit(solution)/shard_map/ppermute | solution.py:31
  17.2 8.5 %collective-permute-start.11 = (f32[16,1024]{1,0:T(8,128)S(1)}, f32[16,1024]{1,0:T(8,128)S(1)}, u32[]{:S(2)}, u32[]{:S(2)}) collective-permute-start(f32[16,1024]{1,0:T(8,128)S(1)} %get-tuple-element.35), channel_id=1, source_target_pairs={{0,3},{1,0},{2,1},{3,2},{4,7},{5,4},{6,5},{7,6},{8,11},{9,8},{10,9... | collective-permute-start | bytes 196616 | tf_op jit(solution)/shard_map/ppermute | solution.py:31
  19.9 7.0 %collective-permute-start.9 = (f32[16,1024]{1,0:T(8,128)S(1)}, f32[16,1024]{1,0:T(8,128)S(1)}, u32[]{:S(2)}, u32[]{:S(2)}) collective-permute-start(f32[16,1024]{1,0:T(8,128)S(1)} %get-tuple-element.33), channel_id=1, source_target_pairs={{0,1},{1,2},{2,3},{3,0},{4,5},{5,6},{6,7},{7,4},{8,9},{9,10},{10,1... | collective-permute-start | bytes 196616 | tf_op jit(solution)/shard_map/ppermute | solution.py:31
  20.0 8.8 %collective-permute-start.4 = (f32[24,1024]{1,0:T(8,128)S(1)}, f32[24,1024]{1,0:T(8,128)S(1)}, u32[]{:S(2)}, u32[]{:S(2)}) collective-permute-start(f32[24,1024]{1,0:T(8,128)S(1)} %maximum_maximum_fusion.refs_0_), channel_id=1, source_target_pairs={{0,1},{1,2},{2,3},{3,0},{4,5},{5,6},{6,7},{7,4},{8,9},{9,10},{10,1... | collective-permute-start | bytes 294920 | tf_op jit(solution)/shard_map/ppermute | solution.py:31
  21.2 10.5 %collective-permute-start.5 = (f32[24,1024]{1,0:T(8,128)S(1)}, f32[24,1024]{1,0:T(8,128)S(1)}, u32[]{:S(2)}, u32[]{:S(2)}) collective-permute-start(f32[24,1024]{1,0:T(8,128)S(1)} %maximum_maximum_fusion.refs_0_), channel_id=1, source_target_pairs={{0,2},{1,3},{2,0},{3,1},{4,6},{5,7},{6,4},{7,5},{8,10},{9,11},{10,... | collective-permute-start | bytes 294920 | tf_op jit(solution)/shard_map/ppermute | solution.py:31
  24.4 7.2 %collective-permute-start.6 = (f32[24,1024]{1,0:T(8,128)S(1)}, f32[24,1024]{1,0:T(8,128)S(1)}, u32[]{:S(2)}, u32[]{:S(2)}) collective-permute-start(f32[24,1024]{1,0:T(8,128)S(1)} %maximum_maximum_fusion.refs_0_), channel_id=1, source_target_pairs={{0,3},{1,0},{2,1},{3,2},{4,7},{5,4},{6,5},{7,6},{8,11},{9,8},{10,9... | collective-permute-start | bytes 294920 | tf_op jit(solution)/shard_map/ppermute | solution.py:31
  25.7 57.1 %collective-permute-start.7 = (bf16[256,1024]{1,0:T(8,128)(2,1)S(1)}, bf16[256,1024]{1,0:T(8,128)(2,1)S(1)}, u32[]{:S(2)}, u32[]{:S(2)}) collective-permute-start(bf16[256,1024]{1,0:T(8,128)(2,1)S(1)} %shard_map.65.refs_1_), channel_id=1, source_target_pairs={{0,16},{4,20},{8,24},{12,28},{1,17},{5,21},{9,25},{13,29},{2,18},{... | collective-permute-start | bytes 1572872 | tf_op jit(solution)/shard_map/ppermute | solution.py:23
  27.0 56.2 %collective-permute-start.3 = (bf16[256,1024]{1,0:T(8,128)(2,1)S(1)}, bf16[256,1024]{1,0:T(8,128)(2,1)S(1)}, u32[]{:S(2)}, u32[]{:S(2)}) collective-permute-start(bf16[256,1024]{1,0:T(8,128)(2,1)S(1)} %shard_map.64.refs_0_), channel_id=1, source_target_pairs={{0,16},{4,20},{8,24},{12,28},{1,17},{5,21},{9,25},{13,29},{2,18},{... | collective-permute-start | bytes 1572872 | tf_op jit(solution)/shard_map/ppermute | solution.py:23
  28.8 6.6 %collective-permute-start.13 = (f32[16,1024]{1,0:T(8,128)S(1)}, f32[16,1024]{1,0:T(8,128)S(1)}, u32[]{:S(2)}, u32[]{:S(2)}) collective-permute-start(f32[16,1024]{1,0:T(8,128)S(1)} %get-tuple-element.38), channel_id=1, source_target_pairs={{0,4},{4,8},{8,12},{12,16},{16,20},{20,24},{24,28},{1,5},{5,9},{9,... | collective-permute-start | bytes 196616 | tf_op jit(solution)/shard_map/ppermute | solution.py:23
  31.7 61.5 %collective-permute-start.8 = (bf16[256,1024]{1,0:T(8,128)(2,1)S(1)}, bf16[256,1024]{1,0:T(8,128)(2,1)S(1)}, u32[]{:S(2)}, u32[]{:S(2)}) collective-permute-start(bf16[256,1024]{1,0:T(8,128)(2,1)S(1)} %shard_map.71), channel_id=1, source_target_pairs={{0,16},{4,20},{8,24},{12,28},{1,17},{5,21},{9,25},{13,29},{2,18},{... | collective-permute-start | bytes 1572872 | tf_op jit(solution)/shard_map/ppermute | solution.py:23
  33.0 72.0 %collective-permute-start.19 = (bf16[256,1024]{1,0:T(8,128)(2,1)S(1)}, bf16[256,1024]{1,0:T(8,128)(2,1)S(1)}, u32[]{:S(2)}, u32[]{:S(2)}) collective-permute-start(bf16[256,1024]{1,0:T(8,128)(2,1)S(1)} %shard_map.75), channel_id=1, source_target_pairs={{0,16},{4,20},{8,24},{12,28},{1,17},{5,21},{9,25},{13,29},{2,18},{... | collective-permute-start | bytes 1572872 | tf_op jit(solution)/shard_map/ppermute | solution.py:23
  35.4 10.4 %collective-permute-start.14 = (f32[16,1024]{1,0:T(8,128)S(1)}, f32[16,1024]{1,0:T(8,128)S(1)}, u32[]{:S(2)}, u32[]{:S(2)}) collective-permute-start(f32[16,1024]{1,0:T(8,128)S(1)} %get-tuple-element.38), channel_id=1, source_target_pairs={{0,8},{4,12},{8,16},{12,20},{16,24},{20,28},{1,9},{5,13},{9,17},{1... | collective-permute-start | bytes 196616 | tf_op jit(solution)/shard_map/ppermute | solution.py:23
  45.8 25.8 %collective-permute-start.15 = (f32[16,1024]{1,0:T(8,128)S(1)}, f32[16,1024]{1,0:T(8,128)S(1)}, u32[]{:S(2)}, u32[]{:S(2)}) collective-permute-start(f32[16,1024]{1,0:T(8,128)S(1)} %get-tuple-element.38), channel_id=1, source_target_pairs={{0,12},{4,16},{8,20},{12,24},{16,28},{1,13},{5,17},{9,21},{13,25},... | collective-permute-start | bytes 196616 | tf_op jit(solution)/shard_map/ppermute | solution.py:23
  71.6 9.2 %collective-permute-start.12 = (f32[4,16,1024]{2,1,0:T(8,128)S(1)}, f32[4,16,1024]{2,1,0:T(8,128)S(1)}, u32[]{:S(2)}, u32[]{:S(2)}) collective-permute-start(f32[4,16,1024]{2,1,0:T(8,128)S(1)} %get-tuple-element.37), channel_id=1, source_target_pairs={{0,16},{4,20},{8,24},{12,28},{1,17},{5,21},{9,25},{13,29},{2,18},{... | collective-permute-start | bytes 786440 | tf_op jit(solution)/shard_map/ppermute | solution.py:23
  81.0 12.2 %collective-permute-start.16 = (f32[16,1024]{1,0:T(8,128)S(1)}, f32[16,1024]{1,0:T(8,128)S(1)}, u32[]{:S(2)}, u32[]{:S(2)}) collective-permute-start(f32[16,1024]{1,0:T(8,128)S(1)} %get-tuple-element.40), channel_id=1, source_target_pairs={{0,1},{1,2},{2,3},{3,0},{4,5},{5,6},{6,7},{7,4},{8,9},{9,10},{10,1... | collective-permute-start | bytes 196616 | tf_op jit(solution)/shard_map/ppermute | solution.py:31
  82.8 10.4 %collective-permute-start.17 = (f32[16,1024]{1,0:T(8,128)S(1)}, f32[16,1024]{1,0:T(8,128)S(1)}, u32[]{:S(2)}, u32[]{:S(2)}) collective-permute-start(f32[16,1024]{1,0:T(8,128)S(1)} %get-tuple-element.41), channel_id=1, source_target_pairs={{0,2},{1,3},{2,0},{3,1},{4,6},{5,7},{6,4},{7,5},{8,10},{9,11},{10,... | collective-permute-start | bytes 196616 | tf_op jit(solution)/shard_map/ppermute | solution.py:31
  83.2 10.0 %copy-start.2 = (bf16[256,4096]{1,0:T(8,128)(2,1)S(1)}, bf16[256,4096]{1,0:T(8,128)(2,1)}, u32[]{:S(2)}) copy-start(bf16[256,4096]{1,0:T(8,128)(2,1)} %value.1) | copy-start | bytes 6291460
  83.2 10.0 %collective-permute-start.18 = (f32[16,1024]{1,0:T(8,128)S(1)}, f32[16,1024]{1,0:T(8,128)S(1)}, u32[]{:S(2)}, u32[]{:S(2)}) collective-permute-start(f32[16,1024]{1,0:T(8,128)S(1)} %get-tuple-element.42), channel_id=1, source_target_pairs={{0,3},{1,0},{2,1},{3,2},{4,7},{5,4},{6,5},{7,6},{8,11},{9,8},{10,9... | collective-permute-start | bytes 196616 | tf_op jit(solution)/shard_map/ppermute | solution.py:31

commit v5 on v4

--- a/solution.py
+++ b/solution.py
@@ -12,8 +12,8 @@
 FILTER_PARTS = 4
 LANES = 128
 SEGMENTS = 8
-RAW_SHARES = (2, 2)
-DONE_SHARES = (2, 2)
+RAW_SHARES = (5, 5)
+DONE_SHARES = (6,)
 VMEM_BYTES = 16 << 20
 F32 = jnp.float32
 
@@ -136,6 +136,24 @@
                 order[...], product, preferred_element_type=F32
             ).astype(jnp.bfloat16)
         start += width
+
+
+def first_product_kernel(query, key_in, out, order, left, right, sems):
+    width = out.shape[1]
+    wide = width // sems.shape[0]
+    copies = []
+    for k in range(sems.shape[0]):
+        cols = pl.ds(k * wide, wide)
+        for j, (source, into) in enumerate(((query, left), (key_in, right))):
+            copies.append(pltpu.make_async_copy(source.at[:, cols], into.at[:, cols], sems.at[k, j]))
+            copies[-1].start()
+    fill_order(order)
+    for k in range(sems.shape[0]):
+        cols = pl.ds(k * wide, wide)
+        copies[2 * k].wait()
+        copies[2 * k + 1].wait()
+        product = (left[:, cols].astype(F32) * right[:, cols].astype(F32)).astype(jnp.bfloat16)
+        out[:, cols] = jnp.dot(order[...], product, preferred_element_type=F32).astype(jnp.bfloat16)
 
 
 def states_kernel(*refs, count, n_ch):
@@ -356,6 +374,7 @@
 
     vmem = pl.BlockSpec(memory_space=pltpu.VMEM)
     anywhere = pl.BlockSpec(memory_space=pl.ANY)
+    hbm = pl.BlockSpec(memory_space=pltpu.HBM)
 
     def shape(rows, columns, dtype=F32):
         return jax.ShapeDtypeStruct((rows, columns), dtype)
@@ -385,12 +404,23 @@
     products, pasts = [], []
     batches = [[k] for k in range(n_raw)] + [list(range(n_raw, count))]
     for k, batch in enumerate(batches):
-        products += call(
-            functools.partial(product_kernel, first=firsts[batch[0]]),
-            [shape(length, widths[j], bf16) for j in batch],
-            [order_scr],
-            (query, key_in),
-        )
+        if k == 0:
+            read = pltpu.VMEM((length, widths[0]), bf16)
+            product = call(
+                first_product_kernel,
+                shape(length, widths[0], bf16),
+                [order_scr, read, read, pltpu.SemaphoreType.DMA((2, 2))],
+                tuple(pltpu.with_memory_space_constraint(x, pltpu.HBM) for x in (query, key_in)),
+                in_specs=[hbm, hbm],
+            )
+            products.append(product)
+        else:
+            products += call(
+                functools.partial(product_kernel, first=firsts[batch[0]]),
+                [shape(length, widths[j], bf16) for j in batch],
+                [order_scr],
+                (query, key_in),
+            )
         if k < n_raw:
             pasts.append(from_behind(products[k], "ctx", FILTER_PARTS))
 
@@ -454,7 +484,7 @@
     )
     befores = ring(heads, "ch")
 
-    widest = max(widths)
+    widest = max(widths[:-1])
     partial, rest = call(
         functools.partial(finish_kernel, count=count, n_ch=n_ch),
         [shape(length, channels, bf16), shape(length, widths[-1])],

time: 107 us -> 124 us (1.16)
  waiting for transfers between devices: 42.3 us -> 60.1 us
  local copies, waits for them, and re-layouts: 3.63 us -> 0.1 us
  Pallas kernels: 28.2 us -> 30.2 us
    ppermute x12, waiting for transfers between devices: 1.4 us -> 12.5 us  [ring(): moved.append(lax.ppermute(part, axis, pairs) if k else part)]
    ppermute x8 -> x7, waiting for transfers between devices: 40.9 us -> 47.6 us  [from_behind(): lax.ppermute(value, axis, [(source, source + steps) for source in range(c...]
    unnamed x12 -> x8, local copies, waits for them, and re-layouts: 3.55 us -> 0.02 us
    pallas_call x13 -> x12, Pallas kernels: 28.2 us -> 30.2 us  [call(): pl.pallas_call(kernel, out_shape=out_shape, scratch_shapes=scratch, compi...]
    ppermute x12, starting transfers between devices: 19 us -> 20.7 us  [ring(): moved.append(lax.ppermute(part, axis, pairs) if k else part)]
    ppermute x8 -> x7, starting transfers between devices: 12.7 us -> 11.7 us  [from_behind(): lax.ppermute(value, axis, [(source, source + steps) for source in range(c...]
  transfers between devices with their start and end apart: 20 -> 19, of which waited for: 6 -> 7; matrix products, arithmetic and copies ran while one was open for 0% -> 1% of each run, Pallas kernels for 19% -> 23%
where the time goes in v5:
time: 124 us
  waiting for transfers between devices  60.1 us (48%)
  starting transfers between devices  32.4 us (26%)
  Pallas kernels  30.2 us (24%)
    ppermute x7, waiting for transfers between devices, from_behind(): lax.ppermute(value, axis, [(source, source + steps) for source in range(c...  47.6 us
    pallas_call x12, Pallas kernels, call(): pl.pallas_call(kernel, out_shape=out_shape, scratch_shapes=scratch, compi...  30.2 us
    ppermute x12, starting transfers between devices, ring(): moved.append(lax.ppermute(part, axis, pairs) if k else part)  20.7 us
    ppermute x12, waiting for transfers between devices, ring(): moved.append(lax.ppermute(part, axis, pairs) if k else part)  12.5 us
    ppermute x7, starting transfers between devices, from_behind(): lax.ppermute(value, axis, [(source, source + steps) for source in range(c...  11.7 us
  transfers between devices with their start and end apart: 19, of which 7 were waited for; matrix products, arithmetic and copies ran while one was open for 1% of the time, Pallas kernels for 23%

profile of v5, /device:TPU:4, one launch (start us, length us, event | category | flops | bytes accessed | tf_op | source)
XLA Modules:
  0.0 123.9 jit_solution(4398170907890209129)
XLA Ops:
  0.0 3.6 %collective-permute-start.2 = (f32[16,1024]{1,0:T(8,128)}, f32[16,1024]{1,0:T(8,128)S(1)}, u32[]{:S(2)}, u32[]{:S(2)}) collective-permute-start(f32[16,1024]{1,0:T(8,128)} %bitcast.3), channel_id=1, source_target_pairs={{0,3},{1,0},{2,1},{3,2},{4,7},{5,4},{6,5},{7,6},{8,11},{9,8},{10,9... | collective-permute-start | bytes 196616 | tf_op jit(solution)/shard_map/ppermute | solution.py:31
  3.7 0.9 maximum_maximum_fusion.refs_0_
  4.6 0.5 collective-permute-start.6
  5.1 1.6 %collective-permute-start.4 = (f32[24,1024]{1,0:T(8,128)S(1)}, f32[24,1024]{1,0:T(8,128)S(1)}, u32[]{:S(2)}, u32[]{:S(2)}) collective-permute-start(f32[24,1024]{1,0:T(8,128)S(1)} %maximum_maximum_fusion.refs_0_), channel_id=1, source_target_pairs={{0,1},{1,2},{2,3},{3,0},{4,5},{5,6},{6,7},{7,4},{8,9},{9,10},{10,1... | collective-permute-start | bytes 294920 | tf_op jit(solution)/shard_map/ppermute | solution.py:31
  6.7 2.9 %collective-permute-start.1 = (f32[16,1024]{1,0:T(8,128)}, f32[16,1024]{1,0:T(8,128)S(1)}, u32[]{:S(2)}, u32[]{:S(2)}) collective-permute-start(f32[16,1024]{1,0:T(8,128)} %bitcast.4), channel_id=1, source_target_pairs={{0,2},{1,3},{2,0},{3,1},{4,6},{5,7},{6,4},{7,5},{8,10},{9,11},{10,... | collective-permute-start | bytes 196616 | tf_op jit(solution)/shard_map/ppermute | solution.py:31
  9.6 1.7 %shard_map.64.refs_0_ = bf16[256,1280]{1,0:T(8,128)(2,1)S(1)} custom-call(bf16[256,4096]{1,0:T(8,128)(2,1)} %query.5, bf16[256,4096]{1,0:T(8,128)(2,1)} %key_in.5), custom_call_target="tpu_custom_call" | custom-call | tf_op jit(solution)/shard_map/pallas_call | solution.py:393
  11.8 0.4 shard_map.66.refs_2_.product
  12.2 6.2 %collective-permute-done.1.refs_5_ = f32[16,1024]{1,0:T(8,128)S(1)} collective-permute-done((f32[16,1024]{1,0:T(8,128)}, f32[16,1024]{1,0:T(8,128)S(1)}, u32[]{:S(2)}, u32[]{:S(2)}) %collective-permute-start.1) | collective-permute-done | bytes 65568 | tf_op jit(solution)/shard_map/ppermute | solution.py:31
  18.4 6.0 %shard_map.67 = (f32[128,1280]{1,0:T(8,128)S(1)}, f32[128,1280]{1,0:T(8,128)S(1)}, f32[128,1536]{1,0:T(8,128)S(1)}, f32[16,1024]{1,0:T(8,128)S(1)}, f32[16,1024]...) custom-call(bf16[256,1280]{1,0:T(8,128)(2,1)S(1)} %shard_map.64.refs_0_, ...), custom_call_target="tpu_custom_call" | custom-call | tf_op jit(solution)/shard_map/pallas_call | solution.py:393
  24.6 1.3 %collective-permute-start.18 = (bf16[256,1536]{1,0:T(8,128)(2,1)S(1)}, bf16[256,1536]{1,0:T(8,128)(2,1)S(1)}, u32[]{:S(2)}, u32[]{:S(2)}) collective-permute-start(bf16[256,1536]{1,0:T(8,128)(2,1)S(1)} %shard_map.74), channel_id=1, source_target_pairs={{0,16},{4,20},{8,24},{12,28},{1,17},{5,21},{9,25},{13,29},{2,18},{... | collective-permute-start | bytes 2359304 | tf_op jit(solution)/shard_map/ppermute | solution.py:23
  25.9 1.3 %collective-permute-start.7 = (bf16[256,1280]{1,0:T(8,128)(2,1)S(1)}, bf16[256,1280]{1,0:T(8,128)(2,1)S(1)}, u32[]{:S(2)}, u32[]{:S(2)}) collective-permute-start(bf16[256,1280]{1,0:T(8,128)(2,1)S(1)} %shard_map.65.refs_1_), channel_id=1, source_target_pairs={{0,16},{4,20},{8,24},{12,28},{1,17},{5,21},{9,25},{13,29},{2,18},{... | collective-permute-start | bytes 1966088 | tf_op jit(solution)/shard_map/ppermute | solution.py:23
  27.2 1.3 %collective-permute-start.3 = (bf16[256,1280]{1,0:T(8,128)(2,1)S(1)}, bf16[256,1280]{1,0:T(8,128)(2,1)S(1)}, u32[]{:S(2)}, u32[]{:S(2)}) collective-permute-start(bf16[256,1280]{1,0:T(8,128)(2,1)S(1)} %shard_map.64.refs_0_), channel_id=1, source_target_pairs={{0,16},{4,20},{8,24},{12,28},{1,17},{5,21},{9,25},{13,29},{2,18},{... | collective-permute-start | bytes 1966088 | tf_op jit(solution)/shard_map/ppermute | solution.py:23
  28.5 1.3 %collective-permute-start.8 = (f32[16,1024]{1,0:T(8,128)S(1)}, f32[16,1024]{1,0:T(8,128)S(1)}, u32[]{:S(2)}, u32[]{:S(2)}) collective-permute-start(f32[16,1024]{1,0:T(8,128)S(1)} %get-tuple-element.27), channel_id=1, source_target_pairs={{0,1},{1,2},{2,3},{3,0},{4,5},{5,6},{6,7},{7,4},{8,9},{9,10},{10,1... | collective-permute-start | bytes 196616 | tf_op jit(solution)/shard_map/ppermute | solution.py:31
  29.8 2.0 %collective-permute-start.9 = (f32[16,1024]{1,0:T(8,128)S(1)}, f32[16,1024]{1,0:T(8,128)S(1)}, u32[]{:S(2)}, u32[]{:S(2)}) collective-permute-start(f32[16,1024]{1,0:T(8,128)S(1)} %get-tuple-element.28), channel_id=1, source_target_pairs={{0,2},{1,3},{2,0},{3,1},{4,6},{5,7},{6,4},{7,5},{8,10},{9,11},{10,... | collective-permute-start | bytes 196616 | tf_op jit(solution)/shard_map/ppermute | solution.py:31
  31.8 2.9 %collective-permute-done.8.refs_1_ = f32[16,1024]{1,0:T(8,128)S(1)} collective-permute-done((f32[16,1024]{1,0:T(8,128)S(1)}, f32[16,1024]{1,0:T(8,128)S(1)}, u32[]{:S(2)}, u32[]{:S(2)}) %collective-permute-start.8) | collective-permute-done | bytes 65568 | tf_op jit(solution)/shard_map/ppermute | solution.py:31
  34.6 0.8 collective-permute-start.10
  35.5 0.6 collective-permute-done.9.refs_2_
  36.1 2.8 %collective-permute-done.10.refs_3_ = f32[16,1024]{1,0:T(8,128)S(1)} collective-permute-done((f32[16,1024]{1,0:T(8,128)S(1)}, f32[16,1024]{1,0:T(8,128)S(1)}, u32[]{:S(2)}, u32[]{:S(2)}) %collective-permute-start.10) | collective-permute-done | bytes 65568 | tf_op jit(solution)/shard_map/ppermute | solution.py:31
  39.0 1.3 %collective-permute-start.11 = (f32[4,16,1024]{2,1,0:T(8,128)S(1)}, f32[4,16,1024]{2,1,0:T(8,128)S(1)}, u32[]{:S(2)}, u32[]{:S(2)}) collective-permute-start(f32[4,16,1024]{2,1,0:T(8,128)S(1)} %get-tuple-element.31), channel_id=1, source_target_pairs={{0,16},{4,20},{8,24},{12,28},{1,17},{5,21},{9,25},{13,29},{2,18},{... | collective-permute-start | bytes 786440 | tf_op jit(solution)/shard_map/ppermute | solution.py:23
  40.3 1.9 %collective-permute-start.14 = (f32[16,1024]{1,0:T(8,128)S(1)}, f32[16,1024]{1,0:T(8,128)S(1)}, u32[]{:S(2)}, u32[]{:S(2)}) collective-permute-start(f32[16,1024]{1,0:T(8,128)S(1)} %get-tuple-element.32), channel_id=1, source_target_pairs={{0,12},{4,16},{8,20},{12,24},{16,28},{1,13},{5,17},{9,21},{13,25},... | collective-permute-start | bytes 196616 | tf_op jit(solution)/shard_map/ppermute | solution.py:23
  42.2 38.7 %collective-permute-done.14.refs_5_ = f32[16,1024]{1,0:T(8,128)S(1)} collective-permute-done((f32[16,1024]{1,0:T(8,128)S(1)}, f32[16,1024]{1,0:T(8,128)S(1)}, u32[]{:S(2)}, u32[]{:S(2)}) %collective-permute-start.14) | collective-permute-done | bytes 65568 | tf_op jit(solution)/shard_map/ppermute | solution.py:23
  80.9 2.7 %collective-permute-start.13 = (f32[16,1024]{1,0:T(8,128)S(1)}, f32[16,1024]{1,0:T(8,128)S(1)}, u32[]{:S(2)}, u32[]{:S(2)}) collective-permute-start(f32[16,1024]{1,0:T(8,128)S(1)} %get-tuple-element.32), channel_id=1, source_target_pairs={{0,8},{4,12},{8,16},{12,20},{16,24},{20,28},{1,9},{5,13},{9,17},{1... | collective-permute-start | bytes 196616 | tf_op jit(solution)/shard_map/ppermute | solution.py:23
  83.6 4.4 %collective-permute-done.13.refs_4_ = f32[16,1024]{1,0:T(8,128)S(1)} collective-permute-done((f32[16,1024]{1,0:T(8,128)S(1)}, f32[16,1024]{1,0:T(8,128)S(1)}, u32[]{:S(2)}, u32[]{:S(2)}) %collective-permute-start.13) | collective-permute-done | bytes 65568 | tf_op jit(solution)/shard_map/ppermute | solution.py:23
  87.9 1.9 %collective-permute-start.12 = (f32[16,1024]{1,0:T(8,128)S(1)}, f32[16,1024]{1,0:T(8,128)S(1)}, u32[]{:S(2)}, u32[]{:S(2)}) collective-permute-start(f32[16,1024]{1,0:T(8,128)S(1)} %get-tuple-element.32), channel_id=1, source_target_pairs={{0,4},{4,8},{8,12},{12,16},{16,20},{20,24},{24,28},{1,5},{5,9},{9,... | collective-permute-start | bytes 196616 | tf_op jit(solution)/shard_map/ppermute | solution.py:23
  89.8 4.6 %collective-permute-done.12.refs_3_ = f32[16,1024]{1,0:T(8,128)S(1)} collective-permute-done((f32[16,1024]{1,0:T(8,128)S(1)}, f32[16,1024]{1,0:T(8,128)S(1)}, u32[]{:S(2)}, u32[]{:S(2)}) %collective-permute-start.12) | collective-permute-done | bytes 65568 | tf_op jit(solution)/shard_map/ppermute | solution.py:23
  94.5 3.2 %collective-permute-start.15 = (f32[16,1024]{1,0:T(8,128)S(1)}, f32[16,1024]{1,0:T(8,128)S(1)}, u32[]{:S(2)}, u32[]{:S(2)}) collective-permute-start(f32[16,1024]{1,0:T(8,128)S(1)} %get-tuple-element.34), channel_id=1, source_target_pairs={{0,1},{1,2},{2,3},{3,0},{4,5},{5,6},{6,7},{7,4},{8,9},{9,10},{10,1... | collective-permute-start | bytes 196616 | tf_op jit(solution)/shard_map/ppermute | solution.py:31
  97.7 1.9 %collective-permute-start.16 = (f32[16,1024]{1,0:T(8,128)S(1)}, f32[16,1024]{1,0:T(8,128)S(1)}, u32[]{:S(2)}, u32[]{:S(2)}) collective-permute-start(f32[16,1024]{1,0:T(8,128)S(1)} %get-tuple-element.35), channel_id=1, source_target_pairs={{0,2},{1,3},{2,0},{3,1},{4,6},{5,7},{6,4},{7,5},{8,10},{9,11},{10,... | collective-permute-start | bytes 196616 | tf_op jit(solution)/shard_map/ppermute | solution.py:31
  99.6 2.8 %collective-permute-start.17 = (f32[16,1024]{1,0:T(8,128)S(1)}, f32[16,1024]{1,0:T(8,128)S(1)}, u32[]{:S(2)}, u32[]{:S(2)}) collective-permute-start(f32[16,1024]{1,0:T(8,128)S(1)} %get-tuple-element.36), channel_id=1, source_target_pairs={{0,3},{1,0},{2,1},{3,2},{4,7},{5,4},{6,5},{7,6},{8,11},{9,8},{10,9... | collective-permute-start | bytes 196616 | tf_op jit(solution)/shard_map/ppermute | solution.py:31
  102.5 4.6 %shard_map.70.refs_7_ = f32[256,1280]{1,0:T(8,128)S(1)} custom-call(bf16[256,1280]{1,0:T(8,128)(2,1)S(1)} %collective-permute-done.7.past, f32[4,16,1024]{2,1,0:T(8,128)S(1)} %get-tuple-element.25.rates.refs_12_, f32[4,24,1024]{2,1,0:T(8,128)S(1)} %shard_map.68.weighing.refs_13_), custom_call_target="tpu_custom_call" | custom-call | tf_op jit(solution)/shard_map/pallas_call | solution.py:393
  107.1 4.6 %shard_map.69.refs_6_ = f32[256,1280]{1,0:T(8,128)S(1)} custom-call(bf16[256,1280]{1,0:T(8,128)(2,1)S(1)} %collective-permute-done.3.past, f32[4,16,1024]{2,1,0:T(8,128)S(1)} %get-tuple-element.25.rates.refs_12_, f32[4,24,1024]{2,1,0:T(8,128)S(1)} %shard_map.68.weighing.refs_13_), custom_call_target="tpu_custom_call" | custom-call | tf_op jit(solution)/shard_map/pallas_call | solution.py:393
  111.7 11.0 %shard_map.73 = (bf16[256,4096]{1,0:T(8,128)(2,1)}, f32[256,1536]{1,0:T(8,128)S(1)}) custom-call(bf16[256,1280]{1,0:T(8,128)(2,1)S(1)} %shard_map.64.refs_0_, bf16[256,1280]{1,0:T(8,128)(2,1)S(1)} %shard_map.65.refs_1_, bf16[256,1536]{1,0:T(8,128)(2,1)S(1)} %shard_map.66.refs_2_.product, f32[128,1280]{1,0:T(8,128)S(1)} %get-tuple-element.22.refs_3_, ...), custom_call_target="tpu_custom_call" | custom-call | tf_op jit(solution)/shard_map/pallas_call | solution.py:393
  122.7 1.2 shard_map.75
  (29 shorter events, 0.8 us)
Async XLA Ops:
  0.0 9.6 %collective-permute-start.2 = (f32[16,1024]{1,0:T(8,128)}, f32[16,1024]{1,0:T(8,128)S(1)}, u32[]{:S(2)}, u32[]{:S(2)}) collective-permute-start(f32[16,1024]{1,0:T(8,128)} %bitcast.3), channel_id=1, source_target_pairs={{0,3},{1,0},{2,1},{3,2},{4,7},{5,4},{6,5},{7,6},{8,11},{9,8},{10,9... | collective-permute-start | bytes 196616 | tf_op jit(solution)/shard_map/ppermute | solution.py:31
  4.6 6.8 %copy-start = (bf16[256,4096]{1,0:T(8,128)(2,1)S(1)}, bf16[256,4096]{1,0:T(8,128)(2,1)}, u32[]{:S(2)}) copy-start(bf16[256,4096]{1,0:T(8,128)(2,1)} %query.5) | copy-start | bytes 6291460
  4.6 6.8 %copy-start.1 = (bf16[256,4096]{1,0:T(8,128)(2,1)S(1)}, bf16[256,4096]{1,0:T(8,128)(2,1)}, u32[]{:S(2)}) copy-start(bf16[256,4096]{1,0:T(8,128)(2,1)} %key_in.5) | copy-start | bytes 6291460
  4.6 19.9 %collective-permute-start.6 = (f32[24,1024]{1,0:T(8,128)S(1)}, f32[24,1024]{1,0:T(8,128)S(1)}, u32[]{:S(2)}, u32[]{:S(2)}) collective-permute-start(f32[24,1024]{1,0:T(8,128)S(1)} %maximum_maximum_fusion.refs_0_), channel_id=1, source_target_pairs={{0,3},{1,0},{2,1},{3,2},{4,7},{5,4},{6,5},{7,6},{8,11},{9,8},{10,9... | collective-permute-start | bytes 294920 | tf_op jit(solution)/shard_map/ppermute | solution.py:31
  5.1 19.4 %collective-permute-start.5 = (f32[24,1024]{1,0:T(8,128)S(1)}, f32[24,1024]{1,0:T(8,128)S(1)}, u32[]{:S(2)}, u32[]{:S(2)}) collective-permute-start(f32[24,1024]{1,0:T(8,128)S(1)} %maximum_maximum_fusion.refs_0_), channel_id=1, source_target_pairs={{0,2},{1,3},{2,0},{3,1},{4,6},{5,7},{6,4},{7,5},{8,10},{9,11},{10,... | collective-permute-start | bytes 294920 | tf_op jit(solution)/shard_map/ppermute | solution.py:31
  5.1 19.4 %collective-permute-start.4 = (f32[24,1024]{1,0:T(8,128)S(1)}, f32[24,1024]{1,0:T(8,128)S(1)}, u32[]{:S(2)}, u32[]{:S(2)}) collective-permute-start(f32[24,1024]{1,0:T(8,128)S(1)} %maximum_maximum_fusion.refs_0_), channel_id=1, source_target_pairs={{0,1},{1,2},{2,3},{3,0},{4,5},{5,6},{6,7},{7,4},{8,9},{9,10},{10,1... | collective-permute-start | bytes 294920 | tf_op jit(solution)/shard_map/ppermute | solution.py:31
  6.7 11.7 %collective-permute-start.1 = (f32[16,1024]{1,0:T(8,128)}, f32[16,1024]{1,0:T(8,128)S(1)}, u32[]{:S(2)}, u32[]{:S(2)}) collective-permute-start(f32[16,1024]{1,0:T(8,128)} %bitcast.4), channel_id=1, source_target_pairs={{0,2},{1,3},{2,0},{3,1},{4,6},{5,7},{6,4},{7,5},{8,10},{9,11},{10,... | collective-permute-start | bytes 196616 | tf_op jit(solution)/shard_map/ppermute | solution.py:31
  9.6 8.8 %collective-permute-start = (f32[16,1024]{1,0:T(8,128)}, f32[16,1024]{1,0:T(8,128)S(1)}, u32[]{:S(2)}, u32[]{:S(2)}) collective-permute-start(f32[16,1024]{1,0:T(8,128)} %bitcast.5), channel_id=1, source_target_pairs={{0,1},{1,2},{2,3},{3,0},{4,5},{5,6},{6,7},{7,4},{8,9},{9,10},{10,1... | collective-permute-start | bytes 196616 | tf_op jit(solution)/shard_map/ppermute | solution.py:31
  11.8 6.7 %copy-start.3 = (f32[1024,16]{0,1:T(8,128)S(1)}, f32[1024,16]{0,1:T(8,128)}, u32[]{:S(2)}) copy-start(f32[1024,16]{0,1:T(8,128)} %param.10) | copy-start | bytes 196612
  24.6 98.1 %collective-permute-start.18 = (bf16[256,1536]{1,0:T(8,128)(2,1)S(1)}, bf16[256,1536]{1,0:T(8,128)(2,1)S(1)}, u32[]{:S(2)}, u32[]{:S(2)}) collective-permute-start(bf16[256,1536]{1,0:T(8,128)(2,1)S(1)} %shard_map.74), channel_id=1, source_target_pairs={{0,16},{4,20},{8,24},{12,28},{1,17},{5,21},{9,25},{13,29},{2,18},{... | collective-permute-start | bytes 2359304 | tf_op jit(solution)/shard_map/ppermute | solution.py:23
  25.9 73.7 %collective-permute-start.7 = (bf16[256,1280]{1,0:T(8,128)(2,1)S(1)}, bf16[256,1280]{1,0:T(8,128)(2,1)S(1)}, u32[]{:S(2)}, u32[]{:S(2)}) collective-permute-start(bf16[256,1280]{1,0:T(8,128)(2,1)S(1)} %shard_map.65.refs_1_), channel_id=1, source_target_pairs={{0,16},{4,20},{8,24},{12,28},{1,17},{5,21},{9,25},{13,29},{2,18},{... | collective-permute-start | bytes 1966088 | tf_op jit(solution)/shard_map/ppermute | solution.py:23
  27.2 79.9 %collective-permute-start.3 = (bf16[256,1280]{1,0:T(8,128)(2,1)S(1)}, bf16[256,1280]{1,0:T(8,128)(2,1)S(1)}, u32[]{:S(2)}, u32[]{:S(2)}) collective-permute-start(bf16[256,1280]{1,0:T(8,128)(2,1)S(1)} %shard_map.64.refs_0_), channel_id=1, source_target_pairs={{0,16},{4,20},{8,24},{12,28},{1,17},{5,21},{9,25},{13,29},{2,18},{... | collective-permute-start | bytes 1966088 | tf_op jit(solution)/shard_map/ppermute | solution.py:23
  28.5 6.1 %collective-permute-start.8 = (f32[16,1024]{1,0:T(8,128)S(1)}, f32[16,1024]{1,0:T(8,128)S(1)}, u32[]{:S(2)}, u32[]{:S(2)}) collective-permute-start(f32[16,1024]{1,0:T(8,128)S(1)} %get-tuple-element.27), channel_id=1, source_target_pairs={{0,1},{1,2},{2,3},{3,0},{4,5},{5,6},{6,7},{7,4},{8,9},{9,10},{10,1... | collective-permute-start | bytes 196616 | tf_op jit(solution)/shard_map/ppermute | solution.py:31
  29.8 6.3 %collective-permute-start.9 = (f32[16,1024]{1,0:T(8,128)S(1)}, f32[16,1024]{1,0:T(8,128)S(1)}, u32[]{:S(2)}, u32[]{:S(2)}) collective-permute-start(f32[16,1024]{1,0:T(8,128)S(1)} %get-tuple-element.28), channel_id=1, source_target_pairs={{0,2},{1,3},{2,0},{3,1},{4,6},{5,7},{6,4},{7,5},{8,10},{9,11},{10,... | collective-permute-start | bytes 196616 | tf_op jit(solution)/shard_map/ppermute | solution.py:31
  34.6 4.3 %collective-permute-start.10 = (f32[16,1024]{1,0:T(8,128)S(1)}, f32[16,1024]{1,0:T(8,128)S(1)}, u32[]{:S(2)}, u32[]{:S(2)}) collective-permute-start(f32[16,1024]{1,0:T(8,128)S(1)} %get-tuple-element.29), channel_id=1, source_target_pairs={{0,3},{1,0},{2,1},{3,2},{4,7},{5,4},{6,5},{7,6},{8,11},{9,8},{10,9... | collective-permute-start | bytes 196616 | tf_op jit(solution)/shard_map/ppermute | solution.py:31
  39.0 55.4 %collective-permute-start.11 = (f32[4,16,1024]{2,1,0:T(8,128)S(1)}, f32[4,16,1024]{2,1,0:T(8,128)S(1)}, u32[]{:S(2)}, u32[]{:S(2)}) collective-permute-start(f32[4,16,1024]{2,1,0:T(8,128)S(1)} %get-tuple-element.31), channel_id=1, source_target_pairs={{0,16},{4,20},{8,24},{12,28},{1,17},{5,21},{9,25},{13,29},{2,18},{... | collective-permute-start | bytes 786440 | tf_op jit(solution)/shard_map/ppermute | solution.py:23
  40.3 40.6 %collective-permute-start.14 = (f32[16,1024]{1,0:T(8,128)S(1)}, f32[16,1024]{1,0:T(8,128)S(1)}, u32[]{:S(2)}, u32[]{:S(2)}) collective-permute-start(f32[16,1024]{1,0:T(8,128)S(1)} %get-tuple-element.32), channel_id=1, source_target_pairs={{0,12},{4,16},{8,20},{12,24},{16,28},{1,13},{5,17},{9,21},{13,25},... | collective-permute-start | bytes 196616 | tf_op jit(solution)/shard_map/ppermute | solution.py:23
  80.9 7.0 %collective-permute-start.13 = (f32[16,1024]{1,0:T(8,128)S(1)}, f32[16,1024]{1,0:T(8,128)S(1)}, u32[]{:S(2)}, u32[]{:S(2)}) collective-permute-start(f32[16,1024]{1,0:T(8,128)S(1)} %get-tuple-element.32), channel_id=1, source_target_pairs={{0,8},{4,12},{8,16},{12,20},{16,24},{20,28},{1,9},{5,13},{9,17},{1... | collective-permute-start | bytes 196616 | tf_op jit(solution)/shard_map/ppermute | solution.py:23
  87.9 6.5 %collective-permute-start.12 = (f32[16,1024]{1,0:T(8,128)S(1)}, f32[16,1024]{1,0:T(8,128)S(1)}, u32[]{:S(2)}, u32[]{:S(2)}) collective-permute-start(f32[16,1024]{1,0:T(8,128)S(1)} %get-tuple-element.32), channel_id=1, source_target_pairs={{0,4},{4,8},{8,12},{12,16},{16,20},{20,24},{24,28},{1,5},{5,9},{9,... | collective-permute-start | bytes 196616 | tf_op jit(solution)/shard_map/ppermute | solution.py:23
  94.5 17.1 %collective-permute-start.15 = (f32[16,1024]{1,0:T(8,128)S(1)}, f32[16,1024]{1,0:T(8,128)S(1)}, u32[]{:S(2)}, u32[]{:S(2)}) collective-permute-start(f32[16,1024]{1,0:T(8,128)S(1)} %get-tuple-element.34), channel_id=1, source_target_pairs={{0,1},{1,2},{2,3},{3,0},{4,5},{5,6},{6,7},{7,4},{8,9},{9,10},{10,1... | collective-permute-start | bytes 196616 | tf_op jit(solution)/shard_map/ppermute | solution.py:31
  97.7 13.9 %collective-permute-start.16 = (f32[16,1024]{1,0:T(8,128)S(1)}, f32[16,1024]{1,0:T(8,128)S(1)}, u32[]{:S(2)}, u32[]{:S(2)}) collective-permute-start(f32[16,1024]{1,0:T(8,128)S(1)} %get-tuple-element.35), channel_id=1, source_target_pairs={{0,2},{1,3},{2,0},{3,1},{4,6},{5,7},{6,4},{7,5},{8,10},{9,11},{10,... | collective-permute-start | bytes 196616 | tf_op jit(solution)/shard_map/ppermute | solution.py:31
  99.6 12.0 %copy-start.2 = (bf16[256,4096]{1,0:T(8,128)(2,1)S(1)}, bf16[256,4096]{1,0:T(8,128)(2,1)}, u32[]{:S(2)}) copy-start(bf16[256,4096]{1,0:T(8,128)(2,1)} %value.1) | copy-start | bytes 6291460
  99.6 12.0 %collective-permute-start.17 = (f32[16,1024]{1,0:T(8,128)S(1)}, f32[16,1024]{1,0:T(8,128)S(1)}, u32[]{:S(2)}, u32[]{:S(2)}) collective-permute-start(f32[16,1024]{1,0:T(8,128)S(1)} %get-tuple-element.36), channel_id=1, source_target_pairs={{0,3},{1,0},{2,1},{3,2},{4,7},{5,4},{6,5},{7,6},{8,11},{9,8},{10,9... | collective-permute-start | bytes 196616 | tf_op jit(solution)/shard_map/ppermute | solution.py:31

commit v6 on v5

--- a/solution.py
+++ b/solution.py
@@ -23,11 +23,17 @@
     return lax.ppermute(value, axis, [(source, source + steps) for source in range(count - steps)])
 
 
+def partner(mine, k, count, sign):
+    if count & (count - 1) == 0:
+        return mine ^ k
+    return (mine + sign * k + count) % count
+
+
 def ring(parts, axis):
     count = lax.axis_size(axis)
     moved = []
     for k, part in enumerate(parts):
-        pairs = [(source, (source + k) % count) for source in range(count)]
+        pairs = [(source, partner(source, k, count, 1)) for source in range(count)]
         moved.append(lax.ppermute(part, axis, pairs) if k else part)
     return moved
 
@@ -36,14 +42,14 @@
     count = len(refs)
     mine = lax.axis_index("ch")
     for k, ref in enumerate(refs):
-        out[(mine - k + count) % count] = ref[...]
+        out[partner(mine, k, count, -1)] = ref[...]
 
 
 def to_ring(whole, refs):
     count = len(refs)
     mine = lax.axis_index("ch")
     for k, ref in enumerate(refs):
-        ref[...] = whole[(mine + k) % count]
+        ref[...] = whole[partner(mine, k, count, 1)]
 
 
 def row_of(table, m):

time: 124 us -> 121 us (0.976)
  waiting for transfers between devices: 60.1 us -> 57.9 us
    ppermute x12, waiting for transfers between devices: 12.5 us -> 9.69 us  [ring(): moved.append(lax.ppermute(part, axis, pairs) if k else part)]
  transfers between devices with their start and end apart: 19 -> 19, of which waited for: 7 -> 7; matrix products, arithmetic and copies ran while one was open for 1% -> 1% of each run, Pallas kernels for 23% -> 24%
where the time goes in v6:
time: 121 us
  waiting for transfers between devices  57.9 us (48%)
  starting transfers between devices  31.4 us (26%)
  Pallas kernels  30.2 us (25%)
    ppermute x7, waiting for transfers between devices, from_behind(): lax.ppermute(value, axis, [(source, source + steps) for source in range(c...  48.2 us
    pallas_call x12, Pallas kernels, call(): pl.pallas_call(kernel, out_shape=out_shape, scratch_shapes=scratch, compi...  30.2 us
    ppermute x12, starting transfers between devices, ring(): moved.append(lax.ppermute(part, axis, pairs) if k else part)  19.7 us
    ppermute x7, starting transfers between devices, from_behind(): lax.ppermute(value, axis, [(source, source + steps) for source in range(c...  11.7 us
    ppermute x12, waiting for transfers between devices, ring(): moved.append(lax.ppermute(part, axis, pairs) if k else part)  9.69 us
  transfers between devices with their start and end apart: 19, of which 7 were waited for; matrix products, arithmetic and copies ran while one was open for 1% of the time, Pallas kernels for 24%

profile of v6, /device:TPU:4, one launch (start us, length us, event | category | flops | bytes accessed | tf_op | source)
XLA Modules:
  0.0 120.7 jit_solution(12715380584451982291)
XLA Ops:
  0.0 3.6 %collective-permute-start.2 = (f32[16,1024]{1,0:T(8,128)}, f32[16,1024]{1,0:T(8,128)S(1)}, u32[]{:S(2)}, u32[]{:S(2)}) collective-permute-start(f32[16,1024]{1,0:T(8,128)} %bitcast.3), channel_id=1, source_target_pairs={{0,3},{1,2},{2,1},{3,0},{4,7},{5,6},{6,5},{7,4},{8,11},{9,10},{10,... | collective-permute-start | bytes 196616 | tf_op jit(solution)/shard_map/ppermute | solution.py:37
  3.7 0.9 maximum_maximum_fusion.refs_0_
  4.6 0.3 collective-permute-start.6
  4.9 0.8 collective-permute-start.5
  5.7 3.4 %collective-permute-start.4 = (f32[24,1024]{1,0:T(8,128)S(1)}, f32[24,1024]{1,0:T(8,128)S(1)}, u32[]{:S(2)}, u32[]{:S(2)}) collective-permute-start(f32[24,1024]{1,0:T(8,128)S(1)} %maximum_maximum_fusion.refs_0_), channel_id=1, source_target_pairs={{0,1},{1,0},{2,3},{3,2},{4,5},{5,4},{6,7},{7,6},{8,9},{9,8},{10,11... | collective-permute-start | bytes 294920 | tf_op jit(solution)/shard_map/ppermute | solution.py:37
  9.1 1.5 %collective-permute-start = (f32[16,1024]{1,0:T(8,128)}, f32[16,1024]{1,0:T(8,128)S(1)}, u32[]{:S(2)}, u32[]{:S(2)}) collective-permute-start(f32[16,1024]{1,0:T(8,128)} %bitcast.5), channel_id=1, source_target_pairs={{0,1},{1,0},{2,3},{3,2},{4,5},{5,4},{6,7},{7,6},{8,9},{9,8},{10,11... | collective-permute-start | bytes 196616 | tf_op jit(solution)/shard_map/ppermute | solution.py:37
  10.6 1.7 %shard_map.64.refs_0_ = bf16[256,1280]{1,0:T(8,128)(2,1)S(1)} custom-call(bf16[256,4096]{1,0:T(8,128)(2,1)} %query.5, bf16[256,4096]{1,0:T(8,128)(2,1)} %key_in.5), custom_call_target="tpu_custom_call" | custom-call | tf_op jit(solution)/shard_map/pallas_call | solution.py:399
  12.3 0.4 shard_map.65.refs_1_
  12.7 0.4 shard_map.66.refs_2_.product
  13.1 4.7 %collective-permute-done.1.refs_5_ = f32[16,1024]{1,0:T(8,128)S(1)} collective-permute-done((f32[16,1024]{1,0:T(8,128)}, f32[16,1024]{1,0:T(8,128)S(1)}, u32[]{:S(2)}, u32[]{:S(2)}) %collective-permute-start.1) | collective-permute-done | bytes 65568 | tf_op jit(solution)/shard_map/ppermute | solution.py:37
  17.9 6.0 %shard_map.67 = (f32[128,1280]{1,0:T(8,128)S(1)}, f32[128,1280]{1,0:T(8,128)S(1)}, f32[128,1536]{1,0:T(8,128)S(1)}, f32[16,1024]{1,0:T(8,128)S(1)}, f32[16,1024]...) custom-call(bf16[256,1280]{1,0:T(8,128)(2,1)S(1)} %shard_map.64.refs_0_, ...), custom_call_target="tpu_custom_call" | custom-call | tf_op jit(solution)/shard_map/pallas_call | solution.py:399
  24.0 1.3 %collective-permute-start.18 = (bf16[256,1536]{1,0:T(8,128)(2,1)S(1)}, bf16[256,1536]{1,0:T(8,128)(2,1)S(1)}, u32[]{:S(2)}, u32[]{:S(2)}) collective-permute-start(bf16[256,1536]{1,0:T(8,128)(2,1)S(1)} %shard_map.74), channel_id=1, source_target_pairs={{0,16},{4,20},{8,24},{12,28},{1,17},{5,21},{9,25},{13,29},{2,18},{... | collective-permute-start | bytes 2359304 | tf_op jit(solution)/shard_map/ppermute | solution.py:23
  25.3 1.3 %collective-permute-start.7 = (bf16[256,1280]{1,0:T(8,128)(2,1)S(1)}, bf16[256,1280]{1,0:T(8,128)(2,1)S(1)}, u32[]{:S(2)}, u32[]{:S(2)}) collective-permute-start(bf16[256,1280]{1,0:T(8,128)(2,1)S(1)} %shard_map.65.refs_1_), channel_id=1, source_target_pairs={{0,16},{4,20},{8,24},{12,28},{1,17},{5,21},{9,25},{13,29},{2,18},{... | collective-permute-start | bytes 1966088 | tf_op jit(solution)/shard_map/ppermute | solution.py:23
  26.6 1.3 %collective-permute-start.3 = (bf16[256,1280]{1,0:T(8,128)(2,1)S(1)}, bf16[256,1280]{1,0:T(8,128)(2,1)S(1)}, u32[]{:S(2)}, u32[]{:S(2)}) collective-permute-start(bf16[256,1280]{1,0:T(8,128)(2,1)S(1)} %shard_map.64.refs_0_), channel_id=1, source_target_pairs={{0,16},{4,20},{8,24},{12,28},{1,17},{5,21},{9,25},{13,29},{2,18},{... | collective-permute-start | bytes 1966088 | tf_op jit(solution)/shard_map/ppermute | solution.py:23
  28.0 3.2 %collective-permute-start.9 = (f32[16,1024]{1,0:T(8,128)S(1)}, f32[16,1024]{1,0:T(8,128)S(1)}, u32[]{:S(2)}, u32[]{:S(2)}) collective-permute-start(f32[16,1024]{1,0:T(8,128)S(1)} %get-tuple-element.28), channel_id=1, source_target_pairs={{0,2},{1,3},{2,0},{3,1},{4,6},{5,7},{6,4},{7,5},{8,10},{9,11},{10,... | collective-permute-start | bytes 196616 | tf_op jit(solution)/shard_map/ppermute | solution.py:37
  31.2 1.3 %collective-permute-done.8.refs_1_ = f32[16,1024]{1,0:T(8,128)S(1)} collective-permute-done((f32[16,1024]{1,0:T(8,128)S(1)}, f32[16,1024]{1,0:T(8,128)S(1)}, u32[]{:S(2)}, u32[]{:S(2)}) %collective-permute-start.8) | collective-permute-done | bytes 65568 | tf_op jit(solution)/shard_map/ppermute | solution.py:37
  32.5 2.4 %collective-permute-start.10 = (f32[16,1024]{1,0:T(8,128)S(1)}, f32[16,1024]{1,0:T(8,128)S(1)}, u32[]{:S(2)}, u32[]{:S(2)}) collective-permute-start(f32[16,1024]{1,0:T(8,128)S(1)} %get-tuple-element.29), channel_id=1, source_target_pairs={{0,3},{1,2},{2,1},{3,0},{4,7},{5,6},{6,5},{7,4},{8,11},{9,10},{10,... | collective-permute-start | bytes 196616 | tf_op jit(solution)/shard_map/ppermute | solution.py:37
  35.0 0.8 collective-permute-done.9.refs_2_
  35.7 2.9 %collective-permute-done.10.refs_3_ = f32[16,1024]{1,0:T(8,128)S(1)} collective-permute-done((f32[16,1024]{1,0:T(8,128)S(1)}, f32[16,1024]{1,0:T(8,128)S(1)}, u32[]{:S(2)}, u32[]{:S(2)}) %collective-permute-start.10) | collective-permute-done | bytes 65568 | tf_op jit(solution)/shard_map/ppermute | solution.py:37
  38.6 1.3 %collective-permute-start.11 = (f32[4,16,1024]{2,1,0:T(8,128)S(1)}, f32[4,16,1024]{2,1,0:T(8,128)S(1)}, u32[]{:S(2)}, u32[]{:S(2)}) collective-permute-start(f32[4,16,1024]{2,1,0:T(8,128)S(1)} %get-tuple-element.31), channel_id=1, source_target_pairs={{0,16},{4,20},{8,24},{12,28},{1,17},{5,21},{9,25},{13,29},{2,18},{... | collective-permute-start | bytes 786440 | tf_op jit(solution)/shard_map/ppermute | solution.py:23
  39.9 1.9 %collective-permute-start.14 = (f32[16,1024]{1,0:T(8,128)S(1)}, f32[16,1024]{1,0:T(8,128)S(1)}, u32[]{:S(2)}, u32[]{:S(2)}) collective-permute-start(f32[16,1024]{1,0:T(8,128)S(1)} %get-tuple-element.32), channel_id=1, source_target_pairs={{0,12},{4,16},{8,20},{12,24},{16,28},{1,13},{5,17},{9,21},{13,25},... | collective-permute-start | bytes 196616 | tf_op jit(solution)/shard_map/ppermute | solution.py:23
  41.9 39.3 %collective-permute-done.14.refs_5_ = f32[16,1024]{1,0:T(8,128)S(1)} collective-permute-done((f32[16,1024]{1,0:T(8,128)S(1)}, f32[16,1024]{1,0:T(8,128)S(1)}, u32[]{:S(2)}, u32[]{:S(2)}) %collective-permute-start.14) | collective-permute-done | bytes 65568 | tf_op jit(solution)/shard_map/ppermute | solution.py:23
  81.1 2.7 %collective-permute-start.13 = (f32[16,1024]{1,0:T(8,128)S(1)}, f32[16,1024]{1,0:T(8,128)S(1)}, u32[]{:S(2)}, u32[]{:S(2)}) collective-permute-start(f32[16,1024]{1,0:T(8,128)S(1)} %get-tuple-element.32), channel_id=1, source_target_pairs={{0,8},{4,12},{8,16},{12,20},{16,24},{20,28},{1,9},{5,13},{9,17},{1... | collective-permute-start | bytes 196616 | tf_op jit(solution)/shard_map/ppermute | solution.py:23
  83.8 4.4 %collective-permute-done.13.refs_4_ = f32[16,1024]{1,0:T(8,128)S(1)} collective-permute-done((f32[16,1024]{1,0:T(8,128)S(1)}, f32[16,1024]{1,0:T(8,128)S(1)}, u32[]{:S(2)}, u32[]{:S(2)}) %collective-permute-start.13) | collective-permute-done | bytes 65568 | tf_op jit(solution)/shard_map/ppermute | solution.py:23
  88.2 1.9 %collective-permute-start.12 = (f32[16,1024]{1,0:T(8,128)S(1)}, f32[16,1024]{1,0:T(8,128)S(1)}, u32[]{:S(2)}, u32[]{:S(2)}) collective-permute-start(f32[16,1024]{1,0:T(8,128)S(1)} %get-tuple-element.32), channel_id=1, source_target_pairs={{0,4},{4,8},{8,12},{12,16},{16,20},{20,24},{24,28},{1,5},{5,9},{9,... | collective-permute-start | bytes 196616 | tf_op jit(solution)/shard_map/ppermute | solution.py:23
  90.1 4.6 %collective-permute-done.12.refs_3_ = f32[16,1024]{1,0:T(8,128)S(1)} collective-permute-done((f32[16,1024]{1,0:T(8,128)S(1)}, f32[16,1024]{1,0:T(8,128)S(1)}, u32[]{:S(2)}, u32[]{:S(2)}) %collective-permute-start.12) | collective-permute-done | bytes 65568 | tf_op jit(solution)/shard_map/ppermute | solution.py:23
  94.9 2.9 %collective-permute-start.16 = (f32[16,1024]{1,0:T(8,128)S(1)}, f32[16,1024]{1,0:T(8,128)S(1)}, u32[]{:S(2)}, u32[]{:S(2)}) collective-permute-start(f32[16,1024]{1,0:T(8,128)S(1)} %get-tuple-element.35), channel_id=1, source_target_pairs={{0,2},{1,3},{2,0},{3,1},{4,6},{5,7},{6,4},{7,5},{8,10},{9,11},{10,... | collective-permute-start | bytes 196616 | tf_op jit(solution)/shard_map/ppermute | solution.py:37
  97.8 1.5 %collective-permute-start.17 = (f32[16,1024]{1,0:T(8,128)S(1)}, f32[16,1024]{1,0:T(8,128)S(1)}, u32[]{:S(2)}, u32[]{:S(2)}) collective-permute-start(f32[16,1024]{1,0:T(8,128)S(1)} %get-tuple-element.36), channel_id=1, source_target_pairs={{0,3},{1,2},{2,1},{3,0},{4,7},{5,6},{6,5},{7,4},{8,11},{9,10},{10,... | collective-permute-start | bytes 196616 | tf_op jit(solution)/shard_map/ppermute | solution.py:37
  99.3 4.6 %shard_map.70.refs_7_ = f32[256,1280]{1,0:T(8,128)S(1)} custom-call(bf16[256,1280]{1,0:T(8,128)(2,1)S(1)} %collective-permute-done.7.past, f32[4,16,1024]{2,1,0:T(8,128)S(1)} %get-tuple-element.25.rates.refs_12_, f32[4,24,1024]{2,1,0:T(8,128)S(1)} %shard_map.68.weighing.refs_13_), custom_call_target="tpu_custom_call" | custom-call | tf_op jit(solution)/shard_map/pallas_call | solution.py:399
  103.8 4.6 %shard_map.69.refs_6_ = f32[256,1280]{1,0:T(8,128)S(1)} custom-call(bf16[256,1280]{1,0:T(8,128)(2,1)S(1)} %collective-permute-done.3.past, f32[4,16,1024]{2,1,0:T(8,128)S(1)} %get-tuple-element.25.rates.refs_12_, f32[4,24,1024]{2,1,0:T(8,128)S(1)} %shard_map.68.weighing.refs_13_), custom_call_target="tpu_custom_call" | custom-call | tf_op jit(solution)/shard_map/pallas_call | solution.py:399
  108.4 11.0 %shard_map.73 = (bf16[256,4096]{1,0:T(8,128)(2,1)}, f32[256,1536]{1,0:T(8,128)S(1)}) custom-call(bf16[256,1280]{1,0:T(8,128)(2,1)S(1)} %shard_map.64.refs_0_, bf16[256,1280]{1,0:T(8,128)(2,1)S(1)} %shard_map.65.refs_1_, bf16[256,1536]{1,0:T(8,128)(2,1)S(1)} %shard_map.66.refs_2_.product, f32[128,1280]{1,0:T(8,128)S(1)} %get-tuple-element.22.refs_3_, ...), custom_call_target="tpu_custom_call" | custom-call | tf_op jit(solution)/shard_map/pallas_call | solution.py:399
  119.5 1.2 %shard_map.75 = bf16[256,4096]{1,0:T(8,128)(2,1)} custom-call(f32[256,1536]{1,0:T(8,128)S(1)} %get-tuple-element.37.rest, bf16[256,1536]{1,0:T(8,128)(2,1)S(1)} %collective-permute-done.18.over, bf16[256,4096]{1,0:T(8,128)(2,1)S(1)} %copy-done.2, bf16[256,4096]{1,0:T(8,128)(2,1)} %get-tuple-element.38.partial), custom_call_target="tpu_custom_call", output_to_operand_aliasing={{}: (3, {})} | custom-call | tf_op jit(solution)/shard_map/pallas_call | solution.py:399
  (29 shorter events, 0.5 us)
Async XLA Ops:
  0.0 9.1 %collective-permute-start.2 = (f32[16,1024]{1,0:T(8,128)}, f32[16,1024]{1,0:T(8,128)S(1)}, u32[]{:S(2)}, u32[]{:S(2)}) collective-permute-start(f32[16,1024]{1,0:T(8,128)} %bitcast.3), channel_id=1, source_target_pairs={{0,3},{1,2},{2,1},{3,0},{4,7},{5,6},{6,5},{7,4},{8,11},{9,10},{10,... | collective-permute-start | bytes 196616 | tf_op jit(solution)/shard_map/ppermute | solution.py:37
  4.6 7.7 %copy-start = (bf16[256,4096]{1,0:T(8,128)(2,1)S(1)}, bf16[256,4096]{1,0:T(8,128)(2,1)}, u32[]{:S(2)}) copy-start(bf16[256,4096]{1,0:T(8,128)(2,1)} %query.5) | copy-start | bytes 6291460
  4.6 7.7 %copy-start.1 = (bf16[256,4096]{1,0:T(8,128)(2,1)S(1)}, bf16[256,4096]{1,0:T(8,128)(2,1)}, u32[]{:S(2)}) copy-start(bf16[256,4096]{1,0:T(8,128)(2,1)} %key_in.5) | copy-start | bytes 6291460
  4.6 19.3 %collective-permute-start.6 = (f32[24,1024]{1,0:T(8,128)S(1)}, f32[24,1024]{1,0:T(8,128)S(1)}, u32[]{:S(2)}, u32[]{:S(2)}) collective-permute-start(f32[24,1024]{1,0:T(8,128)S(1)} %maximum_maximum_fusion.refs_0_), channel_id=1, source_target_pairs={{0,3},{1,2},{2,1},{3,0},{4,7},{5,6},{6,5},{7,4},{8,11},{9,10},{10,... | collective-permute-start | bytes 294920 | tf_op jit(solution)/shard_map/ppermute | solution.py:37
  4.9 19.0 %collective-permute-start.5 = (f32[24,1024]{1,0:T(8,128)S(1)}, f32[24,1024]{1,0:T(8,128)S(1)}, u32[]{:S(2)}, u32[]{:S(2)}) collective-permute-start(f32[24,1024]{1,0:T(8,128)S(1)} %maximum_maximum_fusion.refs_0_), channel_id=1, source_target_pairs={{0,2},{1,3},{2,0},{3,1},{4,6},{5,7},{6,4},{7,5},{8,10},{9,11},{10,... | collective-permute-start | bytes 294920 | tf_op jit(solution)/shard_map/ppermute | solution.py:37
  5.7 18.2 %collective-permute-start.4 = (f32[24,1024]{1,0:T(8,128)S(1)}, f32[24,1024]{1,0:T(8,128)S(1)}, u32[]{:S(2)}, u32[]{:S(2)}) collective-permute-start(f32[24,1024]{1,0:T(8,128)S(1)} %maximum_maximum_fusion.refs_0_), channel_id=1, source_target_pairs={{0,1},{1,0},{2,3},{3,2},{4,5},{5,4},{6,7},{7,6},{8,9},{9,8},{10,11... | collective-permute-start | bytes 294920 | tf_op jit(solution)/shard_map/ppermute | solution.py:37
  9.1 8.8 %collective-permute-start.1 = (f32[16,1024]{1,0:T(8,128)}, f32[16,1024]{1,0:T(8,128)S(1)}, u32[]{:S(2)}, u32[]{:S(2)}) collective-permute-start(f32[16,1024]{1,0:T(8,128)} %bitcast.4), channel_id=1, source_target_pairs={{0,2},{1,3},{2,0},{3,1},{4,6},{5,7},{6,4},{7,5},{8,10},{9,11},{10,... | collective-permute-start | bytes 196616 | tf_op jit(solution)/shard_map/ppermute | solution.py:37
  9.1 8.8 %collective-permute-start = (f32[16,1024]{1,0:T(8,128)}, f32[16,1024]{1,0:T(8,128)S(1)}, u32[]{:S(2)}, u32[]{:S(2)}) collective-permute-start(f32[16,1024]{1,0:T(8,128)} %bitcast.5), channel_id=1, source_target_pairs={{0,1},{1,0},{2,3},{3,2},{4,5},{5,4},{6,7},{7,6},{8,9},{9,8},{10,11... | collective-permute-start | bytes 196616 | tf_op jit(solution)/shard_map/ppermute | solution.py:37
  12.7 5.2 %copy-start.3 = (f32[1024,16]{0,1:T(8,128)S(1)}, f32[1024,16]{0,1:T(8,128)}, u32[]{:S(2)}) copy-start(f32[1024,16]{0,1:T(8,128)} %param.10) | copy-start | bytes 196612
  24.0 95.5 %collective-permute-start.18 = (bf16[256,1536]{1,0:T(8,128)(2,1)S(1)}, bf16[256,1536]{1,0:T(8,128)(2,1)S(1)}, u32[]{:S(2)}, u32[]{:S(2)}) collective-permute-start(bf16[256,1536]{1,0:T(8,128)(2,1)S(1)} %shard_map.74), channel_id=1, source_target_pairs={{0,16},{4,20},{8,24},{12,28},{1,17},{5,21},{9,25},{13,29},{2,18},{... | collective-permute-start | bytes 2359304 | tf_op jit(solution)/shard_map/ppermute | solution.py:23
  25.3 72.5 %collective-permute-start.7 = (bf16[256,1280]{1,0:T(8,128)(2,1)S(1)}, bf16[256,1280]{1,0:T(8,128)(2,1)S(1)}, u32[]{:S(2)}, u32[]{:S(2)}) collective-permute-start(bf16[256,1280]{1,0:T(8,128)(2,1)S(1)} %shard_map.65.refs_1_), channel_id=1, source_target_pairs={{0,16},{4,20},{8,24},{12,28},{1,17},{5,21},{9,25},{13,29},{2,18},{... | collective-permute-start | bytes 1966088 | tf_op jit(solution)/shard_map/ppermute | solution.py:23
  26.6 77.2 %collective-permute-start.3 = (bf16[256,1280]{1,0:T(8,128)(2,1)S(1)}, bf16[256,1280]{1,0:T(8,128)(2,1)S(1)}, u32[]{:S(2)}, u32[]{:S(2)}) collective-permute-start(bf16[256,1280]{1,0:T(8,128)(2,1)S(1)} %shard_map.64.refs_0_), channel_id=1, source_target_pairs={{0,16},{4,20},{8,24},{12,28},{1,17},{5,21},{9,25},{13,29},{2,18},{... | collective-permute-start | bytes 1966088 | tf_op jit(solution)/shard_map/ppermute | solution.py:23
  27.9 4.6 %collective-permute-start.8 = (f32[16,1024]{1,0:T(8,128)S(1)}, f32[16,1024]{1,0:T(8,128)S(1)}, u32[]{:S(2)}, u32[]{:S(2)}) collective-permute-start(f32[16,1024]{1,0:T(8,128)S(1)} %get-tuple-element.27), channel_id=1, source_target_pairs={{0,1},{1,0},{2,3},{3,2},{4,5},{5,4},{6,7},{7,6},{8,9},{9,8},{10,11... | collective-permute-start | bytes 196616 | tf_op jit(solution)/shard_map/ppermute | solution.py:37
  28.0 7.7 %collective-permute-start.9 = (f32[16,1024]{1,0:T(8,128)S(1)}, f32[16,1024]{1,0:T(8,128)S(1)}, u32[]{:S(2)}, u32[]{:S(2)}) collective-permute-start(f32[16,1024]{1,0:T(8,128)S(1)} %get-tuple-element.28), channel_id=1, source_target_pairs={{0,2},{1,3},{2,0},{3,1},{4,6},{5,7},{6,4},{7,5},{8,10},{9,11},{10,... | collective-permute-start | bytes 196616 | tf_op jit(solution)/shard_map/ppermute | solution.py:37
  32.5 6.1 %collective-permute-start.10 = (f32[16,1024]{1,0:T(8,128)S(1)}, f32[16,1024]{1,0:T(8,128)S(1)}, u32[]{:S(2)}, u32[]{:S(2)}) collective-permute-start(f32[16,1024]{1,0:T(8,128)S(1)} %get-tuple-element.29), channel_id=1, source_target_pairs={{0,3},{1,2},{2,1},{3,0},{4,7},{5,6},{6,5},{7,4},{8,11},{9,10},{10,... | collective-permute-start | bytes 196616 | tf_op jit(solution)/shard_map/ppermute | solution.py:37
  38.6 56.0 %collective-permute-start.11 = (f32[4,16,1024]{2,1,0:T(8,128)S(1)}, f32[4,16,1024]{2,1,0:T(8,128)S(1)}, u32[]{:S(2)}, u32[]{:S(2)}) collective-permute-start(f32[4,16,1024]{2,1,0:T(8,128)S(1)} %get-tuple-element.31), channel_id=1, source_target_pairs={{0,16},{4,20},{8,24},{12,28},{1,17},{5,21},{9,25},{13,29},{2,18},{... | collective-permute-start | bytes 786440 | tf_op jit(solution)/shard_map/ppermute | solution.py:23
  39.9 41.2 %collective-permute-start.14 = (f32[16,1024]{1,0:T(8,128)S(1)}, f32[16,1024]{1,0:T(8,128)S(1)}, u32[]{:S(2)}, u32[]{:S(2)}) collective-permute-start(f32[16,1024]{1,0:T(8,128)S(1)} %get-tuple-element.32), channel_id=1, source_target_pairs={{0,12},{4,16},{8,20},{12,24},{16,28},{1,13},{5,17},{9,21},{13,25},... | collective-permute-start | bytes 196616 | tf_op jit(solution)/shard_map/ppermute | solution.py:23
  81.1 7.0 %collective-permute-start.13 = (f32[16,1024]{1,0:T(8,128)S(1)}, f32[16,1024]{1,0:T(8,128)S(1)}, u32[]{:S(2)}, u32[]{:S(2)}) collective-permute-start(f32[16,1024]{1,0:T(8,128)S(1)} %get-tuple-element.32), channel_id=1, source_target_pairs={{0,8},{4,12},{8,16},{12,20},{16,24},{20,28},{1,9},{5,13},{9,17},{1... | collective-permute-start | bytes 196616 | tf_op jit(solution)/shard_map/ppermute | solution.py:23
  88.2 6.5 %collective-permute-start.12 = (f32[16,1024]{1,0:T(8,128)S(1)}, f32[16,1024]{1,0:T(8,128)S(1)}, u32[]{:S(2)}, u32[]{:S(2)}) collective-permute-start(f32[16,1024]{1,0:T(8,128)S(1)} %get-tuple-element.32), channel_id=1, source_target_pairs={{0,4},{4,8},{8,12},{12,16},{16,20},{20,24},{24,28},{1,5},{5,9},{9,... | collective-permute-start | bytes 196616 | tf_op jit(solution)/shard_map/ppermute | solution.py:23
  94.8 13.6 %collective-permute-start.15 = (f32[16,1024]{1,0:T(8,128)S(1)}, f32[16,1024]{1,0:T(8,128)S(1)}, u32[]{:S(2)}, u32[]{:S(2)}) collective-permute-start(f32[16,1024]{1,0:T(8,128)S(1)} %get-tuple-element.34), channel_id=1, source_target_pairs={{0,1},{1,0},{2,3},{3,2},{4,5},{5,4},{6,7},{7,6},{8,9},{9,8},{10,11... | collective-permute-start | bytes 196616 | tf_op jit(solution)/shard_map/ppermute | solution.py:37
  94.9 13.5 %collective-permute-start.16 = (f32[16,1024]{1,0:T(8,128)S(1)}, f32[16,1024]{1,0:T(8,128)S(1)}, u32[]{:S(2)}, u32[]{:S(2)}) collective-permute-start(f32[16,1024]{1,0:T(8,128)S(1)} %get-tuple-element.35), channel_id=1, source_target_pairs={{0,2},{1,3},{2,0},{3,1},{4,6},{5,7},{6,4},{7,5},{8,10},{9,11},{10,... | collective-permute-start | bytes 196616 | tf_op jit(solution)/shard_map/ppermute | solution.py:37
  97.8 10.6 %copy-start.2 = (bf16[256,4096]{1,0:T(8,128)(2,1)S(1)}, bf16[256,4096]{1,0:T(8,128)(2,1)}, u32[]{:S(2)}) copy-start(bf16[256,4096]{1,0:T(8,128)(2,1)} %value.1) | copy-start | bytes 6291460
  97.8 10.6 %collective-permute-start.17 = (f32[16,1024]{1,0:T(8,128)S(1)}, f32[16,1024]{1,0:T(8,128)S(1)}, u32[]{:S(2)}, u32[]{:S(2)}) collective-permute-start(f32[16,1024]{1,0:T(8,128)S(1)} %get-tuple-element.36), channel_id=1, source_target_pairs={{0,3},{1,2},{2,1},{3,0},{4,7},{5,6},{6,5},{7,4},{8,11},{9,10},{10,... | collective-permute-start | bytes 196616 | tf_op jit(solution)/shard_map/ppermute | solution.py:37

commit v7 on v6

--- a/solution.py
+++ b/solution.py
@@ -12,7 +12,7 @@
 FILTER_PARTS = 4
 LANES = 128
 SEGMENTS = 8
-RAW_SHARES = (5, 5)
+RAW_SHARES = (4, 6)
 DONE_SHARES = (6,)
 VMEM_BYTES = 16 << 20
 F32 = jnp.float32
@@ -276,71 +276,93 @@
         over_tiles(product.shape[1], body)
 
 
+def local_kernel(product, rates, weighing, carry, out, tokens, table, weights, *, first):
+    modes = rates.shape[1]
+
+    def body(t):
+        cols = lanes(t * LANES)
+        tokens[...] = product[:, cols].astype(F32)
+        table[0] = jnp.exp(-at_tile(rates, first + t)[...])
+        weights[...] = at_tile(weighing, first + t, 0, modes)[...]
+        gain = row_of(at_tile(weighing, first + t, modes, 1), 0)
+        state = [carry[pl.ds(m * SEGMENTS, SEGMENTS), cols] for m in range(modes)]
+
+        def write(i, value, now):
+            out[step_rows(i), cols] = value + gain * now
+
+        emit(table, weights, state, tokens, write)
+
+    over_tiles(product.shape[1], body)
+
+
 def gated(back, mixed, value):
     plain = jnp.dot(back[...], mixed, preferred_element_type=F32)
     return (value.astype(F32) * plain).astype(jnp.bfloat16)
 
 
 def finish_kernel(*refs, count, n_ch):
-    products, carries, overs = refs[:count], refs[count : 2 * count], refs[2 * count : 3 * count - 1]
-    refs = refs[3 * count - 1 :]
-    befores, (rates, weighing, value, out, rest) = refs[:n_ch], refs[n_ch : n_ch + 5]
-    tokens, table, weights, scr, back, before, mixed, done, sems = refs[n_ch + 5 :]
+    products, carries, overs = refs[:count], refs[count : 2 * count], refs[2 * count : 3 * count]
+    refs = refs[3 * count :]
+    befores, (rates, weighing, value, late, out, rest) = refs[:n_ch], refs[n_ch : n_ch + 6]
+    tokens, table, weights, scr, back, before, mixed, done, sems = refs[n_ch + 6 :]
     modes = rates.shape[1]
     length = value.shape[0]
     steps = length // SEGMENTS
     from_ring(befores, before)
     fill_order(back, True)
+
+    def arriving(tile):
+        own, ahead = at_tile(rates, tile), at_tile(before, tile)
+        table[0] = jnp.exp(-own[...])
+        weights[...] = at_tile(weighing, tile, 0, modes)[...]
+        begin = (lax.broadcasted_iota(jnp.int32, (SEGMENTS, LANES), 0) * steps).astype(F32)
+        return [jnp.exp(-row_of(own, m) * begin) * row_of(ahead, m) for m in range(modes)]
+
     copies = [None, None]
     first = 0
     for k in range(count):
         product, carry = products[k], carries[k]
         width = product.shape[1]
         slot = k % 2
-        last = k == count - 1
-
-        def body(t, first=first, product=product, carry=carry, last=last, k=k):
+
+        def body(t, first=first, product=product, carry=carry, k=k):
             cols = lanes(t * LANES)
             tokens[...] = product[:, cols].astype(F32)
-            own = at_tile(rates, first + t)
-            table[0] = jnp.exp(-own[...])
-            weights[...] = at_tile(weighing, first + t, 0, modes)[...]
             gain = row_of(at_tile(weighing, first + t, modes, 1), 0)
-            begin = (lax.broadcasted_iota(jnp.int32, (SEGMENTS, LANES), 0) * steps).astype(F32)
-            ahead = at_tile(before, first + t)
-            state = []
-            for m in range(modes):
-                state.append(
-                    carry[pl.ds(m * SEGMENTS, SEGMENTS), cols]
-                    + jnp.exp(-row_of(own, m) * begin) * row_of(ahead, m)
-                )
-            if last:
-
-                def write(i, value, now):
-                    rest[step_rows(i), cols] = value + gain * now
-
-                emit(table, weights, state, tokens, write)
-            else:
-
-                def write(i, value, now):
-                    scr[step_rows(i), :] = value + gain * now
-
-                emit(table, weights, state, tokens, write)
-                mixed[:, cols] = (scr[...] - overs[k][:, cols].astype(F32)).astype(jnp.bfloat16)
+            state = arriving(first + t)
+            state = [carry[pl.ds(m * SEGMENTS, SEGMENTS), cols] + s for m, s in enumerate(state)]
+
+            def write(i, value, now):
+                scr[step_rows(i), :] = value + gain * now
+
+            emit(table, weights, state, tokens, write)
+            mixed[:, cols] = (scr[...] - overs[k][:, cols].astype(F32)).astype(jnp.bfloat16)
 
         over_tiles(width, body)
-        if not last:
-            if copies[slot] is not None:
-                copies[slot].wait()
-            wide = math.gcd(width, 4 * LANES)
-            for at in range(0, width, wide):
-                cols = pl.ds(at, wide)
-                done[slot, :, cols] = gated(back, mixed[:, cols], value[:, pl.ds(first * LANES + at, wide)])
-            copies[slot] = pltpu.make_async_copy(
-                done.at[slot, :, pl.ds(0, width)], out.at[:, pl.ds(first * LANES, width)], sems.at[slot]
-            )
-            copies[slot].start()
+        if copies[slot] is not None:
+            copies[slot].wait()
+        wide = math.gcd(width, 4 * LANES)
+        for at in range(0, width, wide):
+            cols = pl.ds(at, wide)
+            done[slot, :, cols] = gated(back, mixed[:, cols], value[:, pl.ds(first * LANES + at, wide)])
+        copies[slot] = pltpu.make_async_copy(
+            done.at[slot, :, pl.ds(0, width)], out.at[:, pl.ds(first * LANES, width)], sems.at[slot]
+        )
+        copies[slot].start()
         first += width // LANES
+
+    def add(t):
+        cols = lanes(t * LANES)
+        state = [row_of(weights, m) * s for m, s in enumerate(arriving(first + t))]
+        decay = [row_of(table.at[0], m) for m in range(modes)]
+        for i in range(steps):
+            state = [d * s for d, s in zip(decay, state)]
+            terms = state
+            while len(terms) > 1:
+                terms = [x + y for x, y in zip(terms[::2], terms[1::2])]
+            rest[step_rows(i), cols] = late[step_rows(i), cols] + terms[0]
+
+    over_tiles(late.shape[1], add)
     for copy in copies:
         if copy is not None:
             copy.wait()
@@ -490,9 +512,15 @@
     )
     befores = ring(heads, "ch")
 
+    late = call(
+        functools.partial(local_kernel, first=firsts[-1] // LANES),
+        shape(length, widths[-1]),
+        [tokens_scr, table_scr, weights_scr],
+        (products[-1], rates, weighing, carries[-1]),
+    )
     widest = max(widths[:-1])
     partial, rest = call(
-        functools.partial(finish_kernel, count=count, n_ch=n_ch),
+        functools.partial(finish_kernel, count=count - 1, n_ch=n_ch),
         [shape(length, channels, bf16), shape(length, widths[-1])],
         [
             tokens_scr,
@@ -505,7 +533,7 @@
             pltpu.VMEM((2, length, widest), bf16),
             pltpu.SemaphoreType.DMA((2,)),
         ],
-        (*products, *carries, *overs[:-1], *befores, rates, weighing, value),
+        (*products[:-1], *carries[:-1], *overs[:-1], *befores, rates, weighing, value, late),
         out_specs=[anywhere, vmem],
     )
     return call(

time: 121 us -> 115 us (0.950)
  waiting for transfers between devices: 57.9 us -> 49.7 us
  Pallas kernels: 30.2 us -> 32.2 us
    ppermute x7, waiting for transfers between devices: 48.2 us -> 39.9 us  [from_behind(): lax.ppermute(value, axis, [(source, source + steps) for source in range(c...]
    pallas_call x12 -> x13, Pallas kernels: 30.2 us -> 32.2 us  [call(): pl.pallas_call(kernel, out_shape=out_shape, scratch_shapes=scratch, compi...]
  transfers between devices with their start and end apart: 19 -> 19, of which waited for: 7 -> 7; matrix products, arithmetic and copies ran while one was open for 1% -> 1% of each run, Pallas kernels for 24% -> 27%
where the time goes in v7:
time: 115 us
  waiting for transfers between devices  49.7 us (43%)
  Pallas kernels  32.2 us (28%)
  starting transfers between devices  31.3 us (27%)
    ppermute x7, waiting for transfers between devices, from_behind(): lax.ppermute(value, axis, [(source, source + steps) for source in range(c...  39.9 us
    pallas_call x13, Pallas kernels, call(): pl.pallas_call(kernel, out_shape=out_shape, scratch_shapes=scratch, compi...  32.2 us
    ppermute x12, starting transfers between devices, ring(): moved.append(lax.ppermute(part, axis, pairs) if k else part)  19.7 us
    ppermute x7, starting transfers between devices, from_behind(): lax.ppermute(value, axis, [(source, source + steps) for source in range(c...  11.7 us
    ppermute x12, waiting for transfers between devices, ring(): moved.append(lax.ppermute(part, axis, pairs) if k else part)  9.78 us
  transfers between devices with their start and end apart: 19, of which 7 were waited for; matrix products, arithmetic and copies ran while one was open for 1% of the time, Pallas kernels for 27%

profile of v7, /device:TPU:4, one launch (start us, length us, event | category | flops | bytes accessed | tf_op | source)
XLA Modules:
  0.0 114.6 jit_solution(12079521155418725272)
XLA Ops:
  0.0 3.6 %collective-permute-start.2 = (f32[16,1024]{1,0:T(8,128)}, f32[16,1024]{1,0:T(8,128)S(1)}, u32[]{:S(2)}, u32[]{:S(2)}) collective-permute-start(f32[16,1024]{1,0:T(8,128)} %bitcast.3), channel_id=1, source_target_pairs={{0,3},{1,2},{2,1},{3,0},{4,7},{5,6},{6,5},{7,4},{8,11},{9,10},{10,... | collective-permute-start | bytes 196616 | tf_op jit(solution)/shard_map/ppermute | solution.py:37
  3.7 0.9 maximum_maximum_fusion.refs_0_
  4.6 0.3 collective-permute-start.6
  4.9 0.8 collective-permute-start.5
  5.7 3.4 %collective-permute-start.4 = (f32[24,1024]{1,0:T(8,128)S(1)}, f32[24,1024]{1,0:T(8,128)S(1)}, u32[]{:S(2)}, u32[]{:S(2)}) collective-permute-start(f32[24,1024]{1,0:T(8,128)S(1)} %maximum_maximum_fusion.refs_0_), channel_id=1, source_target_pairs={{0,1},{1,0},{2,3},{3,2},{4,5},{5,4},{6,7},{7,6},{8,9},{9,8},{10,11... | collective-permute-start | bytes 294920 | tf_op jit(solution)/shard_map/ppermute | solution.py:37
  9.1 1.5 %collective-permute-start = (f32[16,1024]{1,0:T(8,128)}, f32[16,1024]{1,0:T(8,128)S(1)}, u32[]{:S(2)}, u32[]{:S(2)}) collective-permute-start(f32[16,1024]{1,0:T(8,128)} %bitcast.5), channel_id=1, source_target_pairs={{0,1},{1,0},{2,3},{3,2},{4,5},{5,4},{6,7},{7,6},{8,9},{9,8},{10,11... | collective-permute-start | bytes 196616 | tf_op jit(solution)/shard_map/ppermute | solution.py:37
  10.6 1.6 %shard_map.64.refs_0_ = bf16[256,1024]{1,0:T(8,128)(2,1)S(1)} custom-call(bf16[256,4096]{1,0:T(8,128)(2,1)} %query.5, bf16[256,4096]{1,0:T(8,128)(2,1)} %key_in.5), custom_call_target="tpu_custom_call" | custom-call | tf_op jit(solution)/shard_map/pallas_call | solution.py:421
  12.2 0.4 shard_map.66.refs_2_.product
  12.6 0.4 shard_map.65.refs_1_
  13.1 4.8 %collective-permute-done.1.refs_5_ = f32[16,1024]{1,0:T(8,128)S(1)} collective-permute-done((f32[16,1024]{1,0:T(8,128)}, f32[16,1024]{1,0:T(8,128)S(1)}, u32[]{:S(2)}, u32[]{:S(2)}) %collective-permute-start.1) | collective-permute-done | bytes 65568 | tf_op jit(solution)/shard_map/ppermute | solution.py:37
  17.9 1.3 %collective-permute-start.7 = (bf16[256,1536]{1,0:T(8,128)(2,1)S(1)}, bf16[256,1536]{1,0:T(8,128)(2,1)S(1)}, u32[]{:S(2)}, u32[]{:S(2)}) collective-permute-start(bf16[256,1536]{1,0:T(8,128)(2,1)S(1)} %shard_map.65.refs_1_), channel_id=1, source_target_pairs={{0,16},{4,20},{8,24},{12,28},{1,17},{5,21},{9,25},{13,29},{2,18},{... | collective-permute-start | bytes 2359304 | tf_op jit(solution)/shard_map/ppermute | solution.py:23
  19.2 6.1 %shard_map.67 = (f32[128,1024]{1,0:T(8,128)S(1)}, f32[128,1536]{1,0:T(8,128)S(1)}, f32[128,1536]{1,0:T(8,128)S(1)}, f32[16,1024]{1,0:T(8,128)S(1)}, f32[16,1024]...) custom-call(bf16[256,1024]{1,0:T(8,128)(2,1)S(1)} %shard_map.64.refs_0_, ...), custom_call_target="tpu_custom_call" | custom-call | tf_op jit(solution)/shard_map/pallas_call | solution.py:421
  25.4 1.3 %collective-permute-start.18 = (bf16[256,1536]{1,0:T(8,128)(2,1)S(1)}, bf16[256,1536]{1,0:T(8,128)(2,1)S(1)}, u32[]{:S(2)}, u32[]{:S(2)}) collective-permute-start(bf16[256,1536]{1,0:T(8,128)(2,1)S(1)} %shard_map.75), channel_id=1, source_target_pairs={{0,16},{4,20},{8,24},{12,28},{1,17},{5,21},{9,25},{13,29},{2,18},{... | collective-permute-start | bytes 2359304 | tf_op jit(solution)/shard_map/ppermute | solution.py:23
  26.7 1.3 %collective-permute-start.3 = (bf16[256,1024]{1,0:T(8,128)(2,1)S(1)}, bf16[256,1024]{1,0:T(8,128)(2,1)S(1)}, u32[]{:S(2)}, u32[]{:S(2)}) collective-permute-start(bf16[256,1024]{1,0:T(8,128)(2,1)S(1)} %shard_map.64.refs_0_), channel_id=1, source_target_pairs={{0,16},{4,20},{8,24},{12,28},{1,17},{5,21},{9,25},{13,29},{2,18},{... | collective-permute-start | bytes 1572872 | tf_op jit(solution)/shard_map/ppermute | solution.py:23
  28.1 3.2 %collective-permute-start.9 = (f32[16,1024]{1,0:T(8,128)S(1)}, f32[16,1024]{1,0:T(8,128)S(1)}, u32[]{:S(2)}, u32[]{:S(2)}) collective-permute-start(f32[16,1024]{1,0:T(8,128)S(1)} %get-tuple-element.27), channel_id=1, source_target_pairs={{0,2},{1,3},{2,0},{3,1},{4,6},{5,7},{6,4},{7,5},{8,10},{9,11},{10,... | collective-permute-start | bytes 196616 | tf_op jit(solution)/shard_map/ppermute | solution.py:37
  31.3 1.3 %collective-permute-done.8.refs_1_ = f32[16,1024]{1,0:T(8,128)S(1)} collective-permute-done((f32[16,1024]{1,0:T(8,128)S(1)}, f32[16,1024]{1,0:T(8,128)S(1)}, u32[]{:S(2)}, u32[]{:S(2)}) %collective-permute-start.8) | collective-permute-done | bytes 65568 | tf_op jit(solution)/shard_map/ppermute | solution.py:37
  32.6 2.4 %collective-permute-start.10 = (f32[16,1024]{1,0:T(8,128)S(1)}, f32[16,1024]{1,0:T(8,128)S(1)}, u32[]{:S(2)}, u32[]{:S(2)}) collective-permute-start(f32[16,1024]{1,0:T(8,128)S(1)} %get-tuple-element.28), channel_id=1, source_target_pairs={{0,3},{1,2},{2,1},{3,0},{4,7},{5,6},{6,5},{7,4},{8,11},{9,10},{10,... | collective-permute-start | bytes 196616 | tf_op jit(solution)/shard_map/ppermute | solution.py:37
  35.1 3.6 %collective-permute-done.10.refs_3_ = f32[16,1024]{1,0:T(8,128)S(1)} collective-permute-done((f32[16,1024]{1,0:T(8,128)S(1)}, f32[16,1024]{1,0:T(8,128)S(1)}, u32[]{:S(2)}, u32[]{:S(2)}) %collective-permute-start.10) | collective-permute-done | bytes 65568 | tf_op jit(solution)/shard_map/ppermute | solution.py:37
  38.7 1.3 %collective-permute-start.11 = (f32[4,16,1024]{2,1,0:T(8,128)S(1)}, f32[4,16,1024]{2,1,0:T(8,128)S(1)}, u32[]{:S(2)}, u32[]{:S(2)}) collective-permute-start(f32[4,16,1024]{2,1,0:T(8,128)S(1)} %get-tuple-element.30), channel_id=1, source_target_pairs={{0,16},{4,20},{8,24},{12,28},{1,17},{5,21},{9,25},{13,29},{2,18},{... | collective-permute-start | bytes 786440 | tf_op jit(solution)/shard_map/ppermute | solution.py:23
  40.0 1.9 %collective-permute-start.14 = (f32[16,1024]{1,0:T(8,128)S(1)}, f32[16,1024]{1,0:T(8,128)S(1)}, u32[]{:S(2)}, u32[]{:S(2)}) collective-permute-start(f32[16,1024]{1,0:T(8,128)S(1)} %get-tuple-element.31), channel_id=1, source_target_pairs={{0,12},{4,16},{8,20},{12,24},{16,28},{1,13},{5,17},{9,21},{13,25},... | collective-permute-start | bytes 196616 | tf_op jit(solution)/shard_map/ppermute | solution.py:23
  42.0 31.0 %collective-permute-done.14.refs_5_ = f32[16,1024]{1,0:T(8,128)S(1)} collective-permute-done((f32[16,1024]{1,0:T(8,128)S(1)}, f32[16,1024]{1,0:T(8,128)S(1)}, u32[]{:S(2)}, u32[]{:S(2)}) %collective-permute-start.14) | collective-permute-done | bytes 65568 | tf_op jit(solution)/shard_map/ppermute | solution.py:23
  73.0 2.7 %collective-permute-start.13 = (f32[16,1024]{1,0:T(8,128)S(1)}, f32[16,1024]{1,0:T(8,128)S(1)}, u32[]{:S(2)}, u32[]{:S(2)}) collective-permute-start(f32[16,1024]{1,0:T(8,128)S(1)} %get-tuple-element.31), channel_id=1, source_target_pairs={{0,8},{4,12},{8,16},{12,20},{16,24},{20,28},{1,9},{5,13},{9,17},{1... | collective-permute-start | bytes 196616 | tf_op jit(solution)/shard_map/ppermute | solution.py:23
  75.7 4.4 %collective-permute-done.13.refs_4_ = f32[16,1024]{1,0:T(8,128)S(1)} collective-permute-done((f32[16,1024]{1,0:T(8,128)S(1)}, f32[16,1024]{1,0:T(8,128)S(1)}, u32[]{:S(2)}, u32[]{:S(2)}) %collective-permute-start.13) | collective-permute-done | bytes 65568 | tf_op jit(solution)/shard_map/ppermute | solution.py:23
  80.0 1.9 %collective-permute-start.12 = (f32[16,1024]{1,0:T(8,128)S(1)}, f32[16,1024]{1,0:T(8,128)S(1)}, u32[]{:S(2)}, u32[]{:S(2)}) collective-permute-start(f32[16,1024]{1,0:T(8,128)S(1)} %get-tuple-element.31), channel_id=1, source_target_pairs={{0,4},{4,8},{8,12},{12,16},{16,20},{20,24},{24,28},{1,5},{5,9},{9,... | collective-permute-start | bytes 196616 | tf_op jit(solution)/shard_map/ppermute | solution.py:23
  82.0 4.6 %collective-permute-done.12.refs_3_ = f32[16,1024]{1,0:T(8,128)S(1)} collective-permute-done((f32[16,1024]{1,0:T(8,128)S(1)}, f32[16,1024]{1,0:T(8,128)S(1)}, u32[]{:S(2)}, u32[]{:S(2)}) %collective-permute-start.12) | collective-permute-done | bytes 65568 | tf_op jit(solution)/shard_map/ppermute | solution.py:23
  86.7 2.9 %collective-permute-start.16 = (f32[16,1024]{1,0:T(8,128)S(1)}, f32[16,1024]{1,0:T(8,128)S(1)}, u32[]{:S(2)}, u32[]{:S(2)}) collective-permute-start(f32[16,1024]{1,0:T(8,128)S(1)} %get-tuple-element.34), channel_id=1, source_target_pairs={{0,2},{1,3},{2,0},{3,1},{4,6},{5,7},{6,4},{7,5},{8,10},{9,11},{10,... | collective-permute-start | bytes 196616 | tf_op jit(solution)/shard_map/ppermute | solution.py:37
  89.6 1.5 %collective-permute-start.17 = (f32[16,1024]{1,0:T(8,128)S(1)}, f32[16,1024]{1,0:T(8,128)S(1)}, u32[]{:S(2)}, u32[]{:S(2)}) collective-permute-start(f32[16,1024]{1,0:T(8,128)S(1)} %get-tuple-element.35), channel_id=1, source_target_pairs={{0,3},{1,2},{2,1},{3,0},{4,7},{5,6},{6,5},{7,4},{8,11},{9,10},{10,... | collective-permute-start | bytes 196616 | tf_op jit(solution)/shard_map/ppermute | solution.py:37
  91.1 3.7 %shard_map.73.refs_13_ = f32[256,1536]{1,0:T(8,128)S(1)} custom-call(bf16[256,1536]{1,0:T(8,128)(2,1)S(1)} %shard_map.66.refs_2_.product, f32[4,16,1024]{2,1,0:T(8,128)S(1)} %get-tuple-element.24.rates.refs_10_, f32[4,24,1024]{2,1,0:T(8,128)S(1)} %shard_map.68.weighing.refs_11_, f32[128,1536]{1,0:T(8,128)S(1)} %get-tuple-element.36.carry), custom_call_target="tpu_custom_call" | custom-call | tf_op jit(solution)/shard_map/pallas_call | solution.py:421
  94.8 3.7 %shard_map.69.refs_4_ = f32[256,1024]{1,0:T(8,128)S(1)} custom-call(bf16[256,1024]{1,0:T(8,128)(2,1)S(1)} %collective-permute-done.3.past, f32[4,16,1024]{2,1,0:T(8,128)S(1)} %get-tuple-element.24.rates.refs_10_, f32[4,24,1024]{2,1,0:T(8,128)S(1)} %shard_map.68.weighing.refs_11_), custom_call_target="tpu_custom_call" | custom-call | tf_op jit(solution)/shard_map/pallas_call | solution.py:421
  98.5 5.5 %shard_map.70.refs_5_ = f32[256,1536]{1,0:T(8,128)S(1)} custom-call(bf16[256,1536]{1,0:T(8,128)(2,1)S(1)} %collective-permute-done.7.past, f32[4,16,1024]{2,1,0:T(8,128)S(1)} %get-tuple-element.24.rates.refs_10_, f32[4,24,1024]{2,1,0:T(8,128)S(1)} %shard_map.68.weighing.refs_11_), custom_call_target="tpu_custom_call" | custom-call | tf_op jit(solution)/shard_map/pallas_call | solution.py:421
  104.0 9.3 %shard_map.74 = (bf16[256,4096]{1,0:T(8,128)(2,1)}, f32[256,1536]{1,0:T(8,128)S(1)}) custom-call(bf16[256,1024]{1,0:T(8,128)(2,1)S(1)} %shard_map.64.refs_0_, bf16[256,1536]{1,0:T(8,128)(2,1)S(1)} %shard_map.65.refs_1_, f32[128,1024]{1,0:T(8,128)S(1)} %get-tuple-element.22.refs_2_, f32[128,1536]{1,0:T(8,128)S(1)} %get-tuple-element.23.refs_3_, ...), custom_call_target="tpu_custom_call" | custom-call | tf_op jit(solution)/shard_map/pallas_call | solution.py:421
  113.4 1.2 %shard_map.76 = bf16[256,4096]{1,0:T(8,128)(2,1)} custom-call(f32[256,1536]{1,0:T(8,128)S(1)} %get-tuple-element.37.rest, bf16[256,1536]{1,0:T(8,128)(2,1)S(1)} %collective-permute-done.18.over, bf16[256,4096]{1,0:T(8,128)(2,1)S(1)} %copy-done.2, bf16[256,4096]{1,0:T(8,128)(2,1)} %get-tuple-element.38.partial), custom_call_target="tpu_custom_call", output_to_operand_aliasing={{}: (3, {})} | custom-call | tf_op jit(solution)/shard_map/pallas_call | solution.py:421
  (30 shorter events, 0.6 us)
Async XLA Ops:
  0.0 9.1 %collective-permute-start.2 = (f32[16,1024]{1,0:T(8,128)}, f32[16,1024]{1,0:T(8,128)S(1)}, u32[]{:S(2)}, u32[]{:S(2)}) collective-permute-start(f32[16,1024]{1,0:T(8,128)} %bitcast.3), channel_id=1, source_target_pairs={{0,3},{1,2},{2,1},{3,0},{4,7},{5,6},{6,5},{7,4},{8,11},{9,10},{10,... | collective-permute-start | bytes 196616 | tf_op jit(solution)/shard_map/ppermute | solution.py:37
  4.6 7.5 %copy-start = (bf16[256,4096]{1,0:T(8,128)(2,1)S(1)}, bf16[256,4096]{1,0:T(8,128)(2,1)}, u32[]{:S(2)}) copy-start(bf16[256,4096]{1,0:T(8,128)(2,1)} %query.5) | copy-start | bytes 6291460
  4.6 7.6 %copy-start.1 = (bf16[256,4096]{1,0:T(8,128)(2,1)S(1)}, bf16[256,4096]{1,0:T(8,128)(2,1)}, u32[]{:S(2)}) copy-start(bf16[256,4096]{1,0:T(8,128)(2,1)} %key_in.5) | copy-start | bytes 6291460
  4.6 20.7 %collective-permute-start.6 = (f32[24,1024]{1,0:T(8,128)S(1)}, f32[24,1024]{1,0:T(8,128)S(1)}, u32[]{:S(2)}, u32[]{:S(2)}) collective-permute-start(f32[24,1024]{1,0:T(8,128)S(1)} %maximum_maximum_fusion.refs_0_), channel_id=1, source_target_pairs={{0,3},{1,2},{2,1},{3,0},{4,7},{5,6},{6,5},{7,4},{8,11},{9,10},{10,... | collective-permute-start | bytes 294920 | tf_op jit(solution)/shard_map/ppermute | solution.py:37
  4.9 20.4 %collective-permute-start.5 = (f32[24,1024]{1,0:T(8,128)S(1)}, f32[24,1024]{1,0:T(8,128)S(1)}, u32[]{:S(2)}, u32[]{:S(2)}) collective-permute-start(f32[24,1024]{1,0:T(8,128)S(1)} %maximum_maximum_fusion.refs_0_), channel_id=1, source_target_pairs={{0,2},{1,3},{2,0},{3,1},{4,6},{5,7},{6,4},{7,5},{8,10},{9,11},{10,... | collective-permute-start | bytes 294920 | tf_op jit(solution)/shard_map/ppermute | solution.py:37
  5.7 19.6 %collective-permute-start.4 = (f32[24,1024]{1,0:T(8,128)S(1)}, f32[24,1024]{1,0:T(8,128)S(1)}, u32[]{:S(2)}, u32[]{:S(2)}) collective-permute-start(f32[24,1024]{1,0:T(8,128)S(1)} %maximum_maximum_fusion.refs_0_), channel_id=1, source_target_pairs={{0,1},{1,0},{2,3},{3,2},{4,5},{5,4},{6,7},{7,6},{8,9},{9,8},{10,11... | collective-permute-start | bytes 294920 | tf_op jit(solution)/shard_map/ppermute | solution.py:37
  9.1 8.8 %collective-permute-start.1 = (f32[16,1024]{1,0:T(8,128)}, f32[16,1024]{1,0:T(8,128)S(1)}, u32[]{:S(2)}, u32[]{:S(2)}) collective-permute-start(f32[16,1024]{1,0:T(8,128)} %bitcast.4), channel_id=1, source_target_pairs={{0,2},{1,3},{2,0},{3,1},{4,6},{5,7},{6,4},{7,5},{8,10},{9,11},{10,... | collective-permute-start | bytes 196616 | tf_op jit(solution)/shard_map/ppermute | solution.py:37
  9.1 10.1 %collective-permute-start = (f32[16,1024]{1,0:T(8,128)}, f32[16,1024]{1,0:T(8,128)S(1)}, u32[]{:S(2)}, u32[]{:S(2)}) collective-permute-start(f32[16,1024]{1,0:T(8,128)} %bitcast.5), channel_id=1, source_target_pairs={{0,1},{1,0},{2,3},{3,2},{4,5},{5,4},{6,7},{7,6},{8,9},{9,8},{10,11... | collective-permute-start | bytes 196616 | tf_op jit(solution)/shard_map/ppermute | solution.py:37
  12.6 6.6 %copy-start.3 = (f32[1024,16]{0,1:T(8,128)S(1)}, f32[1024,16]{0,1:T(8,128)}, u32[]{:S(2)}) copy-start(f32[1024,16]{0,1:T(8,128)} %param.10) | copy-start | bytes 196612
  17.9 80.6 %collective-permute-start.7 = (bf16[256,1536]{1,0:T(8,128)(2,1)S(1)}, bf16[256,1536]{1,0:T(8,128)(2,1)S(1)}, u32[]{:S(2)}, u32[]{:S(2)}) collective-permute-start(bf16[256,1536]{1,0:T(8,128)(2,1)S(1)} %shard_map.65.refs_1_), channel_id=1, source_target_pairs={{0,16},{4,20},{8,24},{12,28},{1,17},{5,21},{9,25},{13,29},{2,18},{... | collective-permute-start | bytes 2359304 | tf_op jit(solution)/shard_map/ppermute | solution.py:23
  25.4 87.9 %collective-permute-start.18 = (bf16[256,1536]{1,0:T(8,128)(2,1)S(1)}, bf16[256,1536]{1,0:T(8,128)(2,1)S(1)}, u32[]{:S(2)}, u32[]{:S(2)}) collective-permute-start(bf16[256,1536]{1,0:T(8,128)(2,1)S(1)} %shard_map.75), channel_id=1, source_target_pairs={{0,16},{4,20},{8,24},{12,28},{1,17},{5,21},{9,25},{13,29},{2,18},{... | collective-permute-start | bytes 2359304 | tf_op jit(solution)/shard_map/ppermute | solution.py:23
  26.7 62.9 %collective-permute-start.3 = (bf16[256,1024]{1,0:T(8,128)(2,1)S(1)}, bf16[256,1024]{1,0:T(8,128)(2,1)S(1)}, u32[]{:S(2)}, u32[]{:S(2)}) collective-permute-start(bf16[256,1024]{1,0:T(8,128)(2,1)S(1)} %shard_map.64.refs_0_), channel_id=1, source_target_pairs={{0,16},{4,20},{8,24},{12,28},{1,17},{5,21},{9,25},{13,29},{2,18},{... | collective-permute-start | bytes 1572872 | tf_op jit(solution)/shard_map/ppermute | solution.py:23
  28.0 4.6 %collective-permute-start.8 = (f32[16,1024]{1,0:T(8,128)S(1)}, f32[16,1024]{1,0:T(8,128)S(1)}, u32[]{:S(2)}, u32[]{:S(2)}) collective-permute-start(f32[16,1024]{1,0:T(8,128)S(1)} %get-tuple-element.26), channel_id=1, source_target_pairs={{0,1},{1,0},{2,3},{3,2},{4,5},{5,4},{6,7},{7,6},{8,9},{9,8},{10,11... | collective-permute-start | bytes 196616 | tf_op jit(solution)/shard_map/ppermute | solution.py:37
  28.1 7.0 %collective-permute-start.9 = (f32[16,1024]{1,0:T(8,128)S(1)}, f32[16,1024]{1,0:T(8,128)S(1)}, u32[]{:S(2)}, u32[]{:S(2)}) collective-permute-start(f32[16,1024]{1,0:T(8,128)S(1)} %get-tuple-element.27), channel_id=1, source_target_pairs={{0,2},{1,3},{2,0},{3,1},{4,6},{5,7},{6,4},{7,5},{8,10},{9,11},{10,... | collective-permute-start | bytes 196616 | tf_op jit(solution)/shard_map/ppermute | solution.py:37
  32.6 6.1 %collective-permute-start.10 = (f32[16,1024]{1,0:T(8,128)S(1)}, f32[16,1024]{1,0:T(8,128)S(1)}, u32[]{:S(2)}, u32[]{:S(2)}) collective-permute-start(f32[16,1024]{1,0:T(8,128)S(1)} %get-tuple-element.28), channel_id=1, source_target_pairs={{0,3},{1,2},{2,1},{3,0},{4,7},{5,6},{6,5},{7,4},{8,11},{9,10},{10,... | collective-permute-start | bytes 196616 | tf_op jit(solution)/shard_map/ppermute | solution.py:37
  38.7 47.8 %collective-permute-start.11 = (f32[4,16,1024]{2,1,0:T(8,128)S(1)}, f32[4,16,1024]{2,1,0:T(8,128)S(1)}, u32[]{:S(2)}, u32[]{:S(2)}) collective-permute-start(f32[4,16,1024]{2,1,0:T(8,128)S(1)} %get-tuple-element.30), channel_id=1, source_target_pairs={{0,16},{4,20},{8,24},{12,28},{1,17},{5,21},{9,25},{13,29},{2,18},{... | collective-permute-start | bytes 786440 | tf_op jit(solution)/shard_map/ppermute | solution.py:23
  40.0 32.9 %collective-permute-start.14 = (f32[16,1024]{1,0:T(8,128)S(1)}, f32[16,1024]{1,0:T(8,128)S(1)}, u32[]{:S(2)}, u32[]{:S(2)}) collective-permute-start(f32[16,1024]{1,0:T(8,128)S(1)} %get-tuple-element.31), channel_id=1, source_target_pairs={{0,12},{4,16},{8,20},{12,24},{16,28},{1,13},{5,17},{9,21},{13,25},... | collective-permute-start | bytes 196616 | tf_op jit(solution)/shard_map/ppermute | solution.py:23
  73.0 7.0 %collective-permute-start.13 = (f32[16,1024]{1,0:T(8,128)S(1)}, f32[16,1024]{1,0:T(8,128)S(1)}, u32[]{:S(2)}, u32[]{:S(2)}) collective-permute-start(f32[16,1024]{1,0:T(8,128)S(1)} %get-tuple-element.31), channel_id=1, source_target_pairs={{0,8},{4,12},{8,16},{12,20},{16,24},{20,28},{1,9},{5,13},{9,17},{1... | collective-permute-start | bytes 196616 | tf_op jit(solution)/shard_map/ppermute | solution.py:23
  80.0 6.5 %collective-permute-start.12 = (f32[16,1024]{1,0:T(8,128)S(1)}, f32[16,1024]{1,0:T(8,128)S(1)}, u32[]{:S(2)}, u32[]{:S(2)}) collective-permute-start(f32[16,1024]{1,0:T(8,128)S(1)} %get-tuple-element.31), channel_id=1, source_target_pairs={{0,4},{4,8},{8,12},{12,16},{16,20},{20,24},{24,28},{1,5},{5,9},{9,... | collective-permute-start | bytes 196616 | tf_op jit(solution)/shard_map/ppermute | solution.py:23
  86.6 17.4 %collective-permute-start.15 = (f32[16,1024]{1,0:T(8,128)S(1)}, f32[16,1024]{1,0:T(8,128)S(1)}, u32[]{:S(2)}, u32[]{:S(2)}) collective-permute-start(f32[16,1024]{1,0:T(8,128)S(1)} %get-tuple-element.33), channel_id=1, source_target_pairs={{0,1},{1,0},{2,3},{3,2},{4,5},{5,4},{6,7},{7,6},{8,9},{9,8},{10,11... | collective-permute-start | bytes 196616 | tf_op jit(solution)/shard_map/ppermute | solution.py:37
  86.7 17.3 %collective-permute-start.16 = (f32[16,1024]{1,0:T(8,128)S(1)}, f32[16,1024]{1,0:T(8,128)S(1)}, u32[]{:S(2)}, u32[]{:S(2)}) collective-permute-start(f32[16,1024]{1,0:T(8,128)S(1)} %get-tuple-element.34), channel_id=1, source_target_pairs={{0,2},{1,3},{2,0},{3,1},{4,6},{5,7},{6,4},{7,5},{8,10},{9,11},{10,... | collective-permute-start | bytes 196616 | tf_op jit(solution)/shard_map/ppermute | solution.py:37
  89.6 14.4 %collective-permute-start.17 = (f32[16,1024]{1,0:T(8,128)S(1)}, f32[16,1024]{1,0:T(8,128)S(1)}, u32[]{:S(2)}, u32[]{:S(2)}) collective-permute-start(f32[16,1024]{1,0:T(8,128)S(1)} %get-tuple-element.35), channel_id=1, source_target_pairs={{0,3},{1,2},{2,1},{3,0},{4,7},{5,6},{6,5},{7,4},{8,11},{9,10},{10,... | collective-permute-start | bytes 196616 | tf_op jit(solution)/shard_map/ppermute | solution.py:37
  94.8 9.3 %copy-start.2 = (bf16[256,4096]{1,0:T(8,128)(2,1)S(1)}, bf16[256,4096]{1,0:T(8,128)(2,1)}, u32[]{:S(2)}) copy-start(bf16[256,4096]{1,0:T(8,128)(2,1)} %value.1) | copy-start | bytes 6291460

commit v8 on v7

--- a/solution.py
+++ b/solution.py
@@ -14,6 +14,7 @@
 SEGMENTS = 8
 RAW_SHARES = (4, 6)
 DONE_SHARES = (6,)
+RUN = 8
 VMEM_BYTES = 16 << 20
 F32 = jnp.float32
 
@@ -83,12 +84,26 @@
     return table.at[tile // per, pl.ds(first, count), lanes(tile % per * LANES)]
 
 
-def scan_segments(table, tokens):
+def runs_of(length):
+    steps = length // SEGMENTS
+    run = min(RUN, steps)
+    return run, steps // run
+
+
+def mode_rows(run, m, modes):
+    return pl.ds((run * modes + m) * SEGMENTS, SEGMENTS)
+
+
+def scan_segments(table, tokens, keep):
     modes = table.shape[1]
     steps = tokens.shape[0] // SEGMENTS
+    run, _ = runs_of(tokens.shape[0])
     decay = [row_of(table.at[0], m) for m in range(modes)]
     state = [tokens[step_rows(0), :]] * modes
     for i in range(1, steps):
+        if i % run == 0:
+            for m in range(modes):
+                keep(i // run, m, state[m])
         now = tokens[step_rows(i), :]
         state = [d * s + now for d, s in zip(decay, state)]
     chained = []
@@ -106,18 +121,45 @@
         table[1 + level] = jnp.exp(-rate * float(steps << level))
 
 
-def emit(table, weights, state, tokens, write):
-    modes = table.shape[1]
-    steps = tokens.shape[0] // SEGMENTS
-    decay = [row_of(table.at[0], m) for m in range(modes)]
-    weight = [row_of(weights, m) for m in range(modes)]
-    for i in range(steps):
-        now = tokens[step_rows(i), :]
-        state = [d * s + now for d, s in zip(decay, state)]
-        terms = [w * s for w, s in zip(weight, state)]
-        while len(terms) > 1:
-            terms = [a + b for a, b in zip(terms[::2], terms[1::2])]
-        write(i, terms[0], now)
+def fill_taps(mix, leaps, direct, rate, weight, gain=None):
+    decay = jnp.exp(-rate)
+    tap = jnp.sum(weight, axis=0, keepdims=True)
+    direct[pl.ds(0, 1), :] = tap if gain is None else tap + gain
+    now = weight
+    for i in range(mix.shape[0]):
+        now = now * decay
+        mix[i] = now
+        if i + 1 < mix.shape[0]:
+            direct[pl.ds(i + 1, 1), :] = jnp.sum(now, axis=0, keepdims=True)
+    for r in range(1, leaps.shape[0]):
+        leaps[r] = jnp.exp(-rate * float(mix.shape[0] * r))
+
+
+def emit(mix, leaps, direct, state, kept, tokens, write):
+    run, modes = mix.shape[:2]
+    runs = leaps.shape[0]
+    together = min(2, runs)
+    for begin in range(0, runs, together):
+        group = range(begin, begin + together)
+        starts = []
+        for r in group:
+            if r == 0:
+                starts.append([state(m) for m in range(modes)])
+            else:
+                starts.append([kept(r, m) + row_of(leaps.at[r], m) * state(m) for m in range(modes)])
+        for i in range(run):
+            sums = [None] * together
+            for m in range(modes):
+                weight = row_of(mix.at[i], m)
+                for j in range(together):
+                    term = weight * starts[j][m]
+                    sums[j] = term if sums[j] is None else sums[j] + term
+            for d in range(i + 1):
+                tap = row_of(direct, d)
+                for j, r in enumerate(group):
+                    sums[j] = sums[j] + tap * tokens[step_rows(r * run + i - d), :]
+            for j, r in enumerate(group):
+                write(r * run + i, sums[j])
 
 
 def fill_order(order, back=False):
@@ -176,10 +218,14 @@
             cols = lanes(t * LANES)
             tokens[...] = product[:, cols].astype(F32)
             fill_jumps(table, at_tile(rates, first + t)[...], steps)
-            state = scan_segments(table, tokens)
+
+            def keep(r, m, state, cols=cols, carry_out=carry_out):
+                carry_out[mode_rows(r, m, modes), cols] = state
+
+            state = scan_segments(table, tokens, keep)
             into = at_tile(totals, first + t)
             for m in range(modes):
-                carry_out[pl.ds(m * SEGMENTS, SEGMENTS), cols] = shifted(state[m], 1)
+                carry_out[mode_rows(0, m, modes), cols] = shifted(state[m], 1)
                 into[pl.ds(m, 1), :] = state[m][SEGMENTS - 1 :, :]
 
         over_tiles(product.shape[1], body)
@@ -227,7 +273,7 @@
     to_ring(heads, outs)
 
 
-def over_kernel(past, rates, weighing, out, tokens, table, weights, *, span, first):
+def over_kernel(past, rates, weighing, out, tokens, table, mix, leaps, direct, carry, *, span, first):
     steps = past.shape[0] // SEGMENTS
     modes = rates.shape[1]
     needed = lax.axis_index("ctx") >= FILTER_PARTS
@@ -239,13 +285,22 @@
             tokens[...] = past[:, cols].astype(F32)
             rate = at_tile(rates, first + t)[...]
             fill_jumps(table, rate, steps)
-            weights[...] = at_tile(weighing, first + t, 0, modes)[...] * jnp.exp(-rate * float(span))
-            state = [shifted(s, 1) for s in scan_segments(table, tokens)]
-
-            def write(i, value, now):
+            weight = at_tile(weighing, first + t, 0, modes)[...] * jnp.exp(-rate * float(span))
+            fill_taps(mix, leaps, direct, rate, weight)
+
+            def keep(r, m, state):
+                carry[mode_rows(r, m, modes), :] = state
+
+            for m, state in enumerate(scan_segments(table, tokens, keep)):
+                carry[mode_rows(0, m, modes), :] = shifted(state, 1)
+
+            def kept(r, m):
+                return carry[mode_rows(r, m, modes), :]
+
+            def write(i, value):
                 out[step_rows(i), cols] = value
 
-            emit(table, weights, state, tokens, write)
+            emit(mix, leaps, direct, lambda m: kept(0, m), kept, tokens, write)
 
         over_tiles(past.shape[1], body)
 
@@ -254,7 +309,7 @@
         out[...] = jnp.zeros_like(out)
 
 
-def ahead_kernel(product, rates, weighing, carry, out, tokens, table, weights, scr, *, span, first, n_ctx):
+def ahead_kernel(product, rates, weighing, carry, out, tokens, mix, leaps, direct, scr, *, span, first, n_ctx):
     modes = rates.shape[1]
 
     @pl.when(lax.axis_index("ctx") + FILTER_PARTS < n_ctx)
@@ -263,34 +318,44 @@
             cols = lanes(t * LANES)
             tokens[...] = product[:, cols].astype(F32)
             rate = at_tile(rates, first + t)[...]
-            table[0] = jnp.exp(-rate)
-            weights[...] = at_tile(weighing, first + t, 0, modes)[...] * jnp.exp(-rate * float(span))
-            state = [carry[pl.ds(m * SEGMENTS, SEGMENTS), cols] for m in range(modes)]
-
-            def write(i, value, now):
+            weight = at_tile(weighing, first + t, 0, modes)[...] * jnp.exp(-rate * float(span))
+            fill_taps(mix, leaps, direct, rate, weight)
+
+            def kept(r, m):
+                return carry[mode_rows(r, m, modes), cols]
+
+            def write(i, value):
                 scr[step_rows(i), :] = value
 
-            emit(table, weights, state, tokens, write)
+            emit(mix, leaps, direct, lambda m: kept(0, m), kept, tokens, write)
             out[:, cols] = scr[...].astype(jnp.bfloat16)
 
         over_tiles(product.shape[1], body)
 
 
-def local_kernel(product, rates, weighing, carry, out, tokens, table, weights, *, first):
+def local_kernel(product, rates, weighing, carry, out, tokens, mix, leaps, direct, *, first):
     modes = rates.shape[1]
 
     def body(t):
         cols = lanes(t * LANES)
         tokens[...] = product[:, cols].astype(F32)
-        table[0] = jnp.exp(-at_tile(rates, first + t)[...])
-        weights[...] = at_tile(weighing, first + t, 0, modes)[...]
-        gain = row_of(at_tile(weighing, first + t, modes, 1), 0)
-        state = [carry[pl.ds(m * SEGMENTS, SEGMENTS), cols] for m in range(modes)]
-
-        def write(i, value, now):
-            out[step_rows(i), cols] = value + gain * now
-
-        emit(table, weights, state, tokens, write)
+        own = at_tile(weighing, first + t)
+        fill_taps(
+            mix,
+            leaps,
+            direct,
+            at_tile(rates, first + t)[...],
+            own[pl.ds(0, modes), :],
+            own[pl.ds(modes, 1), :],
+        )
+
+        def kept(r, m):
+            return carry[mode_rows(r, m, modes), cols]
+
+        def write(i, value):
+            out[step_rows(i), cols] = value
+
+        emit(mix, leaps, direct, lambda m: kept(0, m), kept, tokens, write)
 
     over_tiles(product.shape[1], body)
 
@@ -304,7 +369,7 @@
     products, carries, overs = refs[:count], refs[count : 2 * count], refs[2 * count : 3 * count]
     refs = refs[3 * count :]
     befores, (rates, weighing, value, late, out, rest) = refs[:n_ch], refs[n_ch : n_ch + 6]
-    tokens, table, weights, scr, back, before, mixed, done, sems = refs[n_ch + 6 :]
+    tokens, table, weights, scr, back, before, mixed, done, sems, mix, leaps, direct, coming = refs[n_ch + 6 :]
     modes = rates.shape[1]
     length = value.shape[0]
     steps = length // SEGMENTS
@@ -328,14 +393,19 @@
         def body(t, first=first, product=product, carry=carry, k=k):
             cols = lanes(t * LANES)
             tokens[...] = product[:, cols].astype(F32)
-            gain = row_of(at_tile(weighing, first + t, modes, 1), 0)
-            state = arriving(first + t)
-            state = [carry[pl.ds(m * SEGMENTS, SEGMENTS), cols] + s for m, s in enumerate(state)]
-
-            def write(i, value, now):
-                scr[step_rows(i), :] = value + gain * now
-
-            emit(table, weights, state, tokens, write)
+            own = at_tile(weighing, first + t)
+            for m, state in enumerate(arriving(first + t)):
+                coming[step_rows(m), :] = carry[mode_rows(0, m, modes), cols] + state
+            rate = at_tile(rates, first + t)[...]
+            fill_taps(mix, leaps, direct, rate, own[pl.ds(0, modes), :], own[pl.ds(modes, 1), :])
+
+            def kept(r, m):
+                return carry[mode_rows(r, m, modes), cols]
+
+            def write(i, value):
+                scr[step_rows(i), :] = value
+
+            emit(mix, leaps, direct, lambda m: coming[step_rows(m), :], kept, tokens, write)
             mixed[:, cols] = (scr[...] - overs[k][:, cols].astype(F32)).astype(jnp.bfloat16)
 
         over_tiles(width, body)
@@ -414,6 +484,12 @@
     table_scr = pltpu.VMEM((4, modes, LANES), F32)
     weights_scr = pltpu.VMEM((modes, LANES), F32)
     order_scr = pltpu.VMEM((length, length), bf16)
+    run, runs = runs_of(length)
+    taps_scr = [
+        pltpu.VMEM((run, modes, LANES), F32),
+        pltpu.VMEM((runs, modes, LANES), F32),
+        pltpu.VMEM((run, LANES), F32),
+    ]
 
     def call(kernel, out_shape, scratch, args, **options):
         specs = dict(in_specs=[vmem] * len(args), out_specs=jax.tree.map(lambda _: vmem, out_shape))
@@ -460,7 +536,7 @@
 
     outs = call(
         functools.partial(states_kernel, count=count, n_ch=n_ch),
-        [shape(modes * SEGMENTS, width) for width in widths] + [shape(modes, group)] * n_ch + [stack(modes)],
+        [shape(runs * modes * SEGMENTS, width) for width in widths] + [shape(modes, group)] * n_ch + [stack(modes)],
         [tokens_scr, table_scr, pltpu.VMEM((n_ch, modes, group), F32)],
         (*products, *rate_parts),
     )
@@ -475,7 +551,7 @@
             call(
                 functools.partial(over_kernel, span=span, first=firsts[k] // LANES),
                 shape(length, widths[k]),
-                [tokens_scr, table_scr, weights_scr],
+                [tokens_scr, table_scr, *taps_scr, pltpu.VMEM((runs * modes * SEGMENTS, LANES), F32)],
                 (pasts[k], rates, weighing),
             )
         )
@@ -484,7 +560,7 @@
         return call(
             functools.partial(ahead_kernel, span=span, first=firsts[k] // LANES, n_ctx=n_ctx),
             shape(length, widths[k], bf16),
-            [tokens_scr, table_scr, weights_scr, tokens_scr],
+            [tokens_scr, *taps_scr, tokens_scr],
             (products[k], rates, weighing, carries[k]),
         )
 
@@ -515,7 +591,7 @@
     late = call(
         functools.partial(local_kernel, first=firsts[-1] // LANES),
         shape(length, widths[-1]),
-        [tokens_scr, table_scr, weights_scr],
+        [tokens_scr, *taps_scr],
         (products[-1], rates, weighing, carries[-1]),
     )
     widest = max(widths[:-1])
@@ -532,6 +608,8 @@
             pltpu.VMEM((length, widest), bf16),
             pltpu.VMEM((2, length, widest), bf16),
             pltpu.SemaphoreType.DMA((2,)),
+            *taps_scr,
+            pltpu.VMEM((modes * SEGMENTS, LANES), F32),
         ],
         (*products[:-1], *carries[:-1], *overs[:-1], *befores, rates, weighing, value, late),
         out_specs=[anywhere, vmem],

time: 115 us -> 111 us (0.965)
  Pallas kernels: 32.2 us -> 29.1 us
    pallas_call x13, Pallas kernels: 32.2 us -> 29.1 us  [call(): pl.pallas_call(kernel, out_shape=out_shape, scratch_shapes=scratch, compi...]
  transfers between devices with their start and end apart: 19 -> 19, of which waited for: 7 -> 7; matrix products, arithmetic and copies ran while one was open for 1% -> 1% of each run, Pallas kernels for 27% -> 25%
where the time goes in v8:
time: 111 us
  waiting for transfers between devices  49.4 us (45%)
  starting transfers between devices  31.3 us (28%)
  Pallas kernels  29.1 us (26%)
    ppermute x7, waiting for transfers between devices, from_behind(): lax.ppermute(value, axis, [(source, source + steps) for source in range(c...  39.6 us
    pallas_call x13, Pallas kernels, call(): pl.pallas_call(kernel, out_shape=out_shape, scratch_shapes=scratch, compi...  29.1 us
    ppermute x12, starting transfers between devices, ring(): moved.append(lax.ppermute(part, axis, pairs) if k else part)  19.7 us
    ppermute x7, starting transfers between devices, from_behind(): lax.ppermute(value, axis, [(source, source + steps) for source in range(c...  11.7 us
    ppermute x12, waiting for transfers between devices, ring(): moved.append(lax.ppermute(part, axis, pairs) if k else part)  9.78 us
  transfers between devices with their start and end apart: 19, of which 7 were waited for; matrix products, arithmetic and copies ran while one was open for 1% of the time, Pallas kernels for 25%

profile of v8, /device:TPU:4, one launch (start us, length us, event | category | flops | bytes accessed | tf_op | source)
XLA Modules:
  0.0 111.2 jit_solution(7502470310976600828)
XLA Ops:
  0.0 3.6 %collective-permute-start.2 = (f32[16,1024]{1,0:T(8,128)}, f32[16,1024]{1,0:T(8,128)S(1)}, u32[]{:S(2)}, u32[]{:S(2)}) collective-permute-start(f32[16,1024]{1,0:T(8,128)} %bitcast.3), channel_id=1, source_target_pairs={{0,3},{1,2},{2,1},{3,0},{4,7},{5,6},{6,5},{7,4},{8,11},{9,10},{10,... | collective-permute-start | bytes 196616 | tf_op jit(solution)/shard_map/ppermute | solution.py:38
  3.7 0.9 maximum_maximum_fusion.refs_0_
  4.6 0.3 collective-permute-start.6
  4.9 0.8 collective-permute-start.5
  5.7 3.4 %collective-permute-start.4 = (f32[24,1024]{1,0:T(8,128)S(1)}, f32[24,1024]{1,0:T(8,128)S(1)}, u32[]{:S(2)}, u32[]{:S(2)}) collective-permute-start(f32[24,1024]{1,0:T(8,128)S(1)} %maximum_maximum_fusion.refs_0_), channel_id=1, source_target_pairs={{0,1},{1,0},{2,3},{3,2},{4,5},{5,4},{6,7},{7,6},{8,9},{9,8},{10,11... | collective-permute-start | bytes 294920 | tf_op jit(solution)/shard_map/ppermute | solution.py:38
  9.1 1.5 %collective-permute-start = (f32[16,1024]{1,0:T(8,128)}, f32[16,1024]{1,0:T(8,128)S(1)}, u32[]{:S(2)}, u32[]{:S(2)}) collective-permute-start(f32[16,1024]{1,0:T(8,128)} %bitcast.5), channel_id=1, source_target_pairs={{0,1},{1,0},{2,3},{3,2},{4,5},{5,4},{6,7},{7,6},{8,9},{9,8},{10,11... | collective-permute-start | bytes 196616 | tf_op jit(solution)/shard_map/ppermute | solution.py:38
  10.6 1.6 %shard_map.64.refs_0_ = bf16[256,1024]{1,0:T(8,128)(2,1)S(1)} custom-call(bf16[256,4096]{1,0:T(8,128)(2,1)} %query.5, bf16[256,4096]{1,0:T(8,128)(2,1)} %key_in.5), custom_call_target="tpu_custom_call" | custom-call | tf_op jit(solution)/shard_map/pallas_call | solution.py:497
  12.2 0.4 shard_map.66.refs_2_.product
  12.6 0.4 shard_map.65.refs_1_
  13.1 4.8 %collective-permute-done.1.refs_5_ = f32[16,1024]{1,0:T(8,128)S(1)} collective-permute-done((f32[16,1024]{1,0:T(8,128)}, f32[16,1024]{1,0:T(8,128)S(1)}, u32[]{:S(2)}, u32[]{:S(2)}) %collective-permute-start.1) | collective-permute-done | bytes 65568 | tf_op jit(solution)/shard_map/ppermute | solution.py:38
  17.9 1.3 %collective-permute-start.7 = (bf16[256,1536]{1,0:T(8,128)(2,1)S(1)}, bf16[256,1536]{1,0:T(8,128)(2,1)S(1)}, u32[]{:S(2)}, u32[]{:S(2)}) collective-permute-start(bf16[256,1536]{1,0:T(8,128)(2,1)S(1)} %shard_map.65.refs_1_), channel_id=1, source_target_pairs={{0,16},{4,20},{8,24},{12,28},{1,17},{5,21},{9,25},{13,29},{2,18},{... | collective-permute-start | bytes 2359304 | tf_op jit(solution)/shard_map/ppermute | solution.py:24
  19.2 6.4 %shard_map.67 = (f32[512,1024]{1,0:T(8,128)S(1)}, f32[512,1536]{1,0:T(8,128)S(1)}, f32[512,1536]{1,0:T(8,128)S(1)}, f32[16,1024]{1,0:T(8,128)S(1)}, f32[16,1024]...) custom-call(bf16[256,1024]{1,0:T(8,128)(2,1)S(1)} %shard_map.64.refs_0_, ...), custom_call_target="tpu_custom_call" | custom-call | tf_op jit(solution)/shard_map/pallas_call | solution.py:497
  25.7 1.3 %collective-permute-start.18 = (bf16[256,1536]{1,0:T(8,128)(2,1)S(1)}, bf16[256,1536]{1,0:T(8,128)(2,1)S(1)}, u32[]{:S(2)}, u32[]{:S(2)}) collective-permute-start(bf16[256,1536]{1,0:T(8,128)(2,1)S(1)} %shard_map.75), channel_id=1, source_target_pairs={{0,16},{4,20},{8,24},{12,28},{1,17},{5,21},{9,25},{13,29},{2,18},{... | collective-permute-start | bytes 2359304 | tf_op jit(solution)/shard_map/ppermute | solution.py:24
  27.0 1.3 %collective-permute-start.3 = (bf16[256,1024]{1,0:T(8,128)(2,1)S(1)}, bf16[256,1024]{1,0:T(8,128)(2,1)S(1)}, u32[]{:S(2)}, u32[]{:S(2)}) collective-permute-start(bf16[256,1024]{1,0:T(8,128)(2,1)S(1)} %shard_map.64.refs_0_), channel_id=1, source_target_pairs={{0,16},{4,20},{8,24},{12,28},{1,17},{5,21},{9,25},{13,29},{2,18},{... | collective-permute-start | bytes 1572872 | tf_op jit(solution)/shard_map/ppermute | solution.py:24
  28.4 3.2 %collective-permute-start.9 = (f32[16,1024]{1,0:T(8,128)S(1)}, f32[16,1024]{1,0:T(8,128)S(1)}, u32[]{:S(2)}, u32[]{:S(2)}) collective-permute-start(f32[16,1024]{1,0:T(8,128)S(1)} %get-tuple-element.27), channel_id=1, source_target_pairs={{0,2},{1,3},{2,0},{3,1},{4,6},{5,7},{6,4},{7,5},{8,10},{9,11},{10,... | collective-permute-start | bytes 196616 | tf_op jit(solution)/shard_map/ppermute | solution.py:38
  31.6 1.3 %collective-permute-done.8.refs_1_ = f32[16,1024]{1,0:T(8,128)S(1)} collective-permute-done((f32[16,1024]{1,0:T(8,128)S(1)}, f32[16,1024]{1,0:T(8,128)S(1)}, u32[]{:S(2)}, u32[]{:S(2)}) %collective-permute-start.8) | collective-permute-done | bytes 65568 | tf_op jit(solution)/shard_map/ppermute | solution.py:38
  32.9 2.4 %collective-permute-start.10 = (f32[16,1024]{1,0:T(8,128)S(1)}, f32[16,1024]{1,0:T(8,128)S(1)}, u32[]{:S(2)}, u32[]{:S(2)}) collective-permute-start(f32[16,1024]{1,0:T(8,128)S(1)} %get-tuple-element.28), channel_id=1, source_target_pairs={{0,3},{1,2},{2,1},{3,0},{4,7},{5,6},{6,5},{7,4},{8,11},{9,10},{10,... | collective-permute-start | bytes 196616 | tf_op jit(solution)/shard_map/ppermute | solution.py:38
  35.4 3.6 %collective-permute-done.10.refs_3_ = f32[16,1024]{1,0:T(8,128)S(1)} collective-permute-done((f32[16,1024]{1,0:T(8,128)S(1)}, f32[16,1024]{1,0:T(8,128)S(1)}, u32[]{:S(2)}, u32[]{:S(2)}) %collective-permute-start.10) | collective-permute-done | bytes 65568 | tf_op jit(solution)/shard_map/ppermute | solution.py:38
  39.1 1.3 %collective-permute-start.11 = (f32[4,16,1024]{2,1,0:T(8,128)S(1)}, f32[4,16,1024]{2,1,0:T(8,128)S(1)}, u32[]{:S(2)}, u32[]{:S(2)}) collective-permute-start(f32[4,16,1024]{2,1,0:T(8,128)S(1)} %get-tuple-element.30), channel_id=1, source_target_pairs={{0,16},{4,20},{8,24},{12,28},{1,17},{5,21},{9,25},{13,29},{2,18},{... | collective-permute-start | bytes 786440 | tf_op jit(solution)/shard_map/ppermute | solution.py:24
  40.4 1.9 %collective-permute-start.14 = (f32[16,1024]{1,0:T(8,128)S(1)}, f32[16,1024]{1,0:T(8,128)S(1)}, u32[]{:S(2)}, u32[]{:S(2)}) collective-permute-start(f32[16,1024]{1,0:T(8,128)S(1)} %get-tuple-element.31), channel_id=1, source_target_pairs={{0,12},{4,16},{8,20},{12,24},{16,28},{1,13},{5,17},{9,21},{13,25},... | collective-permute-start | bytes 196616 | tf_op jit(solution)/shard_map/ppermute | solution.py:24
  42.3 30.7 %collective-permute-done.14.refs_5_ = f32[16,1024]{1,0:T(8,128)S(1)} collective-permute-done((f32[16,1024]{1,0:T(8,128)S(1)}, f32[16,1024]{1,0:T(8,128)S(1)}, u32[]{:S(2)}, u32[]{:S(2)}) %collective-permute-start.14) | collective-permute-done | bytes 65568 | tf_op jit(solution)/shard_map/ppermute | solution.py:24
  73.0 2.7 %collective-permute-start.13 = (f32[16,1024]{1,0:T(8,128)S(1)}, f32[16,1024]{1,0:T(8,128)S(1)}, u32[]{:S(2)}, u32[]{:S(2)}) collective-permute-start(f32[16,1024]{1,0:T(8,128)S(1)} %get-tuple-element.31), channel_id=1, source_target_pairs={{0,8},{4,12},{8,16},{12,20},{16,24},{20,28},{1,9},{5,13},{9,17},{1... | collective-permute-start | bytes 196616 | tf_op jit(solution)/shard_map/ppermute | solution.py:24
  75.7 4.4 %collective-permute-done.13.refs_4_ = f32[16,1024]{1,0:T(8,128)S(1)} collective-permute-done((f32[16,1024]{1,0:T(8,128)S(1)}, f32[16,1024]{1,0:T(8,128)S(1)}, u32[]{:S(2)}, u32[]{:S(2)}) %collective-permute-start.13) | collective-permute-done | bytes 65568 | tf_op jit(solution)/shard_map/ppermute | solution.py:24
  80.0 1.9 %collective-permute-start.12 = (f32[16,1024]{1,0:T(8,128)S(1)}, f32[16,1024]{1,0:T(8,128)S(1)}, u32[]{:S(2)}, u32[]{:S(2)}) collective-permute-start(f32[16,1024]{1,0:T(8,128)S(1)} %get-tuple-element.31), channel_id=1, source_target_pairs={{0,4},{4,8},{8,12},{12,16},{16,20},{20,24},{24,28},{1,5},{5,9},{9,... | collective-permute-start | bytes 196616 | tf_op jit(solution)/shard_map/ppermute | solution.py:24
  82.0 4.6 %collective-permute-done.12.refs_3_ = f32[16,1024]{1,0:T(8,128)S(1)} collective-permute-done((f32[16,1024]{1,0:T(8,128)S(1)}, f32[16,1024]{1,0:T(8,128)S(1)}, u32[]{:S(2)}, u32[]{:S(2)}) %collective-permute-start.12) | collective-permute-done | bytes 65568 | tf_op jit(solution)/shard_map/ppermute | solution.py:24
  86.7 2.9 %collective-permute-start.16 = (f32[16,1024]{1,0:T(8,128)S(1)}, f32[16,1024]{1,0:T(8,128)S(1)}, u32[]{:S(2)}, u32[]{:S(2)}) collective-permute-start(f32[16,1024]{1,0:T(8,128)S(1)} %get-tuple-element.34), channel_id=1, source_target_pairs={{0,2},{1,3},{2,0},{3,1},{4,6},{5,7},{6,4},{7,5},{8,10},{9,11},{10,... | collective-permute-start | bytes 196616 | tf_op jit(solution)/shard_map/ppermute | solution.py:38
  89.6 1.5 %collective-permute-start.17 = (f32[16,1024]{1,0:T(8,128)S(1)}, f32[16,1024]{1,0:T(8,128)S(1)}, u32[]{:S(2)}, u32[]{:S(2)}) collective-permute-start(f32[16,1024]{1,0:T(8,128)S(1)} %get-tuple-element.35), channel_id=1, source_target_pairs={{0,3},{1,2},{2,1},{3,0},{4,7},{5,6},{6,5},{7,4},{8,11},{9,10},{10,... | collective-permute-start | bytes 196616 | tf_op jit(solution)/shard_map/ppermute | solution.py:38
  91.1 2.9 %shard_map.73.refs_13_ = f32[256,1536]{1,0:T(8,128)S(1)} custom-call(bf16[256,1536]{1,0:T(8,128)(2,1)S(1)} %shard_map.66.refs_2_.product, f32[4,16,1024]{2,1,0:T(8,128)S(1)} %get-tuple-element.24.rates.refs_10_, f32[4,24,1024]{2,1,0:T(8,128)S(1)} %shard_map.68.weighing.refs_11_, f32[512,1536]{1,0:T(8,128)S(1)} %get-tuple-element.36.carry), custom_call_target="tpu_custom_call" | custom-call | tf_op jit(solution)/shard_map/pallas_call | solution.py:497
  94.0 3.1 %shard_map.69.refs_4_ = f32[256,1024]{1,0:T(8,128)S(1)} custom-call(bf16[256,1024]{1,0:T(8,128)(2,1)S(1)} %collective-permute-done.3.past, f32[4,16,1024]{2,1,0:T(8,128)S(1)} %get-tuple-element.24.rates.refs_10_, f32[4,24,1024]{2,1,0:T(8,128)S(1)} %shard_map.68.weighing.refs_11_), custom_call_target="tpu_custom_call" | custom-call | tf_op jit(solution)/shard_map/pallas_call | solution.py:497
  97.1 4.6 %shard_map.70.refs_5_ = f32[256,1536]{1,0:T(8,128)S(1)} custom-call(bf16[256,1536]{1,0:T(8,128)(2,1)S(1)} %collective-permute-done.7.past, f32[4,16,1024]{2,1,0:T(8,128)S(1)} %get-tuple-element.24.rates.refs_10_, f32[4,24,1024]{2,1,0:T(8,128)S(1)} %shard_map.68.weighing.refs_11_), custom_call_target="tpu_custom_call" | custom-call | tf_op jit(solution)/shard_map/pallas_call | solution.py:497
  101.8 8.1 %shard_map.74 = (bf16[256,4096]{1,0:T(8,128)(2,1)}, f32[256,1536]{1,0:T(8,128)S(1)}) custom-call(bf16[256,1024]{1,0:T(8,128)(2,1)S(1)} %shard_map.64.refs_0_, bf16[256,1536]{1,0:T(8,128)(2,1)S(1)} %shard_map.65.refs_1_, f32[512,1024]{1,0:T(8,128)S(1)} %get-tuple-element.22.refs_2_, f32[512,1536]{1,0:T(8,128)S(1)} %get-tuple-element.23.refs_3_, ...), custom_call_target="tpu_custom_call" | custom-call | tf_op jit(solution)/shard_map/pallas_call | solution.py:497
  110.0 1.2 %shard_map.76 = bf16[256,4096]{1,0:T(8,128)(2,1)} custom-call(f32[256,1536]{1,0:T(8,128)S(1)} %get-tuple-element.37.rest, bf16[256,1536]{1,0:T(8,128)(2,1)S(1)} %collective-permute-done.18.over, bf16[256,4096]{1,0:T(8,128)(2,1)S(1)} %copy-done.2, bf16[256,4096]{1,0:T(8,128)(2,1)} %get-tuple-element.38.partial), custom_call_target="tpu_custom_call", output_to_operand_aliasing={{}: (3, {})} | custom-call | tf_op jit(solution)/shard_map/pallas_call | solution.py:497
  (30 shorter events, 0.6 us)
Async XLA Ops:
  0.0 9.1 %collective-permute-start.2 = (f32[16,1024]{1,0:T(8,128)}, f32[16,1024]{1,0:T(8,128)S(1)}, u32[]{:S(2)}, u32[]{:S(2)}) collective-permute-start(f32[16,1024]{1,0:T(8,128)} %bitcast.3), channel_id=1, source_target_pairs={{0,3},{1,2},{2,1},{3,0},{4,7},{5,6},{6,5},{7,4},{8,11},{9,10},{10,... | collective-permute-start | bytes 196616 | tf_op jit(solution)/shard_map/ppermute | solution.py:38
  4.6 7.5 %copy-start = (bf16[256,4096]{1,0:T(8,128)(2,1)S(1)}, bf16[256,4096]{1,0:T(8,128)(2,1)}, u32[]{:S(2)}) copy-start(bf16[256,4096]{1,0:T(8,128)(2,1)} %query.5) | copy-start | bytes 6291460
  4.6 7.6 %copy-start.1 = (bf16[256,4096]{1,0:T(8,128)(2,1)S(1)}, bf16[256,4096]{1,0:T(8,128)(2,1)}, u32[]{:S(2)}) copy-start(bf16[256,4096]{1,0:T(8,128)(2,1)} %key_in.5) | copy-start | bytes 6291460
  4.6 21.0 %collective-permute-start.6 = (f32[24,1024]{1,0:T(8,128)S(1)}, f32[24,1024]{1,0:T(8,128)S(1)}, u32[]{:S(2)}, u32[]{:S(2)}) collective-permute-start(f32[24,1024]{1,0:T(8,128)S(1)} %maximum_maximum_fusion.refs_0_), channel_id=1, source_target_pairs={{0,3},{1,2},{2,1},{3,0},{4,7},{5,6},{6,5},{7,4},{8,11},{9,10},{10,... | collective-permute-start | bytes 294920 | tf_op jit(solution)/shard_map/ppermute | solution.py:38
  4.9 20.7 %collective-permute-start.5 = (f32[24,1024]{1,0:T(8,128)S(1)}, f32[24,1024]{1,0:T(8,128)S(1)}, u32[]{:S(2)}, u32[]{:S(2)}) collective-permute-start(f32[24,1024]{1,0:T(8,128)S(1)} %maximum_maximum_fusion.refs_0_), channel_id=1, source_target_pairs={{0,2},{1,3},{2,0},{3,1},{4,6},{5,7},{6,4},{7,5},{8,10},{9,11},{10,... | collective-permute-start | bytes 294920 | tf_op jit(solution)/shard_map/ppermute | solution.py:38
  5.7 20.0 %collective-permute-start.4 = (f32[24,1024]{1,0:T(8,128)S(1)}, f32[24,1024]{1,0:T(8,128)S(1)}, u32[]{:S(2)}, u32[]{:S(2)}) collective-permute-start(f32[24,1024]{1,0:T(8,128)S(1)} %maximum_maximum_fusion.refs_0_), channel_id=1, source_target_pairs={{0,1},{1,0},{2,3},{3,2},{4,5},{5,4},{6,7},{7,6},{8,9},{9,8},{10,11... | collective-permute-start | bytes 294920 | tf_op jit(solution)/shard_map/ppermute | solution.py:38
  9.1 8.8 %collective-permute-start.1 = (f32[16,1024]{1,0:T(8,128)}, f32[16,1024]{1,0:T(8,128)S(1)}, u32[]{:S(2)}, u32[]{:S(2)}) collective-permute-start(f32[16,1024]{1,0:T(8,128)} %bitcast.4), channel_id=1, source_target_pairs={{0,2},{1,3},{2,0},{3,1},{4,6},{5,7},{6,4},{7,5},{8,10},{9,11},{10,... | collective-permute-start | bytes 196616 | tf_op jit(solution)/shard_map/ppermute | solution.py:38
  9.1 10.1 %collective-permute-start = (f32[16,1024]{1,0:T(8,128)}, f32[16,1024]{1,0:T(8,128)S(1)}, u32[]{:S(2)}, u32[]{:S(2)}) collective-permute-start(f32[16,1024]{1,0:T(8,128)} %bitcast.5), channel_id=1, source_target_pairs={{0,1},{1,0},{2,3},{3,2},{4,5},{5,4},{6,7},{7,6},{8,9},{9,8},{10,11... | collective-permute-start | bytes 196616 | tf_op jit(solution)/shard_map/ppermute | solution.py:38
  12.6 6.6 %copy-start.3 = (f32[1024,16]{0,1:T(8,128)S(1)}, f32[1024,16]{0,1:T(8,128)}, u32[]{:S(2)}) copy-start(f32[1024,16]{0,1:T(8,128)} %param.10) | copy-start | bytes 196612
  17.9 79.2 %collective-permute-start.7 = (bf16[256,1536]{1,0:T(8,128)(2,1)S(1)}, bf16[256,1536]{1,0:T(8,128)(2,1)S(1)}, u32[]{:S(2)}, u32[]{:S(2)}) collective-permute-start(bf16[256,1536]{1,0:T(8,128)(2,1)S(1)} %shard_map.65.refs_1_), channel_id=1, source_target_pairs={{0,16},{4,20},{8,24},{12,28},{1,17},{5,21},{9,25},{13,29},{2,18},{... | collective-permute-start | bytes 2359304 | tf_op jit(solution)/shard_map/ppermute | solution.py:24
  25.7 84.2 %collective-permute-start.18 = (bf16[256,1536]{1,0:T(8,128)(2,1)S(1)}, bf16[256,1536]{1,0:T(8,128)(2,1)S(1)}, u32[]{:S(2)}, u32[]{:S(2)}) collective-permute-start(bf16[256,1536]{1,0:T(8,128)(2,1)S(1)} %shard_map.75), channel_id=1, source_target_pairs={{0,16},{4,20},{8,24},{12,28},{1,17},{5,21},{9,25},{13,29},{2,18},{... | collective-permute-start | bytes 2359304 | tf_op jit(solution)/shard_map/ppermute | solution.py:24
  27.0 62.6 %collective-permute-start.3 = (bf16[256,1024]{1,0:T(8,128)(2,1)S(1)}, bf16[256,1024]{1,0:T(8,128)(2,1)S(1)}, u32[]{:S(2)}, u32[]{:S(2)}) collective-permute-start(bf16[256,1024]{1,0:T(8,128)(2,1)S(1)} %shard_map.64.refs_0_), channel_id=1, source_target_pairs={{0,16},{4,20},{8,24},{12,28},{1,17},{5,21},{9,25},{13,29},{2,18},{... | collective-permute-start | bytes 1572872 | tf_op jit(solution)/shard_map/ppermute | solution.py:24
  28.3 4.6 %collective-permute-start.8 = (f32[16,1024]{1,0:T(8,128)S(1)}, f32[16,1024]{1,0:T(8,128)S(1)}, u32[]{:S(2)}, u32[]{:S(2)}) collective-permute-start(f32[16,1024]{1,0:T(8,128)S(1)} %get-tuple-element.26), channel_id=1, source_target_pairs={{0,1},{1,0},{2,3},{3,2},{4,5},{5,4},{6,7},{7,6},{8,9},{9,8},{10,11... | collective-permute-start | bytes 196616 | tf_op jit(solution)/shard_map/ppermute | solution.py:38
  28.4 7.0 %collective-permute-start.9 = (f32[16,1024]{1,0:T(8,128)S(1)}, f32[16,1024]{1,0:T(8,128)S(1)}, u32[]{:S(2)}, u32[]{:S(2)}) collective-permute-start(f32[16,1024]{1,0:T(8,128)S(1)} %get-tuple-element.27), channel_id=1, source_target_pairs={{0,2},{1,3},{2,0},{3,1},{4,6},{5,7},{6,4},{7,5},{8,10},{9,11},{10,... | collective-permute-start | bytes 196616 | tf_op jit(solution)/shard_map/ppermute | solution.py:38
  32.9 6.1 %collective-permute-start.10 = (f32[16,1024]{1,0:T(8,128)S(1)}, f32[16,1024]{1,0:T(8,128)S(1)}, u32[]{:S(2)}, u32[]{:S(2)}) collective-permute-start(f32[16,1024]{1,0:T(8,128)S(1)} %get-tuple-element.28), channel_id=1, source_target_pairs={{0,3},{1,2},{2,1},{3,0},{4,7},{5,6},{6,5},{7,4},{8,11},{9,10},{10,... | collective-permute-start | bytes 196616 | tf_op jit(solution)/shard_map/ppermute | solution.py:38
  39.1 47.5 %collective-permute-start.11 = (f32[4,16,1024]{2,1,0:T(8,128)S(1)}, f32[4,16,1024]{2,1,0:T(8,128)S(1)}, u32[]{:S(2)}, u32[]{:S(2)}) collective-permute-start(f32[4,16,1024]{2,1,0:T(8,128)S(1)} %get-tuple-element.30), channel_id=1, source_target_pairs={{0,16},{4,20},{8,24},{12,28},{1,17},{5,21},{9,25},{13,29},{2,18},{... | collective-permute-start | bytes 786440 | tf_op jit(solution)/shard_map/ppermute | solution.py:24
  40.4 32.6 %collective-permute-start.14 = (f32[16,1024]{1,0:T(8,128)S(1)}, f32[16,1024]{1,0:T(8,128)S(1)}, u32[]{:S(2)}, u32[]{:S(2)}) collective-permute-start(f32[16,1024]{1,0:T(8,128)S(1)} %get-tuple-element.31), channel_id=1, source_target_pairs={{0,12},{4,16},{8,20},{12,24},{16,28},{1,13},{5,17},{9,21},{13,25},... | collective-permute-start | bytes 196616 | tf_op jit(solution)/shard_map/ppermute | solution.py:24
  73.0 7.0 %collective-permute-start.13 = (f32[16,1024]{1,0:T(8,128)S(1)}, f32[16,1024]{1,0:T(8,128)S(1)}, u32[]{:S(2)}, u32[]{:S(2)}) collective-permute-start(f32[16,1024]{1,0:T(8,128)S(1)} %get-tuple-element.31), channel_id=1, source_target_pairs={{0,8},{4,12},{8,16},{12,20},{16,24},{20,28},{1,9},{5,13},{9,17},{1... | collective-permute-start | bytes 196616 | tf_op jit(solution)/shard_map/ppermute | solution.py:24
  80.0 6.5 %collective-permute-start.12 = (f32[16,1024]{1,0:T(8,128)S(1)}, f32[16,1024]{1,0:T(8,128)S(1)}, u32[]{:S(2)}, u32[]{:S(2)}) collective-permute-start(f32[16,1024]{1,0:T(8,128)S(1)} %get-tuple-element.31), channel_id=1, source_target_pairs={{0,4},{4,8},{8,12},{12,16},{16,20},{20,24},{24,28},{1,5},{5,9},{9,... | collective-permute-start | bytes 196616 | tf_op jit(solution)/shard_map/ppermute | solution.py:24
  86.6 15.1 %collective-permute-start.15 = (f32[16,1024]{1,0:T(8,128)S(1)}, f32[16,1024]{1,0:T(8,128)S(1)}, u32[]{:S(2)}, u32[]{:S(2)}) collective-permute-start(f32[16,1024]{1,0:T(8,128)S(1)} %get-tuple-element.33), channel_id=1, source_target_pairs={{0,1},{1,0},{2,3},{3,2},{4,5},{5,4},{6,7},{7,6},{8,9},{9,8},{10,11... | collective-permute-start | bytes 196616 | tf_op jit(solution)/shard_map/ppermute | solution.py:38
  86.7 15.1 %collective-permute-start.16 = (f32[16,1024]{1,0:T(8,128)S(1)}, f32[16,1024]{1,0:T(8,128)S(1)}, u32[]{:S(2)}, u32[]{:S(2)}) collective-permute-start(f32[16,1024]{1,0:T(8,128)S(1)} %get-tuple-element.34), channel_id=1, source_target_pairs={{0,2},{1,3},{2,0},{3,1},{4,6},{5,7},{6,4},{7,5},{8,10},{9,11},{10,... | collective-permute-start | bytes 196616 | tf_op jit(solution)/shard_map/ppermute | solution.py:38
  89.6 12.1 %collective-permute-start.17 = (f32[16,1024]{1,0:T(8,128)S(1)}, f32[16,1024]{1,0:T(8,128)S(1)}, u32[]{:S(2)}, u32[]{:S(2)}) collective-permute-start(f32[16,1024]{1,0:T(8,128)S(1)} %get-tuple-element.35), channel_id=1, source_target_pairs={{0,3},{1,2},{2,1},{3,0},{4,7},{5,6},{6,5},{7,4},{8,11},{9,10},{10,... | collective-permute-start | bytes 196616 | tf_op jit(solution)/shard_map/ppermute | solution.py:38
  94.0 7.8 %copy-start.2 = (bf16[256,4096]{1,0:T(8,128)(2,1)S(1)}, bf16[256,4096]{1,0:T(8,128)(2,1)}, u32[]{:S(2)}) copy-start(bf16[256,4096]{1,0:T(8,128)(2,1)} %value.1) | copy-start | bytes 6291460

commit v9 on v8

--- a/solution.py
+++ b/solution.py
@@ -12,8 +12,8 @@
 FILTER_PARTS = 4
 LANES = 128
 SEGMENTS = 8
-RAW_SHARES = (4, 6)
-DONE_SHARES = (6,)
+RAW_SHARES = (4, 5)
+DONE_SHARES = (7,)
 RUN = 8
 VMEM_BYTES = 16 << 20
 F32 = jnp.float32
@@ -251,14 +251,15 @@
     whole[...] = running
 
 
+def pair_kernel(whole, earlier, rate, out, *, part):
+    out[...] = whole[...] + jnp.exp(-rate[...] * float(part)) * earlier[...]
+
+
 def heads_kernel(*refs, length, parts):
-    blocks, rate, oldest, *rest = refs
-    wholes, outs, heads = rest[: parts - 1], rest[parts - 1 : -1], rest[-1]
+    blocks, rate, oldest, newer, pairs, *outs, heads = refs
     count = blocks.shape[0]
     rates = rate[...]
-    older = wholes[0][...]
-    for j in range(1, parts - 1):
-        older = older + jnp.exp(-rates * float(length * count * j)) * wholes[j][...]
+    older = newer[...] + jnp.exp(-rates * float(length * count)) * pairs[...]
     last = jnp.exp(-rates * float(length * count * (parts - 1)))
     jump = jnp.exp(-rates * float(length))
     running = None
@@ -574,17 +575,18 @@
         [],
         (*sums, own_rate),
     )
+    assert FILTER_PARTS == 4
+    newer = from_behind(whole, "ctx", 1)
     oldest = from_behind(tails, "ctx", FILTER_PARTS)
-    wholes = []
-    for j in range(1, FILTER_PARTS):
-        wholes.append(from_behind(whole, "ctx", j))
+    pair = call(functools.partial(pair_kernel, part=length * n_ch), shape(modes, group), [], (whole, newer, own_rate))
+    pairs = from_behind(pair, "ctx", 2)
     for ahead in aheads:
         overs.append(from_behind(ahead, "ctx", FILTER_PARTS))
     heads = call(
         functools.partial(heads_kernel, length=length, parts=FILTER_PARTS),
         [shape(modes, group)] * n_ch,
         [pltpu.VMEM((n_ch, modes, group), F32)],
-        (blocks, own_rate, oldest, *wholes),
+        (blocks, own_rate, oldest, newer, pairs),
     )
     befores = ring(heads, "ch")
 

time: 111 us -> 109 us (0.982)
  starting transfers between devices: 31.3 us -> 28 us
  local copies, waits for them, and re-layouts: 0.1 us -> 3.27 us
  waiting for transfers between devices: 49.4 us -> 47.7 us
    ppermute x7 -> x6, waiting for transfers between devices: 39.6 us -> 35.7 us  [from_behind(): lax.ppermute(value, axis, [(source, source + steps) for source in range(c...]
    unnamed x8, local copies, waits for them, and re-layouts: 0.02 us -> 3.19 us
    ppermute x12, waiting for transfers between devices: 9.78 us -> 12 us  [ring(): moved.append(lax.ppermute(part, axis, pairs) if k else part)]
    ppermute x7 -> x6, starting transfers between devices: 11.7 us -> 9.49 us  [from_behind(): lax.ppermute(value, axis, [(source, source + steps) for source in range(c...]
    ppermute x12, starting transfers between devices: 19.7 us -> 18.5 us  [ring(): moved.append(lax.ppermute(part, axis, pairs) if k else part)]
    pallas_call x13 -> x14, Pallas kernels: 29.1 us -> 28.3 us  [call(): pl.pallas_call(kernel, out_shape=out_shape, scratch_shapes=scratch, compi...]
  transfers between devices with their start and end apart: 19 -> 18, of which waited for: 7 -> 6; matrix products, arithmetic and copies ran while one was open for 1% -> 1% of each run, Pallas kernels for 25% -> 25%
where the time goes in v9:
time: 109 us; the launch traced here: 108 us
  waiting for transfers between devices  47.7 us (44%)
  Pallas kernels  28.3 us (26%)
  starting transfers between devices  28 us (26%)
  local copies, waits for them, and re-layouts  3.27 us (3%)
    ppermute x6, waiting for transfers between devices, from_behind(): lax.ppermute(value, axis, [(source, source + steps) for source in range(c...  35.7 us
    pallas_call x14, Pallas kernels, call(): pl.pallas_call(kernel, out_shape=out_shape, scratch_shapes=scratch, compi...  28.3 us
    ppermute x12, starting transfers between devices, ring(): moved.append(lax.ppermute(part, axis, pairs) if k else part)  18.5 us
    ppermute x12, waiting for transfers between devices, ring(): moved.append(lax.ppermute(part, axis, pairs) if k else part)  12 us
    ppermute x6, starting transfers between devices, from_behind(): lax.ppermute(value, axis, [(source, source + steps) for source in range(c...  9.49 us
    unnamed x8, local copies, waits for them, and re-layouts  3.19 us
  transfers between devices with their start and end apart: 18, of which 6 were waited for; matrix products, arithmetic and copies ran while one was open for 1% of the time, Pallas kernels for 25%

profile of v9, /device:TPU:4, one launch (start us, length us, event | category | flops | bytes accessed | tf_op | source)
XLA Modules:
  0.0 108.4 jit_solution(8821412441865483282)
XLA Ops:
  0.0 1.6 %collective-permute-start = (f32[16,1024]{1,0:T(8,128)}, f32[16,1024]{1,0:T(8,128)S(1)}, u32[]{:S(2)}, u32[]{:S(2)}) collective-permute-start(f32[16,1024]{1,0:T(8,128)} %bitcast.3), channel_id=1, source_target_pairs={{0,1},{1,0},{2,3},{3,2},{4,5},{5,4},{6,7},{7,6},{8,9},{9,8},{10,11... | collective-permute-start | bytes 196616 | tf_op jit(solution)/shard_map/ppermute | solution.py:38
  1.7 0.9 maximum_maximum_fusion.refs_0_
  3.1 2.6 %collective-permute-start.5 = (f32[24,1024]{1,0:T(8,128)S(1)}, f32[24,1024]{1,0:T(8,128)S(1)}, u32[]{:S(2)}, u32[]{:S(2)}) collective-permute-start(f32[24,1024]{1,0:T(8,128)S(1)} %maximum_maximum_fusion.refs_0_), channel_id=1, source_target_pairs={{0,2},{1,3},{2,0},{3,1},{4,6},{5,7},{6,4},{7,5},{8,10},{9,11},{10,... | collective-permute-start | bytes 294920 | tf_op jit(solution)/shard_map/ppermute | solution.py:38
  5.7 1.3 %collective-permute-start.6 = (f32[24,1024]{1,0:T(8,128)S(1)}, f32[24,1024]{1,0:T(8,128)S(1)}, u32[]{:S(2)}, u32[]{:S(2)}) collective-permute-start(f32[24,1024]{1,0:T(8,128)S(1)} %maximum_maximum_fusion.refs_0_), channel_id=1, source_target_pairs={{0,3},{1,2},{2,1},{3,0},{4,7},{5,6},{6,5},{7,4},{8,11},{9,10},{10,... | collective-permute-start | bytes 294920 | tf_op jit(solution)/shard_map/ppermute | solution.py:38
  7.0 1.7 %collective-permute-start.1 = (f32[16,1024]{1,0:T(8,128)}, f32[16,1024]{1,0:T(8,128)S(1)}, u32[]{:S(2)}, u32[]{:S(2)}) collective-permute-start(f32[16,1024]{1,0:T(8,128)} %bitcast.4), channel_id=1, source_target_pairs={{0,2},{1,3},{2,0},{3,1},{4,6},{5,7},{6,4},{7,5},{8,10},{9,11},{10,... | collective-permute-start | bytes 196616 | tf_op jit(solution)/shard_map/ppermute | solution.py:38
  8.7 0.9 collective-permute-start.2
  9.6 1.6 %copy-done = bf16[256,4096]{1,0:T(8,128)(2,1)S(1)} copy-done((bf16[256,4096]{1,0:T(8,128)(2,1)S(1)}, bf16[256,4096]{1,0:T(8,128)(2,1)}, u32[]{:S(2)}) %copy-start) | copy-done | bytes 2097176
  11.2 1.6 %copy-done.1 = bf16[256,4096]{1,0:T(8,128)(2,1)S(1)} copy-done((bf16[256,4096]{1,0:T(8,128)(2,1)S(1)}, bf16[256,4096]{1,0:T(8,128)(2,1)}, u32[]{:S(2)}) %copy-start.1) | copy-done | bytes 2097176
  13.7 1.6 %shard_map.64.refs_0_ = bf16[256,1024]{1,0:T(8,128)(2,1)S(1)} custom-call(bf16[256,4096]{1,0:T(8,128)(2,1)} %query.5, bf16[256,4096]{1,0:T(8,128)(2,1)} %key_in.5), custom_call_target="tpu_custom_call" | custom-call | tf_op jit(solution)/shard_map/pallas_call | solution.py:498
  15.3 4.5 %collective-permute-done.1.refs_5_ = f32[16,1024]{1,0:T(8,128)S(1)} collective-permute-done((f32[16,1024]{1,0:T(8,128)}, f32[16,1024]{1,0:T(8,128)S(1)}, u32[]{:S(2)}, u32[]{:S(2)}) %collective-permute-start.1) | collective-permute-done | bytes 65568 | tf_op jit(solution)/shard_map/ppermute | solution.py:38
  19.8 6.3 %shard_map.67 = (f32[512,1024]{1,0:T(8,128)S(1)}, f32[512,1280]{1,0:T(8,128)S(1)}, f32[512,1792]{1,0:T(8,128)S(1)}, f32[16,1024]{1,0:T(8,128)S(1)}, f32[16,1024]...) custom-call(bf16[256,1024]{1,0:T(8,128)(2,1)S(1)} %shard_map.64.refs_0_, ...), custom_call_target="tpu_custom_call" | custom-call | tf_op jit(solution)/shard_map/pallas_call | solution.py:498
  26.1 1.3 %collective-permute-start.17 = (bf16[256,1792]{1,0:T(8,128)(2,1)S(1)}, bf16[256,1792]{1,0:T(8,128)(2,1)S(1)}, u32[]{:S(2)}, u32[]{:S(2)}) collective-permute-start(bf16[256,1792]{1,0:T(8,128)(2,1)S(1)} %shard_map.76), channel_id=1, source_target_pairs={{0,16},{4,20},{8,24},{12,28},{1,17},{5,21},{9,25},{13,29},{2,18},{... | collective-permute-start | bytes 2752520 | tf_op jit(solution)/shard_map/ppermute | solution.py:24
  27.4 1.3 %collective-permute-start.7 = (bf16[256,1280]{1,0:T(8,128)(2,1)S(1)}, bf16[256,1280]{1,0:T(8,128)(2,1)S(1)}, u32[]{:S(2)}, u32[]{:S(2)}) collective-permute-start(bf16[256,1280]{1,0:T(8,128)(2,1)S(1)} %shard_map.65.refs_1_), channel_id=1, source_target_pairs={{0,16},{4,20},{8,24},{12,28},{1,17},{5,21},{9,25},{13,29},{2,18},{... | collective-permute-start | bytes 1966088 | tf_op jit(solution)/shard_map/ppermute | solution.py:24
  28.7 1.3 %collective-permute-start.3 = (bf16[256,1024]{1,0:T(8,128)(2,1)S(1)}, bf16[256,1024]{1,0:T(8,128)(2,1)S(1)}, u32[]{:S(2)}, u32[]{:S(2)}) collective-permute-start(bf16[256,1024]{1,0:T(8,128)(2,1)S(1)} %shard_map.64.refs_0_), channel_id=1, source_target_pairs={{0,16},{4,20},{8,24},{12,28},{1,17},{5,21},{9,25},{13,29},{2,18},{... | collective-permute-start | bytes 1572872 | tf_op jit(solution)/shard_map/ppermute | solution.py:24
  30.0 2.9 %collective-permute-start.10 = (f32[16,1024]{1,0:T(8,128)S(1)}, f32[16,1024]{1,0:T(8,128)S(1)}, u32[]{:S(2)}, u32[]{:S(2)}) collective-permute-start(f32[16,1024]{1,0:T(8,128)S(1)} %get-tuple-element.28), channel_id=1, source_target_pairs={{0,3},{1,2},{2,1},{3,0},{4,7},{5,6},{6,5},{7,4},{8,11},{9,10},{10,... | collective-permute-start | bytes 196616 | tf_op jit(solution)/shard_map/ppermute | solution.py:38
  33.4 2.7 %collective-permute-done.10.refs_3_ = f32[16,1024]{1,0:T(8,128)S(1)} collective-permute-done((f32[16,1024]{1,0:T(8,128)S(1)}, f32[16,1024]{1,0:T(8,128)S(1)}, u32[]{:S(2)}, u32[]{:S(2)}) %collective-permute-start.10) | collective-permute-done | bytes 65568 | tf_op jit(solution)/shard_map/ppermute | solution.py:38
  36.2 1.0 collective-permute-start.9
  37.2 4.7 %collective-permute-done.9.refs_2_ = f32[16,1024]{1,0:T(8,128)S(1)} collective-permute-done((f32[16,1024]{1,0:T(8,128)S(1)}, f32[16,1024]{1,0:T(8,128)S(1)}, u32[]{:S(2)}, u32[]{:S(2)}) %collective-permute-start.9) | collective-permute-done | bytes 65568 | tf_op jit(solution)/shard_map/ppermute | solution.py:38
  42.0 1.3 %collective-permute-start.11 = (f32[4,16,1024]{2,1,0:T(8,128)S(1)}, f32[4,16,1024]{2,1,0:T(8,128)S(1)}, u32[]{:S(2)}, u32[]{:S(2)}) collective-permute-start(f32[4,16,1024]{2,1,0:T(8,128)S(1)} %get-tuple-element.30), channel_id=1, source_target_pairs={{0,16},{4,20},{8,24},{12,28},{1,17},{5,21},{9,25},{13,29},{2,18},{... | collective-permute-start | bytes 786440 | tf_op jit(solution)/shard_map/ppermute | solution.py:24
  43.3 1.9 %collective-permute-start.12 = (f32[16,1024]{1,0:T(8,128)S(1)}, f32[16,1024]{1,0:T(8,128)S(1)}, u32[]{:S(2)}, u32[]{:S(2)}) collective-permute-start(f32[16,1024]{1,0:T(8,128)S(1)} %get-tuple-element.31.whole), channel_id=1, source_target_pairs={{0,4},{4,8},{8,12},{12,16},{16,20},{20,24},{24,28},{1,5},{5,9},{9,... | collective-permute-start | bytes 196616 | tf_op jit(solution)/shard_map/ppermute | solution.py:24
  45.2 4.7 %collective-permute-done.12.earlier.refs_3_ = f32[16,1024]{1,0:T(8,128)S(1)} collective-permute-done((f32[16,1024]{1,0:T(8,128)S(1)}, f32[16,1024]{1,0:T(8,128)S(1)}, u32[]{:S(2)}, u32[]{:S(2)}) %collective-permute-start.12) | collective-permute-done | bytes 65568 | tf_op jit(solution)/shard_map/ppermute | solution.py:24
  49.9 2.4 %collective-permute-start.13 = (f32[16,1024]{1,0:T(8,128)S(1)}, f32[16,1024]{1,0:T(8,128)S(1)}, u32[]{:S(2)}, u32[]{:S(2)}) collective-permute-start(f32[16,1024]{1,0:T(8,128)S(1)} %shard_map.72), channel_id=1, source_target_pairs={{0,8},{4,12},{8,16},{12,20},{16,24},{20,28},{1,9},{5,13},{9,17},{1... | collective-permute-start | bytes 196616 | tf_op jit(solution)/shard_map/ppermute | solution.py:24
  52.3 5.8 %collective-permute-done.13.refs_4_ = f32[16,1024]{1,0:T(8,128)S(1)} collective-permute-done((f32[16,1024]{1,0:T(8,128)S(1)}, f32[16,1024]{1,0:T(8,128)S(1)}, u32[]{:S(2)}, u32[]{:S(2)}) %collective-permute-start.13) | collective-permute-done | bytes 65568 | tf_op jit(solution)/shard_map/ppermute | solution.py:24
  58.1 25.3 %collective-permute-done.11.refs_2_ = f32[4,16,1024]{2,1,0:T(8,128)S(1)} collective-permute-done((f32[4,16,1024]{2,1,0:T(8,128)S(1)}, f32[4,16,1024]{2,1,0:T(8,128)S(1)}, u32[]{:S(2)}, u32[]{:S(2)}) %collective-permute-start.11) | collective-permute-done | bytes 262176 | tf_op jit(solution)/shard_map/ppermute | solution.py:24
  83.5 2.2 %collective-permute-start.14 = (f32[16,1024]{1,0:T(8,128)S(1)}, f32[16,1024]{1,0:T(8,128)S(1)}, u32[]{:S(2)}, u32[]{:S(2)}) collective-permute-start(f32[16,1024]{1,0:T(8,128)S(1)} %get-tuple-element.33), channel_id=1, source_target_pairs={{0,1},{1,0},{2,3},{3,2},{4,5},{5,4},{6,7},{7,6},{8,9},{9,8},{10,11... | collective-permute-start | bytes 196616 | tf_op jit(solution)/shard_map/ppermute | solution.py:38
  85.7 1.9 %collective-permute-start.15 = (f32[16,1024]{1,0:T(8,128)S(1)}, f32[16,1024]{1,0:T(8,128)S(1)}, u32[]{:S(2)}, u32[]{:S(2)}) collective-permute-start(f32[16,1024]{1,0:T(8,128)S(1)} %get-tuple-element.34), channel_id=1, source_target_pairs={{0,2},{1,3},{2,0},{3,1},{4,6},{5,7},{6,4},{7,5},{8,10},{9,11},{10,... | collective-permute-start | bytes 196616 | tf_op jit(solution)/shard_map/ppermute | solution.py:38
  87.6 1.4 %collective-permute-start.16 = (f32[16,1024]{1,0:T(8,128)S(1)}, f32[16,1024]{1,0:T(8,128)S(1)}, u32[]{:S(2)}, u32[]{:S(2)}) collective-permute-start(f32[16,1024]{1,0:T(8,128)S(1)} %get-tuple-element.35), channel_id=1, source_target_pairs={{0,3},{1,2},{2,1},{3,0},{4,7},{5,6},{6,5},{7,4},{8,11},{9,10},{10,... | collective-permute-start | bytes 196616 | tf_op jit(solution)/shard_map/ppermute | solution.py:38
  89.0 3.2 %shard_map.74.refs_13_ = f32[256,1792]{1,0:T(8,128)S(1)} custom-call(bf16[256,1792]{1,0:T(8,128)(2,1)S(1)} %shard_map.66.refs_2_.product, f32[4,16,1024]{2,1,0:T(8,128)S(1)} %get-tuple-element.24.rates.refs_10_, f32[4,24,1024]{2,1,0:T(8,128)S(1)} %shard_map.68.weighing.refs_11_, f32[512,1792]{1,0:T(8,128)S(1)} %get-tuple-element.36.carry), custom_call_target="tpu_custom_call" | custom-call | tf_op jit(solution)/shard_map/pallas_call | solution.py:498
  92.2 3.1 %shard_map.69.refs_4_ = f32[256,1024]{1,0:T(8,128)S(1)} custom-call(bf16[256,1024]{1,0:T(8,128)(2,1)S(1)} %collective-permute-done.3.past, f32[4,16,1024]{2,1,0:T(8,128)S(1)} %get-tuple-element.24.rates.refs_10_, f32[4,24,1024]{2,1,0:T(8,128)S(1)} %shard_map.68.weighing.refs_11_), custom_call_target="tpu_custom_call" | custom-call | tf_op jit(solution)/shard_map/pallas_call | solution.py:498
  95.4 3.9 %shard_map.70.refs_5_ = f32[256,1280]{1,0:T(8,128)S(1)} custom-call(bf16[256,1280]{1,0:T(8,128)(2,1)S(1)} %collective-permute-done.7.past, f32[4,16,1024]{2,1,0:T(8,128)S(1)} %get-tuple-element.24.rates.refs_10_, f32[4,24,1024]{2,1,0:T(8,128)S(1)} %shard_map.68.weighing.refs_11_), custom_call_target="tpu_custom_call" | custom-call | tf_op jit(solution)/shard_map/pallas_call | solution.py:498
  99.3 7.9 %shard_map.75 = (bf16[256,4096]{1,0:T(8,128)(2,1)}, f32[256,1792]{1,0:T(8,128)S(1)}) custom-call(bf16[256,1024]{1,0:T(8,128)(2,1)S(1)} %shard_map.64.refs_0_, bf16[256,1280]{1,0:T(8,128)(2,1)S(1)} %shard_map.65.refs_1_, f32[512,1024]{1,0:T(8,128)S(1)} %get-tuple-element.22.refs_2_, f32[512,1280]{1,0:T(8,128)S(1)} %get-tuple-element.23.refs_3_, ...), custom_call_target="tpu_custom_call" | custom-call | tf_op jit(solution)/shard_map/pallas_call | solution.py:498
  107.2 1.3 %shard_map.77 = bf16[256,4096]{1,0:T(8,128)(2,1)} custom-call(f32[256,1792]{1,0:T(8,128)S(1)} %get-tuple-element.37.rest, bf16[256,1792]{1,0:T(8,128)(2,1)S(1)} %collective-permute-done.17.over, bf16[256,4096]{1,0:T(8,128)(2,1)S(1)} %copy-done.2, bf16[256,4096]{1,0:T(8,128)(2,1)} %get-tuple-element.38.partial), custom_call_target="tpu_custom_call", output_to_operand_aliasing={{}: (3, {})} | custom-call | tf_op jit(solution)/shard_map/pallas_call | solution.py:498
  (29 shorter events, 2.3 us)
Async XLA Ops:
  0.0 8.7 %collective-permute-start = (f32[16,1024]{1,0:T(8,128)}, f32[16,1024]{1,0:T(8,128)S(1)}, u32[]{:S(2)}, u32[]{:S(2)}) collective-permute-start(f32[16,1024]{1,0:T(8,128)} %bitcast.3), channel_id=1, source_target_pairs={{0,1},{1,0},{2,3},{3,2},{4,5},{5,4},{6,7},{7,6},{8,9},{9,8},{10,11... | collective-permute-start | bytes 196616 | tf_op jit(solution)/shard_map/ppermute | solution.py:38
  2.6 23.5 %collective-permute-start.4 = (f32[24,1024]{1,0:T(8,128)S(1)}, f32[24,1024]{1,0:T(8,128)S(1)}, u32[]{:S(2)}, u32[]{:S(2)}) collective-permute-start(f32[24,1024]{1,0:T(8,128)S(1)} %maximum_maximum_fusion.refs_0_), channel_id=1, source_target_pairs={{0,1},{1,0},{2,3},{3,2},{4,5},{5,4},{6,7},{7,6},{8,9},{9,8},{10,11... | collective-permute-start | bytes 294920 | tf_op jit(solution)/shard_map/ppermute | solution.py:38
  3.1 23.0 %collective-permute-start.5 = (f32[24,1024]{1,0:T(8,128)S(1)}, f32[24,1024]{1,0:T(8,128)S(1)}, u32[]{:S(2)}, u32[]{:S(2)}) collective-permute-start(f32[24,1024]{1,0:T(8,128)S(1)} %maximum_maximum_fusion.refs_0_), channel_id=1, source_target_pairs={{0,2},{1,3},{2,0},{3,1},{4,6},{5,7},{6,4},{7,5},{8,10},{9,11},{10,... | collective-permute-start | bytes 294920 | tf_op jit(solution)/shard_map/ppermute | solution.py:38
  5.7 20.4 %collective-permute-start.6 = (f32[24,1024]{1,0:T(8,128)S(1)}, f32[24,1024]{1,0:T(8,128)S(1)}, u32[]{:S(2)}, u32[]{:S(2)}) collective-permute-start(f32[24,1024]{1,0:T(8,128)S(1)} %maximum_maximum_fusion.refs_0_), channel_id=1, source_target_pairs={{0,3},{1,2},{2,1},{3,0},{4,7},{5,6},{6,5},{7,4},{8,11},{9,10},{10,... | collective-permute-start | bytes 294920 | tf_op jit(solution)/shard_map/ppermute | solution.py:38
  7.0 12.7 %collective-permute-start.1 = (f32[16,1024]{1,0:T(8,128)}, f32[16,1024]{1,0:T(8,128)S(1)}, u32[]{:S(2)}, u32[]{:S(2)}) collective-permute-start(f32[16,1024]{1,0:T(8,128)} %bitcast.4), channel_id=1, source_target_pairs={{0,2},{1,3},{2,0},{3,1},{4,6},{5,7},{6,4},{7,5},{8,10},{9,11},{10,... | collective-permute-start | bytes 196616 | tf_op jit(solution)/shard_map/ppermute | solution.py:38
  8.7 11.1 %collective-permute-start.2 = (f32[16,1024]{1,0:T(8,128)}, f32[16,1024]{1,0:T(8,128)S(1)}, u32[]{:S(2)}, u32[]{:S(2)}) collective-permute-start(f32[16,1024]{1,0:T(8,128)} %bitcast.5), channel_id=1, source_target_pairs={{0,3},{1,2},{2,1},{3,0},{4,7},{5,6},{6,5},{7,4},{8,11},{9,10},{10,... | collective-permute-start | bytes 196616 | tf_op jit(solution)/shard_map/ppermute | solution.py:38
  9.6 1.6 %copy-start = (bf16[256,4096]{1,0:T(8,128)(2,1)S(1)}, bf16[256,4096]{1,0:T(8,128)(2,1)}, u32[]{:S(2)}) copy-start(bf16[256,4096]{1,0:T(8,128)(2,1)} %query.5) | copy-start | bytes 6291460
  11.2 1.6 %copy-start.1 = (bf16[256,4096]{1,0:T(8,128)(2,1)S(1)}, bf16[256,4096]{1,0:T(8,128)(2,1)}, u32[]{:S(2)}) copy-start(bf16[256,4096]{1,0:T(8,128)(2,1)} %key_in.5) | copy-start | bytes 6291460
  13.7 6.1 %copy-start.3 = (f32[1024,16]{0,1:T(8,128)S(1)}, f32[1024,16]{0,1:T(8,128)}, u32[]{:S(2)}) copy-start(f32[1024,16]{0,1:T(8,128)} %param.10) | copy-start | bytes 196612
  26.1 81.0 %collective-permute-start.17 = (bf16[256,1792]{1,0:T(8,128)(2,1)S(1)}, bf16[256,1792]{1,0:T(8,128)(2,1)S(1)}, u32[]{:S(2)}, u32[]{:S(2)}) collective-permute-start(bf16[256,1792]{1,0:T(8,128)(2,1)S(1)} %shard_map.76), channel_id=1, source_target_pairs={{0,16},{4,20},{8,24},{12,28},{1,17},{5,21},{9,25},{13,29},{2,18},{... | collective-permute-start | bytes 2752520 | tf_op jit(solution)/shard_map/ppermute | solution.py:24
  27.4 67.9 %collective-permute-start.7 = (bf16[256,1280]{1,0:T(8,128)(2,1)S(1)}, bf16[256,1280]{1,0:T(8,128)(2,1)S(1)}, u32[]{:S(2)}, u32[]{:S(2)}) collective-permute-start(bf16[256,1280]{1,0:T(8,128)(2,1)S(1)} %shard_map.65.refs_1_), channel_id=1, source_target_pairs={{0,16},{4,20},{8,24},{12,28},{1,17},{5,21},{9,25},{13,29},{2,18},{... | collective-permute-start | bytes 1966088 | tf_op jit(solution)/shard_map/ppermute | solution.py:24
  28.7 58.8 %collective-permute-start.3 = (bf16[256,1024]{1,0:T(8,128)(2,1)S(1)}, bf16[256,1024]{1,0:T(8,128)(2,1)S(1)}, u32[]{:S(2)}, u32[]{:S(2)}) collective-permute-start(bf16[256,1024]{1,0:T(8,128)(2,1)S(1)} %shard_map.64.refs_0_), channel_id=1, source_target_pairs={{0,16},{4,20},{8,24},{12,28},{1,17},{5,21},{9,25},{13,29},{2,18},{... | collective-permute-start | bytes 1572872 | tf_op jit(solution)/shard_map/ppermute | solution.py:24
  30.0 6.1 %collective-permute-start.10 = (f32[16,1024]{1,0:T(8,128)S(1)}, f32[16,1024]{1,0:T(8,128)S(1)}, u32[]{:S(2)}, u32[]{:S(2)}) collective-permute-start(f32[16,1024]{1,0:T(8,128)S(1)} %get-tuple-element.28), channel_id=1, source_target_pairs={{0,3},{1,2},{2,1},{3,0},{4,7},{5,6},{6,5},{7,4},{8,11},{9,10},{10,... | collective-permute-start | bytes 196616 | tf_op jit(solution)/shard_map/ppermute | solution.py:38
  32.9 4.3 %collective-permute-start.8 = (f32[16,1024]{1,0:T(8,128)S(1)}, f32[16,1024]{1,0:T(8,128)S(1)}, u32[]{:S(2)}, u32[]{:S(2)}) collective-permute-start(f32[16,1024]{1,0:T(8,128)S(1)} %get-tuple-element.26), channel_id=1, source_target_pairs={{0,1},{1,0},{2,3},{3,2},{4,5},{5,4},{6,7},{7,6},{8,9},{9,8},{10,11... | collective-permute-start | bytes 196616 | tf_op jit(solution)/shard_map/ppermute | solution.py:38
  36.2 5.7 %collective-permute-start.9 = (f32[16,1024]{1,0:T(8,128)S(1)}, f32[16,1024]{1,0:T(8,128)S(1)}, u32[]{:S(2)}, u32[]{:S(2)}) collective-permute-start(f32[16,1024]{1,0:T(8,128)S(1)} %get-tuple-element.27), channel_id=1, source_target_pairs={{0,2},{1,3},{2,0},{3,1},{4,6},{5,7},{6,4},{7,5},{8,10},{9,11},{10,... | collective-permute-start | bytes 196616 | tf_op jit(solution)/shard_map/ppermute | solution.py:38
  42.0 41.4 %collective-permute-start.11 = (f32[4,16,1024]{2,1,0:T(8,128)S(1)}, f32[4,16,1024]{2,1,0:T(8,128)S(1)}, u32[]{:S(2)}, u32[]{:S(2)}) collective-permute-start(f32[4,16,1024]{2,1,0:T(8,128)S(1)} %get-tuple-element.30), channel_id=1, source_target_pairs={{0,16},{4,20},{8,24},{12,28},{1,17},{5,21},{9,25},{13,29},{2,18},{... | collective-permute-start | bytes 786440 | tf_op jit(solution)/shard_map/ppermute | solution.py:24
  43.3 6.6 %collective-permute-start.12 = (f32[16,1024]{1,0:T(8,128)S(1)}, f32[16,1024]{1,0:T(8,128)S(1)}, u32[]{:S(2)}, u32[]{:S(2)}) collective-permute-start(f32[16,1024]{1,0:T(8,128)S(1)} %get-tuple-element.31.whole), channel_id=1, source_target_pairs={{0,4},{4,8},{8,12},{12,16},{16,20},{20,24},{24,28},{1,5},{5,9},{9,... | collective-permute-start | bytes 196616 | tf_op jit(solution)/shard_map/ppermute | solution.py:24
  49.9 8.2 %collective-permute-start.13 = (f32[16,1024]{1,0:T(8,128)S(1)}, f32[16,1024]{1,0:T(8,128)S(1)}, u32[]{:S(2)}, u32[]{:S(2)}) collective-permute-start(f32[16,1024]{1,0:T(8,128)S(1)} %shard_map.72), channel_id=1, source_target_pairs={{0,8},{4,12},{8,16},{12,20},{16,24},{20,28},{1,9},{5,13},{9,17},{1... | collective-permute-start | bytes 196616 | tf_op jit(solution)/shard_map/ppermute | solution.py:24
  83.5 15.8 %collective-permute-start.14 = (f32[16,1024]{1,0:T(8,128)S(1)}, f32[16,1024]{1,0:T(8,128)S(1)}, u32[]{:S(2)}, u32[]{:S(2)}) collective-permute-start(f32[16,1024]{1,0:T(8,128)S(1)} %get-tuple-element.33), channel_id=1, source_target_pairs={{0,1},{1,0},{2,3},{3,2},{4,5},{5,4},{6,7},{7,6},{8,9},{9,8},{10,11... | collective-permute-start | bytes 196616 | tf_op jit(solution)/shard_map/ppermute | solution.py:38
  85.7 13.5 %collective-permute-start.15 = (f32[16,1024]{1,0:T(8,128)S(1)}, f32[16,1024]{1,0:T(8,128)S(1)}, u32[]{:S(2)}, u32[]{:S(2)}) collective-permute-start(f32[16,1024]{1,0:T(8,128)S(1)} %get-tuple-element.34), channel_id=1, source_target_pairs={{0,2},{1,3},{2,0},{3,1},{4,6},{5,7},{6,4},{7,5},{8,10},{9,11},{10,... | collective-permute-start | bytes 196616 | tf_op jit(solution)/shard_map/ppermute | solution.py:38
  87.6 11.7 %collective-permute-start.16 = (f32[16,1024]{1,0:T(8,128)S(1)}, f32[16,1024]{1,0:T(8,128)S(1)}, u32[]{:S(2)}, u32[]{:S(2)}) collective-permute-start(f32[16,1024]{1,0:T(8,128)S(1)} %get-tuple-element.35), channel_id=1, source_target_pairs={{0,3},{1,2},{2,1},{3,0},{4,7},{5,6},{6,5},{7,4},{8,11},{9,10},{10,... | collective-permute-start | bytes 196616 | tf_op jit(solution)/shard_map/ppermute | solution.py:38
  92.2 7.1 %copy-start.2 = (bf16[256,4096]{1,0:T(8,128)(2,1)S(1)}, bf16[256,4096]{1,0:T(8,128)(2,1)}, u32[]{:S(2)}) copy-start(bf16[256,4096]{1,0:T(8,128)(2,1)} %value.1) | copy-start | bytes 6291460

commit v10 on v8

--- a/solution.py
+++ b/solution.py
@@ -333,31 +333,36 @@
         over_tiles(product.shape[1], body)
 
 
-def local_kernel(product, rates, weighing, carry, out, tokens, mix, leaps, direct, *, first):
+def local_kernel(near, product, rates, weighing, near_carry, carry, near_out, out, tokens, mix, leaps, direct, *, first):
     modes = rates.shape[1]
 
-    def body(t):
-        cols = lanes(t * LANES)
-        tokens[...] = product[:, cols].astype(F32)
-        own = at_tile(weighing, first + t)
-        fill_taps(
-            mix,
-            leaps,
-            direct,
-            at_tile(rates, first + t)[...],
-            own[pl.ds(0, modes), :],
-            own[pl.ds(modes, 1), :],
-        )
-
-        def kept(r, m):
-            return carry[mode_rows(r, m, modes), cols]
-
-        def write(i, value):
-            out[step_rows(i), cols] = value
-
-        emit(mix, leaps, direct, lambda m: kept(0, m), kept, tokens, write)
-
-    over_tiles(product.shape[1], body)
+    def part(product, carry, out, first, skip):
+        def body(t):
+            cols = lanes((skip + t) * LANES)
+            tokens[...] = product[:, cols].astype(F32)
+            own = at_tile(weighing, first + t)
+            fill_taps(
+                mix,
+                leaps,
+                direct,
+                at_tile(rates, first + t)[...],
+                own[pl.ds(0, modes), :],
+                own[pl.ds(modes, 1), :],
+            )
+
+            def kept(r, m):
+                return carry[mode_rows(r, m, modes), cols]
+
+            def write(i, value):
+                out[step_rows(i), lanes(t * LANES)] = value
+
+            emit(mix, leaps, direct, lambda m: kept(0, m), kept, tokens, write)
+
+        over_tiles(out.shape[1], body)
+
+    ahead = near_out.shape[1] // LANES
+    part(near, near_carry, near_out, first - ahead, near.shape[1] // LANES - ahead)
+    part(product, carry, out, first, 0)
 
 
 def gated(back, mixed, value):
@@ -368,8 +373,8 @@
 def finish_kernel(*refs, count, n_ch):
     products, carries, overs = refs[:count], refs[count : 2 * count], refs[2 * count : 3 * count]
     refs = refs[3 * count :]
-    befores, (rates, weighing, value, late, out, rest) = refs[:n_ch], refs[n_ch : n_ch + 6]
-    tokens, table, weights, scr, back, before, mixed, done, sems, mix, leaps, direct, coming = refs[n_ch + 6 :]
+    befores, (rates, weighing, value, near, late, out, rest) = refs[:n_ch], refs[n_ch : n_ch + 7]
+    tokens, table, weights, scr, back, before, mixed, done, sems, mix, leaps, direct, coming = refs[n_ch + 7 :]
     modes = rates.shape[1]
     length = value.shape[0]
     steps = length // SEGMENTS
@@ -383,12 +388,32 @@
         begin = (lax.broadcasted_iota(jnp.int32, (SEGMENTS, LANES), 0) * steps).astype(F32)
         return [jnp.exp(-row_of(own, m) * begin) * row_of(ahead, m) for m in range(modes)]
 
+    def add(tile, source, cols, write):
+        state = [row_of(weights, m) * s for m, s in enumerate(arriving(tile))]
+        decay = [row_of(table.at[0], m) for m in range(modes)]
+        for i in range(steps):
+            state = [d * s for d, s in zip(decay, state)]
+            terms = state
+            while len(terms) > 1:
+                terms = [x + y for x, y in zip(terms[::2], terms[1::2])]
+            write(i, source[step_rows(i), cols] + terms[0])
+
     copies = [None, None]
     first = 0
     for k in range(count):
         product, carry = products[k], carries[k]
         width = product.shape[1]
         slot = k % 2
+        soon = near.shape[1] // LANES if k == count - 1 else 0
+        whole = width // LANES - soon
+
+        def write_scr(i, value):
+            scr[step_rows(i), :] = value
+
+        def body_near(t, first=first, whole=whole, k=k):
+            cols = lanes((whole + t) * LANES)
+            add(first + whole + t, near, lanes(t * LANES), write_scr)
+            mixed[:, cols] = (scr[...] - overs[k][:, cols].astype(F32)).astype(jnp.bfloat16)
 
         def body(t, first=first, product=product, carry=carry, k=k):
             cols = lanes(t * LANES)
@@ -402,13 +427,12 @@
             def kept(r, m):
                 return carry[mode_rows(r, m, modes), cols]
 
-            def write(i, value):
-                scr[step_rows(i), :] = value
-
-            emit(mix, leaps, direct, lambda m: coming[step_rows(m), :], kept, tokens, write)
+            emit(mix, leaps, direct, lambda m: coming[step_rows(m), :], kept, tokens, write_scr)
             mixed[:, cols] = (scr[...] - overs[k][:, cols].astype(F32)).astype(jnp.bfloat16)
 
-        over_tiles(width, body)
+        over_tiles(whole * LANES, body)
+        if soon:
+            over_tiles(soon * LANES, body_near)
         if copies[slot] is not None:
             copies[slot].wait()
         wide = math.gcd(width, 4 * LANES)
@@ -421,18 +445,15 @@
         copies[slot].start()
         first += width // LANES
 
-    def add(t):
+    def body_late(t):
         cols = lanes(t * LANES)
-        state = [row_of(weights, m) * s for m, s in enumerate(arriving(first + t))]
-        decay = [row_of(table.at[0], m) for m in range(modes)]
-        for i in range(steps):
-            state = [d * s for d, s in zip(decay, state)]
-            terms = state
-            while len(terms) > 1:
-                terms = [x + y for x, y in zip(terms[::2], terms[1::2])]
-            rest[step_rows(i), cols] = late[step_rows(i), cols] + terms[0]
-
-    over_tiles(late.shape[1], add)
+
+        def write(i, value):
+            rest[step_rows(i), cols] = value
+
+        add(first + t, late, cols, write)
+
+    over_tiles(late.shape[1], body_late)
     for copy in copies:
         if copy is not None:
             copy.wait()
@@ -588,11 +609,12 @@
     )
     befores = ring(heads, "ch")
 
-    late = call(
+    soon = widths[-2] // LANES // 3 * LANES
+    near, late = call(
         functools.partial(local_kernel, first=firsts[-1] // LANES),
-        shape(length, widths[-1]),
+        [shape(length, soon), shape(length, widths[-1])],
         [tokens_scr, *taps_scr],
-        (products[-1], rates, weighing, carries[-1]),
+        (products[-2], products[-1], rates, weighing, carries[-2], carries[-1]),
     )
     widest = max(widths[:-1])
     partial, rest = call(
@@ -611,7 +633,7 @@
             *taps_scr,
             pltpu.VMEM((modes * SEGMENTS, LANES), F32),
         ],
-        (*products[:-1], *carries[:-1], *overs[:-1], *befores, rates, weighing, value, late),
+        (*products[:-1], *carries[:-1], *overs[:-1], *befores, rates, weighing, value, near, late),
         out_specs=[anywhere, vmem],
     )
     return call(

time: 111 us -> 112 us (level)
  transfers between devices with their start and end apart: 19 -> 19, of which waited for: 7 -> 7; matrix products, arithmetic and copies ran while one was open for 1% -> 1% of each run, Pallas kernels for 25% -> 26%
where the time goes in v10:
time: 112 us
  waiting for transfers between devices  49.4 us (44%)
  starting transfers between devices  31.3 us (28%)
  Pallas kernels  29.8 us (27%)
    ppermute x7, waiting for transfers between devices, from_behind(): lax.ppermute(value, axis, [(source, source + steps) for source in range(c...  39.2 us
    pallas_call x13, Pallas kernels, call(): pl.pallas_call(kernel, out_shape=out_shape, scratch_shapes=scratch, compi...  29.8 us
    ppermute x12, starting transfers between devices, ring(): moved.append(lax.ppermute(part, axis, pairs) if k else part)  19.7 us
    ppermute x7, starting transfers between devices, from_behind(): lax.ppermute(value, axis, [(source, source + steps) for source in range(c...  11.7 us
    ppermute x12, waiting for transfers between devices, ring(): moved.append(lax.ppermute(part, axis, pairs) if k else part)  10.2 us
  transfers between devices with their start and end apart: 19, of which 7 were waited for; matrix products, arithmetic and copies ran while one was open for 1% of the time, Pallas kernels for 26%

profile of v10, /device:TPU:4, one launch (start us, length us, event | category | flops | bytes accessed | tf_op | source)
XLA Modules:
  0.0 111.8 jit_solution(6688002628282613765)
XLA Ops:
  0.0 3.6 %collective-permute-start.2 = (f32[16,1024]{1,0:T(8,128)}, f32[16,1024]{1,0:T(8,128)S(1)}, u32[]{:S(2)}, u32[]{:S(2)}) collective-permute-start(f32[16,1024]{1,0:T(8,128)} %bitcast.3), channel_id=1, source_target_pairs={{0,3},{1,2},{2,1},{3,0},{4,7},{5,6},{6,5},{7,4},{8,11},{9,10},{10,... | collective-permute-start | bytes 196616 | tf_op jit(solution)/shard_map/ppermute | solution.py:38
  3.7 0.9 maximum_maximum_fusion.refs_0_
  4.6 0.3 collective-permute-start.6
  4.9 0.8 collective-permute-start.5
  5.7 3.4 %collective-permute-start.4 = (f32[24,1024]{1,0:T(8,128)S(1)}, f32[24,1024]{1,0:T(8,128)S(1)}, u32[]{:S(2)}, u32[]{:S(2)}) collective-permute-start(f32[24,1024]{1,0:T(8,128)S(1)} %maximum_maximum_fusion.refs_0_), channel_id=1, source_target_pairs={{0,1},{1,0},{2,3},{3,2},{4,5},{5,4},{6,7},{7,6},{8,9},{9,8},{10,11... | collective-permute-start | bytes 294920 | tf_op jit(solution)/shard_map/ppermute | solution.py:38
  9.1 1.5 %collective-permute-start = (f32[16,1024]{1,0:T(8,128)}, f32[16,1024]{1,0:T(8,128)S(1)}, u32[]{:S(2)}, u32[]{:S(2)}) collective-permute-start(f32[16,1024]{1,0:T(8,128)} %bitcast.5), channel_id=1, source_target_pairs={{0,1},{1,0},{2,3},{3,2},{4,5},{5,4},{6,7},{7,6},{8,9},{9,8},{10,11... | collective-permute-start | bytes 196616 | tf_op jit(solution)/shard_map/ppermute | solution.py:38
  10.6 1.6 %shard_map.64.refs_0_ = bf16[256,1024]{1,0:T(8,128)(2,1)S(1)} custom-call(bf16[256,4096]{1,0:T(8,128)(2,1)} %query.5, bf16[256,4096]{1,0:T(8,128)(2,1)} %key_in.5), custom_call_target="tpu_custom_call" | custom-call | tf_op jit(solution)/shard_map/pallas_call | solution.py:518
  12.2 0.4 shard_map.65.refs_1_.near
  12.6 5.3 %collective-permute-done.1.refs_5_ = f32[16,1024]{1,0:T(8,128)S(1)} collective-permute-done((f32[16,1024]{1,0:T(8,128)}, f32[16,1024]{1,0:T(8,128)S(1)}, u32[]{:S(2)}, u32[]{:S(2)}) %collective-permute-start.1) | collective-permute-done | bytes 65568 | tf_op jit(solution)/shard_map/ppermute | solution.py:38
  17.9 1.3 %collective-permute-start.7 = (bf16[256,1536]{1,0:T(8,128)(2,1)S(1)}, bf16[256,1536]{1,0:T(8,128)(2,1)S(1)}, u32[]{:S(2)}, u32[]{:S(2)}) collective-permute-start(bf16[256,1536]{1,0:T(8,128)(2,1)S(1)} %shard_map.65.refs_1_.near), channel_id=1, source_target_pairs={{0,16},{4,20},{8,24},{12,28},{1,17},{5,21},{9,25},{13,29},{2,18},{... | collective-permute-start | bytes 2359304 | tf_op jit(solution)/shard_map/ppermute | solution.py:24
  19.2 0.4 shard_map.66.refs_2_.product
  19.6 6.4 %shard_map.67 = (f32[512,1024]{1,0:T(8,128)S(1)}, f32[512,1536]{1,0:T(8,128)S(1)}, f32[512,1536]{1,0:T(8,128)S(1)}, f32[16,1024]{1,0:T(8,128)S(1)}, f32[16,1024]...) custom-call(bf16[256,1024]{1,0:T(8,128)(2,1)S(1)} %shard_map.64.refs_0_, ...), custom_call_target="tpu_custom_call" | custom-call | tf_op jit(solution)/shard_map/pallas_call | solution.py:518
  26.2 1.3 %collective-permute-start.18 = (bf16[256,1536]{1,0:T(8,128)(2,1)S(1)}, bf16[256,1536]{1,0:T(8,128)(2,1)S(1)}, u32[]{:S(2)}, u32[]{:S(2)}) collective-permute-start(bf16[256,1536]{1,0:T(8,128)(2,1)S(1)} %shard_map.75), channel_id=1, source_target_pairs={{0,16},{4,20},{8,24},{12,28},{1,17},{5,21},{9,25},{13,29},{2,18},{... | collective-permute-start | bytes 2359304 | tf_op jit(solution)/shard_map/ppermute | solution.py:24
  27.5 1.3 %collective-permute-start.3 = (bf16[256,1024]{1,0:T(8,128)(2,1)S(1)}, bf16[256,1024]{1,0:T(8,128)(2,1)S(1)}, u32[]{:S(2)}, u32[]{:S(2)}) collective-permute-start(bf16[256,1024]{1,0:T(8,128)(2,1)S(1)} %shard_map.64.refs_0_), channel_id=1, source_target_pairs={{0,16},{4,20},{8,24},{12,28},{1,17},{5,21},{9,25},{13,29},{2,18},{... | collective-permute-start | bytes 1572872 | tf_op jit(solution)/shard_map/ppermute | solution.py:24
  28.9 3.2 %collective-permute-start.9 = (f32[16,1024]{1,0:T(8,128)S(1)}, f32[16,1024]{1,0:T(8,128)S(1)}, u32[]{:S(2)}, u32[]{:S(2)}) collective-permute-start(f32[16,1024]{1,0:T(8,128)S(1)} %get-tuple-element.29), channel_id=1, source_target_pairs={{0,2},{1,3},{2,0},{3,1},{4,6},{5,7},{6,4},{7,5},{8,10},{9,11},{10,... | collective-permute-start | bytes 196616 | tf_op jit(solution)/shard_map/ppermute | solution.py:38
  32.0 1.3 %collective-permute-done.8.refs_1_ = f32[16,1024]{1,0:T(8,128)S(1)} collective-permute-done((f32[16,1024]{1,0:T(8,128)S(1)}, f32[16,1024]{1,0:T(8,128)S(1)}, u32[]{:S(2)}, u32[]{:S(2)}) %collective-permute-start.8) | collective-permute-done | bytes 65568 | tf_op jit(solution)/shard_map/ppermute | solution.py:38
  33.4 2.4 %collective-permute-start.10 = (f32[16,1024]{1,0:T(8,128)S(1)}, f32[16,1024]{1,0:T(8,128)S(1)}, u32[]{:S(2)}, u32[]{:S(2)}) collective-permute-start(f32[16,1024]{1,0:T(8,128)S(1)} %get-tuple-element.30), channel_id=1, source_target_pairs={{0,3},{1,2},{2,1},{3,0},{4,7},{5,6},{6,5},{7,4},{8,11},{9,10},{10,... | collective-permute-start | bytes 196616 | tf_op jit(solution)/shard_map/ppermute | solution.py:38
  35.9 3.6 %collective-permute-done.10.refs_3_ = f32[16,1024]{1,0:T(8,128)S(1)} collective-permute-done((f32[16,1024]{1,0:T(8,128)S(1)}, f32[16,1024]{1,0:T(8,128)S(1)}, u32[]{:S(2)}, u32[]{:S(2)}) %collective-permute-start.10) | collective-permute-done | bytes 65568 | tf_op jit(solution)/shard_map/ppermute | solution.py:38
  39.5 1.3 %collective-permute-start.11 = (f32[4,16,1024]{2,1,0:T(8,128)S(1)}, f32[4,16,1024]{2,1,0:T(8,128)S(1)}, u32[]{:S(2)}, u32[]{:S(2)}) collective-permute-start(f32[4,16,1024]{2,1,0:T(8,128)S(1)} %get-tuple-element.32), channel_id=1, source_target_pairs={{0,16},{4,20},{8,24},{12,28},{1,17},{5,21},{9,25},{13,29},{2,18},{... | collective-permute-start | bytes 786440 | tf_op jit(solution)/shard_map/ppermute | solution.py:24
  40.8 1.9 %collective-permute-start.14 = (f32[16,1024]{1,0:T(8,128)S(1)}, f32[16,1024]{1,0:T(8,128)S(1)}, u32[]{:S(2)}, u32[]{:S(2)}) collective-permute-start(f32[16,1024]{1,0:T(8,128)S(1)} %get-tuple-element.33), channel_id=1, source_target_pairs={{0,12},{4,16},{8,20},{12,24},{16,28},{1,13},{5,17},{9,21},{13,25},... | collective-permute-start | bytes 196616 | tf_op jit(solution)/shard_map/ppermute | solution.py:24
  42.7 30.3 %collective-permute-done.14.refs_5_ = f32[16,1024]{1,0:T(8,128)S(1)} collective-permute-done((f32[16,1024]{1,0:T(8,128)S(1)}, f32[16,1024]{1,0:T(8,128)S(1)}, u32[]{:S(2)}, u32[]{:S(2)}) %collective-permute-start.14) | collective-permute-done | bytes 65568 | tf_op jit(solution)/shard_map/ppermute | solution.py:24
  73.0 2.7 %collective-permute-start.13 = (f32[16,1024]{1,0:T(8,128)S(1)}, f32[16,1024]{1,0:T(8,128)S(1)}, u32[]{:S(2)}, u32[]{:S(2)}) collective-permute-start(f32[16,1024]{1,0:T(8,128)S(1)} %get-tuple-element.33), channel_id=1, source_target_pairs={{0,8},{4,12},{8,16},{12,20},{16,24},{20,28},{1,9},{5,13},{9,17},{1... | collective-permute-start | bytes 196616 | tf_op jit(solution)/shard_map/ppermute | solution.py:24
  75.7 4.4 %collective-permute-done.13.refs_4_ = f32[16,1024]{1,0:T(8,128)S(1)} collective-permute-done((f32[16,1024]{1,0:T(8,128)S(1)}, f32[16,1024]{1,0:T(8,128)S(1)}, u32[]{:S(2)}, u32[]{:S(2)}) %collective-permute-start.13) | collective-permute-done | bytes 65568 | tf_op jit(solution)/shard_map/ppermute | solution.py:24
  80.0 1.9 %collective-permute-start.12 = (f32[16,1024]{1,0:T(8,128)S(1)}, f32[16,1024]{1,0:T(8,128)S(1)}, u32[]{:S(2)}, u32[]{:S(2)}) collective-permute-start(f32[16,1024]{1,0:T(8,128)S(1)} %get-tuple-element.33), channel_id=1, source_target_pairs={{0,4},{4,8},{8,12},{12,16},{16,20},{20,24},{24,28},{1,5},{5,9},{9,... | collective-permute-start | bytes 196616 | tf_op jit(solution)/shard_map/ppermute | solution.py:24
  82.0 4.6 %collective-permute-done.12.refs_3_ = f32[16,1024]{1,0:T(8,128)S(1)} collective-permute-done((f32[16,1024]{1,0:T(8,128)S(1)}, f32[16,1024]{1,0:T(8,128)S(1)}, u32[]{:S(2)}, u32[]{:S(2)}) %collective-permute-start.12) | collective-permute-done | bytes 65568 | tf_op jit(solution)/shard_map/ppermute | solution.py:24
  86.7 2.9 %collective-permute-start.16 = (f32[16,1024]{1,0:T(8,128)S(1)}, f32[16,1024]{1,0:T(8,128)S(1)}, u32[]{:S(2)}, u32[]{:S(2)}) collective-permute-start(f32[16,1024]{1,0:T(8,128)S(1)} %get-tuple-element.36), channel_id=1, source_target_pairs={{0,2},{1,3},{2,0},{3,1},{4,6},{5,7},{6,4},{7,5},{8,10},{9,11},{10,... | collective-permute-start | bytes 196616 | tf_op jit(solution)/shard_map/ppermute | solution.py:38
  89.6 1.5 %collective-permute-start.17 = (f32[16,1024]{1,0:T(8,128)S(1)}, f32[16,1024]{1,0:T(8,128)S(1)}, u32[]{:S(2)}, u32[]{:S(2)}) collective-permute-start(f32[16,1024]{1,0:T(8,128)S(1)} %get-tuple-element.37), channel_id=1, source_target_pairs={{0,3},{1,2},{2,1},{3,0},{4,7},{5,6},{6,5},{7,4},{8,11},{9,10},{10,... | collective-permute-start | bytes 196616 | tf_op jit(solution)/shard_map/ppermute | solution.py:38
  91.1 3.9 %shard_map.73 = (f32[256,512]{1,0:T(8,128)S(1)}, f32[256,1536]{1,0:T(8,128)S(1)}) custom-call(bf16[256,1536]{1,0:T(8,128)(2,1)S(1)} %shard_map.65.refs_1_.near, bf16[256,1536]{1,0:T(8,128)(2,1)S(1)} %shard_map.66.refs_2_.product, f32[4,16,1024]{2,1,0:T(8,128)S(1)} %get-tuple-element.26.rates.refs_10_, f32[4,24,1024]{2,1,0:T(8,128)S(1)} %shard_map.68.weighing.refs_11_, ...), custom_call_target="tpu_custom_call" | custom-call | tf_op jit(solution)/shard_map/pallas_call | solution.py:518
  95.0 3.1 %shard_map.69.refs_4_ = f32[256,1024]{1,0:T(8,128)S(1)} custom-call(bf16[256,1024]{1,0:T(8,128)(2,1)S(1)} %collective-permute-done.3.past, f32[4,16,1024]{2,1,0:T(8,128)S(1)} %get-tuple-element.26.rates.refs_10_, f32[4,24,1024]{2,1,0:T(8,128)S(1)} %shard_map.68.weighing.refs_11_), custom_call_target="tpu_custom_call" | custom-call | tf_op jit(solution)/shard_map/pallas_call | solution.py:518
  98.1 4.6 %shard_map.70.refs_5_ = f32[256,1536]{1,0:T(8,128)S(1)} custom-call(bf16[256,1536]{1,0:T(8,128)(2,1)S(1)} %collective-permute-done.7.past, f32[4,16,1024]{2,1,0:T(8,128)S(1)} %get-tuple-element.26.rates.refs_10_, f32[4,24,1024]{2,1,0:T(8,128)S(1)} %shard_map.68.weighing.refs_11_), custom_call_target="tpu_custom_call" | custom-call | tf_op jit(solution)/shard_map/pallas_call | solution.py:518
  102.8 7.8 %shard_map.74 = (bf16[256,4096]{1,0:T(8,128)(2,1)}, f32[256,1536]{1,0:T(8,128)S(1)}) custom-call(bf16[256,1024]{1,0:T(8,128)(2,1)S(1)} %shard_map.64.refs_0_, bf16[256,1536]{1,0:T(8,128)(2,1)S(1)} %shard_map.65.refs_1_.near, f32[512,1024]{1,0:T(8,128)S(1)} %get-tuple-element.24.refs_2_, f32[512,1536]{1,0:T(8,128)S(1)} %get-tuple-element.25.near_carry.refs_3_, ...), custom_call_target="tpu_custom_call" | custom-call | tf_op jit(solution)/shard_map/pallas_call | solution.py:518
  110.6 1.2 %shard_map.76 = bf16[256,4096]{1,0:T(8,128)(2,1)} custom-call(f32[256,1536]{1,0:T(8,128)S(1)} %get-tuple-element.41.rest, bf16[256,1536]{1,0:T(8,128)(2,1)S(1)} %collective-permute-done.18.over, bf16[256,4096]{1,0:T(8,128)(2,1)S(1)} %copy-done.2, bf16[256,4096]{1,0:T(8,128)(2,1)} %get-tuple-element.42.partial), custom_call_target="tpu_custom_call", output_to_operand_aliasing={{}: (3, {})} | custom-call | tf_op jit(solution)/shard_map/pallas_call | solution.py:518
  (30 shorter events, 0.6 us)
Async XLA Ops:
  0.0 9.1 %collective-permute-start.2 = (f32[16,1024]{1,0:T(8,128)}, f32[16,1024]{1,0:T(8,128)S(1)}, u32[]{:S(2)}, u32[]{:S(2)}) collective-permute-start(f32[16,1024]{1,0:T(8,128)} %bitcast.3), channel_id=1, source_target_pairs={{0,3},{1,2},{2,1},{3,0},{4,7},{5,6},{6,5},{7,4},{8,11},{9,10},{10,... | collective-permute-start | bytes 196616 | tf_op jit(solution)/shard_map/ppermute | solution.py:38
  4.6 7.5 %copy-start = (bf16[256,4096]{1,0:T(8,128)(2,1)S(1)}, bf16[256,4096]{1,0:T(8,128)(2,1)}, u32[]{:S(2)}) copy-start(bf16[256,4096]{1,0:T(8,128)(2,1)} %query.5) | copy-start | bytes 6291460
  4.6 7.6 %copy-start.1 = (bf16[256,4096]{1,0:T(8,128)(2,1)S(1)}, bf16[256,4096]{1,0:T(8,128)(2,1)}, u32[]{:S(2)}) copy-start(bf16[256,4096]{1,0:T(8,128)(2,1)} %key_in.5) | copy-start | bytes 6291460
  4.6 21.4 %collective-permute-start.6 = (f32[24,1024]{1,0:T(8,128)S(1)}, f32[24,1024]{1,0:T(8,128)S(1)}, u32[]{:S(2)}, u32[]{:S(2)}) collective-permute-start(f32[24,1024]{1,0:T(8,128)S(1)} %maximum_maximum_fusion.refs_0_), channel_id=1, source_target_pairs={{0,3},{1,2},{2,1},{3,0},{4,7},{5,6},{6,5},{7,4},{8,11},{9,10},{10,... | collective-permute-start | bytes 294920 | tf_op jit(solution)/shard_map/ppermute | solution.py:38
  4.9 21.2 %collective-permute-start.5 = (f32[24,1024]{1,0:T(8,128)S(1)}, f32[24,1024]{1,0:T(8,128)S(1)}, u32[]{:S(2)}, u32[]{:S(2)}) collective-permute-start(f32[24,1024]{1,0:T(8,128)S(1)} %maximum_maximum_fusion.refs_0_), channel_id=1, source_target_pairs={{0,2},{1,3},{2,0},{3,1},{4,6},{5,7},{6,4},{7,5},{8,10},{9,11},{10,... | collective-permute-start | bytes 294920 | tf_op jit(solution)/shard_map/ppermute | solution.py:38
  5.7 20.4 %collective-permute-start.4 = (f32[24,1024]{1,0:T(8,128)S(1)}, f32[24,1024]{1,0:T(8,128)S(1)}, u32[]{:S(2)}, u32[]{:S(2)}) collective-permute-start(f32[24,1024]{1,0:T(8,128)S(1)} %maximum_maximum_fusion.refs_0_), channel_id=1, source_target_pairs={{0,1},{1,0},{2,3},{3,2},{4,5},{5,4},{6,7},{7,6},{8,9},{9,8},{10,11... | collective-permute-start | bytes 294920 | tf_op jit(solution)/shard_map/ppermute | solution.py:38
  9.1 8.8 %collective-permute-start.1 = (f32[16,1024]{1,0:T(8,128)}, f32[16,1024]{1,0:T(8,128)S(1)}, u32[]{:S(2)}, u32[]{:S(2)}) collective-permute-start(f32[16,1024]{1,0:T(8,128)} %bitcast.4), channel_id=1, source_target_pairs={{0,2},{1,3},{2,0},{3,1},{4,6},{5,7},{6,4},{7,5},{8,10},{9,11},{10,... | collective-permute-start | bytes 196616 | tf_op jit(solution)/shard_map/ppermute | solution.py:38
  9.1 10.5 %collective-permute-start = (f32[16,1024]{1,0:T(8,128)}, f32[16,1024]{1,0:T(8,128)S(1)}, u32[]{:S(2)}, u32[]{:S(2)}) collective-permute-start(f32[16,1024]{1,0:T(8,128)} %bitcast.5), channel_id=1, source_target_pairs={{0,1},{1,0},{2,3},{3,2},{4,5},{5,4},{6,7},{7,6},{8,9},{9,8},{10,11... | collective-permute-start | bytes 196616 | tf_op jit(solution)/shard_map/ppermute | solution.py:38
  12.6 7.0 %copy-start.3 = (f32[1024,16]{0,1:T(8,128)S(1)}, f32[1024,16]{0,1:T(8,128)}, u32[]{:S(2)}) copy-start(f32[1024,16]{0,1:T(8,128)} %param.10) | copy-start | bytes 196612
  17.9 80.2 %collective-permute-start.7 = (bf16[256,1536]{1,0:T(8,128)(2,1)S(1)}, bf16[256,1536]{1,0:T(8,128)(2,1)S(1)}, u32[]{:S(2)}, u32[]{:S(2)}) collective-permute-start(bf16[256,1536]{1,0:T(8,128)(2,1)S(1)} %shard_map.65.refs_1_.near), channel_id=1, source_target_pairs={{0,16},{4,20},{8,24},{12,28},{1,17},{5,21},{9,25},{13,29},{2,18},{... | collective-permute-start | bytes 2359304 | tf_op jit(solution)/shard_map/ppermute | solution.py:24
  26.2 84.4 %collective-permute-start.18 = (bf16[256,1536]{1,0:T(8,128)(2,1)S(1)}, bf16[256,1536]{1,0:T(8,128)(2,1)S(1)}, u32[]{:S(2)}, u32[]{:S(2)}) collective-permute-start(bf16[256,1536]{1,0:T(8,128)(2,1)S(1)} %shard_map.75), channel_id=1, source_target_pairs={{0,16},{4,20},{8,24},{12,28},{1,17},{5,21},{9,25},{13,29},{2,18},{... | collective-permute-start | bytes 2359304 | tf_op jit(solution)/shard_map/ppermute | solution.py:24
  27.5 62.2 %collective-permute-start.3 = (bf16[256,1024]{1,0:T(8,128)(2,1)S(1)}, bf16[256,1024]{1,0:T(8,128)(2,1)S(1)}, u32[]{:S(2)}, u32[]{:S(2)}) collective-permute-start(bf16[256,1024]{1,0:T(8,128)(2,1)S(1)} %shard_map.64.refs_0_), channel_id=1, source_target_pairs={{0,16},{4,20},{8,24},{12,28},{1,17},{5,21},{9,25},{13,29},{2,18},{... | collective-permute-start | bytes 1572872 | tf_op jit(solution)/shard_map/ppermute | solution.py:24
  28.8 4.6 %collective-permute-start.8 = (f32[16,1024]{1,0:T(8,128)S(1)}, f32[16,1024]{1,0:T(8,128)S(1)}, u32[]{:S(2)}, u32[]{:S(2)}) collective-permute-start(f32[16,1024]{1,0:T(8,128)S(1)} %get-tuple-element.28), channel_id=1, source_target_pairs={{0,1},{1,0},{2,3},{3,2},{4,5},{5,4},{6,7},{7,6},{8,9},{9,8},{10,11... | collective-permute-start | bytes 196616 | tf_op jit(solution)/shard_map/ppermute | solution.py:38
  28.9 7.0 %collective-permute-start.9 = (f32[16,1024]{1,0:T(8,128)S(1)}, f32[16,1024]{1,0:T(8,128)S(1)}, u32[]{:S(2)}, u32[]{:S(2)}) collective-permute-start(f32[16,1024]{1,0:T(8,128)S(1)} %get-tuple-element.29), channel_id=1, source_target_pairs={{0,2},{1,3},{2,0},{3,1},{4,6},{5,7},{6,4},{7,5},{8,10},{9,11},{10,... | collective-permute-start | bytes 196616 | tf_op jit(solution)/shard_map/ppermute | solution.py:38
  33.4 6.1 %collective-permute-start.10 = (f32[16,1024]{1,0:T(8,128)S(1)}, f32[16,1024]{1,0:T(8,128)S(1)}, u32[]{:S(2)}, u32[]{:S(2)}) collective-permute-start(f32[16,1024]{1,0:T(8,128)S(1)} %get-tuple-element.30), channel_id=1, source_target_pairs={{0,3},{1,2},{2,1},{3,0},{4,7},{5,6},{6,5},{7,4},{8,11},{9,10},{10,... | collective-permute-start | bytes 196616 | tf_op jit(solution)/shard_map/ppermute | solution.py:38
  39.5 47.0 %collective-permute-start.11 = (f32[4,16,1024]{2,1,0:T(8,128)S(1)}, f32[4,16,1024]{2,1,0:T(8,128)S(1)}, u32[]{:S(2)}, u32[]{:S(2)}) collective-permute-start(f32[4,16,1024]{2,1,0:T(8,128)S(1)} %get-tuple-element.32), channel_id=1, source_target_pairs={{0,16},{4,20},{8,24},{12,28},{1,17},{5,21},{9,25},{13,29},{2,18},{... | collective-permute-start | bytes 786440 | tf_op jit(solution)/shard_map/ppermute | solution.py:24
  40.8 32.2 %collective-permute-start.14 = (f32[16,1024]{1,0:T(8,128)S(1)}, f32[16,1024]{1,0:T(8,128)S(1)}, u32[]{:S(2)}, u32[]{:S(2)}) collective-permute-start(f32[16,1024]{1,0:T(8,128)S(1)} %get-tuple-element.33), channel_id=1, source_target_pairs={{0,12},{4,16},{8,20},{12,24},{16,28},{1,13},{5,17},{9,21},{13,25},... | collective-permute-start | bytes 196616 | tf_op jit(solution)/shard_map/ppermute | solution.py:24
  73.0 7.0 %collective-permute-start.13 = (f32[16,1024]{1,0:T(8,128)S(1)}, f32[16,1024]{1,0:T(8,128)S(1)}, u32[]{:S(2)}, u32[]{:S(2)}) collective-permute-start(f32[16,1024]{1,0:T(8,128)S(1)} %get-tuple-element.33), channel_id=1, source_target_pairs={{0,8},{4,12},{8,16},{12,20},{16,24},{20,28},{1,9},{5,13},{9,17},{1... | collective-permute-start | bytes 196616 | tf_op jit(solution)/shard_map/ppermute | solution.py:24
  80.0 6.5 %collective-permute-start.12 = (f32[16,1024]{1,0:T(8,128)S(1)}, f32[16,1024]{1,0:T(8,128)S(1)}, u32[]{:S(2)}, u32[]{:S(2)}) collective-permute-start(f32[16,1024]{1,0:T(8,128)S(1)} %get-tuple-element.33), channel_id=1, source_target_pairs={{0,4},{4,8},{8,12},{12,16},{16,20},{20,24},{24,28},{1,5},{5,9},{9,... | collective-permute-start | bytes 196616 | tf_op jit(solution)/shard_map/ppermute | solution.py:24
  86.6 16.1 %collective-permute-start.15 = (f32[16,1024]{1,0:T(8,128)S(1)}, f32[16,1024]{1,0:T(8,128)S(1)}, u32[]{:S(2)}, u32[]{:S(2)}) collective-permute-start(f32[16,1024]{1,0:T(8,128)S(1)} %get-tuple-element.35), channel_id=1, source_target_pairs={{0,1},{1,0},{2,3},{3,2},{4,5},{5,4},{6,7},{7,6},{8,9},{9,8},{10,11... | collective-permute-start | bytes 196616 | tf_op jit(solution)/shard_map/ppermute | solution.py:38
  86.7 16.1 %collective-permute-start.16 = (f32[16,1024]{1,0:T(8,128)S(1)}, f32[16,1024]{1,0:T(8,128)S(1)}, u32[]{:S(2)}, u32[]{:S(2)}) collective-permute-start(f32[16,1024]{1,0:T(8,128)S(1)} %get-tuple-element.36), channel_id=1, source_target_pairs={{0,2},{1,3},{2,0},{3,1},{4,6},{5,7},{6,4},{7,5},{8,10},{9,11},{10,... | collective-permute-start | bytes 196616 | tf_op jit(solution)/shard_map/ppermute | solution.py:38
  89.6 13.1 %collective-permute-start.17 = (f32[16,1024]{1,0:T(8,128)S(1)}, f32[16,1024]{1,0:T(8,128)S(1)}, u32[]{:S(2)}, u32[]{:S(2)}) collective-permute-start(f32[16,1024]{1,0:T(8,128)S(1)} %get-tuple-element.37), channel_id=1, source_target_pairs={{0,3},{1,2},{2,1},{3,0},{4,7},{5,6},{6,5},{7,4},{8,11},{9,10},{10,... | collective-permute-start | bytes 196616 | tf_op jit(solution)/shard_map/ppermute | solution.py:38
  95.0 7.8 %copy-start.2 = (bf16[256,4096]{1,0:T(8,128)(2,1)S(1)}, bf16[256,4096]{1,0:T(8,128)(2,1)}, u32[]{:S(2)}) copy-start(bf16[256,4096]{1,0:T(8,128)(2,1)} %value.1) | copy-start | bytes 6291460

commit v11 on v10

--- a/solution.py
+++ b/solution.py
@@ -1,5 +1,4 @@
 import functools
-import math
 
 import jax
 import jax.numpy as jnp
@@ -12,8 +11,8 @@
 FILTER_PARTS = 4
 LANES = 128
 SEGMENTS = 8
-RAW_SHARES = (4, 6)
-DONE_SHARES = (6,)
+RAW_SHARES = (8, 11)
+DONE_SHARES = (13,)
 RUN = 8
 VMEM_BYTES = 16 << 20
 F32 = jnp.float32
@@ -64,6 +63,11 @@
 
 def step_rows(i):
     return pl.ds(i * SEGMENTS, SEGMENTS)
+
+
+def pieces(width):
+    wide = 4 * LANES
+    return [(at, min(wide, width - at)) for at in range(0, width, wide)]
 
 
 def lanes(start):
@@ -176,8 +180,7 @@
     start = first
     for out in outs:
         width = out.shape[1]
-        wide = math.gcd(width, 4 * LANES)
-        for at in range(0, width, wide):
+        for at, wide in pieces(width):
             cols = pl.ds(start + at, wide)
             product = (query[:, cols].astype(F32) * key_in[:, cols].astype(F32)).astype(jnp.bfloat16)
             out[:, pl.ds(at, wide)] = jnp.dot(
@@ -435,8 +438,7 @@
             over_tiles(soon * LANES, body_near)
         if copies[slot] is not None:
             copies[slot].wait()
-        wide = math.gcd(width, 4 * LANES)
-        for at in range(0, width, wide):
+        for at, wide in pieces(width):
             cols = pl.ds(at, wide)
             done[slot, :, cols] = gated(back, mixed[:, cols], value[:, pl.ds(first * LANES + at, wide)])
         copies[slot] = pltpu.make_async_copy(
@@ -464,9 +466,8 @@
     _, width = rest.shape
     first = value.shape[1] - width
     fill_order(back, True)
-    wide = math.gcd(width, 4 * LANES)
     copies = []
-    for k, at in enumerate(range(0, width, wide)):
+    for k, (at, wide) in enumerate(pieces(width)):
         cols = pl.ds(at, wide)
         mixed = (rest[:, cols] - over[:, cols].astype(F32)).astype(jnp.bfloat16)
         done[:, cols] = gated(back, mixed, value[:, pl.ds(first + at, wide)])
@@ -639,7 +640,7 @@
     return call(
         last_kernel,
         shape(length, channels, bf16),
-        [order_scr, pltpu.VMEM((length, widths[-1]), bf16), pltpu.SemaphoreType.DMA((8,))],
+        [order_scr, pltpu.VMEM((length, widths[-1]), bf16), pltpu.SemaphoreType.DMA((len(pieces(widths[-1])),))],
         (rest, overs[-1], value, partial),
         in_specs=[vmem, vmem, vmem, anywhere],
         out_specs=anywhere,

time: 112 us -> 111 us (level)
  local copies, waits for them, and re-layouts: 0.1 us -> 3.27 us
  waiting for transfers between devices: 49.4 us -> 46.9 us
  starting transfers between devices: 31.3 us -> 29.9 us
    ppermute x7, waiting for transfers between devices: 39.2 us -> 35 us  [from_behind(): lax.ppermute(value, axis, [(source, source + steps) for source in range(c...]
    unnamed x8, local copies, waits for them, and re-layouts: 0.02 us -> 3.19 us
    ppermute x12, waiting for transfers between devices: 10.2 us -> 11.9 us  [ring(): moved.append(lax.ppermute(part, axis, pairs) if k else part)]
    ppermute x12, starting transfers between devices: 19.7 us -> 18.5 us  [ring(): moved.append(lax.ppermute(part, axis, pairs) if k else part)]
  transfers between devices with their start and end apart: 19 -> 19, of which waited for: 7 -> 7; matrix products, arithmetic and copies ran while one was open for 1% -> 1% of each run, Pallas kernels for 26% -> 25%
where the time goes in v11:
time: 111 us; the launch traced here: 110 us
  waiting for transfers between devices  46.9 us (42%)
  starting transfers between devices  29.9 us (27%)
  Pallas kernels  29.1 us (26%)
  local copies, waits for them, and re-layouts  3.27 us (3%)
    ppermute x7, waiting for transfers between devices, from_behind(): lax.ppermute(value, axis, [(source, source + steps) for source in range(c...  35 us
    pallas_call x13, Pallas kernels, call(): pl.pallas_call(kernel, out_shape=out_shape, scratch_shapes=scratch, compi...  29.1 us
    ppermute x12, starting transfers between devices, ring(): moved.append(lax.ppermute(part, axis, pairs) if k else part)  18.5 us
    ppermute x12, waiting for transfers between devices, ring(): moved.append(lax.ppermute(part, axis, pairs) if k else part)  11.9 us
    ppermute x7, starting transfers between devices, from_behind(): lax.ppermute(value, axis, [(source, source + steps) for source in range(c...  11.4 us
    unnamed x8, local copies, waits for them, and re-layouts  3.19 us
  transfers between devices with their start and end apart: 19, of which 7 were waited for; matrix products, arithmetic and copies ran while one was open for 1% of the time, Pallas kernels for 25%

profile of v11, /device:TPU:4, one launch (start us, length us, event | category | flops | bytes accessed | tf_op | source)
XLA Modules:
  0.0 110.2 jit_solution(18282541620914588204)
XLA Ops:
  0.0 1.6 %collective-permute-start = (f32[16,1024]{1,0:T(8,128)}, f32[16,1024]{1,0:T(8,128)S(1)}, u32[]{:S(2)}, u32[]{:S(2)}) collective-permute-start(f32[16,1024]{1,0:T(8,128)} %bitcast.3), channel_id=1, source_target_pairs={{0,1},{1,0},{2,3},{3,2},{4,5},{5,4},{6,7},{7,6},{8,9},{9,8},{10,11... | collective-permute-start | bytes 196616 | tf_op jit(solution)/shard_map/ppermute | solution.py:37
  3.1 2.6 %collective-permute-start.5 = (f32[24,1024]{1,0:T(8,128)S(1)}, f32[24,1024]{1,0:T(8,128)S(1)}, u32[]{:S(2)}, u32[]{:S(2)}) collective-permute-start(f32[24,1024]{1,0:T(8,128)S(1)} %maximum_maximum_fusion.refs_0_), channel_id=1, source_target_pairs={{0,2},{1,3},{2,0},{3,1},{4,6},{5,7},{6,4},{7,5},{8,10},{9,11},{10,... | collective-permute-start | bytes 294920 | tf_op jit(solution)/shard_map/ppermute | solution.py:37
  5.7 1.3 %collective-permute-start.6 = (f32[24,1024]{1,0:T(8,128)S(1)}, f32[24,1024]{1,0:T(8,128)S(1)}, u32[]{:S(2)}, u32[]{:S(2)}) collective-permute-start(f32[24,1024]{1,0:T(8,128)S(1)} %maximum_maximum_fusion.refs_0_), channel_id=1, source_target_pairs={{0,3},{1,2},{2,1},{3,0},{4,7},{5,6},{6,5},{7,4},{8,11},{9,10},{10,... | collective-permute-start | bytes 294920 | tf_op jit(solution)/shard_map/ppermute | solution.py:37
  7.0 1.7 %collective-permute-start.1 = (f32[16,1024]{1,0:T(8,128)}, f32[16,1024]{1,0:T(8,128)S(1)}, u32[]{:S(2)}, u32[]{:S(2)}) collective-permute-start(f32[16,1024]{1,0:T(8,128)} %bitcast.4), channel_id=1, source_target_pairs={{0,2},{1,3},{2,0},{3,1},{4,6},{5,7},{6,4},{7,5},{8,10},{9,11},{10,... | collective-permute-start | bytes 196616 | tf_op jit(solution)/shard_map/ppermute | solution.py:37
  9.6 1.6 %copy-done = bf16[256,4096]{1,0:T(8,128)(2,1)S(1)} copy-done((bf16[256,4096]{1,0:T(8,128)(2,1)S(1)}, bf16[256,4096]{1,0:T(8,128)(2,1)}, u32[]{:S(2)}) %copy-start) | copy-done | bytes 2097176
  11.2 1.6 %copy-done.1 = bf16[256,4096]{1,0:T(8,128)(2,1)S(1)} copy-done((bf16[256,4096]{1,0:T(8,128)(2,1)S(1)}, bf16[256,4096]{1,0:T(8,128)(2,1)}, u32[]{:S(2)}) %copy-start.1) | copy-done | bytes 2097176
  13.7 1.6 %shard_map.64.refs_0_ = bf16[256,1024]{1,0:T(8,128)(2,1)S(1)} custom-call(bf16[256,4096]{1,0:T(8,128)(2,1)} %query.5, bf16[256,4096]{1,0:T(8,128)(2,1)} %key_in.5), custom_call_target="tpu_custom_call" | custom-call | tf_op jit(solution)/shard_map/pallas_call | solution.py:519
  15.4 4.4 %collective-permute-done.1.refs_5_ = f32[16,1024]{1,0:T(8,128)S(1)} collective-permute-done((f32[16,1024]{1,0:T(8,128)}, f32[16,1024]{1,0:T(8,128)S(1)}, u32[]{:S(2)}, u32[]{:S(2)}) %collective-permute-start.1) | collective-permute-done | bytes 65568 | tf_op jit(solution)/shard_map/ppermute | solution.py:37
  19.8 6.3 %shard_map.67 = (f32[512,1024]{1,0:T(8,128)S(1)}, f32[512,1408]{1,0:T(8,128)S(1)}, f32[512,1664]{1,0:T(8,128)S(1)}, f32[16,1024]{1,0:T(8,128)S(1)}, f32[16,1024]...) custom-call(bf16[256,1024]{1,0:T(8,128)(2,1)S(1)} %shard_map.64.refs_0_, ...), custom_call_target="tpu_custom_call" | custom-call | tf_op jit(solution)/shard_map/pallas_call | solution.py:519
  26.2 1.3 %collective-permute-start.18 = (bf16[256,1664]{1,0:T(8,128)(2,1)S(1)}, bf16[256,1664]{1,0:T(8,128)(2,1)S(1)}, u32[]{:S(2)}, u32[]{:S(2)}) collective-permute-start(bf16[256,1664]{1,0:T(8,128)(2,1)S(1)} %shard_map.75), channel_id=1, source_target_pairs={{0,16},{4,20},{8,24},{12,28},{1,17},{5,21},{9,25},{13,29},{2,18},{... | collective-permute-start | bytes 2555912 | tf_op jit(solution)/shard_map/ppermute | solution.py:23
  27.5 1.3 %collective-permute-start.7 = (bf16[256,1408]{1,0:T(8,128)(2,1)S(1)}, bf16[256,1408]{1,0:T(8,128)(2,1)S(1)}, u32[]{:S(2)}, u32[]{:S(2)}) collective-permute-start(bf16[256,1408]{1,0:T(8,128)(2,1)S(1)} %shard_map.65.refs_1_.near), channel_id=1, source_target_pairs={{0,16},{4,20},{8,24},{12,28},{1,17},{5,21},{9,25},{13,29},{2,18},{... | collective-permute-start | bytes 2162696 | tf_op jit(solution)/shard_map/ppermute | solution.py:23
  28.8 1.3 %collective-permute-start.3 = (bf16[256,1024]{1,0:T(8,128)(2,1)S(1)}, bf16[256,1024]{1,0:T(8,128)(2,1)S(1)}, u32[]{:S(2)}, u32[]{:S(2)}) collective-permute-start(bf16[256,1024]{1,0:T(8,128)(2,1)S(1)} %shard_map.64.refs_0_), channel_id=1, source_target_pairs={{0,16},{4,20},{8,24},{12,28},{1,17},{5,21},{9,25},{13,29},{2,18},{... | collective-permute-start | bytes 1572872 | tf_op jit(solution)/shard_map/ppermute | solution.py:23
  30.1 2.9 %collective-permute-start.10 = (f32[16,1024]{1,0:T(8,128)S(1)}, f32[16,1024]{1,0:T(8,128)S(1)}, u32[]{:S(2)}, u32[]{:S(2)}) collective-permute-start(f32[16,1024]{1,0:T(8,128)S(1)} %get-tuple-element.30), channel_id=1, source_target_pairs={{0,3},{1,2},{2,1},{3,0},{4,7},{5,6},{6,5},{7,4},{8,11},{9,10},{10,... | collective-permute-start | bytes 196616 | tf_op jit(solution)/shard_map/ppermute | solution.py:37
  33.5 2.7 %collective-permute-done.10.refs_3_ = f32[16,1024]{1,0:T(8,128)S(1)} collective-permute-done((f32[16,1024]{1,0:T(8,128)S(1)}, f32[16,1024]{1,0:T(8,128)S(1)}, u32[]{:S(2)}, u32[]{:S(2)}) %collective-permute-start.10) | collective-permute-done | bytes 65568 | tf_op jit(solution)/shard_map/ppermute | solution.py:37
  36.2 1.0 collective-permute-start.9
  37.2 4.7 %collective-permute-done.9.refs_2_ = f32[16,1024]{1,0:T(8,128)S(1)} collective-permute-done((f32[16,1024]{1,0:T(8,128)S(1)}, f32[16,1024]{1,0:T(8,128)S(1)}, u32[]{:S(2)}, u32[]{:S(2)}) %collective-permute-start.9) | collective-permute-done | bytes 65568 | tf_op jit(solution)/shard_map/ppermute | solution.py:37
  42.0 1.3 %collective-permute-start.11 = (f32[4,16,1024]{2,1,0:T(8,128)S(1)}, f32[4,16,1024]{2,1,0:T(8,128)S(1)}, u32[]{:S(2)}, u32[]{:S(2)}) collective-permute-start(f32[4,16,1024]{2,1,0:T(8,128)S(1)} %get-tuple-element.32), channel_id=1, source_target_pairs={{0,16},{4,20},{8,24},{12,28},{1,17},{5,21},{9,25},{13,29},{2,18},{... | collective-permute-start | bytes 786440 | tf_op jit(solution)/shard_map/ppermute | solution.py:23
  43.3 1.9 %collective-permute-start.12 = (f32[16,1024]{1,0:T(8,128)S(1)}, f32[16,1024]{1,0:T(8,128)S(1)}, u32[]{:S(2)}, u32[]{:S(2)}) collective-permute-start(f32[16,1024]{1,0:T(8,128)S(1)} %get-tuple-element.33), channel_id=1, source_target_pairs={{0,4},{4,8},{8,12},{12,16},{16,20},{20,24},{24,28},{1,5},{5,9},{9,... | collective-permute-start | bytes 196616 | tf_op jit(solution)/shard_map/ppermute | solution.py:23
  45.2 4.7 %collective-permute-done.12.refs_3_ = f32[16,1024]{1,0:T(8,128)S(1)} collective-permute-done((f32[16,1024]{1,0:T(8,128)S(1)}, f32[16,1024]{1,0:T(8,128)S(1)}, u32[]{:S(2)}, u32[]{:S(2)}) %collective-permute-start.12) | collective-permute-done | bytes 65568 | tf_op jit(solution)/shard_map/ppermute | solution.py:23
  49.9 2.4 %collective-permute-start.13 = (f32[16,1024]{1,0:T(8,128)S(1)}, f32[16,1024]{1,0:T(8,128)S(1)}, u32[]{:S(2)}, u32[]{:S(2)}) collective-permute-start(f32[16,1024]{1,0:T(8,128)S(1)} %get-tuple-element.33), channel_id=1, source_target_pairs={{0,8},{4,12},{8,16},{12,20},{16,24},{20,28},{1,9},{5,13},{9,17},{1... | collective-permute-start | bytes 196616 | tf_op jit(solution)/shard_map/ppermute | solution.py:23
  52.3 5.5 %collective-permute-done.13.refs_4_ = f32[16,1024]{1,0:T(8,128)S(1)} collective-permute-done((f32[16,1024]{1,0:T(8,128)S(1)}, f32[16,1024]{1,0:T(8,128)S(1)}, u32[]{:S(2)}, u32[]{:S(2)}) %collective-permute-start.13) | collective-permute-done | bytes 65568 | tf_op jit(solution)/shard_map/ppermute | solution.py:23
  57.8 1.9 %collective-permute-start.14 = (f32[16,1024]{1,0:T(8,128)S(1)}, f32[16,1024]{1,0:T(8,128)S(1)}, u32[]{:S(2)}, u32[]{:S(2)}) collective-permute-start(f32[16,1024]{1,0:T(8,128)S(1)} %get-tuple-element.33), channel_id=1, source_target_pairs={{0,12},{4,16},{8,20},{12,24},{16,28},{1,13},{5,17},{9,21},{13,25},... | collective-permute-start | bytes 196616 | tf_op jit(solution)/shard_map/ppermute | solution.py:23
  59.7 23.7 %collective-permute-done.14.refs_5_ = f32[16,1024]{1,0:T(8,128)S(1)} collective-permute-done((f32[16,1024]{1,0:T(8,128)S(1)}, f32[16,1024]{1,0:T(8,128)S(1)}, u32[]{:S(2)}, u32[]{:S(2)}) %collective-permute-start.14) | collective-permute-done | bytes 65568 | tf_op jit(solution)/shard_map/ppermute | solution.py:23
  83.4 1.1 collective-permute-done.11.refs_2_
  84.6 2.2 %collective-permute-start.15 = (f32[16,1024]{1,0:T(8,128)S(1)}, f32[16,1024]{1,0:T(8,128)S(1)}, u32[]{:S(2)}, u32[]{:S(2)}) collective-permute-start(f32[16,1024]{1,0:T(8,128)S(1)} %get-tuple-element.35), channel_id=1, source_target_pairs={{0,1},{1,0},{2,3},{3,2},{4,5},{5,4},{6,7},{7,6},{8,9},{9,8},{10,11... | collective-permute-start | bytes 196616 | tf_op jit(solution)/shard_map/ppermute | solution.py:37
  86.9 1.9 %collective-permute-start.16 = (f32[16,1024]{1,0:T(8,128)S(1)}, f32[16,1024]{1,0:T(8,128)S(1)}, u32[]{:S(2)}, u32[]{:S(2)}) collective-permute-start(f32[16,1024]{1,0:T(8,128)S(1)} %get-tuple-element.36), channel_id=1, source_target_pairs={{0,2},{1,3},{2,0},{3,1},{4,6},{5,7},{6,4},{7,5},{8,10},{9,11},{10,... | collective-permute-start | bytes 196616 | tf_op jit(solution)/shard_map/ppermute | solution.py:37
  88.7 1.4 %collective-permute-start.17 = (f32[16,1024]{1,0:T(8,128)S(1)}, f32[16,1024]{1,0:T(8,128)S(1)}, u32[]{:S(2)}, u32[]{:S(2)}) collective-permute-start(f32[16,1024]{1,0:T(8,128)S(1)} %get-tuple-element.37), channel_id=1, source_target_pairs={{0,3},{1,2},{2,1},{3,0},{4,7},{5,6},{6,5},{7,4},{8,11},{9,10},{10,... | collective-permute-start | bytes 196616 | tf_op jit(solution)/shard_map/ppermute | solution.py:37
  90.1 3.7 %shard_map.73 = (f32[256,384]{1,0:T(8,128)S(1)}, f32[256,1664]{1,0:T(8,128)S(1)}) custom-call(bf16[256,1408]{1,0:T(8,128)(2,1)S(1)} %shard_map.65.refs_1_.near, bf16[256,1664]{1,0:T(8,128)(2,1)S(1)} %shard_map.66.refs_2_.product, f32[4,16,1024]{2,1,0:T(8,128)S(1)} %get-tuple-element.26.rates.refs_10_, f32[4,24,1024]{2,1,0:T(8,128)S(1)} %shard_map.68.weighing.refs_11_, ...), custom_call_target="tpu_custom_call" | custom-call | tf_op jit(solution)/shard_map/pallas_call | solution.py:519
  93.9 3.1 %shard_map.69.refs_4_ = f32[256,1024]{1,0:T(8,128)S(1)} custom-call(bf16[256,1024]{1,0:T(8,128)(2,1)S(1)} %collective-permute-done.3.past, f32[4,16,1024]{2,1,0:T(8,128)S(1)} %get-tuple-element.26.rates.refs_10_, f32[4,24,1024]{2,1,0:T(8,128)S(1)} %shard_map.68.weighing.refs_11_), custom_call_target="tpu_custom_call" | custom-call | tf_op jit(solution)/shard_map/pallas_call | solution.py:519
  97.0 4.2 %shard_map.70.refs_5_ = f32[256,1408]{1,0:T(8,128)S(1)} custom-call(bf16[256,1408]{1,0:T(8,128)(2,1)S(1)} %collective-permute-done.7.past, f32[4,16,1024]{2,1,0:T(8,128)S(1)} %get-tuple-element.26.rates.refs_10_, f32[4,24,1024]{2,1,0:T(8,128)S(1)} %shard_map.68.weighing.refs_11_), custom_call_target="tpu_custom_call" | custom-call | tf_op jit(solution)/shard_map/pallas_call | solution.py:519
  101.3 7.7 %shard_map.74 = (bf16[256,4096]{1,0:T(8,128)(2,1)}, f32[256,1664]{1,0:T(8,128)S(1)}) custom-call(bf16[256,1024]{1,0:T(8,128)(2,1)S(1)} %shard_map.64.refs_0_, bf16[256,1408]{1,0:T(8,128)(2,1)S(1)} %shard_map.65.refs_1_.near, f32[512,1024]{1,0:T(8,128)S(1)} %get-tuple-element.24.refs_2_, f32[512,1408]{1,0:T(8,128)S(1)} %get-tuple-element.25.near_carry.refs_3_, ...), custom_call_target="tpu_custom_call" | custom-call | tf_op jit(solution)/shard_map/pallas_call | solution.py:519
  109.0 1.2 %shard_map.76 = bf16[256,4096]{1,0:T(8,128)(2,1)} custom-call(f32[256,1664]{1,0:T(8,128)S(1)} %get-tuple-element.41.rest, bf16[256,1664]{1,0:T(8,128)(2,1)S(1)} %collective-permute-done.18.over, bf16[256,4096]{1,0:T(8,128)(2,1)S(1)} %copy-done.2, bf16[256,4096]{1,0:T(8,128)(2,1)} %get-tuple-element.42.partial), custom_call_target="tpu_custom_call", output_to_operand_aliasing={{}: (3, {})} | custom-call | tf_op jit(solution)/shard_map/pallas_call | solution.py:519
  (30 shorter events, 4.2 us)
Async XLA Ops:
  0.0 8.7 %collective-permute-start = (f32[16,1024]{1,0:T(8,128)}, f32[16,1024]{1,0:T(8,128)S(1)}, u32[]{:S(2)}, u32[]{:S(2)}) collective-permute-start(f32[16,1024]{1,0:T(8,128)} %bitcast.3), channel_id=1, source_target_pairs={{0,1},{1,0},{2,3},{3,2},{4,5},{5,4},{6,7},{7,6},{8,9},{9,8},{10,11... | collective-permute-start | bytes 196616 | tf_op jit(solution)/shard_map/ppermute | solution.py:37
  2.6 23.5 %collective-permute-start.4 = (f32[24,1024]{1,0:T(8,128)S(1)}, f32[24,1024]{1,0:T(8,128)S(1)}, u32[]{:S(2)}, u32[]{:S(2)}) collective-permute-start(f32[24,1024]{1,0:T(8,128)S(1)} %maximum_maximum_fusion.refs_0_), channel_id=1, source_target_pairs={{0,1},{1,0},{2,3},{3,2},{4,5},{5,4},{6,7},{7,6},{8,9},{9,8},{10,11... | collective-permute-start | bytes 294920 | tf_op jit(solution)/shard_map/ppermute | solution.py:37
  3.1 23.0 %collective-permute-start.5 = (f32[24,1024]{1,0:T(8,128)S(1)}, f32[24,1024]{1,0:T(8,128)S(1)}, u32[]{:S(2)}, u32[]{:S(2)}) collective-permute-start(f32[24,1024]{1,0:T(8,128)S(1)} %maximum_maximum_fusion.refs_0_), channel_id=1, source_target_pairs={{0,2},{1,3},{2,0},{3,1},{4,6},{5,7},{6,4},{7,5},{8,10},{9,11},{10,... | collective-permute-start | bytes 294920 | tf_op jit(solution)/shard_map/ppermute | solution.py:37
  5.7 20.4 %collective-permute-start.6 = (f32[24,1024]{1,0:T(8,128)S(1)}, f32[24,1024]{1,0:T(8,128)S(1)}, u32[]{:S(2)}, u32[]{:S(2)}) collective-permute-start(f32[24,1024]{1,0:T(8,128)S(1)} %maximum_maximum_fusion.refs_0_), channel_id=1, source_target_pairs={{0,3},{1,2},{2,1},{3,0},{4,7},{5,6},{6,5},{7,4},{8,11},{9,10},{10,... | collective-permute-start | bytes 294920 | tf_op jit(solution)/shard_map/ppermute | solution.py:37
  7.0 12.7 %collective-permute-start.1 = (f32[16,1024]{1,0:T(8,128)}, f32[16,1024]{1,0:T(8,128)S(1)}, u32[]{:S(2)}, u32[]{:S(2)}) collective-permute-start(f32[16,1024]{1,0:T(8,128)} %bitcast.4), channel_id=1, source_target_pairs={{0,2},{1,3},{2,0},{3,1},{4,6},{5,7},{6,4},{7,5},{8,10},{9,11},{10,... | collective-permute-start | bytes 196616 | tf_op jit(solution)/shard_map/ppermute | solution.py:37
  8.7 11.1 %collective-permute-start.2 = (f32[16,1024]{1,0:T(8,128)}, f32[16,1024]{1,0:T(8,128)S(1)}, u32[]{:S(2)}, u32[]{:S(2)}) collective-permute-start(f32[16,1024]{1,0:T(8,128)} %bitcast.5), channel_id=1, source_target_pairs={{0,3},{1,2},{2,1},{3,0},{4,7},{5,6},{6,5},{7,4},{8,11},{9,10},{10,... | collective-permute-start | bytes 196616 | tf_op jit(solution)/shard_map/ppermute | solution.py:37
  9.6 1.6 %copy-start = (bf16[256,4096]{1,0:T(8,128)(2,1)S(1)}, bf16[256,4096]{1,0:T(8,128)(2,1)}, u32[]{:S(2)}) copy-start(bf16[256,4096]{1,0:T(8,128)(2,1)} %query.5) | copy-start | bytes 6291460
  11.2 1.6 %copy-start.1 = (bf16[256,4096]{1,0:T(8,128)(2,1)S(1)}, bf16[256,4096]{1,0:T(8,128)(2,1)}, u32[]{:S(2)}) copy-start(bf16[256,4096]{1,0:T(8,128)(2,1)} %key_in.5) | copy-start | bytes 6291460
  13.7 6.0 %copy-start.3 = (f32[1024,16]{0,1:T(8,128)S(1)}, f32[1024,16]{0,1:T(8,128)}, u32[]{:S(2)}) copy-start(f32[1024,16]{0,1:T(8,128)} %param.10) | copy-start | bytes 196612
  26.2 82.8 %collective-permute-start.18 = (bf16[256,1664]{1,0:T(8,128)(2,1)S(1)}, bf16[256,1664]{1,0:T(8,128)(2,1)S(1)}, u32[]{:S(2)}, u32[]{:S(2)}) collective-permute-start(bf16[256,1664]{1,0:T(8,128)(2,1)S(1)} %shard_map.75), channel_id=1, source_target_pairs={{0,16},{4,20},{8,24},{12,28},{1,17},{5,21},{9,25},{13,29},{2,18},{... | collective-permute-start | bytes 2555912 | tf_op jit(solution)/shard_map/ppermute | solution.py:23
  27.5 69.5 %collective-permute-start.7 = (bf16[256,1408]{1,0:T(8,128)(2,1)S(1)}, bf16[256,1408]{1,0:T(8,128)(2,1)S(1)}, u32[]{:S(2)}, u32[]{:S(2)}) collective-permute-start(bf16[256,1408]{1,0:T(8,128)(2,1)S(1)} %shard_map.65.refs_1_.near), channel_id=1, source_target_pairs={{0,16},{4,20},{8,24},{12,28},{1,17},{5,21},{9,25},{13,29},{2,18},{... | collective-permute-start | bytes 2162696 | tf_op jit(solution)/shard_map/ppermute | solution.py:23
  28.8 60.0 %collective-permute-start.3 = (bf16[256,1024]{1,0:T(8,128)(2,1)S(1)}, bf16[256,1024]{1,0:T(8,128)(2,1)S(1)}, u32[]{:S(2)}, u32[]{:S(2)}) collective-permute-start(bf16[256,1024]{1,0:T(8,128)(2,1)S(1)} %shard_map.64.refs_0_), channel_id=1, source_target_pairs={{0,16},{4,20},{8,24},{12,28},{1,17},{5,21},{9,25},{13,29},{2,18},{... | collective-permute-start | bytes 1572872 | tf_op jit(solution)/shard_map/ppermute | solution.py:23
  30.1 6.1 %collective-permute-start.10 = (f32[16,1024]{1,0:T(8,128)S(1)}, f32[16,1024]{1,0:T(8,128)S(1)}, u32[]{:S(2)}, u32[]{:S(2)}) collective-permute-start(f32[16,1024]{1,0:T(8,128)S(1)} %get-tuple-element.30), channel_id=1, source_target_pairs={{0,3},{1,2},{2,1},{3,0},{4,7},{5,6},{6,5},{7,4},{8,11},{9,10},{10,... | collective-permute-start | bytes 196616 | tf_op jit(solution)/shard_map/ppermute | solution.py:37
  32.9 4.3 %collective-permute-start.8 = (f32[16,1024]{1,0:T(8,128)S(1)}, f32[16,1024]{1,0:T(8,128)S(1)}, u32[]{:S(2)}, u32[]{:S(2)}) collective-permute-start(f32[16,1024]{1,0:T(8,128)S(1)} %get-tuple-element.28), channel_id=1, source_target_pairs={{0,1},{1,0},{2,3},{3,2},{4,5},{5,4},{6,7},{7,6},{8,9},{9,8},{10,11... | collective-permute-start | bytes 196616 | tf_op jit(solution)/shard_map/ppermute | solution.py:37
  36.2 5.7 %collective-permute-start.9 = (f32[16,1024]{1,0:T(8,128)S(1)}, f32[16,1024]{1,0:T(8,128)S(1)}, u32[]{:S(2)}, u32[]{:S(2)}) collective-permute-start(f32[16,1024]{1,0:T(8,128)S(1)} %get-tuple-element.29), channel_id=1, source_target_pairs={{0,2},{1,3},{2,0},{3,1},{4,6},{5,7},{6,4},{7,5},{8,10},{9,11},{10,... | collective-permute-start | bytes 196616 | tf_op jit(solution)/shard_map/ppermute | solution.py:37
  42.0 42.5 %collective-permute-start.11 = (f32[4,16,1024]{2,1,0:T(8,128)S(1)}, f32[4,16,1024]{2,1,0:T(8,128)S(1)}, u32[]{:S(2)}, u32[]{:S(2)}) collective-permute-start(f32[4,16,1024]{2,1,0:T(8,128)S(1)} %get-tuple-element.32), channel_id=1, source_target_pairs={{0,16},{4,20},{8,24},{12,28},{1,17},{5,21},{9,25},{13,29},{2,18},{... | collective-permute-start | bytes 786440 | tf_op jit(solution)/shard_map/ppermute | solution.py:23
  43.3 6.6 %collective-permute-start.12 = (f32[16,1024]{1,0:T(8,128)S(1)}, f32[16,1024]{1,0:T(8,128)S(1)}, u32[]{:S(2)}, u32[]{:S(2)}) collective-permute-start(f32[16,1024]{1,0:T(8,128)S(1)} %get-tuple-element.33), channel_id=1, source_target_pairs={{0,4},{4,8},{8,12},{12,16},{16,20},{20,24},{24,28},{1,5},{5,9},{9,... | collective-permute-start | bytes 196616 | tf_op jit(solution)/shard_map/ppermute | solution.py:23
  49.9 7.9 %collective-permute-start.13 = (f32[16,1024]{1,0:T(8,128)S(1)}, f32[16,1024]{1,0:T(8,128)S(1)}, u32[]{:S(2)}, u32[]{:S(2)}) collective-permute-start(f32[16,1024]{1,0:T(8,128)S(1)} %get-tuple-element.33), channel_id=1, source_target_pairs={{0,8},{4,12},{8,16},{12,20},{16,24},{20,28},{1,9},{5,13},{9,17},{1... | collective-permute-start | bytes 196616 | tf_op jit(solution)/shard_map/ppermute | solution.py:23
  57.8 25.6 %collective-permute-start.14 = (f32[16,1024]{1,0:T(8,128)S(1)}, f32[16,1024]{1,0:T(8,128)S(1)}, u32[]{:S(2)}, u32[]{:S(2)}) collective-permute-start(f32[16,1024]{1,0:T(8,128)S(1)} %get-tuple-element.33), channel_id=1, source_target_pairs={{0,12},{4,16},{8,20},{12,24},{16,28},{1,13},{5,17},{9,21},{13,25},... | collective-permute-start | bytes 196616 | tf_op jit(solution)/shard_map/ppermute | solution.py:23
  84.6 16.6 %collective-permute-start.15 = (f32[16,1024]{1,0:T(8,128)S(1)}, f32[16,1024]{1,0:T(8,128)S(1)}, u32[]{:S(2)}, u32[]{:S(2)}) collective-permute-start(f32[16,1024]{1,0:T(8,128)S(1)} %get-tuple-element.35), channel_id=1, source_target_pairs={{0,1},{1,0},{2,3},{3,2},{4,5},{5,4},{6,7},{7,6},{8,9},{9,8},{10,11... | collective-permute-start | bytes 196616 | tf_op jit(solution)/shard_map/ppermute | solution.py:37
  86.9 14.4 %collective-permute-start.16 = (f32[16,1024]{1,0:T(8,128)S(1)}, f32[16,1024]{1,0:T(8,128)S(1)}, u32[]{:S(2)}, u32[]{:S(2)}) collective-permute-start(f32[16,1024]{1,0:T(8,128)S(1)} %get-tuple-element.36), channel_id=1, source_target_pairs={{0,2},{1,3},{2,0},{3,1},{4,6},{5,7},{6,4},{7,5},{8,10},{9,11},{10,... | collective-permute-start | bytes 196616 | tf_op jit(solution)/shard_map/ppermute | solution.py:37
  88.7 12.5 %collective-permute-start.17 = (f32[16,1024]{1,0:T(8,128)S(1)}, f32[16,1024]{1,0:T(8,128)S(1)}, u32[]{:S(2)}, u32[]{:S(2)}) collective-permute-start(f32[16,1024]{1,0:T(8,128)S(1)} %get-tuple-element.37), channel_id=1, source_target_pairs={{0,3},{1,2},{2,1},{3,0},{4,7},{5,6},{6,5},{7,4},{8,11},{9,10},{10,... | collective-permute-start | bytes 196616 | tf_op jit(solution)/shard_map/ppermute | solution.py:37
  93.9 7.4 %copy-start.2 = (bf16[256,4096]{1,0:T(8,128)(2,1)S(1)}, bf16[256,4096]{1,0:T(8,128)(2,1)}, u32[]{:S(2)}) copy-start(bf16[256,4096]{1,0:T(8,128)(2,1)} %value.1) | copy-start | bytes 6291460
